TPU v7x, 32 devices: a whole 2x2x4 slice. The times are simulated.
32 devices in a mesh: fam: 4 (over z), ctx: 8 (over y, x, core).
Axes of the slice: x: 2, y: 2, z: 4, core: 2. Of those that a mesh axis runs over, the one named last changes fastest.
Arguments:
- queries: bfloat16 [4, 4096, 1024], P('fam', 'ctx'), may hold values from -7 to 7
- key_rows: bfloat16 [4, 4096, 1024], P('fam', 'ctx'), may hold values from -4 to 4
- value_rows: bfloat16 [4, 4096, 1024], P('fam', 'ctx'), may hold values from -6 to 6
- cotangent: bfloat16 [4, 4096, 1024], P('fam', 'ctx'), may hold values from -6 to 6
- out_weight: bfloat16 [1024, 1024], replicated, may hold values from -0.1875 to 0.1875
- prot_blocks: int32 [4, 8], P('fam'), may hold values from 1 to 8, 32 in all within a row
- last_fill: int32 [4, 8], P('fam'), may hold values from 1 to 128
- memory_slots: int32 [4, 128], P('fam'), may hold values from 0 to 511
Outputs:
- query_grad: bfloat16 [4, 4096, 1024], P('fam', 'ctx')
- key_grad: bfloat16 [4, 4096, 1024], P('fam', 'ctx')
- value_grad: bfloat16 [4, 4096, 1024], P('fam', 'ctx')
- weight_grad: float32 [1024, 1024], replicated
Inputs may be any that keep to these rules, and one draw needn't show every extreme that they name: `prot_blocks`: each family's protein lengths, in blocks, sum to 32, and the longest has exactly 8 blocks.
All inputs are finite; a program needn't handle non-finite values.
Results may differ from a plain program's by a relative error of at most 0.015.
Values may be sent and summed in bfloat16 or wider, within the bound.
No kernel may reach another device: no remote copies, remote signals or barrier semaphores. Data moves between devices by JAX's collectives and lax.ppermute only.
A program may use at most 128 MiB of HBM per device.

v0:
```python
import functools
import math

import jax
import jax.numpy as jnp
from jax import lax
from jax.experimental import pallas as pl
from jax.experimental.pallas import tpu as pltpu
from jax.sharding import PartitionSpec as P


HEAD_DIM = 64
W = 512
BLK = 128
SPAN = 2 * HEAD_DIM
TWO = 2 * BLK
FAR = W // BLK
NEG = -1e30
NT = (((1,), (1,)), ((), ()))
NN = (((1,), (0,)), ((), ()))
TN = (((0,), (0,)), ((), ()))
f32 = jnp.float32
bf16 = jnp.bfloat16


def dot(a, b, dims):
    return lax.dot_general(a, b, dims, preferred_element_type=f32)


def by_head(x, first):
    zero = jnp.zeros_like(x)
    return jnp.concatenate([jnp.where(first, x, zero), jnp.where(first, zero, x)], 0)


def join_heads(x, first):
    return jnp.where(first, x[:BLK], x[BLK:])


def fill_keys(dst, halo, own, memory):
    h, o = halo.shape[0], own.shape[0]
    dst[0:h, :SPAN] = halo[...]
    dst[h : h + o, :SPAN] = own[...]
    dst[h + o :, :SPAN] = memory[...]


def forward_kernel(
    info_ref, q_ref, g_ref, ko_ref, vo_ref, kh_ref, vh_ref, km_ref, vm_ref, mb_ref, *rest, nb
):
    at_ref, pt, ga_ref, ke, ve = rest[-5:]
    ext = kh_ref.shape[0] + ko_ref.shape[0]
    fill_keys(ke, kh_ref, ko_ref, km_ref)
    fill_keys(ve, vh_ref, vo_ref, vm_ref)
    ve[:, SPAN:] = jnp.ones((ve.shape[0], SPAN), bf16)
    first = lax.broadcasted_iota(jnp.int32, (BLK, SPAN), 1) < HEAD_DIM
    tri = (
        lax.broadcasted_iota(jnp.int32, (BLK, TWO), 0)
        <= lax.broadcasted_iota(jnp.int32, (BLK, TWO), 1) % BLK
    )
    lane = lax.broadcasted_iota(jnp.int32, (TWO, SPAN), 1)
    row = lax.broadcasted_iota(jnp.int32, (TWO, SPAN), 0) % BLK
    for b in range(nb):
        rows, cols = slice(b * BLK, (b + 1) * BLK), slice(b * TWO, (b + 1) * TWO)
        band = slice(b * BLK, (b + FAR + 1) * BLK)
        q2 = by_head(q_ref[rows, :] * jnp.asarray(HEAD_DIM**-0.5, bf16), first)
        s = dot(ke[band, :], q2, NT)
        sm = dot(ke[ext:, :], q2, NT) + jnp.concatenate([mb_ref[b], mb_ref[b]], 1)
        lo = info_ref[0, b]
        off = [jnp.where(e + b >= lo, 0.0, NEG).astype(f32) for e in range(FAR)]
        ends = jnp.where(tri, s[FAR * BLK :, :], s[:BLK, :] + off[0])
        mid = [s[e * BLK : (e + 1) * BLK, :] for e in range(1, FAR)]
        m = jnp.maximum(jnp.max(ends, 0, keepdims=True), jnp.max(sm, 0, keepdims=True))
        for e in range(1, FAR):
            m = jnp.maximum(m, jnp.max(mid[e - 1], 0, keepdims=True) + off[e])
        p = jnp.exp(ends - m).astype(bf16)
        zero = jnp.zeros_like(p)
        pt[0, b * BLK : (b + 1) * BLK, cols] = jnp.where(tri, zero, p)
        pt[0, (b + FAR) * BLK : (b + FAR + 1) * BLK, cols] = jnp.where(tri, p, zero)
        for e in range(1, FAR):
            pt[0, (b + e) * BLK : (b + e + 1) * BLK, cols] = jnp.exp(
                mid[e - 1] - (m - off[e])
            ).astype(bf16)
        pt[0, ext:, cols] = jnp.exp(sm - m).astype(bf16)
        o = dot(pt[0, band, cols], ve[band, :], TN) + dot(pt[0, ext:, cols], ve[ext:, :], TN)
        scale = jnp.where(row < info_ref[1, b], 1.0 / o[:, SPAN:], 0.0)
        o = o[:, :SPAN] * scale
        at_ref[rows, :] = join_heads(o, first).astype(bf16)
        g2 = (by_head(g_ref[rows, :].astype(f32), first) * scale).astype(bf16)
        d = -jnp.sum(g2.astype(f32) * o, 1, keepdims=True)
        high = d.astype(bf16).astype(f32)
        ga_ref[0, cols, :SPAN] = g2
        ga_ref[0, cols, SPAN:] = jnp.where(
            lane == 0, high, jnp.where(lane == 1, d - high, 0.0)
        ).astype(bf16)


def backward_kernel(
    q_ref, pt_ref, ga_ref, ko_ref, vo_ref, kh_ref, vh_ref, km_ref, vm_ref, *rest, nb
):
    dq_ref, dko_ref, dvo_ref, dm_ref, dh_ref, ke, ve, q2, ds = rest[-9:]
    hrows, slots = kh_ref.shape[0], km_ref.shape[0]
    ext = hrows + ko_ref.shape[0]
    fill_keys(ke, kh_ref, ko_ref, km_ref)
    fill_keys(ve, vh_ref, vo_ref, vm_ref)
    ve[:, SPAN:] = jnp.ones((ve.shape[0], SPAN), bf16)
    first = lax.broadcasted_iota(jnp.int32, (BLK, SPAN), 1) < HEAD_DIM
    unit = HEAD_DIM**-0.5
    for b in range(nb):
        rows, cols = slice(b * BLK, (b + 1) * BLK), slice(b * TWO, (b + 1) * TWO)
        band = slice(b * BLK, (b + FAR + 1) * BLK)
        q2[cols, :] = by_head(q_ref[rows, :] * jnp.asarray(unit, bf16), first)
        ga = ga_ref[0, cols, :]
        dp = dot(ve[band, :], ga, NT)
        ds[band, cols] = (pt_ref[0, band, cols].astype(f32) * dp).astype(bf16)
        dp = dot(ve[ext:, :], ga, NT)
        ds[ext:, cols] = (pt_ref[0, ext:, cols].astype(f32) * dp).astype(bf16)
        dq = dot(ds[band, cols], ke[band, :], TN) + dot(ds[ext:, cols], ke[ext:, :], TN)
        dq_ref[rows, :] = (join_heads(dq, first) * unit).astype(bf16)
    for e in range(ext // BLK):
        cols = slice(max(0, e - FAR) * TWO, (min(nb - 1, e) + 1) * TWO)
        rows = slice(e * BLK, (e + 1) * BLK)
        dv = dot(pt_ref[0, rows, cols], ga_ref[0, cols, :SPAN], NN)
        dk = dot(ds[rows, cols], q2[cols, :], NN)
        if e * BLK < hrows:
            dh_ref[rows, :] = dk.astype(bf16)
            dh_ref[hrows + e * BLK : hrows + (e + 1) * BLK, :] = dv.astype(bf16)
        else:
            own = slice(e * BLK - hrows, (e + 1) * BLK - hrows)
            dko_ref[own, :] = dk
            dvo_ref[own, :] = dv
    dm_ref[:slots, :] = dot(ds[ext:, :], q2[...], NN).astype(bf16)
    dm_ref[slots:, :] = dot(pt_ref[0, ext:, :], ga_ref[0, :, :SPAN], NN).astype(bf16)


def columns(rows, start):
    return pl.BlockSpec((rows, SPAN), lambda p, *_: (0, p + start))


ANY = pl.BlockSpec(memory_space=pl.ANY)


def forward(info, q, g, ko, vo, kh, vh, km, vm, bias, start, count, base, halo_at, carry):
    tokens, width = q.shape
    slots, hrows, nb = km.shape[0], kh.shape[0], tokens // BLK
    keys = hrows + tokens + slots
    kc, vc = halo_at
    mk, mv = base
    args = [info, q, g, ko, vo, kh, vh, km, vm, bias]
    specs = [
        columns(tokens, start), columns(tokens, start), columns(tokens, start), columns(tokens, start),
        columns(hrows, kc), columns(hrows, vc), columns(slots, mk + start), columns(slots, mv + start),
        pl.BlockSpec(bias.shape, lambda p, *_: (0, 0, 0)),
    ]
    alias = {}
    if carry is not None:
        alias = {len(args): 0}
        args.append(carry)
        specs.append(ANY)
    return pl.pallas_call(
        functools.partial(forward_kernel, nb=nb),
        grid_spec=pltpu.PrefetchScalarGridSpec(
            num_scalar_prefetch=1,
            grid=(count,),
            in_specs=specs,
            out_specs=[
                columns(tokens, start),
                pl.BlockSpec((1, keys, nb * TWO), lambda p, *_: (p, 0, 0)),
                pl.BlockSpec((1, nb * TWO, 2 * SPAN), lambda p, *_: (p, 0, 0)),
            ],
            scratch_shapes=[pltpu.VMEM((keys, SPAN), bf16), pltpu.VMEM((keys, 2 * SPAN), bf16)],
        ),
        out_shape=[
            jax.ShapeDtypeStruct((tokens, width), bf16),
            jax.ShapeDtypeStruct((count, keys, nb * TWO), bf16),
            jax.ShapeDtypeStruct((count, nb * TWO, 2 * SPAN), bf16),
        ],
        input_output_aliases=alias,
        compiler_params=pltpu.CompilerParams(vmem_limit_bytes=60 << 20),
        cost_estimate=pl.CostEstimate(
            flops=count * nb * 12 * TWO * BLK * 1024, bytes_accessed=count * (4 << 20), transcendentals=count << 20
        ),
        name="band_forward",
    )(*args)


def backward(q, pt, ga, ko, vo, kh, vh, km, vm, start, count, base, halo_at, at, carry):
    tokens, width = q.shape
    slots, hrows, nb = km.shape[0], kh.shape[0], tokens // BLK
    keys = hrows + tokens + slots
    kc, vc = halo_at
    mk, mv = base
    args = [q, pt, ga, ko, vo, kh, vh, km, vm]
    specs = [
        columns(tokens, start),
        pl.BlockSpec((1, keys, nb * TWO), lambda p, *_: (p + at, 0, 0)),
        pl.BlockSpec((1, nb * TWO, 2 * SPAN), lambda p, *_: (p + at, 0, 0)),
        columns(tokens, start), columns(tokens, start),
        columns(hrows, kc), columns(hrows, vc), columns(slots, mk + start), columns(slots, mv + start),
    ]
    alias = {}
    if carry is not None:
        alias = {len(args) + i: i for i in range(len(carry))}
        args += carry
        specs += [ANY] * len(carry)
    return pl.pallas_call(
        functools.partial(backward_kernel, nb=nb),
        grid=(count,),
        in_specs=specs,
        out_specs=[
            columns(tokens, start), columns(tokens, start), columns(tokens, start),
            columns(2 * slots, start), columns(2 * hrows, 0),
        ],
        scratch_shapes=[
            pltpu.VMEM((keys, SPAN), bf16), pltpu.VMEM((keys, 2 * SPAN), bf16),
            pltpu.VMEM((nb * TWO, SPAN), bf16), pltpu.VMEM((keys, nb * TWO), bf16),
        ],
        out_shape=[
            jax.ShapeDtypeStruct((tokens, width), bf16),
            jax.ShapeDtypeStruct((tokens, width), f32),
            jax.ShapeDtypeStruct((tokens, width), f32),
            jax.ShapeDtypeStruct((2 * slots, width), bf16),
            jax.ShapeDtypeStruct((2 * hrows, count * SPAN), bf16),
        ],
        input_output_aliases=alias,
        compiler_params=pltpu.CompilerParams(vmem_limit_bytes=60 << 20),
        cost_estimate=pl.CostEstimate(
            flops=count * nb * 20 * TWO * BLK * 1024, bytes_accessed=count * (6 << 20), transcendentals=0
        ),
        name="band_backward",
    )(*args)


def finish_kernel(slot_ref, dk_in, dv_in, mk_ref, mv_ref, *rest):
    backs, (dk_ref, dv_ref) = rest[:-2], rest[-2:]
    tokens = dk_in.shape[0]
    mine = slot_ref.shape[1]
    pick = (lax.broadcasted_iota(jnp.int32, (tokens, mine), 0) == slot_ref[...]).astype(f32).astype(bf16)
    dk = dk_in[...] + dot(pick, mk_ref[...], NN)
    dv = dv_in[...] + dot(pick, mv_ref[...], NN)
    edge = tokens - W
    for i, back in enumerate(backs):

        @pl.when(pl.program_id(0) == i)
        def _():
            dk_ref[edge:, :] = (dk[edge:] + back[:W, :].astype(f32)).astype(bf16)
            dv_ref[edge:, :] = (dv[edge:] + back[W:, :].astype(f32)).astype(bf16)


def finish(slots, dko, dvo, dmem, backs):
    tokens, width = dko.shape
    mine, n = slots.shape[0], len(backs)
    step = width // n
    col = lambda r, j: pl.BlockSpec((r, step), lambda i: (j, i))
    return pl.pallas_call(
        finish_kernel,
        grid=(n,),
        in_specs=[pl.BlockSpec((1, mine), lambda i: (0, 0)), col(tokens, 0), col(tokens, 0), col(mine, 0), col(mine, 1)]
        + [pl.BlockSpec((2 * W, step), lambda i: (0, 0))] * n,
        out_specs=[col(tokens, 0), col(tokens, 0)],
        out_shape=[jax.ShapeDtypeStruct((tokens, width), bf16)] * 2,
        compiler_params=pltpu.CompilerParams(vmem_limit_bytes=60 << 20),
        cost_estimate=pl.CostEstimate(flops=1 << 26, bytes_accessed=8 << 20, transcendentals=0),
        name="finish_rows",
    )(slots[None, :], dko, dvo, dmem, dmem, *backs)


def protein_tables(prot_blocks, last_fill):
    prot_ends = jnp.cumsum(prot_blocks)
    starts = prot_ends - prot_blocks
    valid_len = (prot_blocks - 1) * BLK + last_fill
    return prot_ends, starts, valid_len


def token_info(positions, tables):
    prot_ends, starts, valid_len = tables
    count = prot_ends.shape[0]
    blocks = jnp.floor_divide(positions, BLK)
    protein = jnp.sum((blocks[:, None] >= prot_ends[None, :]).astype(jnp.int32), axis=1)
    onehot = protein[:, None] == jnp.arange(count, dtype=jnp.int32)[None, :]
    first = jnp.sum(jnp.where(onehot, starts[None, :], 0), axis=1)
    length = jnp.sum(jnp.where(onehot, valid_len[None, :], 0), axis=1)
    return protein, first, length - (positions - first * BLK)


def swap(x, axis, bits):
    return lax.ppermute(x, axis, [(i, i ^ bits) for i in range(lax.axis_size(axis))])


def bits_of(n):
    out, b = [], 1
    while b < n:
        out.append(b)
        b *= 2
    return out


def gather_rows(x, axis, me):
    for bit in bits_of(lax.axis_size(axis)):
        other = swap(x, axis, bit)
        upper = (me & bit) != 0
        x = jnp.where(upper, jnp.concatenate([other, x], 0), jnp.concatenate([x, other], 0))
    return x


def halve(x, axis, me):
    for bit in bits_of(lax.axis_size(axis)):
        lead, n = x.shape[0], x.shape[1]
        x = x.reshape(lead, n // 2, 2, *x.shape[2:])
        upper = (me & bit) != 0
        keep = jnp.where(upper, x[:, :, 1], x[:, :, 0])
        send = jnp.where(upper, x[:, :, 0], x[:, :, 1])
        x = keep.astype(f32) + swap(send.astype(bf16), axis, bit).astype(f32)
    return x


def exchange(parts, axis, shift, me, n):
    rows = parts.shape[0] // n
    part = lambda j: lax.dynamic_slice_in_dim(parts, j * rows, rows)
    got = [swap(part(me ^ k).astype(bf16), axis, k << shift) for k in range(1, n)]
    return sum([g.astype(f32) for g in got], part(me).astype(f32))


def spread(x, axis, shift, me, n):
    parts = [x] + [swap(x, axis, k << shift) for k in range(1, n)]
    for bit in bits_of(n):
        upper = (me & bit) != 0
        parts = [jnp.where(upper, parts[j ^ bit], parts[j]) for j in range(n)]
    return jnp.concatenate(parts, 0)


def per_device(queries, key_rows, value_rows, cotangent, out_weight, prot_blocks, last_fill, memory_slots):
    q, k, v, cot = queries[0], key_rows[0], value_rows[0], cotangent[0]
    tables = protein_tables(prot_blocks[0], last_fill[0])
    slots = memory_slots[0]
    tokens, width = q.shape
    nctx, nfam = lax.axis_size("ctx"), lax.axis_size("fam")
    me, fam = lax.axis_index("ctx"), lax.axis_index("fam")
    total = slots.shape[0]
    mine = total // nctx
    nb = tokens // BLK
    pairs = width // SPAN
    fgroups, bgroups = math.gcd(pairs, 2), math.gcd(pairs, 4)
    fcount, bcount = pairs // fgroups, pairs // bgroups
    step = fcount * SPAN
    shift = [(i, i + 1) for i in range(nctx - 1)]
    back = [(i + 1, i) for i in range(nctx - 1)]
    edge = tokens - W
    halos = []
    for i in range(fgroups):
        cols = slice(i * step, (i + 1) * step)
        halos.append(lax.ppermute(jnp.concatenate([k[edge:, cols], v[edge:, cols]], 1), "ctx", shift))
    own_slots = lax.dynamic_slice_in_dim(slots, me * mine, mine)
    pick = (own_slots[:, None] == jnp.arange(tokens, dtype=jnp.int32)[None, :]).astype(bf16)
    rows = jnp.concatenate([dot(pick, k, NN).astype(bf16), dot(pick, v, NN).astype(bf16)], 1)
    mem = gather_rows(rows, "ctx", me)
    grad_attn = dot(cot, out_weight, NT).astype(bf16)
    heads = me * tokens + jnp.arange(nb, dtype=jnp.int32) * BLK
    source = jnp.arange(total, dtype=jnp.int32) // mine * tokens + slots
    prot, first, left = token_info(jnp.concatenate([heads, source]), tables)
    lo = jnp.clip(first[:nb] - (me * tokens - W) // BLK, 0, nb + FAR)
    info = jnp.stack([lo, jnp.clip(left[:nb], 0, BLK)])
    seen = (left[nb:] > 0)[None, :] & (prot[None, nb:] < prot[:nb, None])
    bias = jnp.broadcast_to(jnp.where(seen, 0.0, NEG).astype(f32)[:, :, None], (nb, total, BLK))
    base = (0, pairs)
    att, saved = None, []
    for i in range(fgroups):
        att, pt, ga = forward(
            info, q, grad_attn, k, v, halos[i], halos[i], mem, mem, bias,
            i * fcount, fcount, base, (0, fcount), att)
        saved.append((pt, ga))
    core = me & 1
    half = width // 2
    mine_att = lax.dynamic_slice_in_dim(att, core * half, half, 1)
    your_att = lax.dynamic_slice_in_dim(att, (1 - core) * half, half, 1)
    sent = swap(dot(your_att, cot, TN).astype(bf16), "ctx", 1)
    kept = dot(mine_att, cot, TN)

    carry = None

    def run(i, carry):
        at = i * bcount
        j = at // fcount
        r = at - j * fcount
        pt, ga = saved[j]
        out = backward(
            q, pt, ga, k, v, halos[j], halos[j], mem, mem,
            at, bcount, base, (r, fcount + r), r, carry)
        return list(out[:4]), out[4]

    backs = []
    for i in range(bgroups):
        carry, dh = run(i, carry)
        backs.append(lax.ppermute(dh, "ctx", back))
    plane = nctx // 2
    total_w = kept + sent.astype(f32)
    total_w = exchange(total_w, "ctx", 1, me >> 1, plane)
    total_w = exchange(total_w, "fam", 0, fam, nfam)
    w = spread(total_w.astype(bf16), "fam", 0, fam, nfam)
    w = spread(w, "ctx", 1, me >> 1, plane)
    other = swap(w, "ctx", 1)
    scale = (nfam * nctx * tokens) ** -0.5
    upper = core != 0
    weight = jnp.concatenate([jnp.where(upper, other, w), jnp.where(upper, w, other)], 0).astype(f32) * scale
    dq, dko, dvo, dm = carry
    dmem = halve(dm.reshape(2, nctx, mine, width), "ctx", me).reshape(2 * mine, width).astype(bf16)
    dk, dv = finish(own_slots, dko, dvo, dmem, backs)
    return dq[None], dk[None], dv[None], weight


def solution(mesh):
    row = P("fam", "ctx", None)
    small = P("fam", None)

    return jax.shard_map(
        per_device,
        mesh=mesh,
        in_specs=(row, row, row, row, P(), small, small, small),
        out_specs=(row, row, row, P()),
        check_vma=False,
    )
```

profile of v0, /device:TPU:3, one launch (start us, length us, event | category | flops | bytes accessed | tf_op | source)
XLA Modules:
  0.0 182.7 jit_solution(8013109116851099459)
XLA Ops:
  6.8 3.0 %collective-permute-start = (bf16[512,1024]{1,0:T(8,128)(2,1)}, bf16[512,1024]{1,0:T(8,128)(2,1)S(1)}, u32[]{:S(2)}, u32[]{:S(2)}) collective-permute-start(bf16[512,1024]{1,0:T(8,128)(2,1)} %pad_maximum_fusion), channel_id=1, source_target_pairs={{0,1},{1,2},{2,3},{3,4},{4,5},{5,6},{6,7},{8,9},{9,10},{10,11},{11... | collective-permute-start | bytes 3145736 | tf_op jit(solution)/shard_map/ppermute | solution.py:350
  10.9 2.4 %collective-permute-start.4 = (bf16[512,1024]{1,0:T(8,128)(2,1)}, bf16[512,1024]{1,0:T(8,128)(2,1)}, u32[]{:S(2)}, u32[]{:S(2)}) collective-permute-start(bf16[512,1024]{1,0:T(8,128)(2,1)} %pad_maximum_fusion.1), channel_id=1, source_target_pairs={{0,1},{1,2},{2,3},{3,4},{4,5},{5,6},{6,7},{8,9},{9,10},{10,11},{11... | collective-permute-start | bytes 3145736 | tf_op jit(solution)/shard_map/ppermute | solution.py:350
  13.9 3.5 %convolution_convert_fusion.g_ref = bf16[512,1024]{1,0:T(8,128)(2,1)} fusion(bf16[1024,1024]{1,0:T(8,128)(2,1)S(1)} %copy-done, bf16[1,512,1024]{2,1,0:T(8,128)(2,1)} %param.11), kind=kOutput, calls=%fused_computation.2 | convolution fusion | flops 1074266112 | bytes 4194304 | tf_op jit(solution)/shard_map/dot_general | solution.py:27
  17.8 18.7 %collective-permute-done.2 = bf16[32,2048]{1,0:T(8,128)(2,1)S(1)} collective-permute-done((bf16[32,2048]{1,0:T(8,128)(2,1)S(1)}, bf16[32,2048]{1,0:T(8,128)(2,1)S(1)}, u32[]{:S(2)}, u32[]{:S(2)}) %collective-permute-start.2) | collective-permute-done | bytes 131104 | tf_op jit(solution)/shard_map/ppermute | solution.py:285
  38.5 3.3 %collective-permute-done.3 = bf16[64,2048]{1,0:T(8,128)(2,1)S(1)} collective-permute-done((bf16[64,2048]{1,0:T(8,128)(2,1)S(1)}, bf16[64,2048]{1,0:T(8,128)(2,1)S(1)}, u32[]{:S(2)}, u32[]{:S(2)}) %collective-permute-start.3) | collective-permute-done | bytes 262176 | tf_op jit(solution)/shard_map/ppermute | solution.py:285
  43.5 13.5 %band_forward.2 = (bf16[512,1024]{1,0:T(8,128)(2,1)}, bf16[4,1152,1024]{2,1,0:T(8,128)(2,1)}, bf16[4,1024,256]{2,1,0:T(8,128)(2,1)}) custom-call(s32[2,4]{1,0:T(2,128)} %pad_add_fusion.1.info_ref, bf16[512,1024]{1,0:T(8,128)(2,1)} %bitcast.122, bf16[512,1024]{1,0:T(8,128)(2,1)} %convolution_convert_fusion.g_ref, bf16[512,1024]{1,0:T(8,128)(2,1)} %bitcast.106, ...), custom_call_target="tpu_custom_call" | custom-call | flops 6442450944 | bytes 16777216 | tf_op jit(solution)/shard_map/band_forward/pallas_call | solution.py:158
  58.0 13.5 %band_forward.3 = (bf16[512,1024]{1,0:T(8,128)(2,1)}, bf16[4,1152,1024]{2,1,0:T(8,128)(2,1)}, bf16[4,1024,256]{2,1,0:T(8,128)(2,1)}) custom-call(s32[2,4]{1,0:T(2,128)} %pad_add_fusion.1.info_ref, bf16[512,1024]{1,0:T(8,128)(2,1)} %bitcast.123, bf16[512,1024]{1,0:T(8,128)(2,1)} %convolution_convert_fusion.g_ref, ...), custom_call_target="tpu_custom_call", output_to_operand_aliasing={{0}: (10, {})} | custom-call | flops 6442450944 | bytes 16777216 | tf_op jit(solution)/shard_map/band_forward/pallas_call | solution.py:158
  73.4 8.0 %band_backward.4 = (bf16[512,1024]{1,0:T(8,128)(2,1)}, f32[512,1024]{1,0:T(8,128)}, f32[512,1024]{1,0:T(8,128)}, bf16[256,1024]{1,0:T(8,128)(2,1)}, bf16[1024,256]{1,0:T(8,128)(2,1)}) custom-call(bf16[512,1024]{1,0:T(8,128)(2,1)} %bitcast.124, bf16[4,1152,1024]{2,1,0:T(8,128)(2,1)} %get-tuple-element.35.pt_ref, ...), custom_call_target="tpu_custom_call" | custom-call | flops 5368709120 | bytes 12582912 | tf_op jit(solution)/shard_map/band_backward/pallas_call | solution.py:204
  81.5 8.1 %band_backward.5 = (bf16[512,1024]{1,0:T(8,128)(2,1)}, f32[512,1024]{1,0:T(8,128)}, f32[512,1024]{1,0:T(8,128)}, bf16[256,1024]{1,0:T(8,128)(2,1)}, bf16[1024,256]{1,0:T(8,128)(2,1)}) custom-call(bf16[512,1024]{1,0:T(8,128)(2,1)} %bitcast.125, ...), custom_call_target="tpu_custom_call", output_to_operand_aliasing={{0}: (9, {}), {1}: (10, {}), {2}: (11, {}), {3}: (12, {})} | custom-call | flops 5368709120 | bytes 12582912 | tf_op jit(solution)/shard_map/band_backward/pallas_call | solution.py:204
  89.6 2.1 %convert_add_fusion = f32[512,1024]{1,0:T(8,128)S(1)} fusion(bf16[512,1024]{1,0:T(8,128)(2,1)} %collective-permute-done.12, bf16[1,512,1024]{2,1,0:T(8,128)(2,1)S(1)} %copy-done.7, bf16[512,1024]{1,0:T(8,128)(2,1)} %get-tuple-element.59, s32[]{:T(128)S(6)} %select_n.278), kind=kOutput, calls=%fused_computation.1 | convolution fusion | flops 537919488 | bytes 4718596 | tf_op jit(solution)/shard_map/dot_general | solution.py:27
  94.6 8.2 %band_backward.6 = (bf16[512,1024]{1,0:T(8,128)(2,1)}, f32[512,1024]{1,0:T(8,128)}, f32[512,1024]{1,0:T(8,128)}, bf16[256,1024]{1,0:T(8,128)(2,1)}, bf16[1024,256]{1,0:T(8,128)(2,1)}) custom-call(bf16[512,1024]{1,0:T(8,128)(2,1)} %bitcast.126, ...), custom_call_target="tpu_custom_call", output_to_operand_aliasing={{0}: (9, {}), {1}: (10, {}), {2}: (11, {}), {3}: (12, {})} | custom-call | flops 5368709120 | bytes 12582912 | tf_op jit(solution)/shard_map/band_backward/pallas_call | solution.py:204
  102.8 3.2 %collective-permute-done.15 = bf16[128,1024]{1,0:T(8,128)(2,1)S(1)} collective-permute-done((bf16[128,1024]{1,0:T(8,128)(2,1)S(1)}, bf16[128,1024]{1,0:T(8,128)(2,1)S(1)}, u32[]{:S(2)}, u32[]{:S(2)}) %collective-permute-start.15) | collective-permute-done | bytes 262176 | tf_op jit(solution)/shard_map/ppermute | solution.py:285
  107.5 2.2 %collective-permute-start.18 = (bf16[32,1024]{1,0:T(8,128)(2,1)S(1)}, bf16[32,1024]{1,0:T(8,128)(2,1)S(1)}, u32[]{:S(2)}, u32[]{:S(2)}) collective-permute-start(bf16[32,1024]{1,0:T(8,128)(2,1)S(1)} %get-tuple-element.75), channel_id=1, source_target_pairs={{0,24},{8,16},{16,8},{24,0},{1,25},{9,17},{17,9},{25,1},{2,26},{10... | collective-permute-start | bytes 196616 | tf_op jit(solution)/shard_map/ppermute | solution.py:285
  109.9 8.0 %band_backward.7 = (bf16[512,1024]{1,0:T(8,128)(2,1)}, f32[512,1024]{1,0:T(8,128)}, f32[512,1024]{1,0:T(8,128)}, bf16[256,1024]{1,0:T(8,128)(2,1)}, bf16[1024,256]{1,0:T(8,128)(2,1)}) custom-call(bf16[512,1024]{1,0:T(8,128)(2,1)} %bitcast.127, ...), custom_call_target="tpu_custom_call", output_to_operand_aliasing={{0}: (9, {}), {1}: (10, {}), {2}: (11, {}), {3}: (12, {})} | custom-call | flops 5368709120 | bytes 12582912 | tf_op jit(solution)/shard_map/band_backward/pallas_call | solution.py:204
  122.6 4.2 %collective-permute-start.5 = (bf16[2,4,16,1024]{3,2,1,0:T(8,128)(2,1)S(1)}, bf16[2,4,16,1024]{3,2,1,0:T(8,128)(2,1)S(1)}, u32[]{:S(2)}, u32[]{:S(2)}) collective-permute-start(bf16[2,4,16,1024]{3,2,1,0:T(8,128)(2,1)S(1)} %select_bitcast_fusion), channel_id=1, source_target_pairs={{0,1},{1,0},{2,3},{3,2},{4,5},{5,4},{6,7},{7,6},{8,9},{9,8},{10,11... | collective-permute-start | bytes 786440 | tf_op jit(solution)/shard_map/ppermute | solution.py:285
  129.9 2.3 %collective-permute-done.24 = bf16[128,1024]{1,0:T(8,128)(2,1)S(1)} collective-permute-done((bf16[128,1024]{1,0:T(8,128)(2,1)S(1)}, bf16[128,1024]{1,0:T(8,128)(2,1)S(1)}, u32[]{:S(2)}, u32[]{:S(2)}) %collective-permute-start.24) | collective-permute-done | bytes 262176 | tf_op jit(solution)/shard_map/ppermute | solution.py:285
  137.6 6.5 %collective-permute-start.25 = (bf16[512,1024]{1,0:T(8,128)(2,1)}, bf16[512,1024]{1,0:T(8,128)(2,1)S(1)}, u32[]{:S(2)}, u32[]{:S(2)}) collective-permute-start(bf16[512,1024]{1,0:T(8,128)(2,1)} %pad_maximum_fusion.2), channel_id=1, source_target_pairs={{0,1},{1,0},{2,3},{3,2},{4,5},{5,4},{6,7},{7,6},{8,9},{9,8},{10,11... | collective-permute-start | bytes 3145736 | tf_op jit(solution)/shard_map/ppermute | solution.py:285
  145.5 2.2 %collective-permute-start.9 = (bf16[1024,256]{1,0:T(8,128)(2,1)S(1)}, bf16[1024,256]{1,0:T(8,128)(2,1)S(1)}, u32[]{:S(2)}, u32[]{:S(2)}) collective-permute-start(bf16[1024,256]{1,0:T(8,128)(2,1)S(1)} %copy-done.13), channel_id=1, source_target_pairs={{1,0},{2,1},{3,2},{4,3},{5,4},{6,5},{7,6},{9,8},{10,9},{11,10},{12... | collective-permute-start | bytes 1572872 | tf_op jit(solution)/shard_map/ppermute | solution.py:392
  149.9 2.3 %collective-permute-start.11 = (bf16[1024,256]{1,0:T(8,128)(2,1)S(1)}, bf16[1024,256]{1,0:T(8,128)(2,1)}, u32[]{:S(2)}, u32[]{:S(2)}) collective-permute-start(bf16[1024,256]{1,0:T(8,128)(2,1)S(1)} %copy-done.15), channel_id=1, source_target_pairs={{1,0},{2,1},{3,2},{4,3},{5,4},{6,5},{7,6},{9,8},{10,9},{11,10},{12... | collective-permute-start | bytes 1572872 | tf_op jit(solution)/shard_map/ppermute | solution.py:392
  156.9 5.6 %collective-permute-done.8.rest_0_ = bf16[1024,256]{1,0:T(8,128)(2,1)S(1)} collective-permute-done((bf16[1024,256]{1,0:T(8,128)(2,1)S(1)}, bf16[1024,256]{1,0:T(8,128)(2,1)S(1)}, u32[]{:S(2)}, u32[]{:S(2)}) %collective-permute-start.8) | collective-permute-done | bytes 524320 | tf_op jit(solution)/shard_map/ppermute | solution.py:392
  162.6 5.7 %collective-permute-done.11.rest_3_ = bf16[1024,256]{1,0:T(8,128)(2,1)} collective-permute-done((bf16[1024,256]{1,0:T(8,128)(2,1)S(1)}, bf16[1024,256]{1,0:T(8,128)(2,1)}, u32[]{:S(2)}, u32[]{:S(2)}) %collective-permute-start.11) | collective-permute-done | bytes 524320 | tf_op jit(solution)/shard_map/ppermute | solution.py:392
  168.3 5.6 %collective-permute-done.10.rest_2_ = bf16[1024,256]{1,0:T(8,128)(2,1)} collective-permute-done((bf16[1024,256]{1,0:T(8,128)(2,1)S(1)}, bf16[1024,256]{1,0:T(8,128)(2,1)}, u32[]{:S(2)}, u32[]{:S(2)}) %collective-permute-start.10) | collective-permute-done | bytes 524320 | tf_op jit(solution)/shard_map/ppermute | solution.py:392
  173.9 5.7 %finish_rows.1 = (bf16[512,1024]{1,0:T(8,128)(2,1)}, bf16[512,1024]{1,0:T(8,128)(2,1)}) custom-call(s32[1,16]{1,0:T(1,128)} %constant_dynamic-slice_fusion.slot_ref, f32[512,1024]{1,0:T(8,128)} %get-tuple-element.50.dk_in, f32[512,1024]{1,0:T(8,128)} %get-tuple-element.51.dv_in, bf16[32,1024]{1,0:T(8,128)(2,1)} %bitcast.131, bf16[32,1024]{1,0:T(8,128)(2,1)} %bitcast.132, ...), custom_call_target="tpu_custom_call" | custom-call | flops 67108864 | bytes 8388608 | tf_op jit(solution)/shard_map/finish_rows/pallas_call | solution.py:253
  180.2 2.6 %convert_multiply_fusion = f32[1024,1024]{1,0:T(8,128)} fusion(bf16[512,1024]{1,0:T(8,128)(2,1)S(1)} %get-tuple-element.63, bf16[512,1024]{1,0:T(8,128)(2,1)S(1)} %get-tuple-element.62), kind=kLoop, calls=%fused_computation | loop fusion | flops 5242880 | bytes 6291456 | tf_op jit(solution)/shard_map/mul | solution.py:402
  (115 shorter events, 41.2 us)
Async XLA Ops:
  4.7 12.7 %collective-permute-start.1 = (bf16[16,2048]{1,0:T(8,128)(2,1)S(1)}, bf16[16,2048]{1,0:T(8,128)(2,1)S(1)}, u32[]{:S(2)}, u32[]{:S(2)}) collective-permute-start(bf16[16,2048]{1,0:T(8,128)(2,1)S(1)} %pad_maximum_fusion.4), channel_id=1, source_target_pairs={{0,1},{1,0},{2,3},{3,2},{4,5},{5,4},{6,7},{7,6},{8,9},{9,8},{10,11... | collective-permute-start | bytes 196616 | tf_op jit(solution)/shard_map/ppermute | solution.py:285
  6.8 50.3 %collective-permute-start = (bf16[512,1024]{1,0:T(8,128)(2,1)}, bf16[512,1024]{1,0:T(8,128)(2,1)S(1)}, u32[]{:S(2)}, u32[]{:S(2)}) collective-permute-start(bf16[512,1024]{1,0:T(8,128)(2,1)} %pad_maximum_fusion), channel_id=1, source_target_pairs={{0,1},{1,2},{2,3},{3,4},{4,5},{5,6},{6,7},{8,9},{9,10},{10,11},{11... | collective-permute-start | bytes 3145736 | tf_op jit(solution)/shard_map/ppermute | solution.py:350
  10.9 31.8 %collective-permute-start.4 = (bf16[512,1024]{1,0:T(8,128)(2,1)}, bf16[512,1024]{1,0:T(8,128)(2,1)}, u32[]{:S(2)}, u32[]{:S(2)}) collective-permute-start(bf16[512,1024]{1,0:T(8,128)(2,1)} %pad_maximum_fusion.1), channel_id=1, source_target_pairs={{0,1},{1,2},{2,3},{3,4},{4,5},{5,6},{6,7},{8,9},{9,10},{10,11},{11... | collective-permute-start | bytes 3145736 | tf_op jit(solution)/shard_map/ppermute | solution.py:350
  17.4 19.1 %collective-permute-start.2 = (bf16[32,2048]{1,0:T(8,128)(2,1)S(1)}, bf16[32,2048]{1,0:T(8,128)(2,1)S(1)}, u32[]{:S(2)}, u32[]{:S(2)}) collective-permute-start(bf16[32,2048]{1,0:T(8,128)(2,1)S(1)} %maximum_select_fusion.2), channel_id=1, source_target_pairs={{0,2},{1,3},{2,0},{3,1},{4,6},{5,7},{6,4},{7,5},{8,10},{9,11},{10,... | collective-permute-start | bytes 393224 | tf_op jit(solution)/shard_map/ppermute | solution.py:285
  73.3 16.3 %collective-permute-start.12 = (bf16[512,1024]{1,0:T(8,128)(2,1)S(1)}, bf16[512,1024]{1,0:T(8,128)(2,1)}, u32[]{:S(2)}, u32[]{:S(2)}) collective-permute-start(bf16[512,1024]{1,0:T(8,128)(2,1)S(1)} %convolution_convert_fusion.1), channel_id=1, source_target_pairs={{0,1},{1,0},{2,3},{3,2},{4,5},{5,4},{6,7},{7,6},{8,9},{9,8},{10,11... | collective-permute-start | bytes 3145736 | tf_op jit(solution)/shard_map/ppermute | solution.py:285
  91.9 10.9 %collective-permute-start.13 = (bf16[128,1024]{1,0:T(8,128)(2,1)S(1)}, bf16[128,1024]{1,0:T(8,128)(2,1)S(1)}, u32[]{:S(2)}, u32[]{:S(2)}) collective-permute-start(bf16[128,1024]{1,0:T(8,128)(2,1)S(1)} %get-tuple-element.64), channel_id=1, source_target_pairs={{0,2},{1,3},{2,0},{3,1},{4,6},{5,7},{6,4},{7,5},{8,10},{9,11},{10,... | collective-permute-start | bytes 786440 | tf_op jit(solution)/shard_map/ppermute | solution.py:285
  93.2 12.8 %collective-permute-start.15 = (bf16[128,1024]{1,0:T(8,128)(2,1)S(1)}, bf16[128,1024]{1,0:T(8,128)(2,1)S(1)}, u32[]{:S(2)}, u32[]{:S(2)}) collective-permute-start(bf16[128,1024]{1,0:T(8,128)(2,1)S(1)} %get-tuple-element.65), channel_id=1, source_target_pairs={{0,6},{1,7},{2,4},{3,5},{4,2},{5,3},{6,0},{7,1},{8,14},{9,15},{10,... | collective-permute-start | bytes 786440 | tf_op jit(solution)/shard_map/ppermute | solution.py:285
  94.3 11.6 %collective-permute-start.14 = (bf16[128,1024]{1,0:T(8,128)(2,1)S(1)}, bf16[128,1024]{1,0:T(8,128)(2,1)S(1)}, u32[]{:S(2)}, u32[]{:S(2)}) collective-permute-start(bf16[128,1024]{1,0:T(8,128)(2,1)S(1)} %get-tuple-element.66), channel_id=1, source_target_pairs={{0,4},{1,5},{2,6},{3,7},{4,0},{5,1},{6,2},{7,3},{8,12},{9,13},{10,... | collective-permute-start | bytes 786440 | tf_op jit(solution)/shard_map/ppermute | solution.py:285
  106.2 11.7 %collective-permute-start.16 = (bf16[32,1024]{1,0:T(8,128)(2,1)S(1)}, bf16[32,1024]{1,0:T(8,128)(2,1)S(1)}, u32[]{:S(2)}, u32[]{:S(2)}) collective-permute-start(bf16[32,1024]{1,0:T(8,128)(2,1)S(1)} %get-tuple-element.74), channel_id=1, source_target_pairs={{0,8},{8,0},{16,24},{24,16},{1,9},{9,1},{17,25},{25,17},{2,10},{10... | collective-permute-start | bytes 196616 | tf_op jit(solution)/shard_map/ppermute | solution.py:285
  107.5 10.3 %collective-permute-start.18 = (bf16[32,1024]{1,0:T(8,128)(2,1)S(1)}, bf16[32,1024]{1,0:T(8,128)(2,1)S(1)}, u32[]{:S(2)}, u32[]{:S(2)}) collective-permute-start(bf16[32,1024]{1,0:T(8,128)(2,1)S(1)} %get-tuple-element.75), channel_id=1, source_target_pairs={{0,24},{8,16},{16,8},{24,0},{1,25},{9,17},{17,9},{25,1},{2,26},{10... | collective-permute-start | bytes 196616 | tf_op jit(solution)/shard_map/ppermute | solution.py:285
  109.8 8.1 %collective-permute-start.17 = (bf16[32,1024]{1,0:T(8,128)(2,1)S(1)}, bf16[32,1024]{1,0:T(8,128)(2,1)S(1)}, u32[]{:S(2)}, u32[]{:S(2)}) collective-permute-start(bf16[32,1024]{1,0:T(8,128)(2,1)S(1)} %get-tuple-element.76), channel_id=1, source_target_pairs={{0,16},{8,24},{16,0},{24,8},{1,17},{9,25},{17,1},{25,9},{2,18},{10... | collective-permute-start | bytes 196616 | tf_op jit(solution)/shard_map/ppermute | solution.py:285
  117.9 8.8 %collective-permute-start.21 = (bf16[32,1024]{1,0:T(8,128)(2,1)S(1)}, bf16[32,1024]{1,0:T(8,128)(2,1)S(1)}, u32[]{:S(2)}, u32[]{:S(2)}) collective-permute-start(bf16[32,1024]{1,0:T(8,128)(2,1)S(1)} %add_convert_fusion), channel_id=1, source_target_pairs={{0,8},{8,0},{16,24},{24,16},{1,9},{9,1},{17,25},{25,17},{2,10},{10... | collective-permute-start | bytes 196616 | tf_op jit(solution)/shard_map/ppermute | solution.py:285
  119.2 7.6 %collective-permute-start.20 = (bf16[32,1024]{1,0:T(8,128)(2,1)S(1)}, bf16[32,1024]{1,0:T(8,128)(2,1)S(1)}, u32[]{:S(2)}, u32[]{:S(2)}) collective-permute-start(bf16[32,1024]{1,0:T(8,128)(2,1)S(1)} %add_convert_fusion), channel_id=1, source_target_pairs={{0,16},{8,24},{16,0},{24,8},{1,17},{9,25},{17,1},{25,9},{2,18},{10... | collective-permute-start | bytes 196616 | tf_op jit(solution)/shard_map/ppermute | solution.py:285
  120.7 6.1 %collective-permute-start.19 = (bf16[32,1024]{1,0:T(8,128)(2,1)S(1)}, bf16[32,1024]{1,0:T(8,128)(2,1)S(1)}, u32[]{:S(2)}, u32[]{:S(2)}) collective-permute-start(bf16[32,1024]{1,0:T(8,128)(2,1)S(1)} %add_convert_fusion), channel_id=1, source_target_pairs={{0,24},{8,16},{16,8},{24,0},{1,25},{9,17},{17,9},{25,1},{2,26},{10... | collective-permute-start | bytes 196616 | tf_op jit(solution)/shard_map/ppermute | solution.py:285
  122.6 7.0 %collective-permute-start.5 = (bf16[2,4,16,1024]{3,2,1,0:T(8,128)(2,1)S(1)}, bf16[2,4,16,1024]{3,2,1,0:T(8,128)(2,1)S(1)}, u32[]{:S(2)}, u32[]{:S(2)}) collective-permute-start(bf16[2,4,16,1024]{3,2,1,0:T(8,128)(2,1)S(1)} %select_bitcast_fusion), channel_id=1, source_target_pairs={{0,1},{1,0},{2,3},{3,2},{4,5},{5,4},{6,7},{7,6},{8,9},{9,8},{10,11... | collective-permute-start | bytes 786440 | tf_op jit(solution)/shard_map/ppermute | solution.py:285
  127.0 7.2 %collective-permute-start.23 = (bf16[128,1024]{1,0:T(8,128)(2,1)S(1)}, bf16[128,1024]{1,0:T(8,128)(2,1)S(1)}, u32[]{:S(2)}, u32[]{:S(2)}) collective-permute-start(bf16[128,1024]{1,0:T(8,128)(2,1)S(1)} %pad_maximum_fusion.3), channel_id=1, source_target_pairs={{0,4},{1,5},{2,6},{3,7},{4,0},{5,1},{6,2},{7,3},{8,12},{9,13},{10,... | collective-permute-start | bytes 786440 | tf_op jit(solution)/shard_map/ppermute | solution.py:285
  128.4 7.7 %collective-permute-start.22 = (bf16[128,1024]{1,0:T(8,128)(2,1)S(1)}, bf16[128,1024]{1,0:T(8,128)(2,1)S(1)}, u32[]{:S(2)}, u32[]{:S(2)}) collective-permute-start(bf16[128,1024]{1,0:T(8,128)(2,1)S(1)} %pad_maximum_fusion.3), channel_id=1, source_target_pairs={{0,6},{1,7},{2,4},{3,5},{4,2},{5,3},{6,0},{7,1},{8,14},{9,15},{10,... | collective-permute-start | bytes 786440 | tf_op jit(solution)/shard_map/ppermute | solution.py:285
  129.7 14.4 %collective-permute-start.6 = (bf16[2,2,16,1024]{3,2,1,0:T(8,128)(2,1)S(1)}, bf16[2,2,16,1024]{3,2,1,0:T(8,128)(2,1)S(1)}, u32[]{:S(2)}, u32[]{:S(2)}) collective-permute-start(bf16[2,2,16,1024]{3,2,1,0:T(8,128)(2,1)S(1)} %fusion.8), channel_id=1, source_target_pairs={{0,2},{1,3},{2,0},{3,1},{4,6},{5,7},{6,4},{7,5},{8,10},{9,11},{10,... | collective-permute-start | bytes 393224 | tf_op jit(solution)/shard_map/ppermute | solution.py:285
  137.6 42.0 %collective-permute-start.25 = (bf16[512,1024]{1,0:T(8,128)(2,1)}, bf16[512,1024]{1,0:T(8,128)(2,1)S(1)}, u32[]{:S(2)}, u32[]{:S(2)}) collective-permute-start(bf16[512,1024]{1,0:T(8,128)(2,1)} %pad_maximum_fusion.2), channel_id=1, source_target_pairs={{0,1},{1,0},{2,3},{3,2},{4,5},{5,4},{6,7},{7,6},{8,9},{9,8},{10,11... | collective-permute-start | bytes 3145736 | tf_op jit(solution)/shard_map/ppermute | solution.py:285
  144.2 7.9 %collective-permute-start.7 = (bf16[2,1,16,1024]{3,2,0,1:T(8,128)(2,1)S(1)}, bf16[2,1,16,1024]{3,2,0,1:T(8,128)(2,1)S(1)}, u32[]{:S(2)}, u32[]{:S(2)}) collective-permute-start(bf16[2,1,16,1024]{3,2,0,1:T(8,128)(2,1)S(1)} %fusion.12), channel_id=1, source_target_pairs={{0,4},{1,5},{2,6},{3,7},{4,0},{5,1},{6,2},{7,3},{8,12},{9,13},{10,... | collective-permute-start | bytes 196616 | tf_op jit(solution)/shard_map/ppermute | solution.py:285
  145.5 11.4 %collective-permute-start.9 = (bf16[1024,256]{1,0:T(8,128)(2,1)S(1)}, bf16[1024,256]{1,0:T(8,128)(2,1)S(1)}, u32[]{:S(2)}, u32[]{:S(2)}) collective-permute-start(bf16[1024,256]{1,0:T(8,128)(2,1)S(1)} %copy-done.13), channel_id=1, source_target_pairs={{1,0},{2,1},{3,2},{4,3},{5,4},{6,5},{7,6},{9,8},{10,9},{11,10},{12... | collective-permute-start | bytes 1572872 | tf_op jit(solution)/shard_map/ppermute | solution.py:392
  147.7 14.8 %collective-permute-start.8 = (bf16[1024,256]{1,0:T(8,128)(2,1)S(1)}, bf16[1024,256]{1,0:T(8,128)(2,1)S(1)}, u32[]{:S(2)}, u32[]{:S(2)}) collective-permute-start(bf16[1024,256]{1,0:T(8,128)(2,1)S(1)} %copy-done.12), channel_id=1, source_target_pairs={{1,0},{2,1},{3,2},{4,3},{5,4},{6,5},{7,6},{9,8},{10,9},{11,10},{12... | collective-permute-start | bytes 1572872 | tf_op jit(solution)/shard_map/ppermute | solution.py:392
  149.9 18.4 %collective-permute-start.11 = (bf16[1024,256]{1,0:T(8,128)(2,1)S(1)}, bf16[1024,256]{1,0:T(8,128)(2,1)}, u32[]{:S(2)}, u32[]{:S(2)}) collective-permute-start(bf16[1024,256]{1,0:T(8,128)(2,1)S(1)} %copy-done.15), channel_id=1, source_target_pairs={{1,0},{2,1},{3,2},{4,3},{5,4},{6,5},{7,6},{9,8},{10,9},{11,10},{12... | collective-permute-start | bytes 1572872 | tf_op jit(solution)/shard_map/ppermute | solution.py:392
  152.2 21.7 %collective-permute-start.10 = (bf16[1024,256]{1,0:T(8,128)(2,1)S(1)}, bf16[1024,256]{1,0:T(8,128)(2,1)}, u32[]{:S(2)}, u32[]{:S(2)}) collective-permute-start(bf16[1024,256]{1,0:T(8,128)(2,1)S(1)} %copy-done.14), channel_id=1, source_target_pairs={{1,0},{2,1},{3,2},{4,3},{5,4},{6,5},{7,6},{9,8},{10,9},{11,10},{12... | collective-permute-start | bytes 1572872 | tf_op jit(solution)/shard_map/ppermute | solution.py:392
  (19 other events, 172.0 us)
where the time goes:
time: 183 us
  Pallas kernels  65 us (36%)
  waiting for transfers between devices  50 us (27%)
  starting transfers between devices  41.2 us (23%)
  other arithmetic  11.1 us (6%)
  matrix products  10.5 us (6%)
  local copies, waits for them, and re-layouts  3.74 us (2%)
    pallas_call x4, Pallas kernels, backward(): pl.pallas_call(functools.partial(backward_kernel, nb=nb), grid=(count,),...  32.3 us
    ppermute x20, waiting for transfers between devices, swap(): lax.ppermute(x, axis, [(i, i ^ bits) for i in range(lax.axis_size(axis))])  31.4 us
    ppermute x20, starting transfers between devices, swap(): lax.ppermute(x, axis, [(i, i ^ bits) for i in range(lax.axis_size(axis))])  27.3 us
    pallas_call x2, Pallas kernels, forward(): pl.pallas_call(functools.partial(forward_kernel, nb=nb), grid_spec=pltpu....  27 us
    ppermute x4, waiting for transfers between devices, per_device(): backs.append(lax.ppermute(dh, 'ctx', back))  18.6 us
    dot_general x5, matrix products, dot(): return lax.dot_general(a, b, dims, preferred_element_type=f32)  10.5 us
    ppermute x4, starting transfers between devices, per_device(): backs.append(lax.ppermute(dh, 'ctx', back))  8.48 us
    pallas_call x1, Pallas kernels, finish(): pl.pallas_call(finish_kernel, grid=(n,), in_specs=[pl.BlockSpec((1, mine)...  5.68 us
  transfers between devices with their start and end apart: 26, of which 10 were waited for; matrix products, arithmetic and copies ran while one was open for 7% of the time, Pallas kernels for 28%

commit v1 on v0

--- a/solution.py
+++ b/solution.py
@@ -1,5 +1,4 @@
 import functools
-import math
 
 import jax
 import jax.numpy as jnp
@@ -174,7 +173,7 @@
             jax.ShapeDtypeStruct((count, nb * TWO, 2 * SPAN), bf16),
         ],
         input_output_aliases=alias,
-        compiler_params=pltpu.CompilerParams(vmem_limit_bytes=60 << 20),
+        compiler_params=pltpu.CompilerParams(vmem_limit_bytes=67_000_000),
         cost_estimate=pl.CostEstimate(
             flops=count * nb * 12 * TWO * BLK * 1024, bytes_accessed=count * (4 << 20), transcendentals=count << 20
         ),
@@ -182,7 +181,7 @@
     )(*args)
 
 
-def backward(q, pt, ga, ko, vo, kh, vh, km, vm, start, count, base, halo_at, at, carry):
+def backward(q, pt, ga, ko, vo, kh, vh, km, vm, start, count, base, halo_at, at, carry, dh_total, dh_at):
     tokens, width = q.shape
     slots, hrows, nb = km.shape[0], kh.shape[0], tokens // BLK
     keys = hrows + tokens + slots
@@ -207,7 +206,7 @@
         in_specs=specs,
         out_specs=[
             columns(tokens, start), columns(tokens, start), columns(tokens, start),
-            columns(2 * slots, start), columns(2 * hrows, 0),
+            columns(2 * slots, start), columns(2 * hrows, dh_at),
         ],
         scratch_shapes=[
             pltpu.VMEM((keys, SPAN), bf16), pltpu.VMEM((keys, 2 * SPAN), bf16),
@@ -218,10 +217,10 @@
             jax.ShapeDtypeStruct((tokens, width), f32),
             jax.ShapeDtypeStruct((tokens, width), f32),
             jax.ShapeDtypeStruct((2 * slots, width), bf16),
-            jax.ShapeDtypeStruct((2 * hrows, count * SPAN), bf16),
+            jax.ShapeDtypeStruct((2 * hrows, dh_total * SPAN), bf16),
         ],
         input_output_aliases=alias,
-        compiler_params=pltpu.CompilerParams(vmem_limit_bytes=60 << 20),
+        compiler_params=pltpu.CompilerParams(vmem_limit_bytes=67_000_000),
         cost_estimate=pl.CostEstimate(
             flops=count * nb * 20 * TWO * BLK * 1024, bytes_accessed=count * (6 << 20), transcendentals=0
         ),
@@ -229,7 +228,7 @@
     )(*args)
 
 
-def finish_kernel(slot_ref, dk_in, dv_in, mk_ref, mv_ref, *rest):
+def finish_kernel(slot_ref, dk_in, dv_in, mk_ref, mv_ref, *rest, groups):
     backs, (dk_ref, dv_ref) = rest[:-2], rest[-2:]
     tokens = dk_in.shape[0]
     mine = slot_ref.shape[1]
@@ -237,27 +236,34 @@
     dk = dk_in[...] + dot(pick, mk_ref[...], NN)
     dv = dv_in[...] + dot(pick, mv_ref[...], NN)
     edge = tokens - W
-    for i, back in enumerate(backs):
-
-        @pl.when(pl.program_id(0) == i)
+    if edge:
+        dk_ref[:edge, :] = dk[:edge].astype(bf16)
+        dv_ref[:edge, :] = dv[:edge].astype(bf16)
+    pair = pl.program_id(0)
+    for back, (at, count) in zip(backs, groups):
+
+        @pl.when((pair >= at) & (pair < at + count))
         def _():
             dk_ref[edge:, :] = (dk[edge:] + back[:W, :].astype(f32)).astype(bf16)
             dv_ref[edge:, :] = (dv[edge:] + back[W:, :].astype(f32)).astype(bf16)
 
 
-def finish(slots, dko, dvo, dmem, backs):
+def finish(slots, dko, dvo, dmem, backs, groups):
     tokens, width = dko.shape
-    mine, n = slots.shape[0], len(backs)
-    step = width // n
-    col = lambda r, j: pl.BlockSpec((r, step), lambda i: (j, i))
+    mine = slots.shape[0]
+
+    def back_columns(at, count):
+        return pl.BlockSpec((2 * W, SPAN), lambda p: (0, jnp.clip(p - at, 0, count - 1)))
+
+    col = lambda rows, j: pl.BlockSpec((rows, SPAN), lambda p: (j, p))
     return pl.pallas_call(
-        finish_kernel,
-        grid=(n,),
-        in_specs=[pl.BlockSpec((1, mine), lambda i: (0, 0)), col(tokens, 0), col(tokens, 0), col(mine, 0), col(mine, 1)]
-        + [pl.BlockSpec((2 * W, step), lambda i: (0, 0))] * n,
+        functools.partial(finish_kernel, groups=groups),
+        grid=(width // SPAN,),
+        in_specs=[pl.BlockSpec((1, mine), lambda p: (0, 0)), col(tokens, 0), col(tokens, 0), col(mine, 0), col(mine, 1)]
+        + [back_columns(*g) for g in groups],
         out_specs=[col(tokens, 0), col(tokens, 0)],
         out_shape=[jax.ShapeDtypeStruct((tokens, width), bf16)] * 2,
-        compiler_params=pltpu.CompilerParams(vmem_limit_bytes=60 << 20),
+        compiler_params=pltpu.CompilerParams(vmem_limit_bytes=67_000_000),
         cost_estimate=pl.CostEstimate(flops=1 << 26, bytes_accessed=8 << 20, transcendentals=0),
         name="finish_rows",
     )(slots[None, :], dko, dvo, dmem, dmem, *backs)
@@ -325,6 +331,13 @@
         upper = (me & bit) != 0
         parts = [jnp.where(upper, parts[j ^ bit], parts[j]) for j in range(n)]
     return jnp.concatenate(parts, 0)
+
+
+def groups_of(pairs):
+    if pairs % 8:
+        return [pairs], [(0, 0, pairs)], [pairs]
+    u = pairs // 8
+    return [u, 3 * u, 4 * u], [(0, 0, u), (1, 0, 3 * u), (2, 0, 2 * u), (2, 2 * u, 2 * u)], [4 * u, 2 * u, 2 * u]
 
 
 def per_device(queries, key_rows, value_rows, cotangent, out_weight, prot_blocks, last_fill, memory_slots):
@@ -338,15 +351,14 @@
     mine = total // nctx
     nb = tokens // BLK
     pairs = width // SPAN
-    fgroups, bgroups = math.gcd(pairs, 2), math.gcd(pairs, 4)
-    fcount, bcount = pairs // fgroups, pairs // bgroups
-    step = fcount * SPAN
+    fsizes, bplan, dhs = groups_of(pairs)
+    fstarts = [sum(fsizes[:i]) for i in range(len(fsizes))]
     shift = [(i, i + 1) for i in range(nctx - 1)]
     back = [(i + 1, i) for i in range(nctx - 1)]
     edge = tokens - W
     halos = []
-    for i in range(fgroups):
-        cols = slice(i * step, (i + 1) * step)
+    for i, (at, count) in enumerate(zip(fstarts, fsizes)):
+        cols = slice(at * SPAN, (at + count) * SPAN)
         halos.append(lax.ppermute(jnp.concatenate([k[edge:, cols], v[edge:, cols]], 1), "ctx", shift))
     own_slots = lax.dynamic_slice_in_dim(slots, me * mine, mine)
     pick = (own_slots[:, None] == jnp.arange(tokens, dtype=jnp.int32)[None, :]).astype(bf16)
@@ -362,10 +374,10 @@
     bias = jnp.broadcast_to(jnp.where(seen, 0.0, NEG).astype(f32)[:, :, None], (nb, total, BLK))
     base = (0, pairs)
     att, saved = None, []
-    for i in range(fgroups):
+    for i, (at, count) in enumerate(zip(fstarts, fsizes)):
         att, pt, ga = forward(
             info, q, grad_attn, k, v, halos[i], halos[i], mem, mem, bias,
-            i * fcount, fcount, base, (0, fcount), att)
+            at, count, base, (0, count), att)
         saved.append((pt, ga))
     core = me & 1
     half = width // 2
@@ -374,22 +386,18 @@
     sent = swap(dot(your_att, cot, TN).astype(bf16), "ctx", 1)
     kept = dot(mine_att, cot, TN)
 
-    carry = None
-
-    def run(i, carry):
-        at = i * bcount
-        j = at // fcount
-        r = at - j * fcount
-        pt, ga = saved[j]
-        out = backward(
-            q, pt, ga, k, v, halos[j], halos[j], mem, mem,
-            at, bcount, base, (r, fcount + r), r, carry)
-        return list(out[:4]), out[4]
-
-    backs = []
-    for i in range(bgroups):
-        carry, dh = run(i, carry)
-        backs.append(lax.ppermute(dh, "ctx", back))
+    carry, backs, i = [], [], 0
+    for total_dh in dhs:
+        done = 0
+        while done < total_dh:
+            j, r, count = bplan[i]
+            pt, ga = saved[j]
+            out = backward(
+                q, pt, ga, k, v, halos[j], halos[j], mem, mem, fstarts[j] + r, count,
+                base, (r, fsizes[j] + r), r, carry, total_dh, done)
+            carry = list(out)
+            done, i = done + count, i + 1
+        backs.append(lax.ppermute(carry.pop(), "ctx", back))
     plane = nctx // 2
     total_w = kept + sent.astype(f32)
     total_w = exchange(total_w, "ctx", 1, me >> 1, plane)
@@ -402,7 +410,8 @@
     weight = jnp.concatenate([jnp.where(upper, other, w), jnp.where(upper, w, other)], 0).astype(f32) * scale
     dq, dko, dvo, dm = carry
     dmem = halve(dm.reshape(2, nctx, mine, width), "ctx", me).reshape(2 * mine, width).astype(bf16)
-    dk, dv = finish(own_slots, dko, dvo, dmem, backs)
+    dk, dv = finish(
+        own_slots, dko, dvo, dmem, backs, [(sum(dhs[:i]), n) for i, n in enumerate(dhs)])
     return dq[None], dk[None], dv[None], weight
 
 

time: 183 us -> 195 us (1.066)
  the two profiles are of different devices: /device:TPU:3 before, /device:TPU:11 now
where the time goes in v1:
time: 195 us; the launch traced here: 194 us
  Pallas kernels  69.6 us (36%)
  starting transfers between devices  53.6 us (27%)
  waiting for transfers between devices  35.1 us (18%)
  other arithmetic  15.8 us (8%)
  matrix products  12.4 us (6%)
  local copies, waits for them, and re-layouts  6.39 us (3%)
    ppermute x20, waiting for transfers between devices, swap(): lax.ppermute(x, axis, [(i, i ^ bits) for i in range(lax.axis_size(axis))])  35 us
    ppermute x20, starting transfers between devices, swap(): lax.ppermute(x, axis, [(i, i ^ bits) for i in range(lax.axis_size(axis))])  34 us
    pallas_call x4, Pallas kernels, backward(): pl.pallas_call(functools.partial(backward_kernel, nb=nb), grid=(count,),...  32.1 us
    pallas_call x3, Pallas kernels, forward(): pl.pallas_call(functools.partial(forward_kernel, nb=nb), grid_spec=pltpu....  30 us
    dot_general x5, matrix products, dot(): return lax.dot_general(a, b, dims, preferred_element_type=f32)  12.4 us
    ppermute x3, starting transfers between devices, per_device(): backs.append(lax.ppermute(carry.pop(), 'ctx', back))  11 us
    ppermute x3, starting transfers between devices, per_device(): lax.ppermute(jnp.concatenate([k[edge:, cols], v[edge:, cols]], 1), 'ctx',...  8.58 us
    pallas_call x1, Pallas kernels, finish(): pl.pallas_call(functools.partial(finish_kernel, groups=groups), grid=(wid...  7.46 us
  transfers between devices with their start and end apart: 26, of which 5 were waited for; matrix products, arithmetic and copies ran while one was open for 7% of the time, Pallas kernels for 29%

profile of v1, /device:TPU:11, one launch (start us, length us, event | category | flops | bytes accessed | tf_op | source)
XLA Modules:
  0.0 194.0 jit_solution(6395631791833151264)
XLA Ops:
  5.4 3.0 %collective-permute-start.5 = (bf16[512,256]{1,0:T(8,128)(2,1)S(1)}, bf16[512,256]{1,0:T(8,128)(2,1)}, u32[]{:S(2)}, u32[]{:S(2)}) collective-permute-start(bf16[512,256]{1,0:T(8,128)(2,1)S(1)} %pad_maximum_fusion.3), channel_id=1, source_target_pairs={{0,1},{1,2},{2,3},{3,4},{4,5},{5,6},{6,7},{8,9},{9,10},{10,11},{11... | collective-permute-start | bytes 786440 | tf_op jit(solution)/shard_map/ppermute | solution.py:362
  9.5 2.5 %collective-permute-start.4 = (bf16[512,768]{1,0:T(8,128)(2,1)}, bf16[512,768]{1,0:T(8,128)(2,1)}, u32[]{:S(2)}, u32[]{:S(2)}) collective-permute-start(bf16[512,768]{1,0:T(8,128)(2,1)} %pad_maximum_fusion.2), channel_id=1, source_target_pairs={{0,1},{1,2},{2,3},{3,4},{4,5},{5,6},{6,7},{8,9},{9,10},{10,11},{11... | collective-permute-start | bytes 2359304 | tf_op jit(solution)/shard_map/ppermute | solution.py:362
  13.3 3.0 %collective-permute-start = (bf16[512,1024]{1,0:T(8,128)(2,1)}, bf16[512,1024]{1,0:T(8,128)(2,1)}, u32[]{:S(2)}, u32[]{:S(2)}) collective-permute-start(bf16[512,1024]{1,0:T(8,128)(2,1)} %pad_maximum_fusion), channel_id=1, source_target_pairs={{0,1},{1,2},{2,3},{3,4},{4,5},{5,6},{6,7},{8,9},{9,10},{10,11},{11... | collective-permute-start | bytes 3145736 | tf_op jit(solution)/shard_map/ppermute | solution.py:362
  16.9 3.8 %convolution_convert_fusion.g_ref = bf16[512,1024]{1,0:T(8,128)(2,1)} fusion(bf16[1024,1024]{1,0:T(8,128)(2,1)} %param.12, bf16[1,512,1024]{2,1,0:T(8,128)(2,1)S(1)} %copy-done.9), kind=kOutput, calls=%fused_computation.2 | convolution fusion | flops 1074266112 | bytes 4194304 | tf_op jit(solution)/shard_map/dot_general | solution.py:26
  22.2 13.7 %collective-permute-done.2 = bf16[32,2048]{1,0:T(8,128)(2,1)S(1)} collective-permute-done((bf16[32,2048]{1,0:T(8,128)(2,1)S(1)}, bf16[32,2048]{1,0:T(8,128)(2,1)S(1)}, u32[]{:S(2)}, u32[]{:S(2)}) %collective-permute-start.2) | collective-permute-done | bytes 131104 | tf_op jit(solution)/shard_map/ppermute | solution.py:291
  37.8 3.4 %collective-permute-done.3 = bf16[64,2048]{1,0:T(8,128)(2,1)S(1)} collective-permute-done((bf16[64,2048]{1,0:T(8,128)(2,1)S(1)}, bf16[64,2048]{1,0:T(8,128)(2,1)S(1)}, u32[]{:S(2)}, u32[]{:S(2)}) %collective-permute-start.3) | collective-permute-done | bytes 262176 | tf_op jit(solution)/shard_map/ppermute | solution.py:291
  43.0 5.6 %band_forward.3 = (bf16[512,1024]{1,0:T(8,128)(2,1)}, bf16[1,1152,1024]{2,1,0:T(8,128)(2,1)}, bf16[1,1024,256]{2,1,0:T(8,128)(2,1)}) custom-call(s32[2,4]{1,0:T(2,128)} %pad_add_fusion.1.info_ref, bf16[512,1024]{1,0:T(8,128)(2,1)} %bitcast.126, bf16[512,1024]{1,0:T(8,128)(2,1)} %convolution_convert_fusion.g_ref, bf16[512,1024]{1,0:T(8,128)(2,1)} %bitcast.106, ...), custom_call_target="tpu_custom_call" | custom-call | flops 1610612736 | bytes 4194304 | tf_op jit(solution)/shard_map/band_forward/pallas_call | solution.py:157
  48.6 11.0 %band_forward.4 = (bf16[512,1024]{1,0:T(8,128)(2,1)}, bf16[3,1152,1024]{2,1,0:T(8,128)(2,1)}, bf16[3,1024,256]{2,1,0:T(8,128)(2,1)}) custom-call(s32[2,4]{1,0:T(2,128)} %pad_add_fusion.1.info_ref, bf16[512,1024]{1,0:T(8,128)(2,1)} %bitcast.127, bf16[512,1024]{1,0:T(8,128)(2,1)} %convolution_convert_fusion.g_ref, ...), custom_call_target="tpu_custom_call", output_to_operand_aliasing={{0}: (10, {})} | custom-call | flops 4831838208 | bytes 12582912 | tf_op jit(solution)/shard_map/band_forward/pallas_call | solution.py:157
  59.6 13.5 %band_forward.5 = (bf16[512,1024]{1,0:T(8,128)(2,1)}, bf16[4,1152,1024]{2,1,0:T(8,128)(2,1)}, bf16[4,1024,256]{2,1,0:T(8,128)(2,1)}) custom-call(s32[2,4]{1,0:T(2,128)} %pad_add_fusion.1.info_ref, bf16[512,1024]{1,0:T(8,128)(2,1)} %bitcast.128, bf16[512,1024]{1,0:T(8,128)(2,1)} %convolution_convert_fusion.g_ref, ...), custom_call_target="tpu_custom_call", output_to_operand_aliasing={{0}: (10, {})} | custom-call | flops 6442450944 | bytes 16777216 | tf_op jit(solution)/shard_map/band_forward/pallas_call | solution.py:157
  73.1 3.1 %convolution_convert_fusion.1 = bf16[512,1024]{1,0:T(8,128)(2,1)} fusion(bf16[1,512,1024]{2,1,0:T(8,128)(2,1)} %param.11, bf16[512,1024]{1,0:T(8,128)(2,1)} %get-tuple-element.65, s32[]{:T(128)S(6)} %select_n.279), kind=kOutput, calls=%fused_computation.3 | convolution fusion | flops 537395200 | bytes 2621444 | tf_op jit(solution)/shard_map/dot_general | solution.py:26
  76.2 5.3 %band_backward.4 = (bf16[512,1024]{1,0:T(8,128)(2,1)}, f32[512,1024]{1,0:T(8,128)}, f32[512,1024]{1,0:T(8,128)}, bf16[256,1024]{1,0:T(8,128)(2,1)}, bf16[1024,512]{1,0:T(8,128)(2,1)}) custom-call(bf16[512,1024]{1,0:T(8,128)(2,1)} %bitcast.129, bf16[1,1152,1024]{2,1,0:T(8,128)(2,1)} %get-tuple-element.41.pt_ref, ...), custom_call_target="tpu_custom_call" | custom-call | flops 2684354560 | bytes 6291456 | tf_op jit(solution)/shard_map/band_backward/pallas_call | solution.py:203
  81.4 10.6 %band_backward.5 = (bf16[512,1024]{1,0:T(8,128)(2,1)}, f32[512,1024]{1,0:T(8,128)}, f32[512,1024]{1,0:T(8,128)}, bf16[256,1024]{1,0:T(8,128)(2,1)}, bf16[1024,512]{1,0:T(8,128)(2,1)}) custom-call(bf16[512,1024]{1,0:T(8,128)(2,1)} %bitcast.130, ...), custom_call_target="tpu_custom_call", output_to_operand_aliasing={{0}: (9, {}), {1}: (10, {}), {2}: (11, {}), {3}: (12, {}), ... | custom-call | flops 8053063680 | bytes 18874368 | tf_op jit(solution)/shard_map/band_backward/pallas_call | solution.py:203
  92.1 2.4 %convert_add_fusion = f32[512,1024]{1,0:T(8,128)S(1)} fusion(bf16[512,1024]{1,0:T(8,128)(2,1)} %collective-permute-done.12, bf16[1,512,1024]{2,1,0:T(8,128)(2,1)} %param.11, bf16[512,1024]{1,0:T(8,128)(2,1)} %get-tuple-element.65, s32[]{:T(128)S(6)} %select_n.278), kind=kOutput, calls=%fused_computation.1 | convolution fusion | flops 537919488 | bytes 4718596 | tf_op jit(solution)/shard_map/dot_general | solution.py:26
  99.4 8.2 %band_backward.6 = (bf16[512,1024]{1,0:T(8,128)(2,1)}, f32[512,1024]{1,0:T(8,128)}, f32[512,1024]{1,0:T(8,128)}, bf16[256,1024]{1,0:T(8,128)(2,1)}, bf16[1024,256]{1,0:T(8,128)(2,1)}) custom-call(bf16[512,1024]{1,0:T(8,128)(2,1)} %bitcast.131, ...), custom_call_target="tpu_custom_call", output_to_operand_aliasing={{0}: (9, {}), {1}: (10, {}), {2}: (11, {}), {3}: (12, {})} | custom-call | flops 5368709120 | bytes 12582912 | tf_op jit(solution)/shard_map/band_backward/pallas_call | solution.py:203
  107.6 3.5 %collective-permute-done.15 = bf16[128,1024]{1,0:T(8,128)(2,1)} collective-permute-done((bf16[128,1024]{1,0:T(8,128)(2,1)}, bf16[128,1024]{1,0:T(8,128)(2,1)}, u32[]{:S(2)}, u32[]{:S(2)}) %collective-permute-start.15) | collective-permute-done | bytes 262176 | tf_op jit(solution)/shard_map/ppermute | solution.py:291
  114.2 2.4 %collective-permute-start.18 = (bf16[32,1024]{1,0:T(8,128)(2,1)}, bf16[32,1024]{1,0:T(8,128)(2,1)}, u32[]{:S(2)}, u32[]{:S(2)}) collective-permute-start(bf16[32,1024]{1,0:T(8,128)(2,1)} %get-tuple-element.77), channel_id=1, source_target_pairs={{0,24},{8,16},{16,8},{24,0},{1,25},{9,17},{17,9},{25,1},{2,26},{10... | collective-permute-start | bytes 196616 | tf_op jit(solution)/shard_map/ppermute | solution.py:291
  117.5 8.0 %band_backward.7 = (bf16[512,1024]{1,0:T(8,128)(2,1)}, f32[512,1024]{1,0:T(8,128)}, f32[512,1024]{1,0:T(8,128)}, bf16[256,1024]{1,0:T(8,128)(2,1)}, bf16[1024,256]{1,0:T(8,128)(2,1)}) custom-call(bf16[512,1024]{1,0:T(8,128)(2,1)} %bitcast.132, ...), custom_call_target="tpu_custom_call", output_to_operand_aliasing={{0}: (9, {}), {1}: (10, {}), {2}: (11, {}), {3}: (12, {})} | custom-call | flops 5368709120 | bytes 12582912 | tf_op jit(solution)/shard_map/band_backward/pallas_call | solution.py:203
  130.5 4.5 %collective-permute-start.6 = (bf16[2,4,16,1024]{3,2,1,0:T(8,128)(2,1)S(1)}, bf16[2,4,16,1024]{3,2,1,0:T(8,128)(2,1)S(1)}, u32[]{:S(2)}, u32[]{:S(2)}) collective-permute-start(bf16[2,4,16,1024]{3,2,1,0:T(8,128)(2,1)S(1)} %select_bitcast_fusion), channel_id=1, source_target_pairs={{0,1},{1,0},{2,3},{3,2},{4,5},{5,4},{6,7},{7,6},{8,9},{9,8},{10,11... | collective-permute-start | bytes 786440 | tf_op jit(solution)/shard_map/ppermute | solution.py:291
  137.9 5.4 %collective-permute-start.9 = (bf16[1024,512]{1,0:T(8,128)(2,1)S(1)}, bf16[1024,512]{1,0:T(8,128)(2,1)}, u32[]{:S(2)}, u32[]{:S(2)}) collective-permute-start(bf16[1024,512]{1,0:T(8,128)(2,1)S(1)} %copy-done.12), channel_id=1, source_target_pairs={{1,0},{2,1},{3,2},{4,3},{5,4},{6,5},{7,6},{9,8},{10,9},{11,10},{12... | collective-permute-start | bytes 3145736 | tf_op jit(solution)/shard_map/ppermute | solution.py:400
  147.2 15.2 %collective-permute-start.25 = (bf16[512,1024]{1,0:T(8,128)(2,1)}, bf16[512,1024]{1,0:T(8,128)(2,1)}, u32[]{:S(2)}, u32[]{:S(2)}) collective-permute-start(bf16[512,1024]{1,0:T(8,128)(2,1)} %pad_maximum_fusion.1), channel_id=1, source_target_pairs={{0,1},{1,0},{2,3},{3,2},{4,5},{5,4},{6,7},{7,6},{8,9},{9,8},{10,11... | collective-permute-start | bytes 3145736 | tf_op jit(solution)/shard_map/ppermute | solution.py:291
  164.5 3.7 %collective-permute-start.10 = (bf16[1024,256]{1,0:T(8,128)(2,1)S(1)}, bf16[1024,256]{1,0:T(8,128)(2,1)}, u32[]{:S(2)}, u32[]{:S(2)}) collective-permute-start(bf16[1024,256]{1,0:T(8,128)(2,1)S(1)} %copy-done.13), channel_id=1, source_target_pairs={{1,0},{2,1},{3,2},{4,3},{5,4},{6,5},{7,6},{9,8},{10,9},{11,10},{12... | collective-permute-start | bytes 1572872 | tf_op jit(solution)/shard_map/ppermute | solution.py:400
  169.1 12.1 %collective-permute-done.8 = bf16[2,1,16,1024]{3,2,0,1:T(8,128)(2,1)S(1)} collective-permute-done((bf16[2,1,16,1024]{3,2,0,1:T(8,128)(2,1)S(1)}, bf16[2,1,16,1024]{3,2,0,1:T(8,128)(2,1)S(1)}, u32[]{:S(2)}, u32[]{:S(2)}) %collective-permute-start.8) | collective-permute-done | bytes 65568 | tf_op jit(solution)/shard_map/ppermute | solution.py:291
  181.9 7.5 %finish_rows.1 = (bf16[512,1024]{1,0:T(8,128)(2,1)}, bf16[512,1024]{1,0:T(8,128)(2,1)}) custom-call(s32[1,16]{1,0:T(1,128)} %constant_dynamic-slice_fusion.slot_ref, f32[512,1024]{1,0:T(8,128)} %get-tuple-element.57.dk_in, f32[512,1024]{1,0:T(8,128)} %get-tuple-element.58.dv_in, bf16[32,1024]{1,0:T(8,128)(2,1)} %bitcast.138, bf16[32,1024]{1,0:T(8,128)(2,1)} %bitcast.139, ...), custom_call_target="tpu_custom_call" | custom-call | flops 67108864 | bytes 8388608 | tf_op jit(solution)/shard_map/finish_rows/pallas_call | solution.py:259
  191.4 2.6 %convert_multiply_fusion = f32[1024,1024]{1,0:T(8,128)} fusion(bf16[512,1024]{1,0:T(8,128)(2,1)S(1)} %get-tuple-element.69, bf16[512,1024]{1,0:T(8,128)(2,1)S(1)} %get-tuple-element.68), kind=kLoop, calls=%fused_computation | loop fusion | flops 5242880 | bytes 6291456 | tf_op jit(solution)/shard_map/mul | solution.py:410
  (120 shorter events, 38.7 us)
Async XLA Ops:
  4.6 16.3 %collective-permute-start.1 = (bf16[16,2048]{1,0:T(8,128)(2,1)S(1)}, bf16[16,2048]{1,0:T(8,128)(2,1)}, u32[]{:S(2)}, u32[]{:S(2)}) collective-permute-start(bf16[16,2048]{1,0:T(8,128)(2,1)S(1)} %pad_maximum_fusion.5), channel_id=1, source_target_pairs={{0,1},{1,0},{2,3},{3,2},{4,5},{5,4},{6,7},{7,6},{8,9},{9,8},{10,11... | collective-permute-start | bytes 196616 | tf_op jit(solution)/shard_map/ppermute | solution.py:291
  5.4 36.7 %collective-permute-start.5 = (bf16[512,256]{1,0:T(8,128)(2,1)S(1)}, bf16[512,256]{1,0:T(8,128)(2,1)}, u32[]{:S(2)}, u32[]{:S(2)}) collective-permute-start(bf16[512,256]{1,0:T(8,128)(2,1)S(1)} %pad_maximum_fusion.3), channel_id=1, source_target_pairs={{0,1},{1,2},{2,3},{3,4},{4,5},{5,6},{6,7},{8,9},{9,10},{10,11},{11... | collective-permute-start | bytes 786440 | tf_op jit(solution)/shard_map/ppermute | solution.py:362
  9.5 39.1 %collective-permute-start.4 = (bf16[512,768]{1,0:T(8,128)(2,1)}, bf16[512,768]{1,0:T(8,128)(2,1)}, u32[]{:S(2)}, u32[]{:S(2)}) collective-permute-start(bf16[512,768]{1,0:T(8,128)(2,1)} %pad_maximum_fusion.2), channel_id=1, source_target_pairs={{0,1},{1,2},{2,3},{3,4},{4,5},{5,6},{6,7},{8,9},{9,10},{10,11},{11... | collective-permute-start | bytes 2359304 | tf_op jit(solution)/shard_map/ppermute | solution.py:362
  13.3 46.4 %collective-permute-start = (bf16[512,1024]{1,0:T(8,128)(2,1)}, bf16[512,1024]{1,0:T(8,128)(2,1)}, u32[]{:S(2)}, u32[]{:S(2)}) collective-permute-start(bf16[512,1024]{1,0:T(8,128)(2,1)} %pad_maximum_fusion), channel_id=1, source_target_pairs={{0,1},{1,2},{2,3},{3,4},{4,5},{5,6},{6,7},{8,9},{9,10},{10,11},{11... | collective-permute-start | bytes 3145736 | tf_op jit(solution)/shard_map/ppermute | solution.py:362
  21.8 14.1 %collective-permute-start.2 = (bf16[32,2048]{1,0:T(8,128)(2,1)S(1)}, bf16[32,2048]{1,0:T(8,128)(2,1)S(1)}, u32[]{:S(2)}, u32[]{:S(2)}) collective-permute-start(bf16[32,2048]{1,0:T(8,128)(2,1)S(1)} %maximum_select_fusion.2), channel_id=1, source_target_pairs={{0,2},{1,3},{2,0},{3,1},{4,6},{5,7},{6,4},{7,5},{8,10},{9,11},{10,... | collective-permute-start | bytes 393224 | tf_op jit(solution)/shard_map/ppermute | solution.py:291
  76.2 15.9 %collective-permute-start.12 = (bf16[512,1024]{1,0:T(8,128)(2,1)}, bf16[512,1024]{1,0:T(8,128)(2,1)}, u32[]{:S(2)}, u32[]{:S(2)}) collective-permute-start(bf16[512,1024]{1,0:T(8,128)(2,1)} %convolution_convert_fusion.1), channel_id=1, source_target_pairs={{0,1},{1,0},{2,3},{3,2},{4,5},{5,4},{6,7},{7,6},{8,9},{9,8},{10,11... | collective-permute-start | bytes 3145736 | tf_op jit(solution)/shard_map/ppermute | solution.py:291
  96.8 10.8 %collective-permute-start.13 = (bf16[128,1024]{1,0:T(8,128)(2,1)}, bf16[128,1024]{1,0:T(8,128)(2,1)}, u32[]{:S(2)}, u32[]{:S(2)}) collective-permute-start(bf16[128,1024]{1,0:T(8,128)(2,1)} %get-tuple-element.70), channel_id=1, source_target_pairs={{0,2},{1,3},{2,0},{3,1},{4,6},{5,7},{6,4},{7,5},{8,10},{9,11},{10,... | collective-permute-start | bytes 786440 | tf_op jit(solution)/shard_map/ppermute | solution.py:291
  98.0 13.1 %collective-permute-start.15 = (bf16[128,1024]{1,0:T(8,128)(2,1)}, bf16[128,1024]{1,0:T(8,128)(2,1)}, u32[]{:S(2)}, u32[]{:S(2)}) collective-permute-start(bf16[128,1024]{1,0:T(8,128)(2,1)} %get-tuple-element.71), channel_id=1, source_target_pairs={{0,6},{1,7},{2,4},{3,5},{4,2},{5,3},{6,0},{7,1},{8,14},{9,15},{10,... | collective-permute-start | bytes 786440 | tf_op jit(solution)/shard_map/ppermute | solution.py:291
  99.2 11.9 %collective-permute-start.14 = (bf16[128,1024]{1,0:T(8,128)(2,1)}, bf16[128,1024]{1,0:T(8,128)(2,1)}, u32[]{:S(2)}, u32[]{:S(2)}) collective-permute-start(bf16[128,1024]{1,0:T(8,128)(2,1)} %get-tuple-element.72), channel_id=1, source_target_pairs={{0,4},{1,5},{2,6},{3,7},{4,0},{5,1},{6,2},{7,3},{8,12},{9,13},{10,... | collective-permute-start | bytes 786440 | tf_op jit(solution)/shard_map/ppermute | solution.py:291
  114.0 11.6 %collective-permute-start.16 = (bf16[32,1024]{1,0:T(8,128)(2,1)}, bf16[32,1024]{1,0:T(8,128)(2,1)}, u32[]{:S(2)}, u32[]{:S(2)}) collective-permute-start(bf16[32,1024]{1,0:T(8,128)(2,1)} %get-tuple-element.76), channel_id=1, source_target_pairs={{0,8},{8,0},{16,24},{24,16},{1,9},{9,1},{17,25},{25,17},{2,10},{10... | collective-permute-start | bytes 196616 | tf_op jit(solution)/shard_map/ppermute | solution.py:291
  114.2 11.4 %collective-permute-start.18 = (bf16[32,1024]{1,0:T(8,128)(2,1)}, bf16[32,1024]{1,0:T(8,128)(2,1)}, u32[]{:S(2)}, u32[]{:S(2)}) collective-permute-start(bf16[32,1024]{1,0:T(8,128)(2,1)} %get-tuple-element.77), channel_id=1, source_target_pairs={{0,24},{8,16},{16,8},{24,0},{1,25},{9,17},{17,9},{25,1},{2,26},{10... | collective-permute-start | bytes 196616 | tf_op jit(solution)/shard_map/ppermute | solution.py:291
  116.6 9.0 %collective-permute-start.17 = (bf16[32,1024]{1,0:T(8,128)(2,1)}, bf16[32,1024]{1,0:T(8,128)(2,1)}, u32[]{:S(2)}, u32[]{:S(2)}) collective-permute-start(bf16[32,1024]{1,0:T(8,128)(2,1)} %get-tuple-element.78), channel_id=1, source_target_pairs={{0,16},{8,24},{16,0},{24,8},{1,17},{9,25},{17,1},{25,9},{2,18},{10... | collective-permute-start | bytes 196616 | tf_op jit(solution)/shard_map/ppermute | solution.py:291
  126.8 8.3 %collective-permute-start.21 = (bf16[32,1024]{1,0:T(8,128)(2,1)S(1)}, bf16[32,1024]{1,0:T(8,128)(2,1)S(1)}, u32[]{:S(2)}, u32[]{:S(2)}) collective-permute-start(bf16[32,1024]{1,0:T(8,128)(2,1)S(1)} %add_convert_fusion), channel_id=1, source_target_pairs={{0,8},{8,0},{16,24},{24,16},{1,9},{9,1},{17,25},{25,17},{2,10},{10... | collective-permute-start | bytes 196616 | tf_op jit(solution)/shard_map/ppermute | solution.py:291
  127.0 8.0 %collective-permute-start.20 = (bf16[32,1024]{1,0:T(8,128)(2,1)S(1)}, bf16[32,1024]{1,0:T(8,128)(2,1)S(1)}, u32[]{:S(2)}, u32[]{:S(2)}) collective-permute-start(bf16[32,1024]{1,0:T(8,128)(2,1)S(1)} %add_convert_fusion), channel_id=1, source_target_pairs={{0,16},{8,24},{16,0},{24,8},{1,17},{9,25},{17,1},{25,9},{2,18},{10... | collective-permute-start | bytes 196616 | tf_op jit(solution)/shard_map/ppermute | solution.py:291
  129.3 5.8 %collective-permute-start.19 = (bf16[32,1024]{1,0:T(8,128)(2,1)S(1)}, bf16[32,1024]{1,0:T(8,128)(2,1)S(1)}, u32[]{:S(2)}, u32[]{:S(2)}) collective-permute-start(bf16[32,1024]{1,0:T(8,128)(2,1)S(1)} %add_convert_fusion), channel_id=1, source_target_pairs={{0,24},{8,16},{16,8},{24,0},{1,25},{9,17},{17,9},{25,1},{2,26},{10... | collective-permute-start | bytes 196616 | tf_op jit(solution)/shard_map/ppermute | solution.py:291
  130.5 12.7 %collective-permute-start.6 = (bf16[2,4,16,1024]{3,2,1,0:T(8,128)(2,1)S(1)}, bf16[2,4,16,1024]{3,2,1,0:T(8,128)(2,1)S(1)}, u32[]{:S(2)}, u32[]{:S(2)}) collective-permute-start(bf16[2,4,16,1024]{3,2,1,0:T(8,128)(2,1)S(1)} %select_bitcast_fusion), channel_id=1, source_target_pairs={{0,1},{1,0},{2,3},{3,2},{4,5},{5,4},{6,7},{7,6},{8,9},{9,8},{10,11... | collective-permute-start | bytes 786440 | tf_op jit(solution)/shard_map/ppermute | solution.py:291
  135.1 8.3 %collective-permute-start.24 = (bf16[128,1024]{1,0:T(8,128)(2,1)S(1)}, bf16[128,1024]{1,0:T(8,128)(2,1)S(1)}, u32[]{:S(2)}, u32[]{:S(2)}) collective-permute-start(bf16[128,1024]{1,0:T(8,128)(2,1)S(1)} %pad_maximum_fusion.4), channel_id=1, source_target_pairs={{0,2},{1,3},{2,0},{3,1},{4,6},{5,7},{6,4},{7,5},{8,10},{9,11},{10,... | collective-permute-start | bytes 786440 | tf_op jit(solution)/shard_map/ppermute | solution.py:291
  135.2 8.2 %collective-permute-start.23 = (bf16[128,1024]{1,0:T(8,128)(2,1)S(1)}, bf16[128,1024]{1,0:T(8,128)(2,1)S(1)}, u32[]{:S(2)}, u32[]{:S(2)}) collective-permute-start(bf16[128,1024]{1,0:T(8,128)(2,1)S(1)} %pad_maximum_fusion.4), channel_id=1, source_target_pairs={{0,4},{1,5},{2,6},{3,7},{4,0},{5,1},{6,2},{7,3},{8,12},{9,13},{10,... | collective-permute-start | bytes 786440 | tf_op jit(solution)/shard_map/ppermute | solution.py:291
  136.7 9.0 %collective-permute-start.22 = (bf16[128,1024]{1,0:T(8,128)(2,1)S(1)}, bf16[128,1024]{1,0:T(8,128)(2,1)S(1)}, u32[]{:S(2)}, u32[]{:S(2)}) collective-permute-start(bf16[128,1024]{1,0:T(8,128)(2,1)S(1)} %pad_maximum_fusion.4), channel_id=1, source_target_pairs={{0,6},{1,7},{2,4},{3,5},{4,2},{5,3},{6,0},{7,1},{8,14},{9,15},{10,... | collective-permute-start | bytes 786440 | tf_op jit(solution)/shard_map/ppermute | solution.py:291
  137.9 44.0 %collective-permute-start.9 = (bf16[1024,512]{1,0:T(8,128)(2,1)S(1)}, bf16[1024,512]{1,0:T(8,128)(2,1)}, u32[]{:S(2)}, u32[]{:S(2)}) collective-permute-start(bf16[1024,512]{1,0:T(8,128)(2,1)S(1)} %copy-done.12), channel_id=1, source_target_pairs={{1,0},{2,1},{3,2},{4,3},{5,4},{6,5},{7,6},{9,8},{10,9},{11,10},{12... | collective-permute-start | bytes 3145736 | tf_op jit(solution)/shard_map/ppermute | solution.py:400
  147.2 42.1 %collective-permute-start.25 = (bf16[512,1024]{1,0:T(8,128)(2,1)}, bf16[512,1024]{1,0:T(8,128)(2,1)}, u32[]{:S(2)}, u32[]{:S(2)}) collective-permute-start(bf16[512,1024]{1,0:T(8,128)(2,1)} %pad_maximum_fusion.1), channel_id=1, source_target_pairs={{0,1},{1,0},{2,3},{3,2},{4,5},{5,4},{6,7},{7,6},{8,9},{9,8},{10,11... | collective-permute-start | bytes 3145736 | tf_op jit(solution)/shard_map/ppermute | solution.py:291
  162.6 19.3 %collective-permute-start.11 = (bf16[1024,256]{1,0:T(8,128)(2,1)S(1)}, bf16[1024,256]{1,0:T(8,128)(2,1)}, u32[]{:S(2)}, u32[]{:S(2)}) collective-permute-start(bf16[1024,256]{1,0:T(8,128)(2,1)S(1)} %copy-done.14), channel_id=1, source_target_pairs={{1,0},{2,1},{3,2},{4,3},{5,4},{6,5},{7,6},{9,8},{10,9},{11,10},{12... | collective-permute-start | bytes 1572872 | tf_op jit(solution)/shard_map/ppermute | solution.py:400
  164.5 17.4 %collective-permute-start.10 = (bf16[1024,256]{1,0:T(8,128)(2,1)S(1)}, bf16[1024,256]{1,0:T(8,128)(2,1)}, u32[]{:S(2)}, u32[]{:S(2)}) collective-permute-start(bf16[1024,256]{1,0:T(8,128)(2,1)S(1)} %copy-done.13), channel_id=1, source_target_pairs={{1,0},{2,1},{3,2},{4,3},{5,4},{6,5},{7,6},{9,8},{10,9},{11,10},{12... | collective-permute-start | bytes 1572872 | tf_op jit(solution)/shard_map/ppermute | solution.py:400
  168.3 12.9 %collective-permute-start.8 = (bf16[2,1,16,1024]{3,2,0,1:T(8,128)(2,1)S(1)}, bf16[2,1,16,1024]{3,2,0,1:T(8,128)(2,1)S(1)}, u32[]{:S(2)}, u32[]{:S(2)}) collective-permute-start(bf16[2,1,16,1024]{3,2,0,1:T(8,128)(2,1)S(1)} %fusion.12), channel_id=1, source_target_pairs={{0,4},{1,5},{2,6},{3,7},{4,0},{5,1},{6,2},{7,3},{8,12},{9,13},{10,... | collective-permute-start | bytes 196616 | tf_op jit(solution)/shard_map/ppermute | solution.py:291
  (18 other events, 199.2 us)

commit v2 on v1

--- a/solution.py
+++ b/solution.py
@@ -43,9 +43,11 @@
 
 
 def forward_kernel(
-    info_ref, q_ref, g_ref, ko_ref, vo_ref, kh_ref, vh_ref, km_ref, vm_ref, mb_ref, *rest, nb
+    info_ref, q_ref, g_ref, ko_ref, vo_ref, kh_ref, vh_ref, km_ref, vm_ref, mb_ref, *rest, nb, members
 ):
-    at_ref, pt, ga_ref, ke, ve = rest[-5:]
+    at_ref, dm_ref, pt, ga_ref, ke, ve, q2s, pm = rest[-8:]
+    slots = km_ref.shape[0]
+    mine = slots // members
     ext = kh_ref.shape[0] + ko_ref.shape[0]
     fill_keys(ke, kh_ref, ko_ref, km_ref)
     fill_keys(ve, vh_ref, vo_ref, vm_ref)
@@ -61,6 +63,7 @@
         rows, cols = slice(b * BLK, (b + 1) * BLK), slice(b * TWO, (b + 1) * TWO)
         band = slice(b * BLK, (b + FAR + 1) * BLK)
         q2 = by_head(q_ref[rows, :] * jnp.asarray(HEAD_DIM**-0.5, bf16), first)
+        q2s[cols, :] = q2
         s = dot(ke[band, :], q2, NT)
         sm = dot(ke[ext:, :], q2, NT) + jnp.concatenate([mb_ref[b], mb_ref[b]], 1)
         lo = info_ref[0, b]
@@ -78,8 +81,8 @@
             pt[0, (b + e) * BLK : (b + e + 1) * BLK, cols] = jnp.exp(
                 mid[e - 1] - (m - off[e])
             ).astype(bf16)
-        pt[0, ext:, cols] = jnp.exp(sm - m).astype(bf16)
-        o = dot(pt[0, band, cols], ve[band, :], TN) + dot(pt[0, ext:, cols], ve[ext:, :], TN)
+        pm[:, cols] = jnp.exp(sm - m).astype(bf16)
+        o = dot(pt[0, band, cols], ve[band, :], TN) + dot(pm[:, cols], ve[ext:, :], TN)
         scale = jnp.where(row < info_ref[1, b], 1.0 / o[:, SPAN:], 0.0)
         o = o[:, :SPAN] * scale
         at_ref[rows, :] = join_heads(o, first).astype(bf16)
@@ -90,16 +93,25 @@
         ga_ref[0, cols, SPAN:] = jnp.where(
             lane == 0, high, jnp.where(lane == 1, d - high, 0.0)
         ).astype(bf16)
+        dp = dot(ve[ext:, :], ga_ref[0, cols, :], NT)
+        pt[0, ext:, cols] = (pm[:, cols].astype(f32) * dp).astype(bf16)
+    dk = dot(pt[0, ext:, :], q2s[...], NN).astype(bf16)
+    dv = dot(pm[...], ga_ref[0, :, :SPAN], NN).astype(bf16)
+    for j in range(members):
+        part = slice(j * mine, (j + 1) * mine)
+        dm_ref[2 * j * mine : (2 * j + 1) * mine, :] = dk[part]
+        dm_ref[(2 * j + 1) * mine : (2 * j + 2) * mine, :] = dv[part]
 
 
 def backward_kernel(
-    q_ref, pt_ref, ga_ref, ko_ref, vo_ref, kh_ref, vh_ref, km_ref, vm_ref, *rest, nb
+    q_ref, pt_ref, ga_ref, ko_ref, vo_ref, kh_ref, vh_ref, km_ref, *rest, nb
 ):
-    dq_ref, dko_ref, dvo_ref, dm_ref, dh_ref, ke, ve, q2, ds = rest[-9:]
-    hrows, slots = kh_ref.shape[0], km_ref.shape[0]
+    dq_ref, dko_ref, dvo_ref, dh_ref, ke, ve, q2, ds = rest[-8:]
+    hrows = kh_ref.shape[0]
     ext = hrows + ko_ref.shape[0]
     fill_keys(ke, kh_ref, ko_ref, km_ref)
-    fill_keys(ve, vh_ref, vo_ref, vm_ref)
+    ve[0:hrows, :SPAN] = vh_ref[...]
+    ve[hrows:, :SPAN] = vo_ref[...]
     ve[:, SPAN:] = jnp.ones((ve.shape[0], SPAN), bf16)
     first = lax.broadcasted_iota(jnp.int32, (BLK, SPAN), 1) < HEAD_DIM
     unit = HEAD_DIM**-0.5
@@ -110,9 +122,7 @@
         ga = ga_ref[0, cols, :]
         dp = dot(ve[band, :], ga, NT)
         ds[band, cols] = (pt_ref[0, band, cols].astype(f32) * dp).astype(bf16)
-        dp = dot(ve[ext:, :], ga, NT)
-        ds[ext:, cols] = (pt_ref[0, ext:, cols].astype(f32) * dp).astype(bf16)
-        dq = dot(ds[band, cols], ke[band, :], TN) + dot(ds[ext:, cols], ke[ext:, :], TN)
+        dq = dot(ds[band, cols], ke[band, :], TN) + dot(pt_ref[0, ext:, cols], ke[ext:, :], TN)
         dq_ref[rows, :] = (join_heads(dq, first) * unit).astype(bf16)
     for e in range(ext // BLK):
         cols = slice(max(0, e - FAR) * TWO, (min(nb - 1, e) + 1) * TWO)
@@ -124,10 +134,8 @@
             dh_ref[hrows + e * BLK : hrows + (e + 1) * BLK, :] = dv.astype(bf16)
         else:
             own = slice(e * BLK - hrows, (e + 1) * BLK - hrows)
-            dko_ref[own, :] = dk
-            dvo_ref[own, :] = dv
-    dm_ref[:slots, :] = dot(ds[ext:, :], q2[...], NN).astype(bf16)
-    dm_ref[slots:, :] = dot(pt_ref[0, ext:, :], ga_ref[0, :, :SPAN], NN).astype(bf16)
+            dko_ref[own, :] = dk.astype(bf16)
+            dvo_ref[own, :] = dv.astype(bf16)
 
 
 def columns(rows, start):
@@ -137,7 +145,7 @@
 ANY = pl.BlockSpec(memory_space=pl.ANY)
 
 
-def forward(info, q, g, ko, vo, kh, vh, km, vm, bias, start, count, base, halo_at, carry):
+def forward(info, q, g, ko, vo, kh, vh, km, vm, bias, members, start, count, base, halo_at, carry):
     tokens, width = q.shape
     slots, hrows, nb = km.shape[0], kh.shape[0], tokens // BLK
     keys = hrows + tokens + slots
@@ -150,25 +158,29 @@
         pl.BlockSpec(bias.shape, lambda p, *_: (0, 0, 0)),
     ]
     alias = {}
-    if carry is not None:
-        alias = {len(args): 0}
-        args.append(carry)
-        specs.append(ANY)
+    if carry:
+        alias = {len(args) + i: i for i in range(len(carry))}
+        args += carry
+        specs += [ANY] * len(carry)
     return pl.pallas_call(
-        functools.partial(forward_kernel, nb=nb),
+        functools.partial(forward_kernel, nb=nb, members=members),
         grid_spec=pltpu.PrefetchScalarGridSpec(
             num_scalar_prefetch=1,
             grid=(count,),
             in_specs=specs,
             out_specs=[
-                columns(tokens, start),
+                columns(tokens, start), columns(2 * slots, start),
                 pl.BlockSpec((1, keys, nb * TWO), lambda p, *_: (p, 0, 0)),
                 pl.BlockSpec((1, nb * TWO, 2 * SPAN), lambda p, *_: (p, 0, 0)),
             ],
-            scratch_shapes=[pltpu.VMEM((keys, SPAN), bf16), pltpu.VMEM((keys, 2 * SPAN), bf16)],
+            scratch_shapes=[
+                pltpu.VMEM((keys, SPAN), bf16), pltpu.VMEM((keys, 2 * SPAN), bf16),
+                pltpu.VMEM((nb * TWO, SPAN), bf16), pltpu.VMEM((slots, nb * TWO), bf16),
+            ],
         ),
         out_shape=[
             jax.ShapeDtypeStruct((tokens, width), bf16),
+            jax.ShapeDtypeStruct((2 * slots, width), bf16),
             jax.ShapeDtypeStruct((count, keys, nb * TWO), bf16),
             jax.ShapeDtypeStruct((count, nb * TWO, 2 * SPAN), bf16),
         ],
@@ -181,22 +193,21 @@
     )(*args)
 
 
-def backward(q, pt, ga, ko, vo, kh, vh, km, vm, start, count, base, halo_at, at, carry, dh_total, dh_at):
+def backward(q, pt, ga, ko, vo, kh, vh, km, start, count, base, halo_at, at, carry, dh_total, dh_at):
     tokens, width = q.shape
     slots, hrows, nb = km.shape[0], kh.shape[0], tokens // BLK
     keys = hrows + tokens + slots
     kc, vc = halo_at
-    mk, mv = base
-    args = [q, pt, ga, ko, vo, kh, vh, km, vm]
+    args = [q, pt, ga, ko, vo, kh, vh, km]
     specs = [
         columns(tokens, start),
         pl.BlockSpec((1, keys, nb * TWO), lambda p, *_: (p + at, 0, 0)),
         pl.BlockSpec((1, nb * TWO, 2 * SPAN), lambda p, *_: (p + at, 0, 0)),
         columns(tokens, start), columns(tokens, start),
-        columns(hrows, kc), columns(hrows, vc), columns(slots, mk + start), columns(slots, mv + start),
+        columns(hrows, kc), columns(hrows, vc), columns(slots, base + start),
     ]
     alias = {}
-    if carry is not None:
+    if carry:
         alias = {len(args) + i: i for i in range(len(carry))}
         args += carry
         specs += [ANY] * len(carry)
@@ -206,17 +217,16 @@
         in_specs=specs,
         out_specs=[
             columns(tokens, start), columns(tokens, start), columns(tokens, start),
-            columns(2 * slots, start), columns(2 * hrows, dh_at),
+            columns(2 * hrows, dh_at),
         ],
         scratch_shapes=[
-            pltpu.VMEM((keys, SPAN), bf16), pltpu.VMEM((keys, 2 * SPAN), bf16),
-            pltpu.VMEM((nb * TWO, SPAN), bf16), pltpu.VMEM((keys, nb * TWO), bf16),
+            pltpu.VMEM((keys, SPAN), bf16), pltpu.VMEM((keys - slots, 2 * SPAN), bf16),
+            pltpu.VMEM((nb * TWO, SPAN), bf16), pltpu.VMEM((keys - slots, nb * TWO), bf16),
         ],
         out_shape=[
             jax.ShapeDtypeStruct((tokens, width), bf16),
-            jax.ShapeDtypeStruct((tokens, width), f32),
-            jax.ShapeDtypeStruct((tokens, width), f32),
-            jax.ShapeDtypeStruct((2 * slots, width), bf16),
+            jax.ShapeDtypeStruct((tokens, width), bf16),
+            jax.ShapeDtypeStruct((tokens, width), bf16),
             jax.ShapeDtypeStruct((2 * hrows, dh_total * SPAN), bf16),
         ],
         input_output_aliases=alias,
@@ -228,45 +238,67 @@
     )(*args)
 
 
-def finish_kernel(slot_ref, dk_in, dv_in, mk_ref, mv_ref, *rest, groups):
+def finish_kernel(slot_ref, dk_in, dv_in, dm_ref, *rest, segments):
     backs, (dk_ref, dv_ref) = rest[:-2], rest[-2:]
-    tokens = dk_in.shape[0]
+    rows = dk_in.shape[0]
     mine = slot_ref.shape[1]
-    pick = (lax.broadcasted_iota(jnp.int32, (tokens, mine), 0) == slot_ref[...]).astype(f32).astype(bf16)
-    dk = dk_in[...] + dot(pick, mk_ref[...], NN)
-    dv = dv_in[...] + dot(pick, mv_ref[...], NN)
-    edge = tokens - W
-    if edge:
-        dk_ref[:edge, :] = dk[:edge].astype(bf16)
-        dv_ref[:edge, :] = dv[:edge].astype(bf16)
-    pair = pl.program_id(0)
-    for back, (at, count) in zip(backs, groups):
-
-        @pl.when((pair >= at) & (pair < at + count))
-        def _():
-            dk_ref[edge:, :] = (dk[edge:] + back[:W, :].astype(f32)).astype(bf16)
-            dv_ref[edge:, :] = (dv[edge:] + back[W:, :].astype(f32)).astype(bf16)
-
-
-def finish(slots, dko, dvo, dmem, backs, groups):
+    at = lax.broadcasted_iota(jnp.int32, (rows, mine), 0) + pl.program_id(0) * rows
+    pick = (at == slot_ref[...]).astype(f32).astype(bf16)
+    for g, pair, pos, count in segments:
+        to, of = slice(pair * SPAN, (pair + count) * SPAN), slice(pos * SPAN, (pos + count) * SPAN)
+        back = backs[g]
+        dk = dk_in[:, to].astype(f32) + dot(pick, dm_ref[:mine, to], NN)
+        dv = dv_in[:, to].astype(f32) + dot(pick, dm_ref[mine:, to], NN)
+        dk_ref[:, to] = (dk + back[0, :, of].astype(f32)).astype(bf16)
+        dv_ref[:, to] = (dv + back[1, :, of].astype(f32)).astype(bf16)
+
+
+def finish(slots, dko, dvo, dmem, backs, segments):
     tokens, width = dko.shape
     mine = slots.shape[0]
-
-    def back_columns(at, count):
-        return pl.BlockSpec((2 * W, SPAN), lambda p: (0, jnp.clip(p - at, 0, count - 1)))
-
-    col = lambda rows, j: pl.BlockSpec((rows, SPAN), lambda p: (j, p))
+    row = pl.BlockSpec((BLK, width), lambda r: (r, 0))
     return pl.pallas_call(
-        functools.partial(finish_kernel, groups=groups),
-        grid=(width // SPAN,),
-        in_specs=[pl.BlockSpec((1, mine), lambda p: (0, 0)), col(tokens, 0), col(tokens, 0), col(mine, 0), col(mine, 1)]
-        + [back_columns(*g) for g in groups],
-        out_specs=[col(tokens, 0), col(tokens, 0)],
+        functools.partial(finish_kernel, segments=segments),
+        grid=(tokens // BLK,),
+        in_specs=[pl.BlockSpec((1, mine), lambda r: (0, 0)), row, row, pl.BlockSpec((2 * mine, width), lambda r: (0, 0))]
+        + [pl.BlockSpec((2, BLK, b.shape[-1]), lambda r: (0, r, 0)) for b in backs],
+        out_specs=[row, row],
         out_shape=[jax.ShapeDtypeStruct((tokens, width), bf16)] * 2,
         compiler_params=pltpu.CompilerParams(vmem_limit_bytes=67_000_000),
-        cost_estimate=pl.CostEstimate(flops=1 << 26, bytes_accessed=8 << 20, transcendentals=0),
+        cost_estimate=pl.CostEstimate(flops=1 << 26, bytes_accessed=6 << 20, transcendentals=0),
         name="finish_rows",
-    )(slots[None, :], dko, dvo, dmem, dmem, *backs)
+    )(slots[None, :], dko, dvo, dmem, *backs)
+
+
+def place_kernel(where_ref, w_ref, *rest, nfam, scale):
+    out_ref = rest[-1]
+    piece = w_ref.shape[0] // nfam
+    fam = where_ref[2]
+    for k in range(nfam):
+        row = pl.multiple_of((fam ^ k) * piece, piece)
+        out_ref[pl.ds(row, piece), :] = w_ref[k * piece : (k + 1) * piece, :].astype(f32) * scale
+
+
+def place(where, w, plane, nfam, scale, carry):
+    half, width = w.shape
+    rows = half // plane
+    args, specs, alias = [w], [pl.BlockSpec((rows, width), lambda k, s: (k, 0))], {}
+    if carry is not None:
+        args, specs, alias = args + [carry], specs + [ANY], {2: 0}
+    return pl.pallas_call(
+        functools.partial(place_kernel, nfam=nfam, scale=scale),
+        grid_spec=pltpu.PrefetchScalarGridSpec(
+            num_scalar_prefetch=1,
+            grid=(plane,),
+            in_specs=specs,
+            out_specs=pl.BlockSpec((rows, width), lambda k, s: (s[0] * plane + (s[1] ^ k), 0)),
+        ),
+        out_shape=jax.ShapeDtypeStruct((2 * half, width), f32),
+        input_output_aliases=alias,
+        compiler_params=pltpu.CompilerParams(vmem_limit_bytes=67_000_000),
+        cost_estimate=pl.CostEstimate(flops=1 << 20, bytes_accessed=3 << 20, transcendentals=0),
+        name="place_rows",
+    )(where, *args)
 
 
 def protein_tables(prot_blocks, last_fill):
@@ -307,37 +339,20 @@
     return x
 
 
-def halve(x, axis, me):
-    for bit in bits_of(lax.axis_size(axis)):
-        lead, n = x.shape[0], x.shape[1]
-        x = x.reshape(lead, n // 2, 2, *x.shape[2:])
-        upper = (me & bit) != 0
-        keep = jnp.where(upper, x[:, :, 1], x[:, :, 0])
-        send = jnp.where(upper, x[:, :, 0], x[:, :, 1])
-        x = keep.astype(f32) + swap(send.astype(bf16), axis, bit).astype(f32)
-    return x
-
-
-def exchange(parts, axis, shift, me, n):
-    rows = parts.shape[0] // n
-    part = lambda j: lax.dynamic_slice_in_dim(parts, j * rows, rows)
+def exchange(part, axis, shift, me, n):
     got = [swap(part(me ^ k).astype(bf16), axis, k << shift) for k in range(1, n)]
-    return sum([g.astype(f32) for g in got], part(me).astype(f32))
-
-
-def spread(x, axis, shift, me, n):
-    parts = [x] + [swap(x, axis, k << shift) for k in range(1, n)]
-    for bit in bits_of(n):
-        upper = (me & bit) != 0
-        parts = [jnp.where(upper, parts[j ^ bit], parts[j]) for j in range(n)]
-    return jnp.concatenate(parts, 0)
+    return sum([g.astype(f32) for g in got], part(me))
+
+
+def spread(x, axis, shift, n):
+    return jnp.concatenate([x] + [swap(x, axis, k << shift) for k in range(1, n)], 0)
 
 
 def groups_of(pairs):
     if pairs % 8:
         return [pairs], [(0, 0, pairs)], [pairs]
     u = pairs // 8
-    return [u, 3 * u, 4 * u], [(0, 0, u), (1, 0, 3 * u), (2, 0, 2 * u), (2, 2 * u, 2 * u)], [4 * u, 2 * u, 2 * u]
+    return [3 * u, 3 * u, 2 * u], [(0, 0, u), (1, 0, 3 * u), (0, u, 2 * u), (2, 0, 2 * u)], [4 * u, 2 * u, 2 * u]
 
 
 def per_device(queries, key_rows, value_rows, cotangent, out_weight, prot_blocks, last_fill, memory_slots):
@@ -373,45 +388,47 @@
     seen = (left[nb:] > 0)[None, :] & (prot[None, nb:] < prot[:nb, None])
     bias = jnp.broadcast_to(jnp.where(seen, 0.0, NEG).astype(f32)[:, :, None], (nb, total, BLK))
     base = (0, pairs)
-    att, saved = None, []
+    carry, saved = [], []
     for i, (at, count) in enumerate(zip(fstarts, fsizes)):
-        att, pt, ga = forward(
-            info, q, grad_attn, k, v, halos[i], halos[i], mem, mem, bias,
-            at, count, base, (0, count), att)
+        att, dm, pt, ga = forward(
+            info, q, grad_attn, k, v, halos[i], halos[i], mem, mem, bias, nctx,
+            at, count, base, (0, count), carry)
+        carry = [att, dm]
         saved.append((pt, ga))
-    core = me & 1
-    half = width // 2
-    mine_att = lax.dynamic_slice_in_dim(att, core * half, half, 1)
-    your_att = lax.dynamic_slice_in_dim(att, (1 - core) * half, half, 1)
-    sent = swap(dot(your_att, cot, TN).astype(bf16), "ctx", 1)
-    kept = dot(mine_att, cot, TN)
-
-    carry, backs, i = [], [], 0
+    core, spot, plane = me & 1, me >> 1, nctx // 2
+    w = dot(att, cot, TN).astype(bf16).reshape(2, plane, width // nctx, width)
+    dm = dm.reshape(plane, 2, 2 * mine, width)
+    at = lambda x, j, axis: lax.dynamic_index_in_dim(x, j, axis, keepdims=False)
+    side = lambda c: jnp.concatenate([at(w, c, 0), at(dm, c, 1)], 1)
+    sent = swap(side(1 - core), "ctx", 1)
+    kept = side(core)
+    carry, backs, segments, i = [], [], [], 0
     for total_dh in dhs:
         done = 0
         while done < total_dh:
             j, r, count = bplan[i]
             pt, ga = saved[j]
             out = backward(
-                q, pt, ga, k, v, halos[j], halos[j], mem, mem, fstarts[j] + r, count,
-                base, (r, fsizes[j] + r), r, carry, total_dh, done)
+                q, pt, ga, k, v, halos[j], halos[j], mem, fstarts[j] + r, count,
+                0, (r, fsizes[j] + r), r, carry, total_dh, done)
             carry = list(out)
+            segments.append((len(backs), fstarts[j] + r, done, count))
             done, i = done + count, i + 1
         backs.append(lax.ppermute(carry.pop(), "ctx", back))
-    plane = nctx // 2
-    total_w = kept + sent.astype(f32)
-    total_w = exchange(total_w, "ctx", 1, me >> 1, plane)
-    total_w = exchange(total_w, "fam", 0, fam, nfam)
-    w = spread(total_w.astype(bf16), "fam", 0, fam, nfam)
-    w = spread(w, "ctx", 1, me >> 1, plane)
+    total_w = exchange(
+        lambda j: at(sent, j, 0).astype(f32) + at(kept, j, 0).astype(f32), "ctx", 1, spot, plane)
+    mem_grad, total_w = total_w[width // nctx :].astype(bf16), total_w[: width // nctx].reshape(nfam, -1, width)
+    total_w = exchange(lambda j: at(total_w, j, 0), "fam", 0, fam, nfam)
+    w = spread(total_w.astype(bf16), "fam", 0, nfam)
+    w = spread(w, "ctx", 1, plane)
     other = swap(w, "ctx", 1)
     scale = (nfam * nctx * tokens) ** -0.5
-    upper = core != 0
-    weight = jnp.concatenate([jnp.where(upper, other, w), jnp.where(upper, w, other)], 0).astype(f32) * scale
-    dq, dko, dvo, dm = carry
-    dmem = halve(dm.reshape(2, nctx, mine, width), "ctx", me).reshape(2 * mine, width).astype(bf16)
-    dk, dv = finish(
-        own_slots, dko, dvo, dmem, backs, [(sum(dhs[:i]), n) for i, n in enumerate(dhs)])
+    where = lambda c: jnp.stack([c, spot, fam]).astype(jnp.int32)
+    weight = place(where(core), w, plane, nfam, scale, None)
+    weight = place(where(1 - core), other, plane, nfam, scale, weight)
+    dq, dko, dvo = carry
+    backs = [x.reshape(2, W, -1) for x in backs]
+    dk, dv = finish(own_slots, dko, dvo, mem_grad, backs, segments)
     return dq[None], dk[None], dv[None], weight
 
 

time: 195 us -> 215 us (1.10)
  the two profiles are of different devices: /device:TPU:11 before, /device:TPU:3 now
where the time goes in v2:
time: 215 us; the launch traced here: 213 us
  Pallas kernels  85.7 us (40%)
  waiting for transfers between devices  59.4 us (28%)
  starting transfers between devices  33.7 us (16%)
  local copies, waits for them, and re-layouts  13.3 us (6%)
  other arithmetic  10.9 us (5%)
  matrix products  9.44 us (4%)
    ppermute x17, waiting for transfers between devices, swap(): lax.ppermute(x, axis, [(i, i ^ bits) for i in range(lax.axis_size(axis))])  54.4 us
    pallas_call x3, Pallas kernels, forward(): pl.pallas_call(functools.partial(forward_kernel, nb=nb, members=members),...  46.7 us
    pallas_call x4, Pallas kernels, backward(): pl.pallas_call(functools.partial(backward_kernel, nb=nb), grid=(count,),...  25.9 us
    ppermute x17, starting transfers between devices, swap(): lax.ppermute(x, axis, [(i, i ^ bits) for i in range(lax.axis_size(axis))])  15.5 us
    ppermute x3, starting transfers between devices, per_device(): backs.append(lax.ppermute(carry.pop(), 'ctx', back))  9.75 us
    dot_general x4, matrix products, dot(): return lax.dot_general(a, b, dims, preferred_element_type=f32)  9.44 us
    pallas_call x2, Pallas kernels, place(): pl.pallas_call(functools.partial(place_kernel, nfam=nfam, scale=scale), g...  8.51 us
    ppermute x3, starting transfers between devices, per_device(): lax.ppermute(jnp.concatenate([k[edge:, cols], v[edge:, cols]], 1), 'ctx',...  8.43 us
  transfers between devices with their start and end apart: 23, of which 10 were waited for; matrix products, arithmetic and copies ran while one was open for 9% of the time, Pallas kernels for 32%

profile of v2, /device:TPU:3, one launch (start us, length us, event | category | flops | bytes accessed | tf_op | source)
XLA Modules:
  0.0 213.5 jit_solution(2520816269451359675)
XLA Ops:
  6.2 3.0 %collective-permute-start = (bf16[512,512]{1,0:T(8,128)(2,1)}, bf16[512,512]{1,0:T(8,128)(2,1)}, u32[]{:S(2)}, u32[]{:S(2)}) collective-permute-start(bf16[512,512]{1,0:T(8,128)(2,1)} %pad_maximum_fusion.3), channel_id=1, source_target_pairs={{0,1},{1,2},{2,3},{3,4},{4,5},{5,6},{6,7},{8,9},{9,10},{10,11},{11... | collective-permute-start | bytes 1572872 | tf_op jit(solution)/shard_map/ppermute | solution.py:377
  12.9 3.0 %collective-permute-start.5 = (bf16[512,768]{1,0:T(8,128)(2,1)S(1)}, bf16[512,768]{1,0:T(8,128)(2,1)}, u32[]{:S(2)}, u32[]{:S(2)}) collective-permute-start(bf16[512,768]{1,0:T(8,128)(2,1)S(1)} %pad_maximum_fusion.2), channel_id=1, source_target_pairs={{0,1},{1,2},{2,3},{3,4},{4,5},{5,6},{6,7},{8,9},{9,10},{10,11},{11... | collective-permute-start | bytes 2359304 | tf_op jit(solution)/shard_map/ppermute | solution.py:377
  16.5 3.5 %convolution_convert_fusion.1.g_ref = bf16[512,1024]{1,0:T(8,128)(2,1)} fusion(bf16[1024,1024]{1,0:T(8,128)(2,1)S(1)} %copy-done.7, bf16[1,512,1024]{2,1,0:T(8,128)(2,1)} %param.11), kind=kOutput, calls=%fused_computation.5 | convolution fusion | flops 1074266112 | bytes 4194304 | tf_op jit(solution)/shard_map/dot_general | solution.py:26
  20.6 15.3 %collective-permute-done.2 = bf16[32,2048]{1,0:T(8,128)(2,1)S(1)} collective-permute-done((bf16[32,2048]{1,0:T(8,128)(2,1)S(1)}, bf16[32,2048]{1,0:T(8,128)(2,1)S(1)}, u32[]{:S(2)}, u32[]{:S(2)}) %collective-permute-start.2) | collective-permute-done | bytes 131104 | tf_op jit(solution)/shard_map/ppermute | solution.py:323
  37.9 3.4 %collective-permute-done.3 = bf16[64,2048]{1,0:T(8,128)(2,1)S(1)} collective-permute-done((bf16[64,2048]{1,0:T(8,128)(2,1)S(1)}, bf16[64,2048]{1,0:T(8,128)(2,1)S(1)}, u32[]{:S(2)}, u32[]{:S(2)}) %collective-permute-start.3) | collective-permute-done | bytes 262176 | tf_op jit(solution)/shard_map/ppermute | solution.py:323
  43.0 17.0 %band_forward.3 = (bf16[512,1024]{1,0:T(8,128)(2,1)}, bf16[256,1024]{1,0:T(8,128)(2,1)}, bf16[3,1152,1024]{2,1,0:T(8,128)(2,1)}, bf16[3,1024,256]{2,1,0:T(8,128)(2,1)}) custom-call(s32[2,4]{1,0:T(2,128)} %pad_add_fusion.1.info_ref, bf16[512,1024]{1,0:T(8,128)(2,1)} %bitcast.105, bf16[512,1024]{1,0:T(8,128)(2,1)} %convolution_convert_fusion.1.g_ref, ...), custom_call_target="tpu_custom_call" | custom-call | flops 4831838208 | bytes 12582912 | tf_op jit(solution)/shard_map/band_forward/pallas_call | solution.py:165
  60.0 17.1 %band_forward.4 = (bf16[512,1024]{1,0:T(8,128)(2,1)}, bf16[256,1024]{1,0:T(8,128)(2,1)}, bf16[3,1152,1024]{2,1,0:T(8,128)(2,1)}, bf16[3,1024,256]{2,1,0:T(8,128)(2,1)}) custom-call(s32[2,4]{1,0:T(2,128)} %pad_add_fusion.1.info_ref, bf16[512,1024]{1,0:T(8,128)(2,1)} %bitcast.106, ...), custom_call_target="tpu_custom_call", output_to_operand_aliasing={{0}: (10, {}), {1}: (11, {})} | custom-call | flops 4831838208 | bytes 12582912 | tf_op jit(solution)/shard_map/band_forward/pallas_call | solution.py:165
  77.1 12.6 %band_forward.5 = (bf16[512,1024]{1,0:T(8,128)(2,1)}, bf16[256,1024]{1,0:T(8,128)(2,1)}, bf16[2,1152,1024]{2,1,0:T(8,128)(2,1)}, bf16[2,1024,256]{2,1,0:T(8,128)(2,1)}) custom-call(s32[2,4]{1,0:T(2,128)} %pad_add_fusion.1.info_ref, bf16[512,1024]{1,0:T(8,128)(2,1)} %bitcast.107, ...), custom_call_target="tpu_custom_call", output_to_operand_aliasing={{0}: (10, {}), {1}: (11, {})} | custom-call | flops 3221225472 | bytes 8388608 | tf_op jit(solution)/shard_map/band_forward/pallas_call | solution.py:165
  89.7 2.9 %convolution_convert_fusion = bf16[1024,1024]{1,0:T(8,128)(2,1)S(1)} fusion(bf16[512,1024]{1,0:T(8,128)(2,1)} %get-tuple-element.57, bf16[1,512,1024]{2,1,0:T(8,128)(2,1)} %param.11), kind=kOutput, calls=%fused_computation.4 | convolution fusion | flops 1074790400 | bytes 4194304 | tf_op jit(solution)/shard_map/dot_general | solution.py:26
  93.1 3.1 %collective-permute-done.6 = bf16[4,160,1024]{2,1,0:T(8,128)(2,1)} collective-permute-done((bf16[4,160,1024]{2,1,0:T(8,128)(2,1)S(1)}, bf16[4,160,1024]{2,1,0:T(8,128)(2,1)}, u32[]{:S(2)}, u32[]{:S(2)}) %collective-permute-start.6) | collective-permute-done | bytes 1310752 | tf_op jit(solution)/shard_map/ppermute | solution.py:323
  100.5 6.5 %collective-permute-done.7 = bf16[160,1024]{1,0:T(8,128)(2,1)S(1)} collective-permute-done((bf16[160,1024]{1,0:T(8,128)(2,1)S(1)}, bf16[160,1024]{1,0:T(8,128)(2,1)S(1)}, u32[]{:S(2)}, u32[]{:S(2)}) %collective-permute-start.7) | collective-permute-done | bytes 327712 | tf_op jit(solution)/shard_map/ppermute | solution.py:323
  107.9 7.0 %collective-permute-done.9 = bf16[160,1024]{1,0:T(8,128)(2,1)S(1)} collective-permute-done((bf16[160,1024]{1,0:T(8,128)(2,1)S(1)}, bf16[160,1024]{1,0:T(8,128)(2,1)S(1)}, u32[]{:S(2)}, u32[]{:S(2)}) %collective-permute-start.9) | collective-permute-done | bytes 327712 | tf_op jit(solution)/shard_map/ppermute | solution.py:323
  122.2 4.5 %band_backward.4 = (bf16[512,1024]{1,0:T(8,128)(2,1)}, bf16[512,1024]{1,0:T(8,128)(2,1)}, bf16[512,1024]{1,0:T(8,128)(2,1)}, bf16[1024,512]{1,0:T(8,128)(2,1)}) custom-call(bf16[512,1024]{1,0:T(8,128)(2,1)} %bitcast.108, bf16[3,1152,1024]{2,1,0:T(8,128)(2,1)} %get-tuple-element.40.pt_ref, bf16[3,1024,256]{2,1,0:T(8,128)(2,1)} %get-tuple-element.41.ga_ref, ...), custom_call_target="tpu_custom_call" | custom-call | flops 2684354560 | bytes 6291456 | tf_op jit(solution)/shard_map/band_backward/pallas_call | solution.py:214
  133.5 8.4 %band_backward.5 = (bf16[512,1024]{1,0:T(8,128)(2,1)}, bf16[512,1024]{1,0:T(8,128)(2,1)}, bf16[512,1024]{1,0:T(8,128)(2,1)}, bf16[1024,512]{1,0:T(8,128)(2,1)}) custom-call(bf16[512,1024]{1,0:T(8,128)(2,1)} %bitcast.109, bf16[3,1152,1024]{2,1,0:T(8,128)(2,1)} %get-tuple-element.42.pt_ref, ...), custom_call_target="tpu_custom_call", output_to_operand_aliasing={{0}: (8, {}), {1}: (9, {}), {2}: (10, {}), {3}: (11, {})} | custom-call | flops 8053063680 | bytes 18874368 | tf_op jit(solution)/shard_map/band_backward/pallas_call | solution.py:214
  142.0 4.5 %collective-permute-start.10 = (bf16[1024,512]{1,0:T(8,128)(2,1)}, bf16[1024,512]{1,0:T(8,128)(2,1)}, u32[]{:S(2)}, u32[]{:S(2)}) collective-permute-start(bf16[1024,512]{1,0:T(8,128)(2,1)} %get-tuple-element.59), channel_id=1, source_target_pairs={{1,0},{2,1},{3,2},{4,3},{5,4},{6,5},{7,6},{9,8},{10,9},{11,10},{12... | collective-permute-start | bytes 3145736 | tf_op jit(solution)/shard_map/ppermute | solution.py:417
  154.6 7.4 %collective-permute-done.19 = bf16[128,1024]{1,0:T(8,128)(2,1)S(1)} collective-permute-done((bf16[128,1024]{1,0:T(8,128)(2,1)S(1)}, bf16[128,1024]{1,0:T(8,128)(2,1)S(1)}, u32[]{:S(2)}, u32[]{:S(2)}) %collective-permute-start.19) | collective-permute-done | bytes 262176 | tf_op jit(solution)/shard_map/ppermute | solution.py:323
  162.7 9.1 %collective-permute-done.20 = bf16[128,1024]{1,0:T(8,128)(2,1)S(1)} collective-permute-done((bf16[128,1024]{1,0:T(8,128)(2,1)S(1)}, bf16[128,1024]{1,0:T(8,128)(2,1)S(1)}, u32[]{:S(2)}, u32[]{:S(2)}) %collective-permute-start.20) | collective-permute-done | bytes 262176 | tf_op jit(solution)/shard_map/ppermute | solution.py:323
  173.7 6.5 %band_backward.6 = (bf16[512,1024]{1,0:T(8,128)(2,1)}, bf16[512,1024]{1,0:T(8,128)(2,1)}, bf16[512,1024]{1,0:T(8,128)(2,1)}, bf16[1024,256]{1,0:T(8,128)(2,1)}) custom-call(bf16[512,1024]{1,0:T(8,128)(2,1)} %bitcast.110, bf16[3,1152,1024]{2,1,0:T(8,128)(2,1)} %get-tuple-element.40.pt_ref, ...), custom_call_target="tpu_custom_call", output_to_operand_aliasing={{0}: (8, {}), {1}: (9, {}), {2}: (10, {})} | custom-call | flops 5368709120 | bytes 12582912 | tf_op jit(solution)/shard_map/band_backward/pallas_call | solution.py:214
  182.1 6.5 %band_backward.7 = (bf16[512,1024]{1,0:T(8,128)(2,1)}, bf16[512,1024]{1,0:T(8,128)(2,1)}, bf16[512,1024]{1,0:T(8,128)(2,1)}, bf16[1024,256]{1,0:T(8,128)(2,1)}) custom-call(bf16[512,1024]{1,0:T(8,128)(2,1)} %bitcast.111, bf16[2,1152,1024]{2,1,0:T(8,128)(2,1)} %get-tuple-element.38.pt_ref, ...), custom_call_target="tpu_custom_call", output_to_operand_aliasing={{0}: (8, {}), {1}: (9, {}), {2}: (10, {})} | custom-call | flops 5368709120 | bytes 12582912 | tf_op jit(solution)/shard_map/band_backward/pallas_call | solution.py:214
  188.6 3.3 %collective-permute-start.12 = (bf16[1024,256]{1,0:T(8,128)(2,1)}, bf16[1024,256]{1,0:T(8,128)(2,1)}, u32[]{:S(2)}, u32[]{:S(2)}) collective-permute-start(bf16[1024,256]{1,0:T(8,128)(2,1)} %get-tuple-element.61), channel_id=1, source_target_pairs={{1,0},{2,1},{3,2},{4,3},{5,4},{6,5},{7,6},{9,8},{10,9},{11,10},{12... | collective-permute-start | bytes 1572872 | tf_op jit(solution)/shard_map/ppermute | solution.py:417
  195.3 5.0 %collective-permute-done.12 = bf16[1024,256]{1,0:T(8,128)(2,1)} collective-permute-done((bf16[1024,256]{1,0:T(8,128)(2,1)}, bf16[1024,256]{1,0:T(8,128)(2,1)}, u32[]{:S(2)}, u32[]{:S(2)}) %collective-permute-start.12) | collective-permute-done | bytes 524320 | tf_op jit(solution)/shard_map/ppermute | solution.py:417
  200.3 4.6 %finish_rows.1 = (bf16[512,1024]{1,0:T(8,128)(2,1)}, bf16[512,1024]{1,0:T(8,128)(2,1)}) custom-call(s32[1,16]{1,0:T(1,128)} %constant_dynamic-slice_fusion.slot_ref, bf16[512,1024]{1,0:T(8,128)(2,1)} %get-tuple-element.55.dk_in, bf16[512,1024]{1,0:T(8,128)(2,1)} %get-tuple-element.56.dv_in, bf16[32,1024]{1,0:T(8,128)(2,1)} %slice.65.dm_ref, ...), custom_call_target="tpu_custom_call" | custom-call | flops 67108864 | bytes 6291456 | tf_op jit(solution)/shard_map/finish_rows/pallas_call | solution.py:260
  204.9 4.3 %place_rows.2.rest_0_ = f32[1024,1024]{1,0:T(8,128)} custom-call(s32[3]{0:T(128)} %add_add_fusion.1.where_ref, bf16[512,1024]{1,0:T(8,128)(2,1)} %constant_dynamic-update-slice_fusion.w_ref), custom_call_target="tpu_custom_call" | custom-call | flops 1048576 | bytes 3145728 | tf_op jit(solution)/shard_map/place_rows/pallas_call | solution.py:288
  209.2 4.3 %place_rows.3 = f32[1024,1024]{1,0:T(8,128)} custom-call(s32[3]{0:T(128)} %add_add_fusion.where_ref, bf16[512,1024]{1,0:T(8,128)(2,1)} %collective-permute-done.22.w_ref, f32[1024,1024]{1,0:T(8,128)} %place_rows.2.rest_0_), custom_call_target="tpu_custom_call", output_to_operand_aliasing={{}: (2, {})} | custom-call | flops 1048576 | bytes 3145728 | tf_op jit(solution)/shard_map/place_rows/pallas_call | solution.py:288
  (99 shorter events, 49.6 us)
Async XLA Ops:
  4.6 15.6 %collective-permute-start.1 = (bf16[16,2048]{1,0:T(8,128)(2,1)S(1)}, bf16[16,2048]{1,0:T(8,128)(2,1)S(1)}, u32[]{:S(2)}, u32[]{:S(2)}) collective-permute-start(bf16[16,2048]{1,0:T(8,128)(2,1)S(1)} %pad_maximum_fusion.5), channel_id=1, source_target_pairs={{0,1},{1,0},{2,3},{3,2},{4,5},{5,4},{6,7},{7,6},{8,9},{9,8},{10,11... | collective-permute-start | bytes 196616 | tf_op jit(solution)/shard_map/ppermute | solution.py:323
  6.2 70.9 %collective-permute-start = (bf16[512,512]{1,0:T(8,128)(2,1)}, bf16[512,512]{1,0:T(8,128)(2,1)}, u32[]{:S(2)}, u32[]{:S(2)}) collective-permute-start(bf16[512,512]{1,0:T(8,128)(2,1)} %pad_maximum_fusion.3), channel_id=1, source_target_pairs={{0,1},{1,2},{2,3},{3,4},{4,5},{5,6},{6,7},{8,9},{9,10},{10,11},{11... | collective-permute-start | bytes 1572872 | tf_op jit(solution)/shard_map/ppermute | solution.py:377
  9.5 7.0 %copy-start.7 = (bf16[1024,1024]{1,0:T(8,128)(2,1)S(1)}, bf16[1024,1024]{1,0:T(8,128)(2,1)}, u32[]{:S(2)}) copy-start(bf16[1024,1024]{1,0:T(8,128)(2,1)} %param.12) | copy-start | bytes 6291460
  10.4 49.6 %collective-permute-start.4 = (bf16[512,768]{1,0:T(8,128)(2,1)}, bf16[512,768]{1,0:T(8,128)(2,1)}, u32[]{:S(2)}, u32[]{:S(2)}) collective-permute-start(bf16[512,768]{1,0:T(8,128)(2,1)} %pad_maximum_fusion.1), channel_id=1, source_target_pairs={{0,1},{1,2},{2,3},{3,4},{4,5},{5,6},{6,7},{8,9},{9,10},{10,11},{11... | collective-permute-start | bytes 2359304 | tf_op jit(solution)/shard_map/ppermute | solution.py:377
  12.9 29.3 %collective-permute-start.5 = (bf16[512,768]{1,0:T(8,128)(2,1)S(1)}, bf16[512,768]{1,0:T(8,128)(2,1)}, u32[]{:S(2)}, u32[]{:S(2)}) collective-permute-start(bf16[512,768]{1,0:T(8,128)(2,1)S(1)} %pad_maximum_fusion.2), channel_id=1, source_target_pairs={{0,1},{1,2},{2,3},{3,4},{4,5},{5,6},{6,7},{8,9},{9,10},{10,11},{11... | collective-permute-start | bytes 2359304 | tf_op jit(solution)/shard_map/ppermute | solution.py:377
  20.2 15.7 %collective-permute-start.2 = (bf16[32,2048]{1,0:T(8,128)(2,1)S(1)}, bf16[32,2048]{1,0:T(8,128)(2,1)S(1)}, u32[]{:S(2)}, u32[]{:S(2)}) collective-permute-start(bf16[32,2048]{1,0:T(8,128)(2,1)S(1)} %maximum_select_fusion.2), channel_id=1, source_target_pairs={{0,2},{1,3},{2,0},{3,1},{4,6},{5,7},{6,4},{7,5},{8,10},{9,11},{10,... | collective-permute-start | bytes 393224 | tf_op jit(solution)/shard_map/ppermute | solution.py:323
  36.0 5.3 %collective-permute-start.3 = (bf16[64,2048]{1,0:T(8,128)(2,1)S(1)}, bf16[64,2048]{1,0:T(8,128)(2,1)S(1)}, u32[]{:S(2)}, u32[]{:S(2)}) collective-permute-start(bf16[64,2048]{1,0:T(8,128)(2,1)S(1)} %maximum_select_fusion.1), channel_id=1, source_target_pairs={{0,4},{1,5},{2,6},{3,7},{4,0},{5,1},{6,2},{7,3},{8,12},{9,13},{10,... | collective-permute-start | bytes 786440 | tf_op jit(solution)/shard_map/ppermute | solution.py:323
  93.0 3.2 %collective-permute-start.6 = (bf16[4,160,1024]{2,1,0:T(8,128)(2,1)S(1)}, bf16[4,160,1024]{2,1,0:T(8,128)(2,1)}, u32[]{:S(2)}, u32[]{:S(2)}) collective-permute-start(bf16[4,160,1024]{2,1,0:T(8,128)(2,1)S(1)} %pad_maximum_fusion), channel_id=1, source_target_pairs={{0,1},{1,0},{2,3},{3,2},{4,5},{5,4},{6,7},{7,6},{8,9},{9,8},{10,11... | collective-permute-start | bytes 3932168 | tf_op jit(solution)/shard_map/ppermute | solution.py:323
  97.8 9.2 %collective-permute-start.7 = (bf16[160,1024]{1,0:T(8,128)(2,1)S(1)}, bf16[160,1024]{1,0:T(8,128)(2,1)S(1)}, u32[]{:S(2)}, u32[]{:S(2)}) collective-permute-start(bf16[160,1024]{1,0:T(8,128)(2,1)S(1)} %get-tuple-element.68), channel_id=1, source_target_pairs={{0,2},{1,3},{2,0},{3,1},{4,6},{5,7},{6,4},{7,5},{8,10},{9,11},{10,... | collective-permute-start | bytes 983048 | tf_op jit(solution)/shard_map/ppermute | solution.py:323
  99.1 8.9 %collective-permute-start.8 = (bf16[160,1024]{1,0:T(8,128)(2,1)S(1)}, bf16[160,1024]{1,0:T(8,128)(2,1)S(1)}, u32[]{:S(2)}, u32[]{:S(2)}) collective-permute-start(bf16[160,1024]{1,0:T(8,128)(2,1)S(1)} %get-tuple-element.69), channel_id=1, source_target_pairs={{0,4},{1,5},{2,6},{3,7},{4,0},{5,1},{6,2},{7,3},{8,12},{9,13},{10,... | collective-permute-start | bytes 983048 | tf_op jit(solution)/shard_map/ppermute | solution.py:323
  99.1 15.8 %collective-permute-start.9 = (bf16[160,1024]{1,0:T(8,128)(2,1)S(1)}, bf16[160,1024]{1,0:T(8,128)(2,1)S(1)}, u32[]{:S(2)}, u32[]{:S(2)}) collective-permute-start(bf16[160,1024]{1,0:T(8,128)(2,1)S(1)} %get-tuple-element.70), channel_id=1, source_target_pairs={{0,6},{1,7},{2,4},{3,5},{4,2},{5,3},{6,0},{7,1},{8,14},{9,15},{10,... | collective-permute-start | bytes 983048 | tf_op jit(solution)/shard_map/ppermute | solution.py:323
  118.6 8.1 %collective-permute-start.13 = (bf16[32,1024]{1,0:T(8,128)(2,1)}, bf16[32,1024]{1,0:T(8,128)(2,1)}, u32[]{:S(2)}, u32[]{:S(2)}) collective-permute-start(bf16[32,1024]{1,0:T(8,128)(2,1)} %get-tuple-element.77), channel_id=1, source_target_pairs={{0,8},{8,0},{16,24},{24,16},{1,9},{9,1},{17,25},{25,17},{2,10},{10... | collective-permute-start | bytes 196616 | tf_op jit(solution)/shard_map/ppermute | solution.py:323
  119.9 6.8 %collective-permute-start.15 = (bf16[32,1024]{1,0:T(8,128)(2,1)}, bf16[32,1024]{1,0:T(8,128)(2,1)}, u32[]{:S(2)}, u32[]{:S(2)}) collective-permute-start(bf16[32,1024]{1,0:T(8,128)(2,1)} %get-tuple-element.78), channel_id=1, source_target_pairs={{0,24},{8,16},{16,8},{24,0},{1,25},{9,17},{17,9},{25,1},{2,26},{10... | collective-permute-start | bytes 196616 | tf_op jit(solution)/shard_map/ppermute | solution.py:323
  122.1 6.2 %collective-permute-start.14 = (bf16[32,1024]{1,0:T(8,128)(2,1)}, bf16[32,1024]{1,0:T(8,128)(2,1)}, u32[]{:S(2)}, u32[]{:S(2)}) collective-permute-start(bf16[32,1024]{1,0:T(8,128)(2,1)} %get-tuple-element.79), channel_id=1, source_target_pairs={{0,16},{8,24},{16,0},{24,8},{1,17},{9,25},{17,1},{25,9},{2,18},{10... | collective-permute-start | bytes 196616 | tf_op jit(solution)/shard_map/ppermute | solution.py:323
  130.0 16.6 %collective-permute-start.18 = (bf16[32,1024]{1,0:T(8,128)(2,1)}, bf16[32,1024]{1,0:T(8,128)(2,1)}, u32[]{:S(2)}, u32[]{:S(2)}) collective-permute-start(bf16[32,1024]{1,0:T(8,128)(2,1)} %get-tuple-element.67), channel_id=1, source_target_pairs={{0,24},{8,16},{16,8},{24,0},{1,25},{9,17},{17,9},{25,1},{2,26},{10... | collective-permute-start | bytes 196616 | tf_op jit(solution)/shard_map/ppermute | solution.py:323
  132.4 14.2 %collective-permute-start.17 = (bf16[32,1024]{1,0:T(8,128)(2,1)}, bf16[32,1024]{1,0:T(8,128)(2,1)}, u32[]{:S(2)}, u32[]{:S(2)}) collective-permute-start(bf16[32,1024]{1,0:T(8,128)(2,1)} %get-tuple-element.67), channel_id=1, source_target_pairs={{0,16},{8,24},{16,0},{24,8},{1,17},{9,25},{17,1},{25,9},{2,18},{10... | collective-permute-start | bytes 196616 | tf_op jit(solution)/shard_map/ppermute | solution.py:323
  132.4 14.2 %collective-permute-start.16 = (bf16[32,1024]{1,0:T(8,128)(2,1)}, bf16[32,1024]{1,0:T(8,128)(2,1)}, u32[]{:S(2)}, u32[]{:S(2)}) collective-permute-start(bf16[32,1024]{1,0:T(8,128)(2,1)} %get-tuple-element.67), channel_id=1, source_target_pairs={{0,8},{8,0},{16,24},{24,16},{1,9},{9,1},{17,25},{25,17},{2,10},{10... | collective-permute-start | bytes 196616 | tf_op jit(solution)/shard_map/ppermute | solution.py:323
  142.0 58.3 %collective-permute-start.10 = (bf16[1024,512]{1,0:T(8,128)(2,1)}, bf16[1024,512]{1,0:T(8,128)(2,1)}, u32[]{:S(2)}, u32[]{:S(2)}) collective-permute-start(bf16[1024,512]{1,0:T(8,128)(2,1)} %get-tuple-element.59), channel_id=1, source_target_pairs={{1,0},{2,1},{3,2},{4,3},{5,4},{6,5},{7,6},{9,8},{10,9},{11,10},{12... | collective-permute-start | bytes 3145736 | tf_op jit(solution)/shard_map/ppermute | solution.py:417
  147.5 25.0 %collective-permute-start.21 = (bf16[128,1024]{1,0:T(8,128)(2,1)S(1)}, bf16[128,1024]{1,0:T(8,128)(2,1)S(1)}, u32[]{:S(2)}, u32[]{:S(2)}) collective-permute-start(bf16[128,1024]{1,0:T(8,128)(2,1)S(1)} %pad_maximum_fusion.4), channel_id=1, source_target_pairs={{0,6},{1,7},{2,4},{3,5},{4,2},{5,3},{6,0},{7,1},{8,14},{9,15},{10,... | collective-permute-start | bytes 786440 | tf_op jit(solution)/shard_map/ppermute | solution.py:323
  148.8 23.0 %collective-permute-start.20 = (bf16[128,1024]{1,0:T(8,128)(2,1)S(1)}, bf16[128,1024]{1,0:T(8,128)(2,1)S(1)}, u32[]{:S(2)}, u32[]{:S(2)}) collective-permute-start(bf16[128,1024]{1,0:T(8,128)(2,1)S(1)} %pad_maximum_fusion.4), channel_id=1, source_target_pairs={{0,4},{1,5},{2,6},{3,7},{4,0},{5,1},{6,2},{7,3},{8,12},{9,13},{10,... | collective-permute-start | bytes 786440 | tf_op jit(solution)/shard_map/ppermute | solution.py:323
  149.0 13.0 %collective-permute-start.19 = (bf16[128,1024]{1,0:T(8,128)(2,1)S(1)}, bf16[128,1024]{1,0:T(8,128)(2,1)S(1)}, u32[]{:S(2)}, u32[]{:S(2)}) collective-permute-start(bf16[128,1024]{1,0:T(8,128)(2,1)S(1)} %pad_maximum_fusion.4), channel_id=1, source_target_pairs={{0,2},{1,3},{2,0},{3,1},{4,6},{5,7},{6,4},{7,5},{8,10},{9,11},{10,... | collective-permute-start | bytes 786440 | tf_op jit(solution)/shard_map/ppermute | solution.py:323
  173.2 36.0 %collective-permute-start.22 = (bf16[512,1024]{1,0:T(8,128)(2,1)}, bf16[512,1024]{1,0:T(8,128)(2,1)}, u32[]{:S(2)}, u32[]{:S(2)}) collective-permute-start(bf16[512,1024]{1,0:T(8,128)(2,1)} %constant_dynamic-update-slice_fusion.w_ref), channel_id=1, source_target_pairs={{0,1},{1,0},{2,3},{3,2},{4,5},{5,4},{6,7},{7,6},{8,9},{9,8},{10,11... | collective-permute-start | bytes 3145736 | tf_op jit(solution)/shard_map/ppermute | solution.py:323
  180.1 15.1 %collective-permute-start.11 = (bf16[1024,256]{1,0:T(8,128)(2,1)}, bf16[1024,256]{1,0:T(8,128)(2,1)}, u32[]{:S(2)}, u32[]{:S(2)}) collective-permute-start(bf16[1024,256]{1,0:T(8,128)(2,1)} %get-tuple-element.60), channel_id=1, source_target_pairs={{1,0},{2,1},{3,2},{4,3},{5,4},{6,5},{7,6},{9,8},{10,9},{11,10},{12... | collective-permute-start | bytes 1572872 | tf_op jit(solution)/shard_map/ppermute | solution.py:417
  188.6 11.7 %collective-permute-start.12 = (bf16[1024,256]{1,0:T(8,128)(2,1)}, bf16[1024,256]{1,0:T(8,128)(2,1)}, u32[]{:S(2)}, u32[]{:S(2)}) collective-permute-start(bf16[1024,256]{1,0:T(8,128)(2,1)} %get-tuple-element.61), channel_id=1, source_target_pairs={{1,0},{2,1},{3,2},{4,3},{5,4},{6,5},{7,6},{9,8},{10,9},{11,10},{12... | collective-permute-start | bytes 1572872 | tf_op jit(solution)/shard_map/ppermute | solution.py:417
  (8 other events, 33.8 us)

commit v3 on v2

--- a/solution.py
+++ b/solution.py
@@ -43,11 +43,11 @@
 
 
 def forward_kernel(
-    info_ref, q_ref, g_ref, ko_ref, vo_ref, kh_ref, vh_ref, km_ref, vm_ref, mb_ref, *rest, nb, members
+    info_ref, q_ref, g_ref, ko_ref, vo_ref, kh_ref, vh_ref, km_ref, vm_ref, mb_ref, *rest, nb, order
 ):
     at_ref, dm_ref, pt, ga_ref, ke, ve, q2s, pm = rest[-8:]
     slots = km_ref.shape[0]
-    mine = slots // members
+    mine = slots // len(order)
     ext = kh_ref.shape[0] + ko_ref.shape[0]
     fill_keys(ke, kh_ref, ko_ref, km_ref)
     fill_keys(ve, vh_ref, vo_ref, vm_ref)
@@ -59,30 +59,43 @@
     )
     lane = lax.broadcasted_iota(jnp.int32, (TWO, SPAN), 1)
     row = lax.broadcasted_iota(jnp.int32, (TWO, SPAN), 0) % BLK
-    for b in range(nb):
-        rows, cols = slice(b * BLK, (b + 1) * BLK), slice(b * TWO, (b + 1) * TWO)
-        band = slice(b * BLK, (b + FAR + 1) * BLK)
-        q2 = by_head(q_ref[rows, :] * jnp.asarray(HEAD_DIM**-0.5, bf16), first)
+    unit = jnp.asarray(HEAD_DIM**-0.5, bf16)
+    at = lambda b: (slice(b * BLK, (b + 1) * BLK), slice(b * TWO, (b + 1) * TWO), slice(b * BLK, (b + FAR + 1) * BLK))
+    scores, outs = {}, {}
+
+    def score(b):
+        rows, cols, band = at(b)
+        q2 = by_head(q_ref[rows, :] * unit, first)
         q2s[cols, :] = q2
-        s = dot(ke[band, :], q2, NT)
-        sm = dot(ke[ext:, :], q2, NT) + jnp.concatenate([mb_ref[b], mb_ref[b]], 1)
-        lo = info_ref[0, b]
-        off = [jnp.where(e + b >= lo, 0.0, NEG).astype(f32) for e in range(FAR)]
+        scores[b] = (dot(ke[band, :], q2, NT), dot(ke[ext:, :], q2, NT))
+
+    def exponentials(b):
+        _, cols, _ = at(b)
+        s, sm = scores.pop(b)
+        sm = sm + jnp.concatenate([mb_ref[b], mb_ref[b]], 1)
+        off = [jnp.where(e + b >= info_ref[0, b], 0.0, NEG).astype(f32) for e in range(FAR)]
         ends = jnp.where(tri, s[FAR * BLK :, :], s[:BLK, :] + off[0])
         mid = [s[e * BLK : (e + 1) * BLK, :] for e in range(1, FAR)]
         m = jnp.maximum(jnp.max(ends, 0, keepdims=True), jnp.max(sm, 0, keepdims=True))
         for e in range(1, FAR):
             m = jnp.maximum(m, jnp.max(mid[e - 1], 0, keepdims=True) + off[e])
-        p = jnp.exp(ends - m).astype(bf16)
-        zero = jnp.zeros_like(p)
-        pt[0, b * BLK : (b + 1) * BLK, cols] = jnp.where(tri, zero, p)
-        pt[0, (b + FAR) * BLK : (b + FAR + 1) * BLK, cols] = jnp.where(tri, p, zero)
         for e in range(1, FAR):
             pt[0, (b + e) * BLK : (b + e + 1) * BLK, cols] = jnp.exp(
                 mid[e - 1] - (m - off[e])
             ).astype(bf16)
         pm[:, cols] = jnp.exp(sm - m).astype(bf16)
-        o = dot(pt[0, band, cols], ve[band, :], TN) + dot(pm[:, cols], ve[ext:, :], TN)
+        p = jnp.exp(ends - m).astype(bf16)
+        zero = jnp.zeros_like(p)
+        pt[0, b * BLK : (b + 1) * BLK, cols] = jnp.where(tri, zero, p)
+        pt[0, (b + FAR) * BLK : (b + FAR + 1) * BLK, cols] = jnp.where(tri, p, zero)
+
+    def attend(b):
+        _, cols, band = at(b)
+        outs[b] = dot(pt[0, band, cols], ve[band, :], TN) + dot(pm[:, cols], ve[ext:, :], TN)
+
+    def gradients(b):
+        rows, cols, _ = at(b)
+        o = outs.pop(b)
         scale = jnp.where(row < info_ref[1, b], 1.0 / o[:, SPAN:], 0.0)
         o = o[:, :SPAN] * scale
         at_ref[rows, :] = join_heads(o, first).astype(bf16)
@@ -93,12 +106,20 @@
         ga_ref[0, cols, SPAN:] = jnp.where(
             lane == 0, high, jnp.where(lane == 1, d - high, 0.0)
         ).astype(bf16)
+
+    def memory(b):
+        _, cols, _ = at(b)
         dp = dot(ve[ext:, :], ga_ref[0, cols, :], NT)
         pt[0, ext:, cols] = (pm[:, cols].astype(f32) * dp).astype(bf16)
+
+    for t in range(nb + 4):
+        for stage, lag in ((score, 0), (attend, 2), (exponentials, 1), (memory, 4), (gradients, 3)):
+            if 0 <= t - lag < nb:
+                stage(t - lag)
     dk = dot(pt[0, ext:, :], q2s[...], NN).astype(bf16)
     dv = dot(pm[...], ga_ref[0, :, :SPAN], NN).astype(bf16)
-    for j in range(members):
-        part = slice(j * mine, (j + 1) * mine)
+    for i, j in enumerate(order):
+        part = slice(i * mine, (i + 1) * mine)
         dm_ref[2 * j * mine : (2 * j + 1) * mine, :] = dk[part]
         dm_ref[(2 * j + 1) * mine : (2 * j + 2) * mine, :] = dv[part]
 
@@ -145,7 +166,7 @@
 ANY = pl.BlockSpec(memory_space=pl.ANY)
 
 
-def forward(info, q, g, ko, vo, kh, vh, km, vm, bias, members, start, count, base, halo_at, carry):
+def forward(info, q, g, ko, vo, kh, vh, km, vm, bias, order, start, count, base, halo_at, carry):
     tokens, width = q.shape
     slots, hrows, nb = km.shape[0], kh.shape[0], tokens // BLK
     keys = hrows + tokens + slots
@@ -163,7 +184,7 @@
         args += carry
         specs += [ANY] * len(carry)
     return pl.pallas_call(
-        functools.partial(forward_kernel, nb=nb, members=members),
+        functools.partial(forward_kernel, nb=nb, order=order),
         grid_spec=pltpu.PrefetchScalarGridSpec(
             num_scalar_prefetch=1,
             grid=(count,),
@@ -270,35 +291,38 @@
     )(slots[None, :], dko, dvo, dmem, *backs)
 
 
-def place_kernel(where_ref, w_ref, *rest, nfam, scale):
-    out_ref = rest[-1]
-    piece = w_ref.shape[0] // nfam
-    fam = where_ref[2]
-    for k in range(nfam):
-        row = pl.multiple_of((fam ^ k) * piece, piece)
-        out_ref[pl.ds(row, piece), :] = w_ref[k * piece : (k + 1) * piece, :].astype(f32) * scale
-
-
-def place(where, w, plane, nfam, scale, carry):
-    half, width = w.shape
-    rows = half // plane
-    args, specs, alias = [w], [pl.BlockSpec((rows, width), lambda k, s: (k, 0))], {}
-    if carry is not None:
-        args, specs, alias = args + [carry], specs + [ANY], {2: 0}
+def place_kernel(where_ref, *rest, plane, nfam, scale):
+    n = 2 * plane
+    parts, out_ref, buf, sems = rest[:n], rest[n], rest[n + 1], rest[n + 2]
+    rows = parts[0].shape[0]
+    piece = rows // nfam
+    core, spot, fam = where_ref[0], where_ref[1], where_ref[2]
+    copies = []
+    for i, part in enumerate(parts):
+        side = jnp.where(i < plane, core, 1 - core)
+        at = pl.multiple_of((side * plane + (spot ^ (i % plane))) * rows, rows)
+        for k in range(nfam):
+            row = pl.multiple_of((fam ^ k) * piece, piece)
+            buf[i, pl.ds(row, piece), :] = part[k * piece : (k + 1) * piece, :].astype(f32) * scale
+        copies.append(pltpu.make_async_copy(buf.at[i], out_ref.at[pl.ds(at, rows), :], sems.at[i]))
+        copies[-1].start()
+    for copy in copies:
+        copy.wait()
+
+
+def place(where, parts, nfam, scale):
+    rows, width = parts[0].shape
+    n = len(parts)
     return pl.pallas_call(
-        functools.partial(place_kernel, nfam=nfam, scale=scale),
-        grid_spec=pltpu.PrefetchScalarGridSpec(
-            num_scalar_prefetch=1,
-            grid=(plane,),
-            in_specs=specs,
-            out_specs=pl.BlockSpec((rows, width), lambda k, s: (s[0] * plane + (s[1] ^ k), 0)),
-        ),
-        out_shape=jax.ShapeDtypeStruct((2 * half, width), f32),
-        input_output_aliases=alias,
+        functools.partial(place_kernel, plane=n // 2, nfam=nfam, scale=scale),
+        in_specs=[pl.BlockSpec(memory_space=pltpu.SMEM)] + [pl.BlockSpec(memory_space=pltpu.VMEM)] * n,
+        out_specs=pl.BlockSpec(memory_space=pl.ANY),
+        out_shape=jax.ShapeDtypeStruct((n * rows, width), f32),
+        scratch_shapes=[pltpu.VMEM((n, rows, width), f32), pltpu.SemaphoreType.DMA((n,))],
         compiler_params=pltpu.CompilerParams(vmem_limit_bytes=67_000_000),
-        cost_estimate=pl.CostEstimate(flops=1 << 20, bytes_accessed=3 << 20, transcendentals=0),
+        cost_estimate=pl.CostEstimate(flops=1 << 20, bytes_accessed=6 << 20, transcendentals=0),
         name="place_rows",
-    )(where, *args)
+    )(where, *parts)
 
 
 def protein_tables(prot_blocks, last_fill):
@@ -331,8 +355,15 @@
     return out
 
 
+def mirrored(n):
+    order = [0]
+    for bit in reversed(bits_of(n)):
+        order = order + [i + bit for i in order]
+    return order
+
+
 def gather_rows(x, axis, me):
-    for bit in bits_of(lax.axis_size(axis)):
+    for bit in reversed(bits_of(lax.axis_size(axis))):
         other = swap(x, axis, bit)
         upper = (me & bit) != 0
         x = jnp.where(upper, jnp.concatenate([other, x], 0), jnp.concatenate([x, other], 0))
@@ -340,19 +371,22 @@
 
 
 def exchange(part, axis, shift, me, n):
-    got = [swap(part(me ^ k).astype(bf16), axis, k << shift) for k in range(1, n)]
-    return sum([g.astype(f32) for g in got], part(me))
+    return [part(me)] + [swap(part(me ^ k).astype(bf16), axis, k << shift) for k in range(1, n)]
 
 
 def spread(x, axis, shift, n):
-    return jnp.concatenate([x] + [swap(x, axis, k << shift) for k in range(1, n)], 0)
+    return [x] + [swap(x, axis, k << shift) for k in range(1, n)]
+
+
+def total_of(parts):
+    return sum([x.astype(f32) for x in parts[1:]], parts[0].astype(f32))
 
 
 def groups_of(pairs):
     if pairs % 8:
         return [pairs], [(0, 0, pairs)], [pairs]
     u = pairs // 8
-    return [3 * u, 3 * u, 2 * u], [(0, 0, u), (1, 0, 3 * u), (0, u, 2 * u), (2, 0, 2 * u)], [4 * u, 2 * u, 2 * u]
+    return [2 * u, 3 * u, 3 * u], [(0, 0, 2 * u), (1, 0, 3 * u), (2, 0, u), (2, u, 2 * u)], [6 * u, 2 * u]
 
 
 def per_device(queries, key_rows, value_rows, cotangent, out_weight, prot_blocks, last_fill, memory_slots):
@@ -381,7 +415,8 @@
     mem = gather_rows(rows, "ctx", me)
     grad_attn = dot(cot, out_weight, NT).astype(bf16)
     heads = me * tokens + jnp.arange(nb, dtype=jnp.int32) * BLK
-    source = jnp.arange(total, dtype=jnp.int32) // mine * tokens + slots
+    order = mirrored(nctx)
+    source = (jnp.asarray(order, jnp.int32)[:, None] * tokens + slots.reshape(nctx, mine)[jnp.asarray(order)]).reshape(-1)
     prot, first, left = token_info(jnp.concatenate([heads, source]), tables)
     lo = jnp.clip(first[:nb] - (me * tokens - W) // BLK, 0, nb + FAR)
     info = jnp.stack([lo, jnp.clip(left[:nb], 0, BLK)])
@@ -391,7 +426,7 @@
     carry, saved = [], []
     for i, (at, count) in enumerate(zip(fstarts, fsizes)):
         att, dm, pt, ga = forward(
-            info, q, grad_attn, k, v, halos[i], halos[i], mem, mem, bias, nctx,
+            info, q, grad_attn, k, v, halos[i], halos[i], mem, mem, bias, order,
             at, count, base, (0, count), carry)
         carry = [att, dm]
         saved.append((pt, ga))
@@ -415,17 +450,16 @@
             segments.append((len(backs), fstarts[j] + r, done, count))
             done, i = done + count, i + 1
         backs.append(lax.ppermute(carry.pop(), "ctx", back))
-    total_w = exchange(
-        lambda j: at(sent, j, 0).astype(f32) + at(kept, j, 0).astype(f32), "ctx", 1, spot, plane)
-    mem_grad, total_w = total_w[width // nctx :].astype(bf16), total_w[: width // nctx].reshape(nfam, -1, width)
-    total_w = exchange(lambda j: at(total_w, j, 0), "fam", 0, fam, nfam)
-    w = spread(total_w.astype(bf16), "fam", 0, nfam)
-    w = spread(w, "ctx", 1, plane)
-    other = swap(w, "ctx", 1)
+    got = exchange(lambda j: at(sent, j, 0).astype(f32) + at(kept, j, 0).astype(f32), "ctx", 1, spot, plane)
+    rows = width // nctx
+    mem_grad = total_of([x[rows:] for x in got]).astype(bf16)
+    piece = lambda j: total_of([lax.dynamic_slice_in_dim(x, j * (rows // nfam), rows // nfam) for x in got])
+    w = total_of(exchange(piece, "fam", 0, fam, nfam)).astype(bf16)
+    w = jnp.concatenate(spread(w, "fam", 0, nfam), 0)
+    parts = spread(w, "ctx", 1, plane)
+    parts = parts + [swap(x, "ctx", 1) for x in parts]
     scale = (nfam * nctx * tokens) ** -0.5
-    where = lambda c: jnp.stack([c, spot, fam]).astype(jnp.int32)
-    weight = place(where(core), w, plane, nfam, scale, None)
-    weight = place(where(1 - core), other, plane, nfam, scale, weight)
+    weight = place(jnp.stack([core, spot, fam]).astype(jnp.int32), parts, nfam, scale)
     dq, dko, dvo = carry
     backs = [x.reshape(2, W, -1) for x in backs]
     dk, dv = finish(own_slots, dko, dvo, mem_grad, backs, segments)

time: 215 us -> 161 us (0.75)
  waiting for transfers between devices: 59.4 us -> 27.3 us
  Pallas kernels: 85.7 us -> 66.6 us
  local copies, waits for them, and re-layouts: 13.3 us -> 6.58 us
  other arithmetic: 10.9 us -> 14.4 us
    ppermute x17 -> x20, waiting for transfers between devices: 54.4 us -> 27.2 us  [swap(): lax.ppermute(x, axis, [(i, i ^ bits) for i in range(lax.axis_size(axis))])]
    pallas_call x5 -> x4, Pallas kernels: 55.2 us -> 35.9 us  [the longest x3 32.3 us: forward(): pl.pallas_call(functools.partial(forward_kernel, nb=nb, order=order), gri...]
    unnamed x23 -> x21, local copies, waits for them, and re-layouts: 7.49 us -> 1.35 us
    ppermute x3 -> x2, waiting for transfers between devices: 5.04 us -> 0.01 us  [per_device(): backs.append(lax.ppermute(carry.pop(), 'ctx', back))]
    ppermute x3 -> x2, starting transfers between devices: 9.75 us -> 5.59 us  [per_device(): backs.append(lax.ppermute(carry.pop(), 'ctx', back))]
    ppermute x17 -> x20, starting transfers between devices: 15.5 us -> 19.3 us  [swap(): lax.ppermute(x, axis, [(i, i ^ bits) for i in range(lax.axis_size(axis))])]
    convert_element_type x1 -> x2, other arithmetic: 1.55 us -> 5.04 us  [exchange(): part(me ^ k).astype(bf16)]
  transfers between devices with their start and end apart: 23 -> 25, of which waited for: 10 -> 6; matrix products, arithmetic and copies ran while one was open for 9% -> 11% of each run, Pallas kernels for 32% -> 32%
where the time goes in v3:
time: 161 us; the launch traced here: 159 us
  Pallas kernels  66.6 us (41%)
  starting transfers between devices  33.3 us (21%)
  waiting for transfers between devices  27.3 us (17%)
  other arithmetic  14.4 us (9%)
  matrix products  9.8 us (6%)
  local copies, waits for them, and re-layouts  6.58 us (4%)
    pallas_call x3, Pallas kernels, forward(): pl.pallas_call(functools.partial(forward_kernel, nb=nb, order=order), gri...  32.3 us
    ppermute x20, waiting for transfers between devices, swap(): lax.ppermute(x, axis, [(i, i ^ bits) for i in range(lax.axis_size(axis))])  27.2 us
    pallas_call x4, Pallas kernels, backward(): pl.pallas_call(functools.partial(backward_kernel, nb=nb), grid=(count,),...  26.1 us
    ppermute x20, starting transfers between devices, swap(): lax.ppermute(x, axis, [(i, i ^ bits) for i in range(lax.axis_size(axis))])  19.3 us
    dot_general x4, matrix products, dot(): return lax.dot_general(a, b, dims, preferred_element_type=f32)  9.8 us
    ppermute x3, starting transfers between devices, per_device(): lax.ppermute(jnp.concatenate([k[edge:, cols], v[edge:, cols]], 1), 'ctx',...  8.35 us
    ppermute x2, starting transfers between devices, per_device(): backs.append(lax.ppermute(carry.pop(), 'ctx', back))  5.59 us
    convert_element_type x2, other arithmetic, exchange(): part(me ^ k).astype(bf16)  5.04 us
  transfers between devices with their start and end apart: 25, of which 6 were waited for; matrix products, arithmetic and copies ran while one was open for 11% of the time, Pallas kernels for 32%

profile of v3, /device:TPU:3, one launch (start us, length us, event | category | flops | bytes accessed | tf_op | source)
XLA Modules:
  0.0 159.2 jit_solution(826801576811109803)
XLA Ops:
  6.0 2.5 %collective-permute-start.5 = (bf16[512,512]{1,0:T(8,128)(2,1)S(1)}, bf16[512,512]{1,0:T(8,128)(2,1)S(1)}, u32[]{:S(2)}, u32[]{:S(2)}) collective-permute-start(bf16[512,512]{1,0:T(8,128)(2,1)S(1)} %pad_maximum_fusion.3), channel_id=1, source_target_pairs={{0,1},{1,2},{2,3},{3,4},{4,5},{5,6},{6,7},{8,9},{9,10},{10,11},{11... | collective-permute-start | bytes 1572872 | tf_op jit(solution)/shard_map/ppermute | solution.py:411
  12.5 4.0 %collective-permute-start.4 = (bf16[512,768]{1,0:T(8,128)(2,1)}, bf16[512,768]{1,0:T(8,128)(2,1)}, u32[]{:S(2)}, u32[]{:S(2)}) collective-permute-start(bf16[512,768]{1,0:T(8,128)(2,1)} %pad_maximum_fusion.2), channel_id=1, source_target_pairs={{0,1},{1,2},{2,3},{3,4},{4,5},{5,6},{6,7},{8,9},{9,10},{10,11},{11... | collective-permute-start | bytes 2359304 | tf_op jit(solution)/shard_map/ppermute | solution.py:411
  19.1 3.9 %convolution_convert_fusion.1.g_ref = bf16[512,1024]{1,0:T(8,128)(2,1)} fusion(bf16[1024,1024]{1,0:T(8,128)(2,1)} %param.14, bf16[1,512,1024]{2,1,0:T(8,128)(2,1)S(1)} %copy-done.7), kind=kOutput, calls=%fused_computation.6 | convolution fusion | flops 1074266112 | bytes 4194304 | tf_op jit(solution)/shard_map/dot_general | solution.py:26
  23.2 13.3 %collective-permute-done.2 = bf16[32,2048]{1,0:T(8,128)(2,1)S(1)} collective-permute-done((bf16[32,2048]{1,0:T(8,128)(2,1)S(1)}, bf16[32,2048]{1,0:T(8,128)(2,1)S(1)}, u32[]{:S(2)}, u32[]{:S(2)}) %collective-permute-start.2) | collective-permute-done | bytes 131104 | tf_op jit(solution)/shard_map/ppermute | solution.py:347
  40.6 9.1 %band_forward.3 = (bf16[512,1024]{1,0:T(8,128)(2,1)}, bf16[256,1024]{1,0:T(8,128)(2,1)}, bf16[2,1152,1024]{2,1,0:T(8,128)(2,1)}, bf16[2,1024,256]{2,1,0:T(8,128)(2,1)}) custom-call(s32[2,4]{1,0:T(2,128)} %pad_add_fusion.1.info_ref, bf16[512,1024]{1,0:T(8,128)(2,1)} %bitcast.125, bf16[512,1024]{1,0:T(8,128)(2,1)} %convolution_convert_fusion.1.g_ref, ...), custom_call_target="tpu_custom_call" | custom-call | flops 3221225472 | bytes 8388608 | tf_op jit(solution)/shard_map/band_forward/pallas_call | solution.py:186
  49.7 11.6 %band_forward.4 = (bf16[512,1024]{1,0:T(8,128)(2,1)}, bf16[256,1024]{1,0:T(8,128)(2,1)}, bf16[3,1152,1024]{2,1,0:T(8,128)(2,1)}, bf16[3,1024,256]{2,1,0:T(8,128)(2,1)}) custom-call(s32[2,4]{1,0:T(2,128)} %pad_add_fusion.1.info_ref, bf16[512,1024]{1,0:T(8,128)(2,1)} %bitcast.126, ...), custom_call_target="tpu_custom_call", output_to_operand_aliasing={{0}: (10, {}), {1}: (11, {})} | custom-call | flops 4831838208 | bytes 12582912 | tf_op jit(solution)/shard_map/band_forward/pallas_call | solution.py:186
  61.3 11.6 %band_forward.5 = (bf16[512,1024]{1,0:T(8,128)(2,1)}, bf16[256,1024]{1,0:T(8,128)(2,1)}, bf16[3,1152,1024]{2,1,0:T(8,128)(2,1)}, bf16[3,1024,256]{2,1,0:T(8,128)(2,1)}) custom-call(s32[2,4]{1,0:T(2,128)} %pad_add_fusion.1.info_ref, bf16[512,1024]{1,0:T(8,128)(2,1)} %bitcast.127, ...), custom_call_target="tpu_custom_call", output_to_operand_aliasing={{0}: (10, {}), {1}: (11, {})} | custom-call | flops 4831838208 | bytes 12582912 | tf_op jit(solution)/shard_map/band_forward/pallas_call | solution.py:186
  73.0 2.9 %convolution_convert_fusion = bf16[1024,1024]{1,0:T(8,128)(2,1)S(1)} fusion(bf16[512,1024]{1,0:T(8,128)(2,1)} %get-tuple-element.58, bf16[1,512,1024]{2,1,0:T(8,128)(2,1)} %param.13), kind=kOutput, calls=%fused_computation.5 | convolution fusion | flops 1074790400 | bytes 4194304 | tf_op jit(solution)/shard_map/dot_general | solution.py:26
  79.1 6.4 %band_backward.4 = (bf16[512,1024]{1,0:T(8,128)(2,1)}, bf16[512,1024]{1,0:T(8,128)(2,1)}, bf16[512,1024]{1,0:T(8,128)(2,1)}, bf16[1024,768]{1,0:T(8,128)(2,1)}) custom-call(bf16[512,1024]{1,0:T(8,128)(2,1)} %bitcast.128, bf16[2,1152,1024]{2,1,0:T(8,128)(2,1)} %get-tuple-element.42.pt_ref, bf16[2,1024,256]{2,1,0:T(8,128)(2,1)} %get-tuple-element.43.ga_ref, ...), custom_call_target="tpu_custom_call" | custom-call | flops 5368709120 | bytes 12582912 | tf_op jit(solution)/shard_map/band_backward/pallas_call | solution.py:235
  85.5 3.1 %fusion.2 = (bf16[160,1024]{1,0:T(8,128)(2,1)}, f32[1,160,1024]{2,1,0:T(8,128)}, bf16[160,1024]{1,0:T(8,128)(2,1)}, bf16[160,1024]{1,0:T(8,128)(2,1)}) fusion(s32[]{:T(128)S(6)} %select_n.126, bf16[4,128,1024]{2,1,0:T(8,128)(2,1)} %get-tuple-element.71, bf16[4,32,1024]{2,1,0:T(8,128)(2,1)} %get-tuple-element.82, ...), kind=kLoop, calls=%fused_computation.26 | loop fusion | flops 4423680 | bytes 4259856 | tf_op jit(solution)/shard_map/convert_element_type | solution.py:374
  88.9 2.4 %collective-permute-start.9 = (bf16[160,1024]{1,0:T(8,128)(2,1)}, bf16[160,1024]{1,0:T(8,128)(2,1)}, u32[]{:S(2)}, u32[]{:S(2)}) collective-permute-start(bf16[160,1024]{1,0:T(8,128)(2,1)} %get-tuple-element.69), channel_id=1, source_target_pairs={{0,6},{1,7},{2,4},{3,5},{4,2},{5,3},{6,0},{7,1},{8,14},{9,15},{10,... | collective-permute-start | bytes 983048 | tf_op jit(solution)/shard_map/ppermute | solution.py:347
  91.2 8.7 %band_backward.5 = (bf16[512,1024]{1,0:T(8,128)(2,1)}, bf16[512,1024]{1,0:T(8,128)(2,1)}, bf16[512,1024]{1,0:T(8,128)(2,1)}, bf16[1024,768]{1,0:T(8,128)(2,1)}) custom-call(bf16[512,1024]{1,0:T(8,128)(2,1)} %bitcast.129, bf16[3,1152,1024]{2,1,0:T(8,128)(2,1)} %get-tuple-element.40.pt_ref, ...), custom_call_target="tpu_custom_call", output_to_operand_aliasing={{0}: (8, {}), {1}: (9, {}), {2}: (10, {}), {3}: (11, {})} | custom-call | flops 8053063680 | bytes 18874368 | tf_op jit(solution)/shard_map/band_backward/pallas_call | solution.py:235
  99.9 4.5 %band_backward.6 = (bf16[512,1024]{1,0:T(8,128)(2,1)}, bf16[512,1024]{1,0:T(8,128)(2,1)}, bf16[512,1024]{1,0:T(8,128)(2,1)}, bf16[1024,768]{1,0:T(8,128)(2,1)}) custom-call(bf16[512,1024]{1,0:T(8,128)(2,1)} %bitcast.130, bf16[3,1152,1024]{2,1,0:T(8,128)(2,1)} %get-tuple-element.38.pt_ref, ...), custom_call_target="tpu_custom_call", output_to_operand_aliasing={{0}: (8, {}), {1}: (9, {}), {2}: (10, {}), {3}: (11, {})} | custom-call | flops 2684354560 | bytes 6291456 | tf_op jit(solution)/shard_map/band_backward/pallas_call | solution.py:235
  104.4 3.1 %collective-permute-start.10 = (bf16[1024,768]{1,0:T(8,128)(2,1)}, bf16[1024,768]{1,0:T(8,128)(2,1)}, u32[]{:S(2)}, u32[]{:S(2)}) collective-permute-start(bf16[1024,768]{1,0:T(8,128)(2,1)} %get-tuple-element.60), channel_id=1, source_target_pairs={{1,0},{2,1},{3,2},{4,3},{5,4},{6,5},{7,6},{9,8},{10,9},{11,10},{12... | collective-permute-start | bytes 4718600 | tf_op jit(solution)/shard_map/ppermute | solution.py:452
  110.9 2.2 %collective-permute-start.14 = (bf16[32,1024]{1,0:T(8,128)(2,1)}, bf16[32,1024]{1,0:T(8,128)(2,1)}, u32[]{:S(2)}, u32[]{:S(2)}) collective-permute-start(bf16[32,1024]{1,0:T(8,128)(2,1)} %get-tuple-element.75), channel_id=1, source_target_pairs={{0,24},{8,16},{16,8},{24,0},{1,25},{9,17},{17,9},{25,1},{2,26},{10... | collective-permute-start | bytes 196616 | tf_op jit(solution)/shard_map/ppermute | solution.py:347
  113.2 6.5 %band_backward.7 = (bf16[512,1024]{1,0:T(8,128)(2,1)}, bf16[512,1024]{1,0:T(8,128)(2,1)}, bf16[512,1024]{1,0:T(8,128)(2,1)}, bf16[1024,256]{1,0:T(8,128)(2,1)}) custom-call(bf16[512,1024]{1,0:T(8,128)(2,1)} %bitcast.131, bf16[3,1152,1024]{2,1,0:T(8,128)(2,1)} %get-tuple-element.38.pt_ref, ...), custom_call_target="tpu_custom_call", output_to_operand_aliasing={{0}: (8, {}), {1}: (9, {}), {2}: (10, {})} | custom-call | flops 5368709120 | bytes 12582912 | tf_op jit(solution)/shard_map/band_backward/pallas_call | solution.py:235
  119.6 2.5 %collective-permute-start.11 = (bf16[1024,256]{1,0:T(8,128)(2,1)}, bf16[1024,256]{1,0:T(8,128)(2,1)}, u32[]{:S(2)}, u32[]{:S(2)}) collective-permute-start(bf16[1024,256]{1,0:T(8,128)(2,1)} %get-tuple-element.61), channel_id=1, source_target_pairs={{1,0},{2,1},{3,2},{4,3},{5,4},{6,5},{7,6},{9,8},{10,9},{11,10},{12... | collective-permute-start | bytes 1572872 | tf_op jit(solution)/shard_map/ppermute | solution.py:452
  124.1 2.6 %collective-permute-start.17 = (bf16[32,1024]{1,0:T(8,128)(2,1)S(1)}, bf16[32,1024]{1,0:T(8,128)(2,1)S(1)}, u32[]{:S(2)}, u32[]{:S(2)}) collective-permute-start(bf16[32,1024]{1,0:T(8,128)(2,1)S(1)} %get-tuple-element.72), channel_id=1, source_target_pairs={{0,24},{8,16},{16,8},{24,0},{1,25},{9,17},{17,9},{25,1},{2,26},{10... | collective-permute-start | bytes 196616 | tf_op jit(solution)/shard_map/ppermute | solution.py:347
  129.5 3.7 %collective-permute-done.16 = bf16[32,1024]{1,0:T(8,128)(2,1)S(1)} collective-permute-done((bf16[32,1024]{1,0:T(8,128)(2,1)S(1)}, bf16[32,1024]{1,0:T(8,128)(2,1)S(1)}, u32[]{:S(2)}, u32[]{:S(2)}) %collective-permute-start.16) | collective-permute-done | bytes 65568 | tf_op jit(solution)/shard_map/ppermute | solution.py:347
  138.2 3.9 %collective-permute-done.20.rest_3_ = bf16[128,1024]{1,0:T(8,128)(2,1)} collective-permute-done((bf16[128,1024]{1,0:T(8,128)(2,1)}, bf16[128,1024]{1,0:T(8,128)(2,1)}, u32[]{:S(2)}, u32[]{:S(2)}) %collective-permute-start.20) | collective-permute-done | bytes 262176 | tf_op jit(solution)/shard_map/ppermute | solution.py:347
  142.1 3.1 %collective-permute-start.24 = (bf16[128,1024]{1,0:T(8,128)(2,1)}, bf16[128,1024]{1,0:T(8,128)(2,1)}, u32[]{:S(2)}, u32[]{:S(2)}) collective-permute-start(bf16[128,1024]{1,0:T(8,128)(2,1)} %collective-permute-done.20.rest_3_), channel_id=1, source_target_pairs={{0,1},{1,0},{2,3},{3,2},{4,5},{5,4},{6,7},{7,6},{8,9},{9,8},{10,11... | collective-permute-start | bytes 786440 | tf_op jit(solution)/shard_map/ppermute | solution.py:347
  145.2 3.8 %collective-permute-done.19.rest_2_ = bf16[128,1024]{1,0:T(8,128)(2,1)} collective-permute-done((bf16[128,1024]{1,0:T(8,128)(2,1)}, bf16[128,1024]{1,0:T(8,128)(2,1)}, u32[]{:S(2)}, u32[]{:S(2)}) %collective-permute-start.19) | collective-permute-done | bytes 262176 | tf_op jit(solution)/shard_map/ppermute | solution.py:347
  150.7 4.7 %finish_rows.1 = (bf16[512,1024]{1,0:T(8,128)(2,1)}, bf16[512,1024]{1,0:T(8,128)(2,1)}) custom-call(s32[1,16]{1,0:T(1,128)} %constant_dynamic-slice_fusion.slot_ref, bf16[512,1024]{1,0:T(8,128)(2,1)} %get-tuple-element.56.dk_in, bf16[512,1024]{1,0:T(8,128)(2,1)} %get-tuple-element.57.dv_in, bf16[32,1024]{1,0:T(8,128)(2,1)} %get-tuple-element.73.dm_ref, ...), custom_call_target="tpu_custom_call" | custom-call | flops 67108864 | bytes 6291456 | tf_op jit(solution)/shard_map/finish_rows/pallas_call | solution.py:281
  155.4 3.6 %place_rows.1 = f32[1024,1024]{1,0:T(8,128)} custom-call(s32[3]{0:T(128)} %pad_add_fusion.2.where_ref, bf16[128,1024]{1,0:T(8,128)(2,1)} %pad_maximum_fusion.4.rest_0_, bf16[128,1024]{1,0:T(8,128)(2,1)} %collective-permute-done.18.rest_1_, bf16[128,1024]{1,0:T(8,128)(2,1)} %collective-permute-done.19.rest_2_, ...), custom_call_target="tpu_custom_call" | custom-call | flops 1048576 | bytes 6291456 | tf_op jit(solution)/shard_map/place_rows/pallas_call | solution.py:316
  (100 shorter events, 34.6 us)
Async XLA Ops:
  4.6 18.4 %collective-permute-start.1 = (bf16[16,2048]{1,0:T(8,128)(2,1)S(1)}, bf16[16,2048]{1,0:T(8,128)(2,1)S(1)}, u32[]{:S(2)}, u32[]{:S(2)}) collective-permute-start(bf16[16,2048]{1,0:T(8,128)(2,1)S(1)} %pad_maximum_fusion.5), channel_id=1, source_target_pairs={{0,4},{1,5},{2,6},{3,7},{4,0},{5,1},{6,2},{7,3},{8,12},{9,13},{10,... | collective-permute-start | bytes 196616 | tf_op jit(solution)/shard_map/ppermute | solution.py:347
  6.0 33.0 %collective-permute-start.5 = (bf16[512,512]{1,0:T(8,128)(2,1)S(1)}, bf16[512,512]{1,0:T(8,128)(2,1)S(1)}, u32[]{:S(2)}, u32[]{:S(2)}) collective-permute-start(bf16[512,512]{1,0:T(8,128)(2,1)S(1)} %pad_maximum_fusion.3), channel_id=1, source_target_pairs={{0,1},{1,2},{2,3},{3,4},{4,5},{5,6},{6,7},{8,9},{9,10},{10,11},{11... | collective-permute-start | bytes 1572872 | tf_op jit(solution)/shard_map/ppermute | solution.py:411
  9.7 51.6 %collective-permute-start = (bf16[512,768]{1,0:T(8,128)(2,1)}, bf16[512,768]{1,0:T(8,128)(2,1)}, u32[]{:S(2)}, u32[]{:S(2)}) collective-permute-start(bf16[512,768]{1,0:T(8,128)(2,1)} %pad_maximum_fusion.1), channel_id=1, source_target_pairs={{0,1},{1,2},{2,3},{3,4},{4,5},{5,6},{6,7},{8,9},{9,10},{10,11},{11... | collective-permute-start | bytes 2359304 | tf_op jit(solution)/shard_map/ppermute | solution.py:411
  12.5 37.2 %collective-permute-start.4 = (bf16[512,768]{1,0:T(8,128)(2,1)}, bf16[512,768]{1,0:T(8,128)(2,1)}, u32[]{:S(2)}, u32[]{:S(2)}) collective-permute-start(bf16[512,768]{1,0:T(8,128)(2,1)} %pad_maximum_fusion.2), channel_id=1, source_target_pairs={{0,1},{1,2},{2,3},{3,4},{4,5},{5,6},{6,7},{8,9},{9,10},{10,11},{11... | collective-permute-start | bytes 2359304 | tf_op jit(solution)/shard_map/ppermute | solution.py:411
  23.0 13.4 %collective-permute-start.2 = (bf16[32,2048]{1,0:T(8,128)(2,1)S(1)}, bf16[32,2048]{1,0:T(8,128)(2,1)S(1)}, u32[]{:S(2)}, u32[]{:S(2)}) collective-permute-start(bf16[32,2048]{1,0:T(8,128)(2,1)S(1)} %maximum_select_fusion.2), channel_id=1, source_target_pairs={{0,2},{1,3},{2,0},{3,1},{4,6},{5,7},{6,4},{7,5},{8,10},{9,11},{10,... | collective-permute-start | bytes 393224 | tf_op jit(solution)/shard_map/ppermute | solution.py:347
  78.9 6.6 %collective-permute-start.6 = (bf16[4,160,1024]{2,1,0:T(8,128)(2,1)}, bf16[4,160,1024]{2,1,0:T(8,128)(2,1)}, u32[]{:S(2)}, u32[]{:S(2)}) collective-permute-start(bf16[4,160,1024]{2,1,0:T(8,128)(2,1)} %pad_maximum_fusion), channel_id=1, source_target_pairs={{0,1},{1,0},{2,3},{3,2},{4,5},{5,4},{6,7},{7,6},{8,9},{9,8},{10,11... | collective-permute-start | bytes 3932168 | tf_op jit(solution)/shard_map/ppermute | solution.py:347
  88.6 19.0 %collective-permute-start.7 = (bf16[160,1024]{1,0:T(8,128)(2,1)}, bf16[160,1024]{1,0:T(8,128)(2,1)}, u32[]{:S(2)}, u32[]{:S(2)}) collective-permute-start(bf16[160,1024]{1,0:T(8,128)(2,1)} %get-tuple-element.66), channel_id=1, source_target_pairs={{0,2},{1,3},{2,0},{3,1},{4,6},{5,7},{6,4},{7,5},{8,10},{9,11},{10,... | collective-permute-start | bytes 983048 | tf_op jit(solution)/shard_map/ppermute | solution.py:347
  88.6 19.0 %collective-permute-start.8 = (bf16[160,1024]{1,0:T(8,128)(2,1)}, bf16[160,1024]{1,0:T(8,128)(2,1)}, u32[]{:S(2)}, u32[]{:S(2)}) collective-permute-start(bf16[160,1024]{1,0:T(8,128)(2,1)} %get-tuple-element.68), channel_id=1, source_target_pairs={{0,4},{1,5},{2,6},{3,7},{4,0},{5,1},{6,2},{7,3},{8,12},{9,13},{10,... | collective-permute-start | bytes 983048 | tf_op jit(solution)/shard_map/ppermute | solution.py:347
  88.9 18.7 %collective-permute-start.9 = (bf16[160,1024]{1,0:T(8,128)(2,1)}, bf16[160,1024]{1,0:T(8,128)(2,1)}, u32[]{:S(2)}, u32[]{:S(2)}) collective-permute-start(bf16[160,1024]{1,0:T(8,128)(2,1)} %get-tuple-element.69), channel_id=1, source_target_pairs={{0,6},{1,7},{2,4},{3,5},{4,2},{5,3},{6,0},{7,1},{8,14},{9,15},{10,... | collective-permute-start | bytes 983048 | tf_op jit(solution)/shard_map/ppermute | solution.py:347
  104.4 46.2 %collective-permute-start.10 = (bf16[1024,768]{1,0:T(8,128)(2,1)}, bf16[1024,768]{1,0:T(8,128)(2,1)}, u32[]{:S(2)}, u32[]{:S(2)}) collective-permute-start(bf16[1024,768]{1,0:T(8,128)(2,1)} %get-tuple-element.60), channel_id=1, source_target_pairs={{1,0},{2,1},{3,2},{4,3},{5,4},{6,5},{7,6},{9,8},{10,9},{11,10},{12... | collective-permute-start | bytes 4718600 | tf_op jit(solution)/shard_map/ppermute | solution.py:452
  109.5 12.6 %collective-permute-start.12 = (bf16[32,1024]{1,0:T(8,128)(2,1)}, bf16[32,1024]{1,0:T(8,128)(2,1)}, u32[]{:S(2)}, u32[]{:S(2)}) collective-permute-start(bf16[32,1024]{1,0:T(8,128)(2,1)} %get-tuple-element.74), channel_id=1, source_target_pairs={{0,8},{8,0},{16,24},{24,16},{1,9},{9,1},{17,25},{25,17},{2,10},{10... | collective-permute-start | bytes 196616 | tf_op jit(solution)/shard_map/ppermute | solution.py:347
  110.9 11.3 %collective-permute-start.14 = (bf16[32,1024]{1,0:T(8,128)(2,1)}, bf16[32,1024]{1,0:T(8,128)(2,1)}, u32[]{:S(2)}, u32[]{:S(2)}) collective-permute-start(bf16[32,1024]{1,0:T(8,128)(2,1)} %get-tuple-element.75), channel_id=1, source_target_pairs={{0,24},{8,16},{16,8},{24,0},{1,25},{9,17},{17,9},{25,1},{2,26},{10... | collective-permute-start | bytes 196616 | tf_op jit(solution)/shard_map/ppermute | solution.py:347
  113.0 9.1 %collective-permute-start.13 = (bf16[32,1024]{1,0:T(8,128)(2,1)}, bf16[32,1024]{1,0:T(8,128)(2,1)}, u32[]{:S(2)}, u32[]{:S(2)}) collective-permute-start(bf16[32,1024]{1,0:T(8,128)(2,1)} %get-tuple-element.76), channel_id=1, source_target_pairs={{0,16},{8,24},{16,0},{24,8},{1,17},{9,25},{17,1},{25,9},{2,18},{10... | collective-permute-start | bytes 196616 | tf_op jit(solution)/shard_map/ppermute | solution.py:347
  119.6 16.9 %collective-permute-start.11 = (bf16[1024,256]{1,0:T(8,128)(2,1)}, bf16[1024,256]{1,0:T(8,128)(2,1)}, u32[]{:S(2)}, u32[]{:S(2)}) collective-permute-start(bf16[1024,256]{1,0:T(8,128)(2,1)} %get-tuple-element.61), channel_id=1, source_target_pairs={{1,0},{2,1},{3,2},{4,3},{5,4},{6,5},{7,6},{9,8},{10,9},{11,10},{12... | collective-permute-start | bytes 1572872 | tf_op jit(solution)/shard_map/ppermute | solution.py:452
  124.1 5.4 %collective-permute-start.17 = (bf16[32,1024]{1,0:T(8,128)(2,1)S(1)}, bf16[32,1024]{1,0:T(8,128)(2,1)S(1)}, u32[]{:S(2)}, u32[]{:S(2)}) collective-permute-start(bf16[32,1024]{1,0:T(8,128)(2,1)S(1)} %get-tuple-element.72), channel_id=1, source_target_pairs={{0,24},{8,16},{16,8},{24,0},{1,25},{9,17},{17,9},{25,1},{2,26},{10... | collective-permute-start | bytes 196616 | tf_op jit(solution)/shard_map/ppermute | solution.py:347
  126.7 6.4 %collective-permute-start.16 = (bf16[32,1024]{1,0:T(8,128)(2,1)S(1)}, bf16[32,1024]{1,0:T(8,128)(2,1)S(1)}, u32[]{:S(2)}, u32[]{:S(2)}) collective-permute-start(bf16[32,1024]{1,0:T(8,128)(2,1)S(1)} %get-tuple-element.72), channel_id=1, source_target_pairs={{0,16},{8,24},{16,0},{24,8},{1,17},{9,25},{17,1},{25,9},{2,18},{10... | collective-permute-start | bytes 196616 | tf_op jit(solution)/shard_map/ppermute | solution.py:347
  126.8 6.4 %collective-permute-start.15 = (bf16[32,1024]{1,0:T(8,128)(2,1)S(1)}, bf16[32,1024]{1,0:T(8,128)(2,1)S(1)}, u32[]{:S(2)}, u32[]{:S(2)}) collective-permute-start(bf16[32,1024]{1,0:T(8,128)(2,1)S(1)} %get-tuple-element.72), channel_id=1, source_target_pairs={{0,8},{8,0},{16,24},{24,16},{1,9},{9,1},{17,25},{25,17},{2,10},{10... | collective-permute-start | bytes 196616 | tf_op jit(solution)/shard_map/ppermute | solution.py:347
  133.8 8.3 %collective-permute-start.20 = (bf16[128,1024]{1,0:T(8,128)(2,1)}, bf16[128,1024]{1,0:T(8,128)(2,1)}, u32[]{:S(2)}, u32[]{:S(2)}) collective-permute-start(bf16[128,1024]{1,0:T(8,128)(2,1)} %pad_maximum_fusion.4.rest_0_), channel_id=1, source_target_pairs={{0,6},{1,7},{2,4},{3,5},{4,2},{5,3},{6,0},{7,1},{8,14},{9,15},{10,... | collective-permute-start | bytes 786440 | tf_op jit(solution)/shard_map/ppermute | solution.py:347
  135.4 13.5 %collective-permute-start.19 = (bf16[128,1024]{1,0:T(8,128)(2,1)}, bf16[128,1024]{1,0:T(8,128)(2,1)}, u32[]{:S(2)}, u32[]{:S(2)}) collective-permute-start(bf16[128,1024]{1,0:T(8,128)(2,1)} %pad_maximum_fusion.4.rest_0_), channel_id=1, source_target_pairs={{0,4},{1,5},{2,6},{3,7},{4,0},{5,1},{6,2},{7,3},{8,12},{9,13},{10,... | collective-permute-start | bytes 786440 | tf_op jit(solution)/shard_map/ppermute | solution.py:347
  135.4 14.0 %collective-permute-start.18 = (bf16[128,1024]{1,0:T(8,128)(2,1)}, bf16[128,1024]{1,0:T(8,128)(2,1)}, u32[]{:S(2)}, u32[]{:S(2)}) collective-permute-start(bf16[128,1024]{1,0:T(8,128)(2,1)} %pad_maximum_fusion.4.rest_0_), channel_id=1, source_target_pairs={{0,2},{1,3},{2,0},{3,1},{4,6},{5,7},{6,4},{7,5},{8,10},{9,11},{10,... | collective-permute-start | bytes 786440 | tf_op jit(solution)/shard_map/ppermute | solution.py:347
  136.5 18.8 %collective-permute-start.21 = (bf16[128,1024]{1,0:T(8,128)(2,1)}, bf16[128,1024]{1,0:T(8,128)(2,1)}, u32[]{:S(2)}, u32[]{:S(2)}) collective-permute-start(bf16[128,1024]{1,0:T(8,128)(2,1)} %pad_maximum_fusion.4.rest_0_), channel_id=1, source_target_pairs={{0,1},{1,0},{2,3},{3,2},{4,5},{5,4},{6,7},{7,6},{8,9},{9,8},{10,11... | collective-permute-start | bytes 786440 | tf_op jit(solution)/shard_map/ppermute | solution.py:347
  142.1 13.2 %collective-permute-start.24 = (bf16[128,1024]{1,0:T(8,128)(2,1)}, bf16[128,1024]{1,0:T(8,128)(2,1)}, u32[]{:S(2)}, u32[]{:S(2)}) collective-permute-start(bf16[128,1024]{1,0:T(8,128)(2,1)} %collective-permute-done.20.rest_3_), channel_id=1, source_target_pairs={{0,1},{1,0},{2,3},{3,2},{4,5},{5,4},{6,7},{7,6},{8,9},{9,8},{10,11... | collective-permute-start | bytes 786440 | tf_op jit(solution)/shard_map/ppermute | solution.py:347
  148.9 6.4 %collective-permute-start.23 = (bf16[128,1024]{1,0:T(8,128)(2,1)}, bf16[128,1024]{1,0:T(8,128)(2,1)}, u32[]{:S(2)}, u32[]{:S(2)}) collective-permute-start(bf16[128,1024]{1,0:T(8,128)(2,1)} %collective-permute-done.19.rest_2_), channel_id=1, source_target_pairs={{0,1},{1,0},{2,3},{3,2},{4,5},{5,4},{6,7},{7,6},{8,9},{9,8},{10,11... | collective-permute-start | bytes 786440 | tf_op jit(solution)/shard_map/ppermute | solution.py:347
  149.4 6.0 %collective-permute-start.22 = (bf16[128,1024]{1,0:T(8,128)(2,1)}, bf16[128,1024]{1,0:T(8,128)(2,1)}, u32[]{:S(2)}, u32[]{:S(2)}) collective-permute-start(bf16[128,1024]{1,0:T(8,128)(2,1)} %collective-permute-done.18.rest_1_), channel_id=1, source_target_pairs={{0,1},{1,0},{2,3},{3,2},{4,5},{5,4},{6,7},{7,6},{8,9},{9,8},{10,11... | collective-permute-start | bytes 786440 | tf_op jit(solution)/shard_map/ppermute | solution.py:347
  (11 other events, 72.9 us)

commit v4 on v3

--- a/solution.py
+++ b/solution.py
@@ -42,13 +42,52 @@
     dst[h + o :, :SPAN] = memory[...]
 
 
+def tables(me, blocks_ref, fill_ref, slots_ref, info, bias, nb, tokens, order):
+    nprot, slots = blocks_ref.shape[1], slots_ref.shape[1]
+    mine = slots // len(order)
+    begin = jnp.int32(0)
+    first, left, pads = [0] * nb, [0] * nb, []
+    for p in range(nprot):
+        end = begin + blocks_ref[0, p]
+        real = (end - 1) * BLK + fill_ref[0, p]
+        pads.append((real, end * BLK))
+        for b in range(nb):
+            block = me * nb + b
+            inside = (block >= begin) & (block < end)
+            first[b] = jnp.where(inside, begin, first[b])
+            left[b] = jnp.where(inside, real - block * BLK, left[b])
+        begin = end
+    for b in range(nb):
+        info[0, b] = first[b] - (me * nb - FAR)
+        info[1, b] = left[b]
+    row = lax.broadcasted_iota(jnp.int32, (BLK, BLK), 0)
+    for g in range(slots // BLK):
+        lanes = jnp.broadcast_to(slots_ref[:, g * BLK : (g + 1) * BLK], (BLK, BLK))
+        source = lanes.T + (row + g * BLK) // mine * tokens
+        bad = jnp.zeros((BLK, BLK), f32)
+        for lo, hi in pads:
+            bad = jnp.where((source >= lo) & (source < hi), 1.0, bad)
+        for b in range(nb):
+            seen = jnp.where((source < first[b] * BLK) & (bad == 0.0), 0.0, NEG)
+            for j in range(g * BLK // mine, (g + 1) * BLK // mine):
+                i = order.index(j)
+                bias[b, i * mine : (i + 1) * mine, :] = seen[j * mine - g * BLK : (j + 1) * mine - g * BLK]
+
+
 def forward_kernel(
-    info_ref, q_ref, g_ref, ko_ref, vo_ref, kh_ref, vh_ref, km_ref, vm_ref, mb_ref, *rest, nb, order
+    me_ref, blocks_ref, fill_ref, q_ref, cot_ref, w_ref, ko_ref, vo_ref, kh_ref, vh_ref, km_ref, vm_ref, slots_ref,
+    *rest, nb, order
 ):
-    at_ref, dm_ref, pt, ga_ref, ke, ve, q2s, pm = rest[-8:]
+    at_ref, dm_ref, pt, ga_ref, ke, ve, q2s, pm, mb_ref, g_ref, info_ref = rest[-11:]
     slots = km_ref.shape[0]
     mine = slots // len(order)
     ext = kh_ref.shape[0] + ko_ref.shape[0]
+
+    @pl.when(pl.program_id(0) == 0)
+    def _():
+        tables(me_ref[0], blocks_ref, fill_ref, slots_ref, info_ref, mb_ref, nb, ko_ref.shape[0], order)
+
+    g_ref[...] = dot(cot_ref[...], w_ref[...], NT).astype(bf16)
     fill_keys(ke, kh_ref, ko_ref, km_ref)
     fill_keys(ve, vh_ref, vo_ref, vm_ref)
     ve[:, SPAN:] = jnp.ones((ve.shape[0], SPAN), bf16)
@@ -166,17 +205,17 @@
 ANY = pl.BlockSpec(memory_space=pl.ANY)
 
 
-def forward(info, q, g, ko, vo, kh, vh, km, vm, bias, order, start, count, base, halo_at, carry):
+def forward(me, blocks, fill, slot_row, q, cot, weight, ko, vo, halo, mem, order, start, count, carry):
     tokens, width = q.shape
-    slots, hrows, nb = km.shape[0], kh.shape[0], tokens // BLK
+    slots, hrows, nb, pairs = mem.shape[0], halo.shape[0], tokens // BLK, width // SPAN
     keys = hrows + tokens + slots
-    kc, vc = halo_at
-    mk, mv = base
-    args = [info, q, g, ko, vo, kh, vh, km, vm, bias]
+    smem = pl.BlockSpec(memory_space=pltpu.SMEM)
+    args = [me, blocks, fill, q, cot, weight, ko, vo, halo, halo, mem, mem, slot_row]
     specs = [
-        columns(tokens, start), columns(tokens, start), columns(tokens, start), columns(tokens, start),
-        columns(hrows, kc), columns(hrows, vc), columns(slots, mk + start), columns(slots, mv + start),
-        pl.BlockSpec(bias.shape, lambda p, *_: (0, 0, 0)),
+        smem, smem, smem, columns(tokens, start), pl.BlockSpec((tokens, width), lambda p: (0, 0)),
+        pl.BlockSpec((SPAN, width), lambda p: (p + start, 0)), columns(tokens, start), columns(tokens, start),
+        columns(hrows, 0), columns(hrows, count), columns(slots, start), columns(slots, pairs + start),
+        pl.BlockSpec((1, slots), lambda p: (0, 0)),
     ]
     alias = {}
     if carry:
@@ -185,20 +224,18 @@
         specs += [ANY] * len(carry)
     return pl.pallas_call(
         functools.partial(forward_kernel, nb=nb, order=order),
-        grid_spec=pltpu.PrefetchScalarGridSpec(
-            num_scalar_prefetch=1,
-            grid=(count,),
-            in_specs=specs,
-            out_specs=[
-                columns(tokens, start), columns(2 * slots, start),
-                pl.BlockSpec((1, keys, nb * TWO), lambda p, *_: (p, 0, 0)),
-                pl.BlockSpec((1, nb * TWO, 2 * SPAN), lambda p, *_: (p, 0, 0)),
-            ],
-            scratch_shapes=[
-                pltpu.VMEM((keys, SPAN), bf16), pltpu.VMEM((keys, 2 * SPAN), bf16),
-                pltpu.VMEM((nb * TWO, SPAN), bf16), pltpu.VMEM((slots, nb * TWO), bf16),
-            ],
-        ),
+        grid=(count,),
+        in_specs=specs,
+        out_specs=[
+            columns(tokens, start), columns(2 * slots, start),
+            pl.BlockSpec((1, keys, nb * TWO), lambda p: (p, 0, 0)),
+            pl.BlockSpec((1, nb * TWO, 2 * SPAN), lambda p: (p, 0, 0)),
+        ],
+        scratch_shapes=[
+            pltpu.VMEM((keys, SPAN), bf16), pltpu.VMEM((keys, 2 * SPAN), bf16),
+            pltpu.VMEM((nb * TWO, SPAN), bf16), pltpu.VMEM((slots, nb * TWO), bf16),
+            pltpu.VMEM((nb, slots, BLK), f32), pltpu.VMEM((tokens, SPAN), bf16), pltpu.SMEM((2, nb), jnp.int32),
+        ],
         out_shape=[
             jax.ShapeDtypeStruct((tokens, width), bf16),
             jax.ShapeDtypeStruct((2 * slots, width), bf16),
@@ -212,6 +249,61 @@
         ),
         name="band_forward",
     )(*args)
+
+
+def prepare_kernel(me_ref, slots_ref, k_ref, v_ref, rows_ref, *halos, sizes):
+    tokens, width = k_ref.shape
+    mine = rows_ref.shape[0]
+    row = lax.broadcasted_iota(jnp.int32, (mine, tokens), 0)
+    slot = jnp.zeros((mine, tokens), jnp.int32)
+    for r in range(mine):
+        slot = jnp.where(row == r, slots_ref[0, me_ref[0] * mine + r], slot)
+    pick = (slot == lax.broadcasted_iota(jnp.int32, (mine, tokens), 1)).astype(f32).astype(bf16)
+    rows_ref[:, :width] = dot(pick, k_ref[...], NN).astype(bf16)
+    rows_ref[:, width:] = dot(pick, v_ref[...], NN).astype(bf16)
+    at = 0
+    for halo, size in zip(halos, sizes):
+        halo[:, :size] = k_ref[tokens - W :, at : at + size]
+        halo[:, size:] = v_ref[tokens - W :, at : at + size]
+        at += size
+
+
+def prepare(me, slots, k, v, mine, sizes):
+    smem, vmem = pl.BlockSpec(memory_space=pltpu.SMEM), pl.BlockSpec(memory_space=pltpu.VMEM)
+    return pl.pallas_call(
+        functools.partial(prepare_kernel, sizes=sizes),
+        in_specs=[smem, smem, vmem, vmem],
+        out_specs=[vmem] * (1 + len(sizes)),
+        out_shape=[jax.ShapeDtypeStruct((mine, 2 * k.shape[1]), bf16)]
+        + [jax.ShapeDtypeStruct((W, 2 * size), bf16) for size in sizes],
+        compiler_params=pltpu.CompilerParams(vmem_limit_bytes=67_000_000),
+        name="prepare_rows",
+    )(me, slots, k, v)
+
+
+def partial_kernel(core_ref, att_ref, cot_ref, dm_ref, send_ref, keep_ref, *, plane):
+    half = att_ref.shape[1] // 2
+    rows = half // plane
+    for out, c in ((send_ref, 1 - core_ref[0]), (keep_ref, core_ref[0])):
+        w = dot(att_ref[:, pl.ds(pl.multiple_of(c * half, half), half)], cot_ref[...], TN).astype(bf16)
+        for j in range(plane):
+            out[j, :rows, :] = w[j * rows : (j + 1) * rows]
+            out[j, rows:, :] = dm_ref[j, c]
+
+
+def weight_partial(core, att, cot, dm, plane):
+    width, extra = att.shape[1], dm.shape[2]
+    smem, vmem = pl.BlockSpec(memory_space=pltpu.SMEM), pl.BlockSpec(memory_space=pltpu.VMEM)
+    shape = jax.ShapeDtypeStruct((plane, width // 2 // plane + extra, width), bf16)
+    return pl.pallas_call(
+        functools.partial(partial_kernel, plane=plane),
+        in_specs=[smem, vmem, vmem, vmem],
+        out_specs=[vmem, vmem],
+        out_shape=[shape, shape],
+        compiler_params=pltpu.CompilerParams(vmem_limit_bytes=67_000_000),
+        cost_estimate=pl.CostEstimate(flops=1 << 30, bytes_accessed=5 << 20, transcendentals=0),
+        name="weight_partial",
+    )(core, att, cot, dm)
 
 
 def backward(q, pt, ga, ko, vo, kh, vh, km, start, count, base, halo_at, at, carry, dh_total, dh_at):
@@ -325,24 +417,6 @@
     )(where, *parts)
 
 
-def protein_tables(prot_blocks, last_fill):
-    prot_ends = jnp.cumsum(prot_blocks)
-    starts = prot_ends - prot_blocks
-    valid_len = (prot_blocks - 1) * BLK + last_fill
-    return prot_ends, starts, valid_len
-
-
-def token_info(positions, tables):
-    prot_ends, starts, valid_len = tables
-    count = prot_ends.shape[0]
-    blocks = jnp.floor_divide(positions, BLK)
-    protein = jnp.sum((blocks[:, None] >= prot_ends[None, :]).astype(jnp.int32), axis=1)
-    onehot = protein[:, None] == jnp.arange(count, dtype=jnp.int32)[None, :]
-    first = jnp.sum(jnp.where(onehot, starts[None, :], 0), axis=1)
-    length = jnp.sum(jnp.where(onehot, valid_len[None, :], 0), axis=1)
-    return protein, first, length - (positions - first * BLK)
-
-
 def swap(x, axis, bits):
     return lax.ppermute(x, axis, [(i, i ^ bits) for i in range(lax.axis_size(axis))])
 
@@ -386,57 +460,39 @@
     if pairs % 8:
         return [pairs], [(0, 0, pairs)], [pairs]
     u = pairs // 8
-    return [2 * u, 3 * u, 3 * u], [(0, 0, 2 * u), (1, 0, 3 * u), (2, 0, u), (2, u, 2 * u)], [6 * u, 2 * u]
+    return [3 * u, 5 * u], [(0, 0, u), (1, 0, 5 * u), (0, u, 2 * u)], [6 * u, 2 * u]
 
 
 def per_device(queries, key_rows, value_rows, cotangent, out_weight, prot_blocks, last_fill, memory_slots):
     q, k, v, cot = queries[0], key_rows[0], value_rows[0], cotangent[0]
-    tables = protein_tables(prot_blocks[0], last_fill[0])
     slots = memory_slots[0]
     tokens, width = q.shape
     nctx, nfam = lax.axis_size("ctx"), lax.axis_size("fam")
     me, fam = lax.axis_index("ctx"), lax.axis_index("fam")
     total = slots.shape[0]
     mine = total // nctx
-    nb = tokens // BLK
     pairs = width // SPAN
     fsizes, bplan, dhs = groups_of(pairs)
     fstarts = [sum(fsizes[:i]) for i in range(len(fsizes))]
     shift = [(i, i + 1) for i in range(nctx - 1)]
     back = [(i + 1, i) for i in range(nctx - 1)]
-    edge = tokens - W
-    halos = []
-    for i, (at, count) in enumerate(zip(fstarts, fsizes)):
-        cols = slice(at * SPAN, (at + count) * SPAN)
-        halos.append(lax.ppermute(jnp.concatenate([k[edge:, cols], v[edge:, cols]], 1), "ctx", shift))
-    own_slots = lax.dynamic_slice_in_dim(slots, me * mine, mine)
-    pick = (own_slots[:, None] == jnp.arange(tokens, dtype=jnp.int32)[None, :]).astype(bf16)
-    rows = jnp.concatenate([dot(pick, k, NN).astype(bf16), dot(pick, v, NN).astype(bf16)], 1)
+    where = jnp.stack([me]).astype(jnp.int32)
+    rows, *halos = prepare(where, memory_slots, k, v, mine, [n * SPAN for n in fsizes])
     mem = gather_rows(rows, "ctx", me)
-    grad_attn = dot(cot, out_weight, NT).astype(bf16)
-    heads = me * tokens + jnp.arange(nb, dtype=jnp.int32) * BLK
+    halos = [lax.ppermute(x, "ctx", shift) for x in halos]
     order = mirrored(nctx)
-    source = (jnp.asarray(order, jnp.int32)[:, None] * tokens + slots.reshape(nctx, mine)[jnp.asarray(order)]).reshape(-1)
-    prot, first, left = token_info(jnp.concatenate([heads, source]), tables)
-    lo = jnp.clip(first[:nb] - (me * tokens - W) // BLK, 0, nb + FAR)
-    info = jnp.stack([lo, jnp.clip(left[:nb], 0, BLK)])
-    seen = (left[nb:] > 0)[None, :] & (prot[None, nb:] < prot[:nb, None])
-    bias = jnp.broadcast_to(jnp.where(seen, 0.0, NEG).astype(f32)[:, :, None], (nb, total, BLK))
-    base = (0, pairs)
     carry, saved = [], []
     for i, (at, count) in enumerate(zip(fstarts, fsizes)):
         att, dm, pt, ga = forward(
-            info, q, grad_attn, k, v, halos[i], halos[i], mem, mem, bias, order,
-            at, count, base, (0, count), carry)
+            where, prot_blocks, last_fill, memory_slots, q, cot, out_weight, k, v, halos[i], mem, order,
+            at, count, carry)
         carry = [att, dm]
         saved.append((pt, ga))
     core, spot, plane = me & 1, me >> 1, nctx // 2
-    w = dot(att, cot, TN).astype(bf16).reshape(2, plane, width // nctx, width)
-    dm = dm.reshape(plane, 2, 2 * mine, width)
     at = lambda x, j, axis: lax.dynamic_index_in_dim(x, j, axis, keepdims=False)
-    side = lambda c: jnp.concatenate([at(w, c, 0), at(dm, c, 1)], 1)
-    sent = swap(side(1 - core), "ctx", 1)
-    kept = side(core)
+    send, kept = weight_partial(
+        jnp.stack([core]).astype(jnp.int32), att, cot, dm.reshape(plane, 2, 2 * mine, width), plane)
+    sent = swap(send, "ctx", 1)
     carry, backs, segments, i = [], [], [], 0
     for total_dh in dhs:
         done = 0
@@ -462,7 +518,7 @@
     weight = place(jnp.stack([core, spot, fam]).astype(jnp.int32), parts, nfam, scale)
     dq, dko, dvo = carry
     backs = [x.reshape(2, W, -1) for x in backs]
-    dk, dv = finish(own_slots, dko, dvo, mem_grad, backs, segments)
+    dk, dv = finish(lax.dynamic_slice_in_dim(slots, me * mine, mine), dko, dvo, mem_grad, backs, segments)
     return dq[None], dk[None], dv[None], weight
 
 

time: 161 us -> 154 us (0.957)
  matrix products: 9.8 us -> 0 us
  starting transfers between devices: 33.3 us -> 40.1 us
  local copies, waits for them, and re-layouts: 6.58 us -> 0.58 us
  other arithmetic: 14.4 us -> 10.3 us
  waiting for transfers between devices: 27.3 us -> 31.2 us
  Pallas kernels: 66.6 us -> 68.9 us
    ppermute x3 -> x2, waiting for transfers between devices: 0.01 us -> 17.6 us  [per_device(): halos = [lax.ppermute(x, 'ctx', shift) for x in halos]]
    ppermute x20, waiting for transfers between devices: 27.2 us -> 13.6 us  [swap(): lax.ppermute(x, axis, [(i, i ^ bits) for i in range(lax.axis_size(axis))])]
    dot_general x4 -> x0, matrix products: 9.8 us -> none  [dot(): return lax.dot_general(a, b, dims, preferred_element_type=f32)]
    pallas_call x0 -> x2, Pallas kernels: none -> 7.64 us  [the longest x1 4.42 us: weight_partial(): pl.pallas_call(functools.partial(partial_kernel, plane=plane), in_specs=[...]
    ppermute x20, starting transfers between devices: 19.3 us -> 25.8 us  [swap(): lax.ppermute(x, axis, [(i, i ^ bits) for i in range(lax.axis_size(axis))])]
    concatenate x5 -> x0, other arithmetic: 3.11 us -> none  [the longest x3 1.92 us: per_device(): jnp.concatenate([k[edge:, cols], v[edge:, cols]], 1)]
    pallas_call x4 -> x3, Pallas kernels: 26.1 us -> 23.3 us  [backward(): pl.pallas_call(functools.partial(backward_kernel, nb=nb), grid=(count,),...]
    pallas_call x3 -> x2, Pallas kernels: 32.3 us -> 29.6 us  [forward(): pl.pallas_call(functools.partial(forward_kernel, nb=nb, order=order), gri...]
  transfers between devices with their start and end apart: 25 -> 24, of which waited for: 6 -> 8; matrix products, arithmetic and copies ran while one was open for 11% -> 4% of each run, Pallas kernels for 32% -> 26%
where the time goes in v4:
time: 154 us; the launch traced here: 152 us
  Pallas kernels  68.9 us (45%)
  starting transfers between devices  40.1 us (26%)
  waiting for transfers between devices  31.2 us (20%)
  other arithmetic  10.3 us (7%)
    pallas_call x2, Pallas kernels, forward(): pl.pallas_call(functools.partial(forward_kernel, nb=nb, order=order), gri...  29.6 us
    ppermute x20, starting transfers between devices, swap(): lax.ppermute(x, axis, [(i, i ^ bits) for i in range(lax.axis_size(axis))])  25.8 us
    pallas_call x3, Pallas kernels, backward(): pl.pallas_call(functools.partial(backward_kernel, nb=nb), grid=(count,),...  23.3 us
    ppermute x2, waiting for transfers between devices, per_device(): halos = [lax.ppermute(x, 'ctx', shift) for x in halos]  17.6 us
    ppermute x20, waiting for transfers between devices, swap(): lax.ppermute(x, axis, [(i, i ^ bits) for i in range(lax.axis_size(axis))])  13.6 us
    ppermute x2, starting transfers between devices, per_device(): halos = [lax.ppermute(x, 'ctx', shift) for x in halos]  8.2 us
    ppermute x2, starting transfers between devices, per_device(): backs.append(lax.ppermute(carry.pop(), 'ctx', back))  6.14 us
    convert_element_type x2, other arithmetic, exchange(): part(me ^ k).astype(bf16)  5.14 us
  transfers between devices with their start and end apart: 24, of which 8 were waited for; matrix products, arithmetic and copies ran while one was open for 4% of the time, Pallas kernels for 26%

profile of v4, /device:TPU:3, one launch (start us, length us, event | category | flops | bytes accessed | tf_op | source)
XLA Modules:
  0.0 152.1 jit_solution(3994602622126176541)
XLA Ops:
  0.6 3.2 %prepare_rows.1 = (bf16[16,2048]{1,0:T(8,128)(2,1)}, bf16[512,768]{1,0:T(8,128)(2,1)}, bf16[512,1280]{1,0:T(8,128)(2,1)}) custom-call(s32[1]{0:T(128)} %bitcast.1.me_ref, s32[1,128]{1,0:T(1,128)} %slots_ref.5, bf16[512,1024]{1,0:T(8,128)(2,1)} %bitcast.68, bf16[512,1024]{1,0:T(8,128)(2,1)} %bitcast.74), custom_call_target="tpu_custom_call" | custom-call | tf_op jit(solution)/shard_map/prepare_rows/pallas_call | solution.py:273
  5.1 2.1 %collective-permute-done.1 = bf16[16,2048]{1,0:T(8,128)(2,1)S(1)} collective-permute-done((bf16[16,2048]{1,0:T(8,128)(2,1)}, bf16[16,2048]{1,0:T(8,128)(2,1)S(1)}, u32[]{:S(2)}, u32[]{:S(2)}) %collective-permute-start.1) | collective-permute-done | bytes 65568 | tf_op jit(solution)/shard_map/ppermute | solution.py:421
  8.2 6.3 %collective-permute-start.4 = (bf16[512,1280]{1,0:T(8,128)(2,1)}, bf16[512,1280]{1,0:T(8,128)(2,1)}, u32[]{:S(2)}, u32[]{:S(2)}) collective-permute-start(bf16[512,1280]{1,0:T(8,128)(2,1)} %get-tuple-element.35), channel_id=1, source_target_pairs={{0,1},{1,2},{2,3},{3,4},{4,5},{5,6},{6,7},{8,9},{9,10},{10,11},{11... | collective-permute-start | bytes 3932168 | tf_op jit(solution)/shard_map/ppermute | solution.py:482
  17.1 2.2 %collective-permute-done.3 = bf16[64,2048]{1,0:T(8,128)(2,1)S(1)} collective-permute-done((bf16[64,2048]{1,0:T(8,128)(2,1)S(1)}, bf16[64,2048]{1,0:T(8,128)(2,1)S(1)}, u32[]{:S(2)}, u32[]{:S(2)}) %collective-permute-start.3) | collective-permute-done | bytes 262176 | tf_op jit(solution)/shard_map/ppermute | solution.py:421
  20.2 17.6 %collective-permute-done.kh_ref.vh_ref = bf16[512,768]{1,0:T(8,128)(2,1)} collective-permute-done((bf16[512,768]{1,0:T(8,128)(2,1)}, bf16[512,768]{1,0:T(8,128)(2,1)}, u32[]{:S(2)}, u32[]{:S(2)}) %collective-permute-start) | collective-permute-done | bytes 786464 | tf_op jit(solution)/shard_map/ppermute | solution.py:482
  37.8 11.9 %band_forward.2 = (bf16[512,1024]{1,0:T(8,128)(2,1)}, bf16[256,1024]{1,0:T(8,128)(2,1)}, bf16[3,1152,1024]{2,1,0:T(8,128)(2,1)}, bf16[3,1024,256]{2,1,0:T(8,128)(2,1)}) custom-call(s32[1]{0:T(128)} %bitcast.1.me_ref, s32[1,8]{1,0:T(1,128)} %blocks_ref.3, s32[1,8]{1,0:T(1,128)} %fill_ref.3, bf16[512,1024]{1,0:T(8,128)(2,1)} %bitcast.80, ...), custom_call_target="tpu_custom_call" | custom-call | flops 4831838208 | bytes 12582912 | tf_op jit(solution)/shard_map/band_forward/pallas_call | solution.py:225
  49.7 17.7 %band_forward.3 = (bf16[512,1024]{1,0:T(8,128)(2,1)}, bf16[256,1024]{1,0:T(8,128)(2,1)}, bf16[5,1152,1024]{2,1,0:T(8,128)(2,1)}, bf16[5,1024,256]{2,1,0:T(8,128)(2,1)}) custom-call(s32[1]{0:T(128)} %bitcast.1.me_ref, s32[1,8]{1,0:T(1,128)} %blocks_ref.3, s32[1,8]{1,0:T(1,128)} %fill_ref.3, ...), custom_call_target="tpu_custom_call", output_to_operand_aliasing={{0}: (13, {}), {1}: (14, {})} | custom-call | flops 8053063680 | bytes 20971520 | tf_op jit(solution)/shard_map/band_forward/pallas_call | solution.py:225
  67.4 4.4 %weight_partial.1 = (bf16[4,160,1024]{2,1,0:T(8,128)(2,1)}, bf16[4,160,1024]{2,1,0:T(8,128)(2,1)}) custom-call(s32[1]{0:T(128)} %bitcast.6.core_ref, bf16[512,1024]{1,0:T(8,128)(2,1)} %get-tuple-element.50.att_ref, bf16[512,1024]{1,0:T(8,128)(2,1)} %bitcast.87, bf16[4,2,32,1024]{3,2,1,0:T(8,128)(2,1)} %bitcast.91), custom_call_target="tpu_custom_call" | custom-call | flops 1073741824 | bytes 5242880 | tf_op jit(solution)/shard_map/weight_partial/pallas_call | solution.py:298
  71.9 4.5 %band_backward.3 = (bf16[512,1024]{1,0:T(8,128)(2,1)}, bf16[512,1024]{1,0:T(8,128)(2,1)}, bf16[512,1024]{1,0:T(8,128)(2,1)}, bf16[1024,768]{1,0:T(8,128)(2,1)}) custom-call(bf16[512,1024]{1,0:T(8,128)(2,1)} %bitcast.82, bf16[3,1152,1024]{2,1,0:T(8,128)(2,1)} %get-tuple-element.33.pt_ref, bf16[3,1024,256]{2,1,0:T(8,128)(2,1)} %get-tuple-element.34.ga_ref, ...), custom_call_target="tpu_custom_call" | custom-call | flops 2684354560 | bytes 6291456 | tf_op jit(solution)/shard_map/band_backward/pallas_call | solution.py:327
  76.4 3.2 %fusion = (bf16[160,1024]{1,0:T(8,128)(2,1)}, bf16[160,1024]{1,0:T(8,128)(2,1)}, bf16[160,1024]{1,0:T(8,128)(2,1)}, f32[1,160,1024]{2,1,0:T(8,128)}) fusion(bf16[4,160,1024]{2,1,0:T(8,128)(2,1)} %get-tuple-element.53, s32[]{:T(128)S(6)} %select_n.76, bf16[4,160,1024]{2,1,0:T(8,128)(2,1)} %collective-permute-done.5, s32[]{:T(128)S(6)} %select_n.78, ...), kind=kLoop, calls=%fused_computation.5 | loop fusion | flops 2457600 | bytes 4259856 | tf_op jit(solution)/shard_map/convert_element_type | solution.py:448
  79.6 3.5 %collective-permute-start.8 = (bf16[160,1024]{1,0:T(8,128)(2,1)}, bf16[160,1024]{1,0:T(8,128)(2,1)}, u32[]{:S(2)}, u32[]{:S(2)}) collective-permute-start(bf16[160,1024]{1,0:T(8,128)(2,1)} %get-tuple-element.59), channel_id=1, source_target_pairs={{0,6},{1,7},{2,4},{3,5},{4,2},{5,3},{6,0},{7,1},{8,14},{9,15},{10,... | collective-permute-start | bytes 983048 | tf_op jit(solution)/shard_map/ppermute | solution.py:421
  83.4 12.4 %band_backward.4 = (bf16[512,1024]{1,0:T(8,128)(2,1)}, bf16[512,1024]{1,0:T(8,128)(2,1)}, bf16[512,1024]{1,0:T(8,128)(2,1)}, bf16[1024,768]{1,0:T(8,128)(2,1)}) custom-call(bf16[512,1024]{1,0:T(8,128)(2,1)} %bitcast.83, bf16[5,1152,1024]{2,1,0:T(8,128)(2,1)} %get-tuple-element.38.pt_ref, ...), custom_call_target="tpu_custom_call", output_to_operand_aliasing={{0}: (8, {}), {1}: (9, {}), {2}: (10, {}), {3}: (11, {})} | custom-call | flops 13421772800 | bytes 31457280 | tf_op jit(solution)/shard_map/band_backward/pallas_call | solution.py:327
  95.7 2.7 %collective-permute-start.9 = (bf16[1024,768]{1,0:T(8,128)(2,1)}, bf16[1024,768]{1,0:T(8,128)(2,1)}, u32[]{:S(2)}, u32[]{:S(2)}) collective-permute-start(bf16[1024,768]{1,0:T(8,128)(2,1)} %get-tuple-element.54), channel_id=1, source_target_pairs={{1,0},{2,1},{3,2},{4,3},{5,4},{6,5},{7,6},{9,8},{10,9},{11,10},{12... | collective-permute-start | bytes 4718600 | tf_op jit(solution)/shard_map/ppermute | solution.py:508
  100.6 3.3 %collective-permute-start.13 = (bf16[32,1024]{1,0:T(8,128)(2,1)}, bf16[32,1024]{1,0:T(8,128)(2,1)}, u32[]{:S(2)}, u32[]{:S(2)}) collective-permute-start(bf16[32,1024]{1,0:T(8,128)(2,1)} %get-tuple-element.65), channel_id=1, source_target_pairs={{0,24},{8,16},{16,8},{24,0},{1,25},{9,17},{17,9},{25,1},{2,26},{10... | collective-permute-start | bytes 196616 | tf_op jit(solution)/shard_map/ppermute | solution.py:421
  104.2 6.5 %band_backward.5 = (bf16[512,1024]{1,0:T(8,128)(2,1)}, bf16[512,1024]{1,0:T(8,128)(2,1)}, bf16[512,1024]{1,0:T(8,128)(2,1)}, bf16[1024,256]{1,0:T(8,128)(2,1)}) custom-call(bf16[512,1024]{1,0:T(8,128)(2,1)} %bitcast.84, bf16[3,1152,1024]{2,1,0:T(8,128)(2,1)} %get-tuple-element.33.pt_ref, ...), custom_call_target="tpu_custom_call", output_to_operand_aliasing={{0}: (8, {}), {1}: (9, {}), {2}: (10, {})} | custom-call | flops 5368709120 | bytes 12582912 | tf_op jit(solution)/shard_map/band_backward/pallas_call | solution.py:327
  110.7 3.5 %collective-permute-start.10 = (bf16[1024,256]{1,0:T(8,128)(2,1)}, bf16[1024,256]{1,0:T(8,128)(2,1)}, u32[]{:S(2)}, u32[]{:S(2)}) collective-permute-start(bf16[1024,256]{1,0:T(8,128)(2,1)} %get-tuple-element.55), channel_id=1, source_target_pairs={{1,0},{2,1},{3,2},{4,3},{5,4},{6,5},{7,6},{9,8},{10,9},{11,10},{12... | collective-permute-start | bytes 1572872 | tf_op jit(solution)/shard_map/ppermute | solution.py:508
  116.1 3.3 %collective-permute-start.16 = (bf16[32,1024]{1,0:T(8,128)(2,1)S(1)}, bf16[32,1024]{1,0:T(8,128)(2,1)S(1)}, u32[]{:S(2)}, u32[]{:S(2)}) collective-permute-start(bf16[32,1024]{1,0:T(8,128)(2,1)S(1)} %get-tuple-element.62), channel_id=1, source_target_pairs={{0,24},{8,16},{16,8},{24,0},{1,25},{9,17},{17,9},{25,1},{2,26},{10... | collective-permute-start | bytes 196616 | tf_op jit(solution)/shard_map/ppermute | solution.py:421
  119.7 2.0 %collective-permute-done.16 = bf16[32,1024]{1,0:T(8,128)(2,1)S(1)} collective-permute-done((bf16[32,1024]{1,0:T(8,128)(2,1)S(1)}, bf16[32,1024]{1,0:T(8,128)(2,1)S(1)}, u32[]{:S(2)}, u32[]{:S(2)}) %collective-permute-start.16) | collective-permute-done | bytes 65568 | tf_op jit(solution)/shard_map/ppermute | solution.py:421
  121.7 3.3 %collective-permute-done.15 = bf16[32,1024]{1,0:T(8,128)(2,1)S(1)} collective-permute-done((bf16[32,1024]{1,0:T(8,128)(2,1)S(1)}, bf16[32,1024]{1,0:T(8,128)(2,1)S(1)}, u32[]{:S(2)}, u32[]{:S(2)}) %collective-permute-start.15) | collective-permute-done | bytes 65568 | tf_op jit(solution)/shard_map/ppermute | solution.py:421
  130.2 3.2 %collective-permute-done.17.rest_1_ = bf16[128,1024]{1,0:T(8,128)(2,1)} collective-permute-done((bf16[128,1024]{1,0:T(8,128)(2,1)}, bf16[128,1024]{1,0:T(8,128)(2,1)}, u32[]{:S(2)}, u32[]{:S(2)}) %collective-permute-start.17) | collective-permute-done | bytes 262176 | tf_op jit(solution)/shard_map/ppermute | solution.py:421
  133.3 2.5 %collective-permute-start.21 = (bf16[128,1024]{1,0:T(8,128)(2,1)}, bf16[128,1024]{1,0:T(8,128)(2,1)}, u32[]{:S(2)}, u32[]{:S(2)}) collective-permute-start(bf16[128,1024]{1,0:T(8,128)(2,1)} %collective-permute-done.17.rest_1_), channel_id=1, source_target_pairs={{0,1},{1,0},{2,3},{3,2},{4,5},{5,4},{6,7},{7,6},{8,9},{9,8},{10,11... | collective-permute-start | bytes 786440 | tf_op jit(solution)/shard_map/ppermute | solution.py:421
  135.8 4.7 %collective-permute-start.22 = (bf16[128,1024]{1,0:T(8,128)(2,1)}, bf16[128,1024]{1,0:T(8,128)(2,1)}, u32[]{:S(2)}, u32[]{:S(2)}) collective-permute-start(bf16[128,1024]{1,0:T(8,128)(2,1)} %collective-permute-done.18.rest_2_), channel_id=1, source_target_pairs={{0,1},{1,0},{2,3},{3,2},{4,5},{5,4},{6,7},{7,6},{8,9},{9,8},{10,11... | collective-permute-start | bytes 786440 | tf_op jit(solution)/shard_map/ppermute | solution.py:421
  143.6 4.6 %finish_rows.1 = (bf16[512,1024]{1,0:T(8,128)(2,1)}, bf16[512,1024]{1,0:T(8,128)(2,1)}) custom-call(s32[1,16]{1,0:T(1,128)} %constant_dynamic-slice_fusion.slot_ref, bf16[512,1024]{1,0:T(8,128)(2,1)} %get-tuple-element.48.dk_in, bf16[512,1024]{1,0:T(8,128)(2,1)} %get-tuple-element.49.dv_in, bf16[32,1024]{1,0:T(8,128)(2,1)} %get-tuple-element.63.dm_ref, ...), custom_call_target="tpu_custom_call" | custom-call | flops 67108864 | bytes 6291456 | tf_op jit(solution)/shard_map/finish_rows/pallas_call | solution.py:373
  148.3 3.6 %place_rows.1 = f32[1024,1024]{1,0:T(8,128)} custom-call(s32[3]{0:T(128)} %pad_add_fusion.where_ref, bf16[128,1024]{1,0:T(8,128)(2,1)} %pad_maximum_fusion.rest_0_, bf16[128,1024]{1,0:T(8,128)(2,1)} %collective-permute-done.17.rest_1_, bf16[128,1024]{1,0:T(8,128)(2,1)} %collective-permute-done.18.rest_2_, bf16[128,1024]{1,0:T(8,128)(2,1)} %collective-permute-done.19.rest_3_, ...), custom_call_target="tpu_custom_call" | custom-call | flops 1048576 | bytes 6291456 | tf_op jit(solution)/shard_map/place_rows/pallas_call | solution.py:408
  (44 shorter events, 19.0 us)
Async XLA Ops:
  3.9 3.3 %collective-permute-start.1 = (bf16[16,2048]{1,0:T(8,128)(2,1)}, bf16[16,2048]{1,0:T(8,128)(2,1)S(1)}, u32[]{:S(2)}, u32[]{:S(2)}) collective-permute-start(bf16[16,2048]{1,0:T(8,128)(2,1)} %get-tuple-element.32), channel_id=1, source_target_pairs={{0,4},{1,5},{2,6},{3,7},{4,0},{5,1},{6,2},{7,3},{8,12},{9,13},{10,... | collective-permute-start | bytes 196616 | tf_op jit(solution)/shard_map/ppermute | solution.py:421
  8.1 8.3 %collective-permute-start.2 = (bf16[32,2048]{1,0:T(8,128)(2,1)S(1)}, bf16[32,2048]{1,0:T(8,128)(2,1)S(1)}, u32[]{:S(2)}, u32[]{:S(2)}) collective-permute-start(bf16[32,2048]{1,0:T(8,128)(2,1)S(1)} %maximum_select_fusion.2), channel_id=1, source_target_pairs={{0,2},{1,3},{2,0},{3,1},{4,6},{5,7},{6,4},{7,5},{8,10},{9,11},{10,... | collective-permute-start | bytes 393224 | tf_op jit(solution)/shard_map/ppermute | solution.py:421
  8.2 41.5 %collective-permute-start.4 = (bf16[512,1280]{1,0:T(8,128)(2,1)}, bf16[512,1280]{1,0:T(8,128)(2,1)}, u32[]{:S(2)}, u32[]{:S(2)}) collective-permute-start(bf16[512,1280]{1,0:T(8,128)(2,1)} %get-tuple-element.35), channel_id=1, source_target_pairs={{0,1},{1,2},{2,3},{3,4},{4,5},{5,6},{6,7},{8,9},{9,10},{10,11},{11... | collective-permute-start | bytes 3932168 | tf_op jit(solution)/shard_map/ppermute | solution.py:482
  14.5 23.3 %collective-permute-start = (bf16[512,768]{1,0:T(8,128)(2,1)}, bf16[512,768]{1,0:T(8,128)(2,1)}, u32[]{:S(2)}, u32[]{:S(2)}) collective-permute-start(bf16[512,768]{1,0:T(8,128)(2,1)} %get-tuple-element.31), channel_id=1, source_target_pairs={{0,1},{1,2},{2,3},{3,4},{4,5},{5,6},{6,7},{8,9},{9,10},{10,11},{11... | collective-permute-start | bytes 2359304 | tf_op jit(solution)/shard_map/ppermute | solution.py:482
  16.5 2.8 %collective-permute-start.3 = (bf16[64,2048]{1,0:T(8,128)(2,1)S(1)}, bf16[64,2048]{1,0:T(8,128)(2,1)S(1)}, u32[]{:S(2)}, u32[]{:S(2)}) collective-permute-start(bf16[64,2048]{1,0:T(8,128)(2,1)S(1)} %maximum_select_fusion.1), channel_id=1, source_target_pairs={{0,1},{1,0},{2,3},{3,2},{4,5},{5,4},{6,7},{7,6},{8,9},{9,8},{10,11... | collective-permute-start | bytes 786440 | tf_op jit(solution)/shard_map/ppermute | solution.py:421
  71.9 4.5 %collective-permute-start.5 = (bf16[4,160,1024]{2,1,0:T(8,128)(2,1)}, bf16[4,160,1024]{2,1,0:T(8,128)(2,1)}, u32[]{:S(2)}, u32[]{:S(2)}) collective-permute-start(bf16[4,160,1024]{2,1,0:T(8,128)(2,1)} %get-tuple-element.52), channel_id=1, source_target_pairs={{0,1},{1,0},{2,3},{3,2},{4,5},{5,4},{6,7},{7,6},{8,9},{9,8},{10,11... | collective-permute-start | bytes 3932168 | tf_op jit(solution)/shard_map/ppermute | solution.py:421
  79.6 18.8 %collective-permute-start.8 = (bf16[160,1024]{1,0:T(8,128)(2,1)}, bf16[160,1024]{1,0:T(8,128)(2,1)}, u32[]{:S(2)}, u32[]{:S(2)}) collective-permute-start(bf16[160,1024]{1,0:T(8,128)(2,1)} %get-tuple-element.59), channel_id=1, source_target_pairs={{0,6},{1,7},{2,4},{3,5},{4,2},{5,3},{6,0},{7,1},{8,14},{9,15},{10,... | collective-permute-start | bytes 983048 | tf_op jit(solution)/shard_map/ppermute | solution.py:421
  83.1 15.5 %collective-permute-start.7 = (bf16[160,1024]{1,0:T(8,128)(2,1)}, bf16[160,1024]{1,0:T(8,128)(2,1)}, u32[]{:S(2)}, u32[]{:S(2)}) collective-permute-start(bf16[160,1024]{1,0:T(8,128)(2,1)} %get-tuple-element.60), channel_id=1, source_target_pairs={{0,4},{1,5},{2,6},{3,7},{4,0},{5,1},{6,2},{7,3},{8,12},{9,13},{10,... | collective-permute-start | bytes 983048 | tf_op jit(solution)/shard_map/ppermute | solution.py:421
  83.1 15.5 %collective-permute-start.6 = (bf16[160,1024]{1,0:T(8,128)(2,1)}, bf16[160,1024]{1,0:T(8,128)(2,1)}, u32[]{:S(2)}, u32[]{:S(2)}) collective-permute-start(bf16[160,1024]{1,0:T(8,128)(2,1)} %get-tuple-element.58), channel_id=1, source_target_pairs={{0,2},{1,3},{2,0},{3,1},{4,6},{5,7},{6,4},{7,5},{8,10},{9,11},{10,... | collective-permute-start | bytes 983048 | tf_op jit(solution)/shard_map/ppermute | solution.py:421
  95.7 47.9 %collective-permute-start.9 = (bf16[1024,768]{1,0:T(8,128)(2,1)}, bf16[1024,768]{1,0:T(8,128)(2,1)}, u32[]{:S(2)}, u32[]{:S(2)}) collective-permute-start(bf16[1024,768]{1,0:T(8,128)(2,1)} %get-tuple-element.54), channel_id=1, source_target_pairs={{1,0},{2,1},{3,2},{4,3},{5,4},{6,5},{7,6},{9,8},{10,9},{11,10},{12... | collective-permute-start | bytes 4718600 | tf_op jit(solution)/shard_map/ppermute | solution.py:508
  100.6 13.6 %collective-permute-start.13 = (bf16[32,1024]{1,0:T(8,128)(2,1)}, bf16[32,1024]{1,0:T(8,128)(2,1)}, u32[]{:S(2)}, u32[]{:S(2)}) collective-permute-start(bf16[32,1024]{1,0:T(8,128)(2,1)} %get-tuple-element.65), channel_id=1, source_target_pairs={{0,24},{8,16},{16,8},{24,0},{1,25},{9,17},{17,9},{25,1},{2,26},{10... | collective-permute-start | bytes 196616 | tf_op jit(solution)/shard_map/ppermute | solution.py:421
  103.9 10.3 %collective-permute-start.12 = (bf16[32,1024]{1,0:T(8,128)(2,1)}, bf16[32,1024]{1,0:T(8,128)(2,1)}, u32[]{:S(2)}, u32[]{:S(2)}) collective-permute-start(bf16[32,1024]{1,0:T(8,128)(2,1)} %get-tuple-element.66), channel_id=1, source_target_pairs={{0,16},{8,24},{16,0},{24,8},{1,17},{9,25},{17,1},{25,9},{2,18},{10... | collective-permute-start | bytes 196616 | tf_op jit(solution)/shard_map/ppermute | solution.py:421
  103.9 10.3 %collective-permute-start.11 = (bf16[32,1024]{1,0:T(8,128)(2,1)}, bf16[32,1024]{1,0:T(8,128)(2,1)}, u32[]{:S(2)}, u32[]{:S(2)}) collective-permute-start(bf16[32,1024]{1,0:T(8,128)(2,1)} %get-tuple-element.64), channel_id=1, source_target_pairs={{0,8},{8,0},{16,24},{24,16},{1,9},{9,1},{17,25},{25,17},{2,10},{10... | collective-permute-start | bytes 196616 | tf_op jit(solution)/shard_map/ppermute | solution.py:421
  110.7 18.5 %collective-permute-start.10 = (bf16[1024,256]{1,0:T(8,128)(2,1)}, bf16[1024,256]{1,0:T(8,128)(2,1)}, u32[]{:S(2)}, u32[]{:S(2)}) collective-permute-start(bf16[1024,256]{1,0:T(8,128)(2,1)} %get-tuple-element.55), channel_id=1, source_target_pairs={{1,0},{2,1},{3,2},{4,3},{5,4},{6,5},{7,6},{9,8},{10,9},{11,10},{12... | collective-permute-start | bytes 1572872 | tf_op jit(solution)/shard_map/ppermute | solution.py:508
  116.1 5.6 %collective-permute-start.16 = (bf16[32,1024]{1,0:T(8,128)(2,1)S(1)}, bf16[32,1024]{1,0:T(8,128)(2,1)S(1)}, u32[]{:S(2)}, u32[]{:S(2)}) collective-permute-start(bf16[32,1024]{1,0:T(8,128)(2,1)S(1)} %get-tuple-element.62), channel_id=1, source_target_pairs={{0,24},{8,16},{16,8},{24,0},{1,25},{9,17},{17,9},{25,1},{2,26},{10... | collective-permute-start | bytes 196616 | tf_op jit(solution)/shard_map/ppermute | solution.py:421
  119.4 5.6 %collective-permute-start.15 = (bf16[32,1024]{1,0:T(8,128)(2,1)S(1)}, bf16[32,1024]{1,0:T(8,128)(2,1)S(1)}, u32[]{:S(2)}, u32[]{:S(2)}) collective-permute-start(bf16[32,1024]{1,0:T(8,128)(2,1)S(1)} %get-tuple-element.62), channel_id=1, source_target_pairs={{0,16},{8,24},{16,0},{24,8},{1,17},{9,25},{17,1},{25,9},{2,18},{10... | collective-permute-start | bytes 196616 | tf_op jit(solution)/shard_map/ppermute | solution.py:421
  119.4 5.6 %collective-permute-start.14 = (bf16[32,1024]{1,0:T(8,128)(2,1)S(1)}, bf16[32,1024]{1,0:T(8,128)(2,1)S(1)}, u32[]{:S(2)}, u32[]{:S(2)}) collective-permute-start(bf16[32,1024]{1,0:T(8,128)(2,1)S(1)} %get-tuple-element.62), channel_id=1, source_target_pairs={{0,8},{8,0},{16,24},{24,16},{1,9},{9,1},{17,25},{25,17},{2,10},{10... | collective-permute-start | bytes 196616 | tf_op jit(solution)/shard_map/ppermute | solution.py:421
  125.7 7.6 %collective-permute-start.17 = (bf16[128,1024]{1,0:T(8,128)(2,1)}, bf16[128,1024]{1,0:T(8,128)(2,1)}, u32[]{:S(2)}, u32[]{:S(2)}) collective-permute-start(bf16[128,1024]{1,0:T(8,128)(2,1)} %pad_maximum_fusion.rest_0_), channel_id=1, source_target_pairs={{0,2},{1,3},{2,0},{3,1},{4,6},{5,7},{6,4},{7,5},{8,10},{9,11},{10,... | collective-permute-start | bytes 786440 | tf_op jit(solution)/shard_map/ppermute | solution.py:421
  126.7 9.1 %collective-permute-start.18 = (bf16[128,1024]{1,0:T(8,128)(2,1)}, bf16[128,1024]{1,0:T(8,128)(2,1)}, u32[]{:S(2)}, u32[]{:S(2)}) collective-permute-start(bf16[128,1024]{1,0:T(8,128)(2,1)} %pad_maximum_fusion.rest_0_), channel_id=1, source_target_pairs={{0,4},{1,5},{2,6},{3,7},{4,0},{5,1},{6,2},{7,3},{8,12},{9,13},{10,... | collective-permute-start | bytes 786440 | tf_op jit(solution)/shard_map/ppermute | solution.py:421
  128.0 13.1 %collective-permute-start.19 = (bf16[128,1024]{1,0:T(8,128)(2,1)}, bf16[128,1024]{1,0:T(8,128)(2,1)}, u32[]{:S(2)}, u32[]{:S(2)}) collective-permute-start(bf16[128,1024]{1,0:T(8,128)(2,1)} %pad_maximum_fusion.rest_0_), channel_id=1, source_target_pairs={{0,6},{1,7},{2,4},{3,5},{4,2},{5,3},{6,0},{7,1},{8,14},{9,15},{10,... | collective-permute-start | bytes 786440 | tf_op jit(solution)/shard_map/ppermute | solution.py:421
  129.2 19.1 %collective-permute-start.20 = (bf16[128,1024]{1,0:T(8,128)(2,1)}, bf16[128,1024]{1,0:T(8,128)(2,1)}, u32[]{:S(2)}, u32[]{:S(2)}) collective-permute-start(bf16[128,1024]{1,0:T(8,128)(2,1)} %pad_maximum_fusion.rest_0_), channel_id=1, source_target_pairs={{0,1},{1,0},{2,3},{3,2},{4,5},{5,4},{6,7},{7,6},{8,9},{9,8},{10,11... | collective-permute-start | bytes 786440 | tf_op jit(solution)/shard_map/ppermute | solution.py:421
  133.3 15.0 %collective-permute-start.21 = (bf16[128,1024]{1,0:T(8,128)(2,1)}, bf16[128,1024]{1,0:T(8,128)(2,1)}, u32[]{:S(2)}, u32[]{:S(2)}) collective-permute-start(bf16[128,1024]{1,0:T(8,128)(2,1)} %collective-permute-done.17.rest_1_), channel_id=1, source_target_pairs={{0,1},{1,0},{2,3},{3,2},{4,5},{5,4},{6,7},{7,6},{8,9},{9,8},{10,11... | collective-permute-start | bytes 786440 | tf_op jit(solution)/shard_map/ppermute | solution.py:421
  135.8 12.5 %collective-permute-start.22 = (bf16[128,1024]{1,0:T(8,128)(2,1)}, bf16[128,1024]{1,0:T(8,128)(2,1)}, u32[]{:S(2)}, u32[]{:S(2)}) collective-permute-start(bf16[128,1024]{1,0:T(8,128)(2,1)} %collective-permute-done.18.rest_2_), channel_id=1, source_target_pairs={{0,1},{1,0},{2,3},{3,2},{4,5},{5,4},{6,7},{7,6},{8,9},{9,8},{10,11... | collective-permute-start | bytes 786440 | tf_op jit(solution)/shard_map/ppermute | solution.py:421
  141.2 7.2 %collective-permute-start.23 = (bf16[128,1024]{1,0:T(8,128)(2,1)}, bf16[128,1024]{1,0:T(8,128)(2,1)}, u32[]{:S(2)}, u32[]{:S(2)}) collective-permute-start(bf16[128,1024]{1,0:T(8,128)(2,1)} %collective-permute-done.19.rest_3_), channel_id=1, source_target_pairs={{0,1},{1,0},{2,3},{3,2},{4,5},{5,4},{6,7},{7,6},{8,9},{9,8},{10,11... | collective-permute-start | bytes 786440 | tf_op jit(solution)/shard_map/ppermute | solution.py:421
  (1 other events, 38.2 us)

commit v5 on v4

--- a/solution.py
+++ b/solution.py
@@ -76,9 +76,9 @@
 
 def forward_kernel(
     me_ref, blocks_ref, fill_ref, q_ref, cot_ref, w_ref, ko_ref, vo_ref, kh_ref, vh_ref, km_ref, vm_ref, slots_ref,
-    *rest, nb, order
+    *rest, nb, order, start
 ):
-    at_ref, dm_ref, pt, ga_ref, ke, ve, q2s, pm, mb_ref, g_ref, info_ref = rest[-11:]
+    send_ref, keep_ref, pt, ga_ref, ke, ve, q2s, pm, mb_ref, g_ref, at_ref, w_buf, dm_buf, sems, info_ref = rest[-15:]
     slots = km_ref.shape[0]
     mine = slots // len(order)
     ext = kh_ref.shape[0] + ko_ref.shape[0]
@@ -155,12 +155,50 @@
         for stage, lag in ((score, 0), (attend, 2), (exponentials, 1), (memory, 4), (gradients, 3)):
             if 0 <= t - lag < nb:
                 stage(t - lag)
+    step, plane, width = pl.program_id(0), len(order) // 2, cot_ref.shape[1]
+    core, slot, rows = me_ref[0] & 1, lax.rem(step, 2), width // len(order)
     dk = dot(pt[0, ext:, :], q2s[...], NN).astype(bf16)
     dv = dot(pm[...], ga_ref[0, :, :SPAN], NN).astype(bf16)
     for i, j in enumerate(order):
         part = slice(i * mine, (i + 1) * mine)
-        dm_ref[2 * j * mine : (2 * j + 1) * mine, :] = dk[part]
-        dm_ref[(2 * j + 1) * mine : (2 * j + 2) * mine, :] = dv[part]
+        dm_buf[slot, j % 2, j // 2, :mine, :] = dk[part]
+        dm_buf[slot, j % 2, j // 2, mine:, :] = dv[part]
+    w_buf[slot] = dot(at_ref[...], cot_ref[...], TN).astype(bf16)
+
+    def copies(at, slot):
+        pair = start + at
+        out = []
+        for t in range(max(1, SPAN // rows)):
+            block = pair * (SPAN // rows) + t
+            out.append((block // plane == core, lambda ref, t=t, block=block: pltpu.make_async_copy(
+                w_buf.at[slot, pl.ds(t * rows, rows), :], ref.at[lax.rem(block, plane), pl.ds(0, rows), :],
+                sems.at[slot, 2 + t])))
+        for side in range(2):
+            out.append((core == side, lambda ref, side=side: pltpu.make_async_copy(
+                dm_buf.at[slot, side],
+                ref.at[:, pl.ds(rows, 2 * mine), pl.ds(pl.multiple_of(pair * SPAN, SPAN), SPAN)],
+                sems.at[slot, side])))
+        return out
+
+    for stays, copy in copies(step, slot):
+
+        @pl.when(stays)
+        def _():
+            copy(keep_ref).start()
+
+        @pl.when(jnp.logical_not(stays))
+        def _():
+            copy(send_ref).start()
+
+    @pl.when(step > 0)
+    def _():
+        for _, copy in copies(step - 1, 1 - slot):
+            copy(keep_ref).wait()
+
+    @pl.when(step == pl.num_programs(0) - 1)
+    def _():
+        for _, copy in copies(step, slot):
+            copy(keep_ref).wait()
 
 
 def backward_kernel(
@@ -210,6 +248,9 @@
     slots, hrows, nb, pairs = mem.shape[0], halo.shape[0], tokens // BLK, width // SPAN
     keys = hrows + tokens + slots
     smem = pl.BlockSpec(memory_space=pltpu.SMEM)
+    members, plane = len(order), len(order) // 2
+    rows, extra = width // members, 2 * slots // members
+    out = jax.ShapeDtypeStruct((plane, rows + extra, width), bf16)
     args = [me, blocks, fill, q, cot, weight, ko, vo, halo, halo, mem, mem, slot_row]
     specs = [
         smem, smem, smem, columns(tokens, start), pl.BlockSpec((tokens, width), lambda p: (0, 0)),
@@ -223,22 +264,24 @@
         args += carry
         specs += [ANY] * len(carry)
     return pl.pallas_call(
-        functools.partial(forward_kernel, nb=nb, order=order),
+        functools.partial(forward_kernel, nb=nb, order=order, start=start),
         grid=(count,),
         in_specs=specs,
         out_specs=[
-            columns(tokens, start), columns(2 * slots, start),
+            ANY, ANY,
             pl.BlockSpec((1, keys, nb * TWO), lambda p: (p, 0, 0)),
             pl.BlockSpec((1, nb * TWO, 2 * SPAN), lambda p: (p, 0, 0)),
         ],
         scratch_shapes=[
             pltpu.VMEM((keys, SPAN), bf16), pltpu.VMEM((keys, 2 * SPAN), bf16),
             pltpu.VMEM((nb * TWO, SPAN), bf16), pltpu.VMEM((slots, nb * TWO), bf16),
-            pltpu.VMEM((nb, slots, BLK), f32), pltpu.VMEM((tokens, SPAN), bf16), pltpu.SMEM((2, nb), jnp.int32),
+            pltpu.VMEM((nb, slots, BLK), f32), pltpu.VMEM((tokens, SPAN), bf16),
+            pltpu.VMEM((tokens, SPAN), bf16), pltpu.VMEM((2, SPAN, width), bf16),
+            pltpu.VMEM((2, 2, plane, extra, SPAN), bf16), pltpu.SemaphoreType.DMA((2, 2 + SPAN // rows)),
+            pltpu.SMEM((2, nb), jnp.int32),
         ],
         out_shape=[
-            jax.ShapeDtypeStruct((tokens, width), bf16),
-            jax.ShapeDtypeStruct((2 * slots, width), bf16),
+            out, out,
             jax.ShapeDtypeStruct((count, keys, nb * TWO), bf16),
             jax.ShapeDtypeStruct((count, nb * TWO, 2 * SPAN), bf16),
         ],
@@ -279,31 +322,6 @@
         compiler_params=pltpu.CompilerParams(vmem_limit_bytes=67_000_000),
         name="prepare_rows",
     )(me, slots, k, v)
-
-
-def partial_kernel(core_ref, att_ref, cot_ref, dm_ref, send_ref, keep_ref, *, plane):
-    half = att_ref.shape[1] // 2
-    rows = half // plane
-    for out, c in ((send_ref, 1 - core_ref[0]), (keep_ref, core_ref[0])):
-        w = dot(att_ref[:, pl.ds(pl.multiple_of(c * half, half), half)], cot_ref[...], TN).astype(bf16)
-        for j in range(plane):
-            out[j, :rows, :] = w[j * rows : (j + 1) * rows]
-            out[j, rows:, :] = dm_ref[j, c]
-
-
-def weight_partial(core, att, cot, dm, plane):
-    width, extra = att.shape[1], dm.shape[2]
-    smem, vmem = pl.BlockSpec(memory_space=pltpu.SMEM), pl.BlockSpec(memory_space=pltpu.VMEM)
-    shape = jax.ShapeDtypeStruct((plane, width // 2 // plane + extra, width), bf16)
-    return pl.pallas_call(
-        functools.partial(partial_kernel, plane=plane),
-        in_specs=[smem, vmem, vmem, vmem],
-        out_specs=[vmem, vmem],
-        out_shape=[shape, shape],
-        compiler_params=pltpu.CompilerParams(vmem_limit_bytes=67_000_000),
-        cost_estimate=pl.CostEstimate(flops=1 << 30, bytes_accessed=5 << 20, transcendentals=0),
-        name="weight_partial",
-    )(core, att, cot, dm)
 
 
 def backward(q, pt, ga, ko, vo, kh, vh, km, start, count, base, halo_at, at, carry, dh_total, dh_at):
@@ -383,30 +401,27 @@
     )(slots[None, :], dko, dvo, dmem, *backs)
 
 
-def place_kernel(where_ref, *rest, plane, nfam, scale):
+def place_kernel(where_ref, *rest, plane, scale):
     n = 2 * plane
     parts, out_ref, buf, sems = rest[:n], rest[n], rest[n + 1], rest[n + 2]
     rows = parts[0].shape[0]
-    piece = rows // nfam
-    core, spot, fam = where_ref[0], where_ref[1], where_ref[2]
+    core, spot = where_ref[0], where_ref[1]
     copies = []
     for i, part in enumerate(parts):
         side = jnp.where(i < plane, core, 1 - core)
         at = pl.multiple_of((side * plane + (spot ^ (i % plane))) * rows, rows)
-        for k in range(nfam):
-            row = pl.multiple_of((fam ^ k) * piece, piece)
-            buf[i, pl.ds(row, piece), :] = part[k * piece : (k + 1) * piece, :].astype(f32) * scale
+        buf[i] = part[...].astype(f32) * scale
         copies.append(pltpu.make_async_copy(buf.at[i], out_ref.at[pl.ds(at, rows), :], sems.at[i]))
         copies[-1].start()
     for copy in copies:
         copy.wait()
 
 
-def place(where, parts, nfam, scale):
+def place(where, parts, scale):
     rows, width = parts[0].shape
     n = len(parts)
     return pl.pallas_call(
-        functools.partial(place_kernel, plane=n // 2, nfam=nfam, scale=scale),
+        functools.partial(place_kernel, plane=n // 2, scale=scale),
         in_specs=[pl.BlockSpec(memory_space=pltpu.SMEM)] + [pl.BlockSpec(memory_space=pltpu.VMEM)] * n,
         out_specs=pl.BlockSpec(memory_space=pl.ANY),
         out_shape=jax.ShapeDtypeStruct((n * rows, width), f32),
@@ -460,7 +475,7 @@
     if pairs % 8:
         return [pairs], [(0, 0, pairs)], [pairs]
     u = pairs // 8
-    return [3 * u, 5 * u], [(0, 0, u), (1, 0, 5 * u), (0, u, 2 * u)], [6 * u, 2 * u]
+    return [2 * u, 6 * u], [(0, 0, 2 * u), (1, 0, 4 * u), (1, 4 * u, 2 * u)], [6 * u, 2 * u]
 
 
 def per_device(queries, key_rows, value_rows, cotangent, out_weight, prot_blocks, last_fill, memory_slots):
@@ -468,7 +483,7 @@
     slots = memory_slots[0]
     tokens, width = q.shape
     nctx, nfam = lax.axis_size("ctx"), lax.axis_size("fam")
-    me, fam = lax.axis_index("ctx"), lax.axis_index("fam")
+    me = lax.axis_index("ctx")
     total = slots.shape[0]
     mine = total // nctx
     pairs = width // SPAN
@@ -483,15 +498,13 @@
     order = mirrored(nctx)
     carry, saved = [], []
     for i, (at, count) in enumerate(zip(fstarts, fsizes)):
-        att, dm, pt, ga = forward(
+        send, kept, pt, ga = forward(
             where, prot_blocks, last_fill, memory_slots, q, cot, out_weight, k, v, halos[i], mem, order,
             at, count, carry)
-        carry = [att, dm]
+        carry = [send, kept]
         saved.append((pt, ga))
     core, spot, plane = me & 1, me >> 1, nctx // 2
     at = lambda x, j, axis: lax.dynamic_index_in_dim(x, j, axis, keepdims=False)
-    send, kept = weight_partial(
-        jnp.stack([core]).astype(jnp.int32), att, cot, dm.reshape(plane, 2, 2 * mine, width), plane)
     sent = swap(send, "ctx", 1)
     carry, backs, segments, i = [], [], [], 0
     for total_dh in dhs:
@@ -509,13 +522,13 @@
     got = exchange(lambda j: at(sent, j, 0).astype(f32) + at(kept, j, 0).astype(f32), "ctx", 1, spot, plane)
     rows = width // nctx
     mem_grad = total_of([x[rows:] for x in got]).astype(bf16)
-    piece = lambda j: total_of([lax.dynamic_slice_in_dim(x, j * (rows // nfam), rows // nfam) for x in got])
-    w = total_of(exchange(piece, "fam", 0, fam, nfam)).astype(bf16)
-    w = jnp.concatenate(spread(w, "fam", 0, nfam), 0)
+    w = total_of([x[:rows] for x in got]).astype(bf16)
+    for i, bit in enumerate(bits_of(nfam)):
+        w = total_of([w, swap(w, "fam", bit)]).astype(bf16)
     parts = spread(w, "ctx", 1, plane)
     parts = parts + [swap(x, "ctx", 1) for x in parts]
     scale = (nfam * nctx * tokens) ** -0.5
-    weight = place(jnp.stack([core, spot, fam]).astype(jnp.int32), parts, nfam, scale)
+    weight = place(jnp.stack([core, spot]).astype(jnp.int32), parts, scale)
     dq, dko, dvo = carry
     backs = [x.reshape(2, W, -1) for x in backs]
     dk, dv = finish(lax.dynamic_slice_in_dim(slots, me * mine, mine), dko, dvo, mem_grad, backs, segments)

time: 154 us -> 164 us (1.065)
  starting transfers between devices: 40.1 us -> 47.9 us
  other arithmetic: 10.3 us -> 12.6 us
    ppermute x2, waiting for transfers between devices: 17.6 us -> 3.48 us  [per_device(): halos = [lax.ppermute(x, 'ctx', shift) for x in halos]]
    ppermute x20 -> x16, waiting for transfers between devices: 13.6 us -> 24.6 us  [swap(): lax.ppermute(x, axis, [(i, i ^ bits) for i in range(lax.axis_size(axis))])]
    ppermute x20 -> x16, starting transfers between devices: 25.8 us -> 33.3 us  [swap(): lax.ppermute(x, axis, [(i, i ^ bits) for i in range(lax.axis_size(axis))])]
    convert_element_type x1 -> x4, other arithmetic: 1.89 us -> 7.31 us  [the longest x2 3.57 us: per_device(): w = total_of([w, swap(w, 'fam', bit)]).astype(bf16)]
    ppermute x2, waiting for transfers between devices: 0.01 us -> 4.26 us  [per_device(): backs.append(lax.ppermute(carry.pop(), 'ctx', back))]
    convert_element_type x2 -> x1, other arithmetic: 5.14 us -> 2.76 us  [exchange(): part(me ^ k).astype(bf16)]
    pallas_call x4 -> x3, Pallas kernels: 37.7 us -> 36.4 us  [the longest x2 32.8 us: forward(): pl.pallas_call(functools.partial(forward_kernel, nb=nb, order=order, star...]
  transfers between devices with their start and end apart: 24 -> 20, of which waited for: 8 -> 10; matrix products, arithmetic and copies ran while one was open for 4% -> 5% of each run, Pallas kernels for 26% -> 24%
where the time goes in v5:
time: 164 us; the launch traced here: 162 us
  Pallas kernels  67.6 us (41%)
  starting transfers between devices  47.9 us (29%)
  waiting for transfers between devices  32.3 us (20%)
  other arithmetic  12.6 us (8%)
    ppermute x16, starting transfers between devices, swap(): lax.ppermute(x, axis, [(i, i ^ bits) for i in range(lax.axis_size(axis))])  33.3 us
    pallas_call x2, Pallas kernels, forward(): pl.pallas_call(functools.partial(forward_kernel, nb=nb, order=order, star...  32.8 us
    ppermute x16, waiting for transfers between devices, swap(): lax.ppermute(x, axis, [(i, i ^ bits) for i in range(lax.axis_size(axis))])  24.6 us
    pallas_call x3, Pallas kernels, backward(): pl.pallas_call(functools.partial(backward_kernel, nb=nb), grid=(count,),...  23.3 us
    ppermute x2, starting transfers between devices, per_device(): halos = [lax.ppermute(x, 'ctx', shift) for x in halos]  7.36 us
    ppermute x2, starting transfers between devices, per_device(): backs.append(lax.ppermute(carry.pop(), 'ctx', back))  7.22 us
    pallas_call x1, Pallas kernels, finish(): pl.pallas_call(functools.partial(finish_kernel, segments=segments), grid=...  4.64 us
    ppermute x2, waiting for transfers between devices, per_device(): backs.append(lax.ppermute(carry.pop(), 'ctx', back))  4.26 us
  transfers between devices with their start and end apart: 20, of which 10 were waited for; matrix products, arithmetic and copies ran while one was open for 5% of the time, Pallas kernels for 24%

profile of v5, /device:TPU:3, one launch (start us, length us, event | category | flops | bytes accessed | tf_op | source)
XLA Modules:
  0.0 161.9 jit_solution(18056800103583722202)
XLA Ops:
  0.6 3.2 %prepare_rows.1 = (bf16[16,2048]{1,0:T(8,128)(2,1)}, bf16[512,512]{1,0:T(8,128)(2,1)}, bf16[512,1536]{1,0:T(8,128)(2,1)}) custom-call(s32[1]{0:T(128)} %bitcast.1.me_ref, s32[1,128]{1,0:T(1,128)} %slots_ref.5, bf16[512,1024]{1,0:T(8,128)(2,1)} %bitcast.38, bf16[512,1024]{1,0:T(8,128)(2,1)} %bitcast.44), custom_call_target="tpu_custom_call" | custom-call | tf_op jit(solution)/shard_map/prepare_rows/pallas_call | solution.py:316
  3.9 3.7 %collective-permute-start = (bf16[512,1536]{1,0:T(8,128)(2,1)}, bf16[512,1536]{1,0:T(8,128)(2,1)}, u32[]{:S(2)}, u32[]{:S(2)}) collective-permute-start(bf16[512,1536]{1,0:T(8,128)(2,1)} %get-tuple-element.29), channel_id=1, source_target_pairs={{0,1},{1,2},{2,3},{3,4},{4,5},{5,6},{6,7},{8,9},{9,10},{10,11},{11... | collective-permute-start | bytes 4718600 | tf_op jit(solution)/shard_map/ppermute | solution.py:497
  7.6 3.8 %collective-permute-done.1 = bf16[16,2048]{1,0:T(8,128)(2,1)S(1)} collective-permute-done((bf16[16,2048]{1,0:T(8,128)(2,1)}, bf16[16,2048]{1,0:T(8,128)(2,1)S(1)}, u32[]{:S(2)}, u32[]{:S(2)}) %collective-permute-start.1) | collective-permute-done | bytes 65568 | tf_op jit(solution)/shard_map/ppermute | solution.py:436
  12.4 16.2 %collective-permute-start.2 = (bf16[32,2048]{1,0:T(8,128)(2,1)S(1)}, bf16[32,2048]{1,0:T(8,128)(2,1)S(1)}, u32[]{:S(2)}, u32[]{:S(2)}) collective-permute-start(bf16[32,2048]{1,0:T(8,128)(2,1)S(1)} %maximum_select_fusion.2), channel_id=1, source_target_pairs={{0,2},{1,3},{2,0},{3,1},{4,6},{5,7},{6,4},{7,5},{8,10},{9,11},{10,... | collective-permute-start | bytes 393224 | tf_op jit(solution)/shard_map/ppermute | solution.py:436
  28.6 3.7 %collective-permute-start.4 = (bf16[512,512]{1,0:T(8,128)(2,1)}, bf16[512,512]{1,0:T(8,128)(2,1)}, u32[]{:S(2)}, u32[]{:S(2)}) collective-permute-start(bf16[512,512]{1,0:T(8,128)(2,1)} %get-tuple-element.31), channel_id=1, source_target_pairs={{0,1},{1,2},{2,3},{3,4},{4,5},{5,6},{6,7},{8,9},{9,10},{10,11},{11... | collective-permute-start | bytes 1572872 | tf_op jit(solution)/shard_map/ppermute | solution.py:497
  35.2 3.5 %collective-permute-done.4.kh_ref.vh_ref = bf16[512,512]{1,0:T(8,128)(2,1)} collective-permute-done((bf16[512,512]{1,0:T(8,128)(2,1)}, bf16[512,512]{1,0:T(8,128)(2,1)}, u32[]{:S(2)}, u32[]{:S(2)}) %collective-permute-start.4) | collective-permute-done | bytes 524320 | tf_op jit(solution)/shard_map/ppermute | solution.py:497
  38.7 10.3 %band_forward.2 = (bf16[4,160,1024]{2,1,0:T(8,128)(2,1)}, bf16[4,160,1024]{2,1,0:T(8,128)(2,1)}, bf16[2,1152,1024]{2,1,0:T(8,128)(2,1)}, bf16[2,1024,256]{2,1,0:T(8,128)(2,1)}) custom-call(s32[1]{0:T(128)} %bitcast.1.me_ref, s32[1,8]{1,0:T(1,128)} %blocks_ref.3, s32[1,8]{1,0:T(1,128)} %fill_ref.3, bf16[512,1024]{1,0:T(8,128)(2,1)} %bitcast.50, ...), custom_call_target="tpu_custom_call" | custom-call | flops 3221225472 | bytes 8388608 | tf_op jit(solution)/shard_map/band_forward/pallas_call | solution.py:266
  49.0 22.5 %band_forward.3 = (bf16[4,160,1024]{2,1,0:T(8,128)(2,1)}, bf16[4,160,1024]{2,1,0:T(8,128)(2,1)}, bf16[6,1152,1024]{2,1,0:T(8,128)(2,1)}, bf16[6,1024,256]{2,1,0:T(8,128)(2,1)}) custom-call(s32[1]{0:T(128)} %bitcast.1.me_ref, s32[1,8]{1,0:T(1,128)} %blocks_ref.3, s32[1,8]{1,0:T(1,128)} %fill_ref.3, ...), custom_call_target="tpu_custom_call", output_to_operand_aliasing={{0}: (13, {}), {1}: (14, {})} | custom-call | flops 9663676416 | bytes 25165824 | tf_op jit(solution)/shard_map/band_forward/pallas_call | solution.py:266
  72.4 2.9 %collective-permute-done.5 = bf16[4,160,1024]{2,1,0:T(8,128)(2,1)S(1)} collective-permute-done((bf16[4,160,1024]{2,1,0:T(8,128)(2,1)}, bf16[4,160,1024]{2,1,0:T(8,128)(2,1)S(1)}, u32[]{:S(2)}, u32[]{:S(2)}) %collective-permute-start.5) | collective-permute-done | bytes 1310752 | tf_op jit(solution)/shard_map/ppermute | solution.py:436
  75.3 2.8 %fusion.4 = (bf16[160,1024]{1,0:T(8,128)(2,1)}, bf16[160,1024]{1,0:T(8,128)(2,1)}, bf16[160,1024]{1,0:T(8,128)(2,1)}, f32[1,160,1024]{2,1,0:T(8,128)}) fusion(bf16[4,160,1024]{2,1,0:T(8,128)(2,1)} %get-tuple-element.49, s32[]{:T(128)S(6)} %select_n.52, bf16[4,160,1024]{2,1,0:T(8,128)(2,1)S(1)} %collective-permute-done.5, s32[]{:T(128)S(6)} %select_n.54, ...), kind=kLoop, calls=%fused_computation.12 | loop fusion | flops 2457600 | bytes 4259856 | tf_op jit(solution)/shard_map/convert_element_type | solution.py:463
  78.1 3.4 %collective-permute-start.8 = (bf16[160,1024]{1,0:T(8,128)(2,1)}, bf16[160,1024]{1,0:T(8,128)(2,1)}, u32[]{:S(2)}, u32[]{:S(2)}) collective-permute-start(bf16[160,1024]{1,0:T(8,128)(2,1)} %get-tuple-element.55), channel_id=1, source_target_pairs={{0,6},{1,7},{2,4},{3,5},{4,2},{5,3},{6,0},{7,1},{8,14},{9,15},{10,... | collective-permute-start | bytes 983048 | tf_op jit(solution)/shard_map/ppermute | solution.py:436
  81.5 6.5 %band_backward.3 = (bf16[512,1024]{1,0:T(8,128)(2,1)}, bf16[512,1024]{1,0:T(8,128)(2,1)}, bf16[512,1024]{1,0:T(8,128)(2,1)}, bf16[1024,768]{1,0:T(8,128)(2,1)}) custom-call(bf16[512,1024]{1,0:T(8,128)(2,1)} %bitcast.52, bf16[2,1152,1024]{2,1,0:T(8,128)(2,1)} %get-tuple-element.36.pt_ref, bf16[2,1024,256]{2,1,0:T(8,128)(2,1)} %get-tuple-element.37.ga_ref, ...), custom_call_target="tpu_custom_call" | custom-call | flops 5368709120 | bytes 12582912 | tf_op jit(solution)/shard_map/band_backward/pallas_call | solution.py:345
  88.0 8.3 %collective-permute-done.8 = bf16[160,1024]{1,0:T(8,128)(2,1)} collective-permute-done((bf16[160,1024]{1,0:T(8,128)(2,1)}, bf16[160,1024]{1,0:T(8,128)(2,1)}, u32[]{:S(2)}, u32[]{:S(2)}) %collective-permute-start.8) | collective-permute-done | bytes 327712 | tf_op jit(solution)/shard_map/ppermute | solution.py:436
  99.7 10.4 %band_backward.4 = (bf16[512,1024]{1,0:T(8,128)(2,1)}, bf16[512,1024]{1,0:T(8,128)(2,1)}, bf16[512,1024]{1,0:T(8,128)(2,1)}, bf16[1024,768]{1,0:T(8,128)(2,1)}) custom-call(bf16[512,1024]{1,0:T(8,128)(2,1)} %bitcast.53, bf16[6,1152,1024]{2,1,0:T(8,128)(2,1)} %get-tuple-element.34.pt_ref, ...), custom_call_target="tpu_custom_call", output_to_operand_aliasing={{0}: (8, {}), {1}: (9, {}), {2}: (10, {}), {3}: (11, {})} | custom-call | flops 10737418240 | bytes 25165824 | tf_op jit(solution)/shard_map/band_backward/pallas_call | solution.py:345
  110.1 5.0 %collective-permute-start.9 = (bf16[1024,768]{1,0:T(8,128)(2,1)}, bf16[1024,768]{1,0:T(8,128)(2,1)}, u32[]{:S(2)}, u32[]{:S(2)}) collective-permute-start(bf16[1024,768]{1,0:T(8,128)(2,1)} %get-tuple-element.50), channel_id=1, source_target_pairs={{1,0},{2,1},{3,2},{4,3},{5,4},{6,5},{7,6},{9,8},{10,9},{11,10},{12... | collective-permute-start | bytes 4718600 | tf_op jit(solution)/shard_map/ppermute | solution.py:521
  116.9 2.3 %collective-permute-start.12 = (bf16[128,1024]{1,0:T(8,128)(2,1)}, bf16[128,1024]{1,0:T(8,128)(2,1)}, u32[]{:S(2)}, u32[]{:S(2)}) collective-permute-start(bf16[128,1024]{1,0:T(8,128)(2,1)} %add_convert_fusion.4), channel_id=1, source_target_pairs={{0,16},{8,24},{16,0},{24,8},{1,17},{9,25},{17,1},{25,9},{2,18},{10... | collective-permute-start | bytes 786440 | tf_op jit(solution)/shard_map/ppermute | solution.py:436
  119.2 6.5 %band_backward.5 = (bf16[512,1024]{1,0:T(8,128)(2,1)}, bf16[512,1024]{1,0:T(8,128)(2,1)}, bf16[512,1024]{1,0:T(8,128)(2,1)}, bf16[1024,256]{1,0:T(8,128)(2,1)}) custom-call(bf16[512,1024]{1,0:T(8,128)(2,1)} %bitcast.54, bf16[6,1152,1024]{2,1,0:T(8,128)(2,1)} %get-tuple-element.34.pt_ref, ...), custom_call_target="tpu_custom_call", output_to_operand_aliasing={{0}: (8, {}), {1}: (9, {}), {2}: (10, {})} | custom-call | flops 5368709120 | bytes 12582912 | tf_op jit(solution)/shard_map/band_backward/pallas_call | solution.py:345
  125.7 2.2 %collective-permute-start.10 = (bf16[1024,256]{1,0:T(8,128)(2,1)}, bf16[1024,256]{1,0:T(8,128)(2,1)}, u32[]{:S(2)}, u32[]{:S(2)}) collective-permute-start(bf16[1024,256]{1,0:T(8,128)(2,1)} %get-tuple-element.51), channel_id=1, source_target_pairs={{1,0},{2,1},{3,2},{4,3},{5,4},{6,5},{7,6},{9,8},{10,9},{11,10},{12... | collective-permute-start | bytes 1572872 | tf_op jit(solution)/shard_map/ppermute | solution.py:521
  127.9 4.0 %collective-permute-done.12 = bf16[128,1024]{1,0:T(8,128)(2,1)} collective-permute-done((bf16[128,1024]{1,0:T(8,128)(2,1)}, bf16[128,1024]{1,0:T(8,128)(2,1)}, u32[]{:S(2)}, u32[]{:S(2)}) %collective-permute-start.12) | collective-permute-done | bytes 262176 | tf_op jit(solution)/shard_map/ppermute | solution.py:436
  136.9 4.3 %collective-permute-done.10 = bf16[1024,256]{1,0:T(8,128)(2,1)} collective-permute-done((bf16[1024,256]{1,0:T(8,128)(2,1)}, bf16[1024,256]{1,0:T(8,128)(2,1)}, u32[]{:S(2)}, u32[]{:S(2)}) %collective-permute-start.10) | collective-permute-done | bytes 524320 | tf_op jit(solution)/shard_map/ppermute | solution.py:521
  143.3 4.2 %collective-permute-start.19 = (bf16[128,1024]{1,0:T(8,128)(2,1)}, bf16[128,1024]{1,0:T(8,128)(2,1)}, u32[]{:S(2)}, u32[]{:S(2)}) collective-permute-start(bf16[128,1024]{1,0:T(8,128)(2,1)} %collective-permute-done.15.rest_3_), channel_id=1, source_target_pairs={{0,1},{1,0},{2,3},{3,2},{4,5},{5,4},{6,7},{7,6},{8,9},{9,8},{10,11... | collective-permute-start | bytes 786440 | tf_op jit(solution)/shard_map/ppermute | solution.py:436
  147.4 3.2 %collective-permute-done.14.rest_2_ = bf16[128,1024]{1,0:T(8,128)(2,1)} collective-permute-done((bf16[128,1024]{1,0:T(8,128)(2,1)}, bf16[128,1024]{1,0:T(8,128)(2,1)}, u32[]{:S(2)}, u32[]{:S(2)}) %collective-permute-start.14) | collective-permute-done | bytes 262176 | tf_op jit(solution)/shard_map/ppermute | solution.py:436
  153.4 4.6 %finish_rows.1 = (bf16[512,1024]{1,0:T(8,128)(2,1)}, bf16[512,1024]{1,0:T(8,128)(2,1)}) custom-call(s32[1,16]{1,0:T(1,128)} %constant_dynamic-slice_fusion.slot_ref, bf16[512,1024]{1,0:T(8,128)(2,1)} %get-tuple-element.46.dk_in, bf16[512,1024]{1,0:T(8,128)(2,1)} %get-tuple-element.47.dv_in, bf16[32,1024]{1,0:T(8,128)(2,1)} %fusion.10.dm_ref, ...), custom_call_target="tpu_custom_call" | custom-call | flops 67108864 | bytes 6291456 | tf_op jit(solution)/shard_map/finish_rows/pallas_call | solution.py:391
  158.1 3.6 %place_rows.1 = f32[1024,1024]{1,0:T(8,128)} custom-call(s32[2]{0:T(128)} %pad_add_fusion.where_ref, bf16[128,1024]{1,0:T(8,128)(2,1)} %add_convert_fusion.3.rest_0_, bf16[128,1024]{1,0:T(8,128)(2,1)} %collective-permute-done.13.rest_1_, bf16[128,1024]{1,0:T(8,128)(2,1)} %collective-permute-done.14.rest_2_, ...), custom_call_target="tpu_custom_call" | custom-call | flops 1048576 | bytes 6291456 | tf_op jit(solution)/shard_map/place_rows/pallas_call | solution.py:423
  (36 shorter events, 20.0 us)
Async XLA Ops:
  3.9 45.1 %collective-permute-start = (bf16[512,1536]{1,0:T(8,128)(2,1)}, bf16[512,1536]{1,0:T(8,128)(2,1)}, u32[]{:S(2)}, u32[]{:S(2)}) collective-permute-start(bf16[512,1536]{1,0:T(8,128)(2,1)} %get-tuple-element.29), channel_id=1, source_target_pairs={{0,1},{1,2},{2,3},{3,4},{4,5},{5,6},{6,7},{8,9},{9,10},{10,11},{11... | collective-permute-start | bytes 4718600 | tf_op jit(solution)/shard_map/ppermute | solution.py:497
  7.5 3.9 %collective-permute-start.1 = (bf16[16,2048]{1,0:T(8,128)(2,1)}, bf16[16,2048]{1,0:T(8,128)(2,1)S(1)}, u32[]{:S(2)}, u32[]{:S(2)}) collective-permute-start(bf16[16,2048]{1,0:T(8,128)(2,1)} %get-tuple-element.30), channel_id=1, source_target_pairs={{0,4},{1,5},{2,6},{3,7},{4,0},{5,1},{6,2},{7,3},{8,12},{9,13},{10,... | collective-permute-start | bytes 196616 | tf_op jit(solution)/shard_map/ppermute | solution.py:436
  12.4 20.2 %collective-permute-start.2 = (bf16[32,2048]{1,0:T(8,128)(2,1)S(1)}, bf16[32,2048]{1,0:T(8,128)(2,1)S(1)}, u32[]{:S(2)}, u32[]{:S(2)}) collective-permute-start(bf16[32,2048]{1,0:T(8,128)(2,1)S(1)} %maximum_select_fusion.2), channel_id=1, source_target_pairs={{0,2},{1,3},{2,0},{3,1},{4,6},{5,7},{6,4},{7,5},{8,10},{9,11},{10,... | collective-permute-start | bytes 393224 | tf_op jit(solution)/shard_map/ppermute | solution.py:436
  28.6 10.1 %collective-permute-start.4 = (bf16[512,512]{1,0:T(8,128)(2,1)}, bf16[512,512]{1,0:T(8,128)(2,1)}, u32[]{:S(2)}, u32[]{:S(2)}) collective-permute-start(bf16[512,512]{1,0:T(8,128)(2,1)} %get-tuple-element.31), channel_id=1, source_target_pairs={{0,1},{1,2},{2,3},{3,4},{4,5},{5,6},{6,7},{8,9},{9,10},{10,11},{11... | collective-permute-start | bytes 1572872 | tf_op jit(solution)/shard_map/ppermute | solution.py:497
  32.6 1.7 %collective-permute-start.3 = (bf16[64,2048]{1,0:T(8,128)(2,1)S(1)}, bf16[64,2048]{1,0:T(8,128)(2,1)S(1)}, u32[]{:S(2)}, u32[]{:S(2)}) collective-permute-start(bf16[64,2048]{1,0:T(8,128)(2,1)S(1)} %maximum_select_fusion.1), channel_id=1, source_target_pairs={{0,1},{1,0},{2,3},{3,2},{4,5},{5,4},{6,7},{7,6},{8,9},{9,8},{10,11... | collective-permute-start | bytes 786440 | tf_op jit(solution)/shard_map/ppermute | solution.py:436
  71.5 3.8 %collective-permute-start.5 = (bf16[4,160,1024]{2,1,0:T(8,128)(2,1)}, bf16[4,160,1024]{2,1,0:T(8,128)(2,1)S(1)}, u32[]{:S(2)}, u32[]{:S(2)}) collective-permute-start(bf16[4,160,1024]{2,1,0:T(8,128)(2,1)} %get-tuple-element.48), channel_id=1, source_target_pairs={{0,1},{1,0},{2,3},{3,2},{4,5},{5,4},{6,7},{7,6},{8,9},{9,8},{10,11... | collective-permute-start | bytes 3932168 | tf_op jit(solution)/shard_map/ppermute | solution.py:436
  78.1 9.9 %collective-permute-start.6 = (bf16[160,1024]{1,0:T(8,128)(2,1)}, bf16[160,1024]{1,0:T(8,128)(2,1)}, u32[]{:S(2)}, u32[]{:S(2)}) collective-permute-start(bf16[160,1024]{1,0:T(8,128)(2,1)} %get-tuple-element.54), channel_id=1, source_target_pairs={{0,2},{1,3},{2,0},{3,1},{4,6},{5,7},{6,4},{7,5},{8,10},{9,11},{10,... | collective-permute-start | bytes 983048 | tf_op jit(solution)/shard_map/ppermute | solution.py:436
  78.1 18.2 %collective-permute-start.8 = (bf16[160,1024]{1,0:T(8,128)(2,1)}, bf16[160,1024]{1,0:T(8,128)(2,1)}, u32[]{:S(2)}, u32[]{:S(2)}) collective-permute-start(bf16[160,1024]{1,0:T(8,128)(2,1)} %get-tuple-element.55), channel_id=1, source_target_pairs={{0,6},{1,7},{2,4},{3,5},{4,2},{5,3},{6,0},{7,1},{8,14},{9,15},{10,... | collective-permute-start | bytes 983048 | tf_op jit(solution)/shard_map/ppermute | solution.py:436
  81.5 14.8 %collective-permute-start.7 = (bf16[160,1024]{1,0:T(8,128)(2,1)}, bf16[160,1024]{1,0:T(8,128)(2,1)}, u32[]{:S(2)}, u32[]{:S(2)}) collective-permute-start(bf16[160,1024]{1,0:T(8,128)(2,1)} %get-tuple-element.56), channel_id=1, source_target_pairs={{0,4},{1,5},{2,6},{3,7},{4,0},{5,1},{6,2},{7,3},{8,12},{9,13},{10,... | collective-permute-start | bytes 983048 | tf_op jit(solution)/shard_map/ppermute | solution.py:436
  98.4 16.7 %collective-permute-start.11 = (bf16[128,1024]{1,0:T(8,128)(2,1)}, bf16[128,1024]{1,0:T(8,128)(2,1)}, u32[]{:S(2)}, u32[]{:S(2)}) collective-permute-start(bf16[128,1024]{1,0:T(8,128)(2,1)} %fusion.3), channel_id=1, source_target_pairs={{0,8},{8,0},{16,24},{24,16},{1,9},{9,1},{17,25},{25,17},{2,10},{10... | collective-permute-start | bytes 786440 | tf_op jit(solution)/shard_map/ppermute | solution.py:436
  110.1 43.3 %collective-permute-start.9 = (bf16[1024,768]{1,0:T(8,128)(2,1)}, bf16[1024,768]{1,0:T(8,128)(2,1)}, u32[]{:S(2)}, u32[]{:S(2)}) collective-permute-start(bf16[1024,768]{1,0:T(8,128)(2,1)} %get-tuple-element.50), channel_id=1, source_target_pairs={{1,0},{2,1},{3,2},{4,3},{5,4},{6,5},{7,6},{9,8},{10,9},{11,10},{12... | collective-permute-start | bytes 4718600 | tf_op jit(solution)/shard_map/ppermute | solution.py:521
  116.9 15.0 %collective-permute-start.12 = (bf16[128,1024]{1,0:T(8,128)(2,1)}, bf16[128,1024]{1,0:T(8,128)(2,1)}, u32[]{:S(2)}, u32[]{:S(2)}) collective-permute-start(bf16[128,1024]{1,0:T(8,128)(2,1)} %add_convert_fusion.4), channel_id=1, source_target_pairs={{0,16},{8,24},{16,0},{24,8},{1,17},{9,25},{17,1},{25,9},{2,18},{10... | collective-permute-start | bytes 786440 | tf_op jit(solution)/shard_map/ppermute | solution.py:436
  119.2 17.1 %copy-start = (s32[1,128]{1,0:T(1,128)S(1)}, s32[1,128]{1,0:T(1,128)}, u32[]{:S(2)}) copy-start(s32[1,128]{1,0:T(1,128)} %slots_ref.5) | copy-start | bytes 1540
  125.7 15.5 %collective-permute-start.10 = (bf16[1024,256]{1,0:T(8,128)(2,1)}, bf16[1024,256]{1,0:T(8,128)(2,1)}, u32[]{:S(2)}, u32[]{:S(2)}) collective-permute-start(bf16[1024,256]{1,0:T(8,128)(2,1)} %get-tuple-element.51), channel_id=1, source_target_pairs={{1,0},{2,1},{3,2},{4,3},{5,4},{6,5},{7,6},{9,8},{10,9},{11,10},{12... | collective-permute-start | bytes 1572872 | tf_op jit(solution)/shard_map/ppermute | solution.py:521
  133.7 9.6 %collective-permute-start.15 = (bf16[128,1024]{1,0:T(8,128)(2,1)}, bf16[128,1024]{1,0:T(8,128)(2,1)}, u32[]{:S(2)}, u32[]{:S(2)}) collective-permute-start(bf16[128,1024]{1,0:T(8,128)(2,1)} %add_convert_fusion.3.rest_0_), channel_id=1, source_target_pairs={{0,6},{1,7},{2,4},{3,5},{4,2},{5,3},{6,0},{7,1},{8,14},{9,15},{10,... | collective-permute-start | bytes 786440 | tf_op jit(solution)/shard_map/ppermute | solution.py:436
  134.1 16.6 %collective-permute-start.14 = (bf16[128,1024]{1,0:T(8,128)(2,1)}, bf16[128,1024]{1,0:T(8,128)(2,1)}, u32[]{:S(2)}, u32[]{:S(2)}) collective-permute-start(bf16[128,1024]{1,0:T(8,128)(2,1)} %add_convert_fusion.3.rest_0_), channel_id=1, source_target_pairs={{0,4},{1,5},{2,6},{3,7},{4,0},{5,1},{6,2},{7,3},{8,12},{9,13},{10,... | collective-permute-start | bytes 786440 | tf_op jit(solution)/shard_map/ppermute | solution.py:436
  135.4 15.7 %collective-permute-start.13 = (bf16[128,1024]{1,0:T(8,128)(2,1)}, bf16[128,1024]{1,0:T(8,128)(2,1)}, u32[]{:S(2)}, u32[]{:S(2)}) collective-permute-start(bf16[128,1024]{1,0:T(8,128)(2,1)} %add_convert_fusion.3.rest_0_), channel_id=1, source_target_pairs={{0,2},{1,3},{2,0},{3,1},{4,6},{5,7},{6,4},{7,5},{8,10},{9,11},{10,... | collective-permute-start | bytes 786440 | tf_op jit(solution)/shard_map/ppermute | solution.py:436
  141.2 16.9 %collective-permute-start.16 = (bf16[128,1024]{1,0:T(8,128)(2,1)}, bf16[128,1024]{1,0:T(8,128)(2,1)}, u32[]{:S(2)}, u32[]{:S(2)}) collective-permute-start(bf16[128,1024]{1,0:T(8,128)(2,1)} %add_convert_fusion.3.rest_0_), channel_id=1, source_target_pairs={{0,1},{1,0},{2,3},{3,2},{4,5},{5,4},{6,7},{7,6},{8,9},{9,8},{10,11... | collective-permute-start | bytes 786440 | tf_op jit(solution)/shard_map/ppermute | solution.py:436
  143.3 14.8 %collective-permute-start.19 = (bf16[128,1024]{1,0:T(8,128)(2,1)}, bf16[128,1024]{1,0:T(8,128)(2,1)}, u32[]{:S(2)}, u32[]{:S(2)}) collective-permute-start(bf16[128,1024]{1,0:T(8,128)(2,1)} %collective-permute-done.15.rest_3_), channel_id=1, source_target_pairs={{0,1},{1,0},{2,3},{3,2},{4,5},{5,4},{6,7},{7,6},{8,9},{9,8},{10,11... | collective-permute-start | bytes 786440 | tf_op jit(solution)/shard_map/ppermute | solution.py:436
  150.7 7.4 %collective-permute-start.18 = (bf16[128,1024]{1,0:T(8,128)(2,1)}, bf16[128,1024]{1,0:T(8,128)(2,1)}, u32[]{:S(2)}, u32[]{:S(2)}) collective-permute-start(bf16[128,1024]{1,0:T(8,128)(2,1)} %collective-permute-done.14.rest_2_), channel_id=1, source_target_pairs={{0,1},{1,0},{2,3},{3,2},{4,5},{5,4},{6,7},{7,6},{8,9},{9,8},{10,11... | collective-permute-start | bytes 786440 | tf_op jit(solution)/shard_map/ppermute | solution.py:436
  151.1 7.0 %collective-permute-start.17 = (bf16[128,1024]{1,0:T(8,128)(2,1)}, bf16[128,1024]{1,0:T(8,128)(2,1)}, u32[]{:S(2)}, u32[]{:S(2)}) collective-permute-start(bf16[128,1024]{1,0:T(8,128)(2,1)} %collective-permute-done.13.rest_1_), channel_id=1, source_target_pairs={{0,1},{1,0},{2,3},{3,2},{4,5},{5,4},{6,7},{7,6},{8,9},{9,8},{10,11... | collective-permute-start | bytes 786440 | tf_op jit(solution)/shard_map/ppermute | solution.py:436

commit v6 on v5

--- a/solution.py
+++ b/solution.py
@@ -75,10 +75,10 @@
 
 
 def forward_kernel(
-    me_ref, blocks_ref, fill_ref, q_ref, cot_ref, w_ref, ko_ref, vo_ref, kh_ref, vh_ref, km_ref, vm_ref, slots_ref,
+    me_ref, blocks_ref, fill_ref, q_ref, cot_ref, g_ref, ko_ref, vo_ref, kh_ref, vh_ref, km_ref, vm_ref, slots_ref,
     *rest, nb, order, start
 ):
-    send_ref, keep_ref, pt, ga_ref, ke, ve, q2s, pm, mb_ref, g_ref, at_ref, w_buf, dm_buf, sems, info_ref = rest[-15:]
+    send_ref, keep_ref, pt, ga_ref, ke, ve, q2s, pm, mb_ref, at_ref, w_buf, dm_buf, sems, info_ref = rest[-14:]
     slots = km_ref.shape[0]
     mine = slots // len(order)
     ext = kh_ref.shape[0] + ko_ref.shape[0]
@@ -87,7 +87,6 @@
     def _():
         tables(me_ref[0], blocks_ref, fill_ref, slots_ref, info_ref, mb_ref, nb, ko_ref.shape[0], order)
 
-    g_ref[...] = dot(cot_ref[...], w_ref[...], NT).astype(bf16)
     fill_keys(ke, kh_ref, ko_ref, km_ref)
     fill_keys(ve, vh_ref, vo_ref, vm_ref)
     ve[:, SPAN:] = jnp.ones((ve.shape[0], SPAN), bf16)
@@ -243,7 +242,7 @@
 ANY = pl.BlockSpec(memory_space=pl.ANY)
 
 
-def forward(me, blocks, fill, slot_row, q, cot, weight, ko, vo, halo, mem, order, start, count, carry):
+def forward(me, blocks, fill, slot_row, q, cot, g, ko, vo, halo, mem, order, start, count, carry):
     tokens, width = q.shape
     slots, hrows, nb, pairs = mem.shape[0], halo.shape[0], tokens // BLK, width // SPAN
     keys = hrows + tokens + slots
@@ -251,10 +250,10 @@
     members, plane = len(order), len(order) // 2
     rows, extra = width // members, 2 * slots // members
     out = jax.ShapeDtypeStruct((plane, rows + extra, width), bf16)
-    args = [me, blocks, fill, q, cot, weight, ko, vo, halo, halo, mem, mem, slot_row]
+    args = [me, blocks, fill, q, cot, g, ko, vo, halo, halo, mem, mem, slot_row]
     specs = [
         smem, smem, smem, columns(tokens, start), pl.BlockSpec((tokens, width), lambda p: (0, 0)),
-        pl.BlockSpec((SPAN, width), lambda p: (p + start, 0)), columns(tokens, start), columns(tokens, start),
+        columns(tokens, start), columns(tokens, start), columns(tokens, start),
         columns(hrows, 0), columns(hrows, count), columns(slots, start), columns(slots, pairs + start),
         pl.BlockSpec((1, slots), lambda p: (0, 0)),
     ]
@@ -275,7 +274,7 @@
         scratch_shapes=[
             pltpu.VMEM((keys, SPAN), bf16), pltpu.VMEM((keys, 2 * SPAN), bf16),
             pltpu.VMEM((nb * TWO, SPAN), bf16), pltpu.VMEM((slots, nb * TWO), bf16),
-            pltpu.VMEM((nb, slots, BLK), f32), pltpu.VMEM((tokens, SPAN), bf16),
+            pltpu.VMEM((nb, slots, BLK), f32),
             pltpu.VMEM((tokens, SPAN), bf16), pltpu.VMEM((2, SPAN, width), bf16),
             pltpu.VMEM((2, 2, plane, extra, SPAN), bf16), pltpu.SemaphoreType.DMA((2, 2 + SPAN // rows)),
             pltpu.SMEM((2, nb), jnp.int32),
@@ -387,12 +386,13 @@
 def finish(slots, dko, dvo, dmem, backs, segments):
     tokens, width = dko.shape
     mine = slots.shape[0]
-    row = pl.BlockSpec((BLK, width), lambda r: (r, 0))
+    step = 2 * BLK
+    row = pl.BlockSpec((step, width), lambda r: (r, 0))
     return pl.pallas_call(
         functools.partial(finish_kernel, segments=segments),
-        grid=(tokens // BLK,),
+        grid=(tokens // step,),
         in_specs=[pl.BlockSpec((1, mine), lambda r: (0, 0)), row, row, pl.BlockSpec((2 * mine, width), lambda r: (0, 0))]
-        + [pl.BlockSpec((2, BLK, b.shape[-1]), lambda r: (0, r, 0)) for b in backs],
+        + [pl.BlockSpec((2, step, b.shape[-1]), lambda r: (0, r, 0)) for b in backs],
         out_specs=[row, row],
         out_shape=[jax.ShapeDtypeStruct((tokens, width), bf16)] * 2,
         compiler_params=pltpu.CompilerParams(vmem_limit_bytes=67_000_000),
@@ -401,35 +401,38 @@
     )(slots[None, :], dko, dvo, dmem, *backs)
 
 
-def place_kernel(where_ref, *rest, plane, scale):
-    n = 2 * plane
-    parts, out_ref, buf, sems = rest[:n], rest[n], rest[n + 1], rest[n + 2]
+def place_kernel(where_ref, *rest, plane, nfam, scale, flip):
+    parts, (out_ref, buf, sems) = rest[:plane], rest[-3:]
     rows = parts[0].shape[0]
-    core, spot = where_ref[0], where_ref[1]
+    piece = rows // nfam
+    side, spot, fam = (where_ref[0] & 1) ^ flip, lax.div(where_ref[0], 2), where_ref[1]
     copies = []
     for i, part in enumerate(parts):
-        side = jnp.where(i < plane, core, 1 - core)
-        at = pl.multiple_of((side * plane + (spot ^ (i % plane))) * rows, rows)
-        buf[i] = part[...].astype(f32) * scale
+        at = pl.multiple_of((side * plane + (spot ^ i)) * rows, rows)
+        for k in range(nfam):
+            row = pl.multiple_of((fam ^ k) * piece, piece)
+            buf[i, pl.ds(row, piece), :] = part[k * piece : (k + 1) * piece, :].astype(f32) * scale
         copies.append(pltpu.make_async_copy(buf.at[i], out_ref.at[pl.ds(at, rows), :], sems.at[i]))
         copies[-1].start()
     for copy in copies:
         copy.wait()
 
 
-def place(where, parts, scale):
+def place(where, parts, nfam, scale, flip, carry):
     rows, width = parts[0].shape
     n = len(parts)
+    more = [] if carry is None else [carry]
     return pl.pallas_call(
-        functools.partial(place_kernel, plane=n // 2, scale=scale),
-        in_specs=[pl.BlockSpec(memory_space=pltpu.SMEM)] + [pl.BlockSpec(memory_space=pltpu.VMEM)] * n,
-        out_specs=pl.BlockSpec(memory_space=pl.ANY),
-        out_shape=jax.ShapeDtypeStruct((n * rows, width), f32),
+        functools.partial(place_kernel, plane=n, nfam=nfam, scale=scale, flip=flip),
+        in_specs=[pl.BlockSpec(memory_space=pltpu.SMEM)] + [pl.BlockSpec(memory_space=pltpu.VMEM)] * n + [ANY] * len(more),
+        out_specs=ANY,
+        out_shape=jax.ShapeDtypeStruct((2 * n * rows, width), f32),
         scratch_shapes=[pltpu.VMEM((n, rows, width), f32), pltpu.SemaphoreType.DMA((n,))],
+        input_output_aliases={1 + n: 0} if more else {},
         compiler_params=pltpu.CompilerParams(vmem_limit_bytes=67_000_000),
-        cost_estimate=pl.CostEstimate(flops=1 << 20, bytes_accessed=6 << 20, transcendentals=0),
+        cost_estimate=pl.CostEstimate(flops=1 << 20, bytes_accessed=3 << 20, transcendentals=0),
         name="place_rows",
-    )(where, *parts)
+    )(where, *parts, *more)
 
 
 def swap(x, axis, bits):
@@ -475,7 +478,7 @@
     if pairs % 8:
         return [pairs], [(0, 0, pairs)], [pairs]
     u = pairs // 8
-    return [2 * u, 6 * u], [(0, 0, 2 * u), (1, 0, 4 * u), (1, 4 * u, 2 * u)], [6 * u, 2 * u]
+    return [3 * u, 5 * u], [(0, 0, u), (1, 0, 5 * u), (0, u, 2 * u)], [6 * u, 2 * u]
 
 
 def per_device(queries, key_rows, value_rows, cotangent, out_weight, prot_blocks, last_fill, memory_slots):
@@ -483,7 +486,7 @@
     slots = memory_slots[0]
     tokens, width = q.shape
     nctx, nfam = lax.axis_size("ctx"), lax.axis_size("fam")
-    me = lax.axis_index("ctx")
+    me, fam = lax.axis_index("ctx"), lax.axis_index("fam")
     total = slots.shape[0]
     mine = total // nctx
     pairs = width // SPAN
@@ -491,19 +494,20 @@
     fstarts = [sum(fsizes[:i]) for i in range(len(fsizes))]
     shift = [(i, i + 1) for i in range(nctx - 1)]
     back = [(i + 1, i) for i in range(nctx - 1)]
-    where = jnp.stack([me]).astype(jnp.int32)
+    where = jnp.stack([me, fam]).astype(jnp.int32)
     rows, *halos = prepare(where, memory_slots, k, v, mine, [n * SPAN for n in fsizes])
     mem = gather_rows(rows, "ctx", me)
     halos = [lax.ppermute(x, "ctx", shift) for x in halos]
+    grad_attn = dot(cot, out_weight, NT).astype(bf16)
     order = mirrored(nctx)
     carry, saved = [], []
     for i, (at, count) in enumerate(zip(fstarts, fsizes)):
         send, kept, pt, ga = forward(
-            where, prot_blocks, last_fill, memory_slots, q, cot, out_weight, k, v, halos[i], mem, order,
+            where, prot_blocks, last_fill, memory_slots, q, cot, grad_attn, k, v, halos[i], mem, order,
             at, count, carry)
         carry = [send, kept]
         saved.append((pt, ga))
-    core, spot, plane = me & 1, me >> 1, nctx // 2
+    spot, plane = me >> 1, nctx // 2
     at = lambda x, j, axis: lax.dynamic_index_in_dim(x, j, axis, keepdims=False)
     sent = swap(send, "ctx", 1)
     carry, backs, segments, i = [], [], [], 0
@@ -522,13 +526,14 @@
     got = exchange(lambda j: at(sent, j, 0).astype(f32) + at(kept, j, 0).astype(f32), "ctx", 1, spot, plane)
     rows = width // nctx
     mem_grad = total_of([x[rows:] for x in got]).astype(bf16)
-    w = total_of([x[:rows] for x in got]).astype(bf16)
-    for i, bit in enumerate(bits_of(nfam)):
-        w = total_of([w, swap(w, "fam", bit)]).astype(bf16)
+    piece = lambda j: total_of([lax.dynamic_slice_in_dim(x, j * (rows // nfam), rows // nfam) for x in got])
+    w = total_of(exchange(piece, "fam", 0, fam, nfam)).astype(bf16)
+    w = jnp.concatenate(spread(w, "fam", 0, nfam), 0)
     parts = spread(w, "ctx", 1, plane)
-    parts = parts + [swap(x, "ctx", 1) for x in parts]
+    others = [swap(x, "ctx", 1) for x in parts]
     scale = (nfam * nctx * tokens) ** -0.5
-    weight = place(jnp.stack([core, spot]).astype(jnp.int32), parts, scale)
+    weight = place(where, parts, nfam, scale, 0, None)
+    weight = place(where, others, nfam, scale, 1, weight)
     dq, dko, dvo = carry
     backs = [x.reshape(2, W, -1) for x in backs]
     dk, dv = finish(lax.dynamic_slice_in_dim(slots, me * mine, mine), dko, dvo, mem_grad, backs, segments)

time: 164 us -> 152 us (0.927)
  starting transfers between devices: 47.9 us -> 40.3 us
  waiting for transfers between devices: 32.3 us -> 26.9 us
  matrix products: 0 us -> 4.18 us
  other arithmetic: 12.6 us -> 10.3 us
    ppermute x16 -> x20, waiting for transfers between devices: 24.6 us -> 11.3 us  [swap(): lax.ppermute(x, axis, [(i, i ^ bits) for i in range(lax.axis_size(axis))])]
    ppermute x2, waiting for transfers between devices: 3.48 us -> 15.6 us  [per_device(): halos = [lax.ppermute(x, 'ctx', shift) for x in halos]]
    ppermute x16 -> x20, starting transfers between devices: 33.3 us -> 26 us  [swap(): lax.ppermute(x, axis, [(i, i ^ bits) for i in range(lax.axis_size(axis))])]
    convert_element_type x4 -> x1, other arithmetic: 7.31 us -> 1.91 us  [per_device(): w = total_of(exchange(piece, 'fam', 0, fam, nfam)).astype(bf16)]
    ppermute x2, waiting for transfers between devices: 4.26 us -> 0.01 us  [per_device(): backs.append(lax.ppermute(carry.pop(), 'ctx', back))]
    dot_general x0 -> x1, matrix products: none -> 4.18 us  [dot(): return lax.dot_general(a, b, dims, preferred_element_type=f32)]
    convert_element_type x1 -> x2, other arithmetic: 2.76 us -> 5.12 us  [exchange(): part(me ^ k).astype(bf16)]
    pallas_call x1 -> x2, Pallas kernels: 3.62 us -> 5.16 us  [place(): pl.pallas_call(functools.partial(place_kernel, plane=n, nfam=nfam, scale=...]
  transfers between devices with their start and end apart: 20 -> 24, of which waited for: 10 -> 7; matrix products, arithmetic and copies ran while one was open for 5% -> 7% of each run, Pallas kernels for 24% -> 28%
where the time goes in v6:
time: 152 us; the launch traced here: 150 us
  Pallas kernels  67 us (44%)
  starting transfers between devices  40.3 us (27%)
  waiting for transfers between devices  26.9 us (18%)
  other arithmetic  10.3 us (7%)
  matrix products  4.18 us (3%)
    pallas_call x2, Pallas kernels, forward(): pl.pallas_call(functools.partial(forward_kernel, nb=nb, order=order, star...  31.6 us
    ppermute x20, starting transfers between devices, swap(): lax.ppermute(x, axis, [(i, i ^ bits) for i in range(lax.axis_size(axis))])  26 us
    pallas_call x3, Pallas kernels, backward(): pl.pallas_call(functools.partial(backward_kernel, nb=nb), grid=(count,),...  23.3 us
    ppermute x2, waiting for transfers between devices, per_device(): halos = [lax.ppermute(x, 'ctx', shift) for x in halos]  15.6 us
    ppermute x20, waiting for transfers between devices, swap(): lax.ppermute(x, axis, [(i, i ^ bits) for i in range(lax.axis_size(axis))])  11.3 us
    ppermute x2, starting transfers between devices, per_device(): halos = [lax.ppermute(x, 'ctx', shift) for x in halos]  8.2 us
    ppermute x2, starting transfers between devices, per_device(): backs.append(lax.ppermute(carry.pop(), 'ctx', back))  6.16 us
    pallas_call x2, Pallas kernels, place(): pl.pallas_call(functools.partial(place_kernel, plane=n, nfam=nfam, scale=...  5.16 us
  transfers between devices with their start and end apart: 24, of which 7 were waited for; matrix products, arithmetic and copies ran while one was open for 7% of the time, Pallas kernels for 28%

profile of v6, /device:TPU:3, one launch (start us, length us, event | category | flops | bytes accessed | tf_op | source)
XLA Modules:
  0.0 150.3 jit_solution(15904273430972344667)
XLA Ops:
  1.3 3.2 %prepare_rows.1 = (bf16[16,2048]{1,0:T(8,128)(2,1)}, bf16[512,768]{1,0:T(8,128)(2,1)}, bf16[512,1280]{1,0:T(8,128)(2,1)}) custom-call(s32[2]{0:T(128)} %pad_add_fusion.me_ref.where_ref, s32[1,128]{1,0:T(1,128)} %slots_ref.5, bf16[512,1024]{1,0:T(8,128)(2,1)} %bitcast.68, bf16[512,1024]{1,0:T(8,128)(2,1)} %bitcast.74), custom_call_target="tpu_custom_call" | custom-call | tf_op jit(solution)/shard_map/prepare_rows/pallas_call | solution.py:315
  5.7 2.1 %collective-permute-done.1 = bf16[16,2048]{1,0:T(8,128)(2,1)S(1)} collective-permute-done((bf16[16,2048]{1,0:T(8,128)(2,1)}, bf16[16,2048]{1,0:T(8,128)(2,1)S(1)}, u32[]{:S(2)}, u32[]{:S(2)}) %collective-permute-start.1) | collective-permute-done | bytes 65568 | tf_op jit(solution)/shard_map/ppermute | solution.py:439
  8.9 6.3 %collective-permute-start.4 = (bf16[512,1280]{1,0:T(8,128)(2,1)}, bf16[512,1280]{1,0:T(8,128)(2,1)}, u32[]{:S(2)}, u32[]{:S(2)}) collective-permute-start(bf16[512,1280]{1,0:T(8,128)(2,1)} %get-tuple-element.33), channel_id=1, source_target_pairs={{0,1},{1,2},{2,3},{3,4},{4,5},{5,6},{6,7},{8,9},{9,10},{10,11},{11... | collective-permute-start | bytes 3932168 | tf_op jit(solution)/shard_map/ppermute | solution.py:500
  17.7 4.2 %convolution_convert_fusion.g_ref = bf16[512,1024]{1,0:T(8,128)(2,1)} fusion(bf16[1024,1024]{1,0:T(8,128)(2,1)} %param.12, bf16[1,512,1024]{2,1,0:T(8,128)(2,1)} %param.11), kind=kOutput, calls=%fused_computation | convolution fusion | flops 1074266112 | bytes 4194304 | tf_op jit(solution)/shard_map/dot_general | solution.py:26
  22.8 15.6 %collective-permute-done.kh_ref.vh_ref = bf16[512,768]{1,0:T(8,128)(2,1)} collective-permute-done((bf16[512,768]{1,0:T(8,128)(2,1)}, bf16[512,768]{1,0:T(8,128)(2,1)}, u32[]{:S(2)}, u32[]{:S(2)}) %collective-permute-start) | collective-permute-done | bytes 786464 | tf_op jit(solution)/shard_map/ppermute | solution.py:500
  38.4 12.9 %band_forward.2 = (bf16[4,160,1024]{2,1,0:T(8,128)(2,1)}, bf16[4,160,1024]{2,1,0:T(8,128)(2,1)}, bf16[3,1152,1024]{2,1,0:T(8,128)(2,1)}, bf16[3,1024,256]{2,1,0:T(8,128)(2,1)}) custom-call(s32[2]{0:T(128)} %pad_add_fusion.me_ref.where_ref, s32[1,8]{1,0:T(1,128)} %blocks_ref.3, s32[1,8]{1,0:T(1,128)} %fill_ref.3, bf16[512,1024]{1,0:T(8,128)(2,1)} %bitcast.80, ...), custom_call_target="tpu_custom_call" | custom-call | flops 4831838208 | bytes 12582912 | tf_op jit(solution)/shard_map/band_forward/pallas_call | solution.py:265
  51.3 18.7 %band_forward.3 = (bf16[4,160,1024]{2,1,0:T(8,128)(2,1)}, bf16[4,160,1024]{2,1,0:T(8,128)(2,1)}, bf16[5,1152,1024]{2,1,0:T(8,128)(2,1)}, bf16[5,1024,256]{2,1,0:T(8,128)(2,1)}) custom-call(s32[2]{0:T(128)} %pad_add_fusion.me_ref.where_ref, s32[1,8]{1,0:T(1,128)} %blocks_ref.3, s32[1,8]{1,0:T(1,128)} %fill_ref.3, ...), custom_call_target="tpu_custom_call", output_to_operand_aliasing={{0}: (13, {}), {1}: (14, {})} | custom-call | flops 8053063680 | bytes 20971520 | tf_op jit(solution)/shard_map/band_forward/pallas_call | solution.py:265
  70.2 4.5 %band_backward.3 = (bf16[512,1024]{1,0:T(8,128)(2,1)}, bf16[512,1024]{1,0:T(8,128)(2,1)}, bf16[512,1024]{1,0:T(8,128)(2,1)}, bf16[1024,768]{1,0:T(8,128)(2,1)}) custom-call(bf16[512,1024]{1,0:T(8,128)(2,1)} %bitcast.82, bf16[3,1152,1024]{2,1,0:T(8,128)(2,1)} %get-tuple-element.31.pt_ref, bf16[3,1024,256]{2,1,0:T(8,128)(2,1)} %get-tuple-element.32.ga_ref, ...), custom_call_target="tpu_custom_call" | custom-call | flops 2684354560 | bytes 6291456 | tf_op jit(solution)/shard_map/band_backward/pallas_call | solution.py:344
  74.7 3.2 %fusion = (bf16[160,1024]{1,0:T(8,128)(2,1)}, bf16[160,1024]{1,0:T(8,128)(2,1)}, bf16[160,1024]{1,0:T(8,128)(2,1)}, f32[1,160,1024]{2,1,0:T(8,128)}) fusion(bf16[4,160,1024]{2,1,0:T(8,128)(2,1)} %get-tuple-element.49, s32[]{:T(128)S(6)} %select_n.76, bf16[4,160,1024]{2,1,0:T(8,128)(2,1)} %collective-permute-done.5, s32[]{:T(128)S(6)} %select_n.78, ...), kind=kLoop, calls=%fused_computation.6 | loop fusion | flops 2457600 | bytes 4259856 | tf_op jit(solution)/shard_map/convert_element_type | solution.py:466
  77.9 3.4 %collective-permute-start.8 = (bf16[160,1024]{1,0:T(8,128)(2,1)}, bf16[160,1024]{1,0:T(8,128)(2,1)}, u32[]{:S(2)}, u32[]{:S(2)}) collective-permute-start(bf16[160,1024]{1,0:T(8,128)(2,1)} %get-tuple-element.55), channel_id=1, source_target_pairs={{0,6},{1,7},{2,4},{3,5},{4,2},{5,3},{6,0},{7,1},{8,14},{9,15},{10,... | collective-permute-start | bytes 983048 | tf_op jit(solution)/shard_map/ppermute | solution.py:439
  81.6 12.4 %band_backward.4 = (bf16[512,1024]{1,0:T(8,128)(2,1)}, bf16[512,1024]{1,0:T(8,128)(2,1)}, bf16[512,1024]{1,0:T(8,128)(2,1)}, bf16[1024,768]{1,0:T(8,128)(2,1)}) custom-call(bf16[512,1024]{1,0:T(8,128)(2,1)} %bitcast.83, bf16[5,1152,1024]{2,1,0:T(8,128)(2,1)} %get-tuple-element.36.pt_ref, ...), custom_call_target="tpu_custom_call", output_to_operand_aliasing={{0}: (8, {}), {1}: (9, {}), {2}: (10, {}), {3}: (11, {})} | custom-call | flops 13421772800 | bytes 31457280 | tf_op jit(solution)/shard_map/band_backward/pallas_call | solution.py:344
  94.0 2.7 %collective-permute-start.9 = (bf16[1024,768]{1,0:T(8,128)(2,1)}, bf16[1024,768]{1,0:T(8,128)(2,1)}, u32[]{:S(2)}, u32[]{:S(2)}) collective-permute-start(bf16[1024,768]{1,0:T(8,128)(2,1)} %get-tuple-element.50), channel_id=1, source_target_pairs={{1,0},{2,1},{3,2},{4,3},{5,4},{6,5},{7,6},{9,8},{10,9},{11,10},{12... | collective-permute-start | bytes 4718600 | tf_op jit(solution)/shard_map/ppermute | solution.py:525
  98.8 3.3 %collective-permute-start.13 = (bf16[32,1024]{1,0:T(8,128)(2,1)}, bf16[32,1024]{1,0:T(8,128)(2,1)}, u32[]{:S(2)}, u32[]{:S(2)}) collective-permute-start(bf16[32,1024]{1,0:T(8,128)(2,1)} %get-tuple-element.61), channel_id=1, source_target_pairs={{0,24},{8,16},{16,8},{24,0},{1,25},{9,17},{17,9},{25,1},{2,26},{10... | collective-permute-start | bytes 196616 | tf_op jit(solution)/shard_map/ppermute | solution.py:439
  102.5 6.4 %band_backward.5 = (bf16[512,1024]{1,0:T(8,128)(2,1)}, bf16[512,1024]{1,0:T(8,128)(2,1)}, bf16[512,1024]{1,0:T(8,128)(2,1)}, bf16[1024,256]{1,0:T(8,128)(2,1)}) custom-call(bf16[512,1024]{1,0:T(8,128)(2,1)} %bitcast.84, bf16[3,1152,1024]{2,1,0:T(8,128)(2,1)} %get-tuple-element.31.pt_ref, ...), custom_call_target="tpu_custom_call", output_to_operand_aliasing={{0}: (8, {}), {1}: (9, {}), {2}: (10, {})} | custom-call | flops 5368709120 | bytes 12582912 | tf_op jit(solution)/shard_map/band_backward/pallas_call | solution.py:344
  108.9 3.5 %collective-permute-start.10 = (bf16[1024,256]{1,0:T(8,128)(2,1)}, bf16[1024,256]{1,0:T(8,128)(2,1)}, u32[]{:S(2)}, u32[]{:S(2)}) collective-permute-start(bf16[1024,256]{1,0:T(8,128)(2,1)} %get-tuple-element.51), channel_id=1, source_target_pairs={{1,0},{2,1},{3,2},{4,3},{5,4},{6,5},{7,6},{9,8},{10,9},{11,10},{12... | collective-permute-start | bytes 1572872 | tf_op jit(solution)/shard_map/ppermute | solution.py:525
  114.3 3.3 %collective-permute-start.16 = (bf16[32,1024]{1,0:T(8,128)(2,1)S(1)}, bf16[32,1024]{1,0:T(8,128)(2,1)S(1)}, u32[]{:S(2)}, u32[]{:S(2)}) collective-permute-start(bf16[32,1024]{1,0:T(8,128)(2,1)S(1)} %get-tuple-element.58), channel_id=1, source_target_pairs={{0,24},{8,16},{16,8},{24,0},{1,25},{9,17},{17,9},{25,1},{2,26},{10... | collective-permute-start | bytes 196616 | tf_op jit(solution)/shard_map/ppermute | solution.py:439
  118.0 2.0 %collective-permute-done.16 = bf16[32,1024]{1,0:T(8,128)(2,1)S(1)} collective-permute-done((bf16[32,1024]{1,0:T(8,128)(2,1)S(1)}, bf16[32,1024]{1,0:T(8,128)(2,1)S(1)}, u32[]{:S(2)}, u32[]{:S(2)}) %collective-permute-start.16) | collective-permute-done | bytes 65568 | tf_op jit(solution)/shard_map/ppermute | solution.py:439
  120.0 3.3 %collective-permute-done.15 = bf16[32,1024]{1,0:T(8,128)(2,1)S(1)} collective-permute-done((bf16[32,1024]{1,0:T(8,128)(2,1)S(1)}, bf16[32,1024]{1,0:T(8,128)(2,1)S(1)}, u32[]{:S(2)}, u32[]{:S(2)}) %collective-permute-start.15) | collective-permute-done | bytes 65568 | tf_op jit(solution)/shard_map/ppermute | solution.py:439
  128.5 3.1 %collective-permute-done.18.rest_1_ = bf16[128,1024]{1,0:T(8,128)(2,1)} collective-permute-done((bf16[128,1024]{1,0:T(8,128)(2,1)}, bf16[128,1024]{1,0:T(8,128)(2,1)}, u32[]{:S(2)}, u32[]{:S(2)}) %collective-permute-start.18) | collective-permute-done | bytes 262176 | tf_op jit(solution)/shard_map/ppermute | solution.py:439
  131.6 2.5 %collective-permute-start.19 = (bf16[128,1024]{1,0:T(8,128)(2,1)}, bf16[128,1024]{1,0:T(8,128)(2,1)}, u32[]{:S(2)}, u32[]{:S(2)}) collective-permute-start(bf16[128,1024]{1,0:T(8,128)(2,1)} %collective-permute-done.18.rest_1_), channel_id=1, source_target_pairs={{0,1},{1,0},{2,3},{3,2},{4,5},{5,4},{6,7},{7,6},{8,9},{9,8},{10,11... | collective-permute-start | bytes 786440 | tf_op jit(solution)/shard_map/ppermute | solution.py:439
  134.0 4.7 %collective-permute-start.21 = (bf16[128,1024]{1,0:T(8,128)(2,1)}, bf16[128,1024]{1,0:T(8,128)(2,1)}, u32[]{:S(2)}, u32[]{:S(2)}) collective-permute-start(bf16[128,1024]{1,0:T(8,128)(2,1)} %collective-permute-done.20.rest_2_), channel_id=1, source_target_pairs={{0,1},{1,0},{2,3},{3,2},{4,5},{5,4},{6,7},{7,6},{8,9},{9,8},{10,11... | collective-permute-start | bytes 786440 | tf_op jit(solution)/shard_map/ppermute | solution.py:439
  141.3 3.7 %finish_rows.1 = (bf16[512,1024]{1,0:T(8,128)(2,1)}, bf16[512,1024]{1,0:T(8,128)(2,1)}) custom-call(s32[1,16]{1,0:T(1,128)} %constant_dynamic-slice_fusion.slot_ref, bf16[512,1024]{1,0:T(8,128)(2,1)} %get-tuple-element.46.dk_in, bf16[512,1024]{1,0:T(8,128)(2,1)} %get-tuple-element.47.dv_in, bf16[32,1024]{1,0:T(8,128)(2,1)} %get-tuple-element.59.dm_ref, ...), custom_call_target="tpu_custom_call" | custom-call | flops 67108864 | bytes 6291456 | tf_op jit(solution)/shard_map/finish_rows/pallas_call | solution.py:391
  145.0 2.6 %place_rows.2.rest_4_ = f32[1024,1024]{1,0:T(8,128)} custom-call(s32[2]{0:T(128)} %pad_add_fusion.me_ref.where_ref, bf16[128,1024]{1,0:T(8,128)(2,1)} %pad_maximum_fusion.rest_0_, bf16[128,1024]{1,0:T(8,128)(2,1)} %collective-permute-done.18.rest_1_, bf16[128,1024]{1,0:T(8,128)(2,1)} %collective-permute-done.20.rest_2_, ...), custom_call_target="tpu_custom_call" | custom-call | flops 1048576 | bytes 3145728 | tf_op jit(solution)/shard_map/place_rows/pallas_call | solution.py:425
  147.6 2.6 %place_rows.3 = f32[1024,1024]{1,0:T(8,128)} custom-call(s32[2]{0:T(128)} %pad_add_fusion.me_ref.where_ref, bf16[128,1024]{1,0:T(8,128)(2,1)} %collective-permute-done.17.rest_0_, bf16[128,1024]{1,0:T(8,128)(2,1)} %collective-permute-done.19.rest_1_, bf16[128,1024]{1,0:T(8,128)(2,1)} %collective-permute-done.21.rest_2_, ...), custom_call_target="tpu_custom_call", output_to_operand_aliasing={{}: (5, {})} | custom-call | flops 1048576 | bytes 3145728 | tf_op jit(solution)/shard_map/place_rows/pallas_call | solution.py:425
  (45 shorter events, 19.1 us)
Async XLA Ops:
  4.5 3.3 %collective-permute-start.1 = (bf16[16,2048]{1,0:T(8,128)(2,1)}, bf16[16,2048]{1,0:T(8,128)(2,1)S(1)}, u32[]{:S(2)}, u32[]{:S(2)}) collective-permute-start(bf16[16,2048]{1,0:T(8,128)(2,1)} %get-tuple-element.30), channel_id=1, source_target_pairs={{0,4},{1,5},{2,6},{3,7},{4,0},{5,1},{6,2},{7,3},{8,12},{9,13},{10,... | collective-permute-start | bytes 196616 | tf_op jit(solution)/shard_map/ppermute | solution.py:439
  8.8 8.3 %collective-permute-start.2 = (bf16[32,2048]{1,0:T(8,128)(2,1)S(1)}, bf16[32,2048]{1,0:T(8,128)(2,1)S(1)}, u32[]{:S(2)}, u32[]{:S(2)}) collective-permute-start(bf16[32,2048]{1,0:T(8,128)(2,1)S(1)} %maximum_select_fusion.2), channel_id=1, source_target_pairs={{0,2},{1,3},{2,0},{3,1},{4,6},{5,7},{6,4},{7,5},{8,10},{9,11},{10,... | collective-permute-start | bytes 393224 | tf_op jit(solution)/shard_map/ppermute | solution.py:439
  8.9 42.4 %collective-permute-start.4 = (bf16[512,1280]{1,0:T(8,128)(2,1)}, bf16[512,1280]{1,0:T(8,128)(2,1)}, u32[]{:S(2)}, u32[]{:S(2)}) collective-permute-start(bf16[512,1280]{1,0:T(8,128)(2,1)} %get-tuple-element.33), channel_id=1, source_target_pairs={{0,1},{1,2},{2,3},{3,4},{4,5},{5,6},{6,7},{8,9},{9,10},{10,11},{11... | collective-permute-start | bytes 3932168 | tf_op jit(solution)/shard_map/ppermute | solution.py:500
  15.2 23.3 %collective-permute-start = (bf16[512,768]{1,0:T(8,128)(2,1)}, bf16[512,768]{1,0:T(8,128)(2,1)}, u32[]{:S(2)}, u32[]{:S(2)}) collective-permute-start(bf16[512,768]{1,0:T(8,128)(2,1)} %get-tuple-element.29), channel_id=1, source_target_pairs={{0,1},{1,2},{2,3},{3,4},{4,5},{5,6},{6,7},{8,9},{9,10},{10,11},{11... | collective-permute-start | bytes 2359304 | tf_op jit(solution)/shard_map/ppermute | solution.py:500
  17.2 4.7 %collective-permute-start.3 = (bf16[64,2048]{1,0:T(8,128)(2,1)S(1)}, bf16[64,2048]{1,0:T(8,128)(2,1)S(1)}, u32[]{:S(2)}, u32[]{:S(2)}) collective-permute-start(bf16[64,2048]{1,0:T(8,128)(2,1)S(1)} %maximum_select_fusion.1), channel_id=1, source_target_pairs={{0,1},{1,0},{2,3},{3,2},{4,5},{5,4},{6,7},{7,6},{8,9},{9,8},{10,11... | collective-permute-start | bytes 786440 | tf_op jit(solution)/shard_map/ppermute | solution.py:439
  70.1 4.6 %collective-permute-start.5 = (bf16[4,160,1024]{2,1,0:T(8,128)(2,1)}, bf16[4,160,1024]{2,1,0:T(8,128)(2,1)}, u32[]{:S(2)}, u32[]{:S(2)}) collective-permute-start(bf16[4,160,1024]{2,1,0:T(8,128)(2,1)} %get-tuple-element.48), channel_id=1, source_target_pairs={{0,1},{1,0},{2,3},{3,2},{4,5},{5,4},{6,7},{7,6},{8,9},{9,8},{10,11... | collective-permute-start | bytes 3932168 | tf_op jit(solution)/shard_map/ppermute | solution.py:439
  77.9 18.8 %collective-permute-start.8 = (bf16[160,1024]{1,0:T(8,128)(2,1)}, bf16[160,1024]{1,0:T(8,128)(2,1)}, u32[]{:S(2)}, u32[]{:S(2)}) collective-permute-start(bf16[160,1024]{1,0:T(8,128)(2,1)} %get-tuple-element.55), channel_id=1, source_target_pairs={{0,6},{1,7},{2,4},{3,5},{4,2},{5,3},{6,0},{7,1},{8,14},{9,15},{10,... | collective-permute-start | bytes 983048 | tf_op jit(solution)/shard_map/ppermute | solution.py:439
  81.3 15.5 %collective-permute-start.7 = (bf16[160,1024]{1,0:T(8,128)(2,1)}, bf16[160,1024]{1,0:T(8,128)(2,1)}, u32[]{:S(2)}, u32[]{:S(2)}) collective-permute-start(bf16[160,1024]{1,0:T(8,128)(2,1)} %get-tuple-element.56), channel_id=1, source_target_pairs={{0,4},{1,5},{2,6},{3,7},{4,0},{5,1},{6,2},{7,3},{8,12},{9,13},{10,... | collective-permute-start | bytes 983048 | tf_op jit(solution)/shard_map/ppermute | solution.py:439
  81.3 15.5 %collective-permute-start.6 = (bf16[160,1024]{1,0:T(8,128)(2,1)}, bf16[160,1024]{1,0:T(8,128)(2,1)}, u32[]{:S(2)}, u32[]{:S(2)}) collective-permute-start(bf16[160,1024]{1,0:T(8,128)(2,1)} %get-tuple-element.54), channel_id=1, source_target_pairs={{0,2},{1,3},{2,0},{3,1},{4,6},{5,7},{6,4},{7,5},{8,10},{9,11},{10,... | collective-permute-start | bytes 983048 | tf_op jit(solution)/shard_map/ppermute | solution.py:439
  94.0 47.3 %collective-permute-start.9 = (bf16[1024,768]{1,0:T(8,128)(2,1)}, bf16[1024,768]{1,0:T(8,128)(2,1)}, u32[]{:S(2)}, u32[]{:S(2)}) collective-permute-start(bf16[1024,768]{1,0:T(8,128)(2,1)} %get-tuple-element.50), channel_id=1, source_target_pairs={{1,0},{2,1},{3,2},{4,3},{5,4},{6,5},{7,6},{9,8},{10,9},{11,10},{12... | collective-permute-start | bytes 4718600 | tf_op jit(solution)/shard_map/ppermute | solution.py:525
  98.8 13.6 %collective-permute-start.13 = (bf16[32,1024]{1,0:T(8,128)(2,1)}, bf16[32,1024]{1,0:T(8,128)(2,1)}, u32[]{:S(2)}, u32[]{:S(2)}) collective-permute-start(bf16[32,1024]{1,0:T(8,128)(2,1)} %get-tuple-element.61), channel_id=1, source_target_pairs={{0,24},{8,16},{16,8},{24,0},{1,25},{9,17},{17,9},{25,1},{2,26},{10... | collective-permute-start | bytes 196616 | tf_op jit(solution)/shard_map/ppermute | solution.py:439
  102.1 10.3 %collective-permute-start.12 = (bf16[32,1024]{1,0:T(8,128)(2,1)}, bf16[32,1024]{1,0:T(8,128)(2,1)}, u32[]{:S(2)}, u32[]{:S(2)}) collective-permute-start(bf16[32,1024]{1,0:T(8,128)(2,1)} %get-tuple-element.62), channel_id=1, source_target_pairs={{0,16},{8,24},{16,0},{24,8},{1,17},{9,25},{17,1},{25,9},{2,18},{10... | collective-permute-start | bytes 196616 | tf_op jit(solution)/shard_map/ppermute | solution.py:439
  102.1 10.3 %collective-permute-start.11 = (bf16[32,1024]{1,0:T(8,128)(2,1)}, bf16[32,1024]{1,0:T(8,128)(2,1)}, u32[]{:S(2)}, u32[]{:S(2)}) collective-permute-start(bf16[32,1024]{1,0:T(8,128)(2,1)} %get-tuple-element.60), channel_id=1, source_target_pairs={{0,8},{8,0},{16,24},{24,16},{1,9},{9,1},{17,25},{25,17},{2,10},{10... | collective-permute-start | bytes 196616 | tf_op jit(solution)/shard_map/ppermute | solution.py:439
  108.9 18.6 %collective-permute-start.10 = (bf16[1024,256]{1,0:T(8,128)(2,1)}, bf16[1024,256]{1,0:T(8,128)(2,1)}, u32[]{:S(2)}, u32[]{:S(2)}) collective-permute-start(bf16[1024,256]{1,0:T(8,128)(2,1)} %get-tuple-element.51), channel_id=1, source_target_pairs={{1,0},{2,1},{3,2},{4,3},{5,4},{6,5},{7,6},{9,8},{10,9},{11,10},{12... | collective-permute-start | bytes 1572872 | tf_op jit(solution)/shard_map/ppermute | solution.py:525
  114.3 5.6 %collective-permute-start.16 = (bf16[32,1024]{1,0:T(8,128)(2,1)S(1)}, bf16[32,1024]{1,0:T(8,128)(2,1)S(1)}, u32[]{:S(2)}, u32[]{:S(2)}) collective-permute-start(bf16[32,1024]{1,0:T(8,128)(2,1)S(1)} %get-tuple-element.58), channel_id=1, source_target_pairs={{0,24},{8,16},{16,8},{24,0},{1,25},{9,17},{17,9},{25,1},{2,26},{10... | collective-permute-start | bytes 196616 | tf_op jit(solution)/shard_map/ppermute | solution.py:439
  117.7 5.6 %collective-permute-start.15 = (bf16[32,1024]{1,0:T(8,128)(2,1)S(1)}, bf16[32,1024]{1,0:T(8,128)(2,1)S(1)}, u32[]{:S(2)}, u32[]{:S(2)}) collective-permute-start(bf16[32,1024]{1,0:T(8,128)(2,1)S(1)} %get-tuple-element.58), channel_id=1, source_target_pairs={{0,16},{8,24},{16,0},{24,8},{1,17},{9,25},{17,1},{25,9},{2,18},{10... | collective-permute-start | bytes 196616 | tf_op jit(solution)/shard_map/ppermute | solution.py:439
  117.7 5.6 %collective-permute-start.14 = (bf16[32,1024]{1,0:T(8,128)(2,1)S(1)}, bf16[32,1024]{1,0:T(8,128)(2,1)S(1)}, u32[]{:S(2)}, u32[]{:S(2)}) collective-permute-start(bf16[32,1024]{1,0:T(8,128)(2,1)S(1)} %get-tuple-element.58), channel_id=1, source_target_pairs={{0,8},{8,0},{16,24},{24,16},{1,9},{9,1},{17,25},{25,17},{2,10},{10... | collective-permute-start | bytes 196616 | tf_op jit(solution)/shard_map/ppermute | solution.py:439
  124.0 7.6 %collective-permute-start.18 = (bf16[128,1024]{1,0:T(8,128)(2,1)}, bf16[128,1024]{1,0:T(8,128)(2,1)}, u32[]{:S(2)}, u32[]{:S(2)}) collective-permute-start(bf16[128,1024]{1,0:T(8,128)(2,1)} %pad_maximum_fusion.rest_0_), channel_id=1, source_target_pairs={{0,2},{1,3},{2,0},{3,1},{4,6},{5,7},{6,4},{7,5},{8,10},{9,11},{10,... | collective-permute-start | bytes 786440 | tf_op jit(solution)/shard_map/ppermute | solution.py:439
  124.9 9.1 %collective-permute-start.20 = (bf16[128,1024]{1,0:T(8,128)(2,1)}, bf16[128,1024]{1,0:T(8,128)(2,1)}, u32[]{:S(2)}, u32[]{:S(2)}) collective-permute-start(bf16[128,1024]{1,0:T(8,128)(2,1)} %pad_maximum_fusion.rest_0_), channel_id=1, source_target_pairs={{0,4},{1,5},{2,6},{3,7},{4,0},{5,1},{6,2},{7,3},{8,12},{9,13},{10,... | collective-permute-start | bytes 786440 | tf_op jit(solution)/shard_map/ppermute | solution.py:439
  126.3 13.1 %collective-permute-start.22 = (bf16[128,1024]{1,0:T(8,128)(2,1)}, bf16[128,1024]{1,0:T(8,128)(2,1)}, u32[]{:S(2)}, u32[]{:S(2)}) collective-permute-start(bf16[128,1024]{1,0:T(8,128)(2,1)} %pad_maximum_fusion.rest_0_), channel_id=1, source_target_pairs={{0,6},{1,7},{2,4},{3,5},{4,2},{5,3},{6,0},{7,1},{8,14},{9,15},{10,... | collective-permute-start | bytes 786440 | tf_op jit(solution)/shard_map/ppermute | solution.py:439
  127.5 20.0 %collective-permute-start.17 = (bf16[128,1024]{1,0:T(8,128)(2,1)}, bf16[128,1024]{1,0:T(8,128)(2,1)}, u32[]{:S(2)}, u32[]{:S(2)}) collective-permute-start(bf16[128,1024]{1,0:T(8,128)(2,1)} %pad_maximum_fusion.rest_0_), channel_id=1, source_target_pairs={{0,1},{1,0},{2,3},{3,2},{4,5},{5,4},{6,7},{7,6},{8,9},{9,8},{10,11... | collective-permute-start | bytes 786440 | tf_op jit(solution)/shard_map/ppermute | solution.py:439
  131.6 16.0 %collective-permute-start.19 = (bf16[128,1024]{1,0:T(8,128)(2,1)}, bf16[128,1024]{1,0:T(8,128)(2,1)}, u32[]{:S(2)}, u32[]{:S(2)}) collective-permute-start(bf16[128,1024]{1,0:T(8,128)(2,1)} %collective-permute-done.18.rest_1_), channel_id=1, source_target_pairs={{0,1},{1,0},{2,3},{3,2},{4,5},{5,4},{6,7},{7,6},{8,9},{9,8},{10,11... | collective-permute-start | bytes 786440 | tf_op jit(solution)/shard_map/ppermute | solution.py:439
  134.0 13.5 %collective-permute-start.21 = (bf16[128,1024]{1,0:T(8,128)(2,1)}, bf16[128,1024]{1,0:T(8,128)(2,1)}, u32[]{:S(2)}, u32[]{:S(2)}) collective-permute-start(bf16[128,1024]{1,0:T(8,128)(2,1)} %collective-permute-done.20.rest_2_), channel_id=1, source_target_pairs={{0,1},{1,0},{2,3},{3,2},{4,5},{5,4},{6,7},{7,6},{8,9},{9,8},{10,11... | collective-permute-start | bytes 786440 | tf_op jit(solution)/shard_map/ppermute | solution.py:439
  139.4 8.1 %collective-permute-start.23 = (bf16[128,1024]{1,0:T(8,128)(2,1)}, bf16[128,1024]{1,0:T(8,128)(2,1)}, u32[]{:S(2)}, u32[]{:S(2)}) collective-permute-start(bf16[128,1024]{1,0:T(8,128)(2,1)} %collective-permute-done.22.rest_3_), channel_id=1, source_target_pairs={{0,1},{1,0},{2,3},{3,2},{4,5},{5,4},{6,7},{7,6},{8,9},{9,8},{10,11... | collective-permute-start | bytes 786440 | tf_op jit(solution)/shard_map/ppermute | solution.py:439
  (1 other events, 38.2 us)

commit v7 on v6

--- a/solution.py
+++ b/solution.py
@@ -293,7 +293,7 @@
     )(*args)
 
 
-def prepare_kernel(me_ref, slots_ref, k_ref, v_ref, rows_ref, *halos, sizes):
+def rows_kernel(me_ref, slots_ref, k_ref, v_ref, rows_ref):
     tokens, width = k_ref.shape
     mine = rows_ref.shape[0]
     row = lax.broadcasted_iota(jnp.int32, (mine, tokens), 0)
@@ -303,24 +303,39 @@
     pick = (slot == lax.broadcasted_iota(jnp.int32, (mine, tokens), 1)).astype(f32).astype(bf16)
     rows_ref[:, :width] = dot(pick, k_ref[...], NN).astype(bf16)
     rows_ref[:, width:] = dot(pick, v_ref[...], NN).astype(bf16)
-    at = 0
-    for halo, size in zip(halos, sizes):
-        halo[:, :size] = k_ref[tokens - W :, at : at + size]
-        halo[:, size:] = v_ref[tokens - W :, at : at + size]
-        at += size
-
-
-def prepare(me, slots, k, v, mine, sizes):
+
+
+def memory_rows(me, slots, k, v, mine):
     smem, vmem = pl.BlockSpec(memory_space=pltpu.SMEM), pl.BlockSpec(memory_space=pltpu.VMEM)
     return pl.pallas_call(
-        functools.partial(prepare_kernel, sizes=sizes),
+        rows_kernel,
         in_specs=[smem, smem, vmem, vmem],
-        out_specs=[vmem] * (1 + len(sizes)),
-        out_shape=[jax.ShapeDtypeStruct((mine, 2 * k.shape[1]), bf16)]
-        + [jax.ShapeDtypeStruct((W, 2 * size), bf16) for size in sizes],
+        out_specs=vmem,
+        out_shape=jax.ShapeDtypeStruct((mine, 2 * k.shape[1]), bf16),
         compiler_params=pltpu.CompilerParams(vmem_limit_bytes=67_000_000),
-        name="prepare_rows",
+        name="memory_rows",
     )(me, slots, k, v)
+
+
+def halo_kernel(k_ref, v_ref, *halos, sizes):
+    edge, at = k_ref.shape[0] - W, 0
+    for halo, size in zip(halos, sizes):
+        halo[:, :size] = k_ref[edge:, at : at + size]
+        halo[:, size:] = v_ref[edge:, at : at + size]
+        at += size
+
+
+def halo_groups(k, v, sizes):
+    vmem = pl.BlockSpec(memory_space=pltpu.VMEM)
+    return pl.pallas_call(
+        functools.partial(halo_kernel, sizes=sizes),
+        in_specs=[vmem, vmem],
+        out_specs=[vmem] * len(sizes),
+        out_shape=[jax.ShapeDtypeStruct((W, 2 * size), bf16) for size in sizes],
+        compiler_params=pltpu.CompilerParams(vmem_limit_bytes=67_000_000),
+        cost_estimate=pl.CostEstimate(flops=0, bytes_accessed=4 << 20, transcendentals=0),
+        name="halo_groups",
+    )(k, v)
 
 
 def backward(q, pt, ga, ko, vo, kh, vh, km, start, count, base, halo_at, at, carry, dh_total, dh_at):
@@ -494,8 +509,9 @@
     fstarts = [sum(fsizes[:i]) for i in range(len(fsizes))]
     shift = [(i, i + 1) for i in range(nctx - 1)]
     back = [(i + 1, i) for i in range(nctx - 1)]
-    where = jnp.stack([me, fam]).astype(jnp.int32)
-    rows, *halos = prepare(where, memory_slots, k, v, mine, [n * SPAN for n in fsizes])
+    where = jnp.stack([me]).astype(jnp.int32)
+    rows = memory_rows(where, memory_slots, k, v, mine)
+    halos = halo_groups(k, v, [n * SPAN for n in fsizes])
     mem = gather_rows(rows, "ctx", me)
     halos = [lax.ppermute(x, "ctx", shift) for x in halos]
     grad_attn = dot(cot, out_weight, NT).astype(bf16)
@@ -532,6 +548,7 @@
     parts = spread(w, "ctx", 1, plane)
     others = [swap(x, "ctx", 1) for x in parts]
     scale = (nfam * nctx * tokens) ** -0.5
+    where = jnp.stack([me, fam]).astype(jnp.int32)
     weight = place(where, parts, nfam, scale, 0, None)
     weight = place(where, others, nfam, scale, 1, weight)
     dq, dko, dvo = carry

time: 152 us -> 155 us (1.020)
  Pallas kernels: 67 us -> 69.2 us
  other arithmetic: 10.3 us -> 12 us
    pallas_call x1 -> x2, Pallas kernels: 3.22 us -> 5.5 us  [the longest x1 2.93 us: halo_groups(): pl.pallas_call(functools.partial(halo_kernel, sizes=sizes), in_specs=[vme...]
    select_n x3, other arithmetic: 1.92 us -> 3.69 us  [gather_rows(): jnp.where(upper, jnp.concatenate([other, x], 0), jnp.concatenate([x, othe...]
  transfers between devices with their start and end apart: 24 -> 24, of which waited for: 7 -> 7; matrix products, arithmetic and copies ran while one was open for 7% -> 8% of each run, Pallas kernels for 28% -> 30%
where the time goes in v7:
time: 155 us; the launch traced here: 153 us
  Pallas kernels  69.2 us (45%)
  starting transfers between devices  40.2 us (26%)
  waiting for transfers between devices  25.8 us (17%)
  other arithmetic  12 us (8%)
  matrix products  4.18 us (3%)
    pallas_call x2, Pallas kernels, forward(): pl.pallas_call(functools.partial(forward_kernel, nb=nb, order=order, star...  31.6 us
    ppermute x20, starting transfers between devices, swap(): lax.ppermute(x, axis, [(i, i ^ bits) for i in range(lax.axis_size(axis))])  25.9 us
    pallas_call x3, Pallas kernels, backward(): pl.pallas_call(functools.partial(backward_kernel, nb=nb), grid=(count,),...  23.3 us
    ppermute x2, waiting for transfers between devices, per_device(): halos = [lax.ppermute(x, 'ctx', shift) for x in halos]  14.5 us
    ppermute x20, waiting for transfers between devices, swap(): lax.ppermute(x, axis, [(i, i ^ bits) for i in range(lax.axis_size(axis))])  11.3 us
    ppermute x2, starting transfers between devices, per_device(): halos = [lax.ppermute(x, 'ctx', shift) for x in halos]  8.2 us
    ppermute x2, starting transfers between devices, per_device(): backs.append(lax.ppermute(carry.pop(), 'ctx', back))  6.18 us
    pallas_call x2, Pallas kernels, place(): pl.pallas_call(functools.partial(place_kernel, plane=n, nfam=nfam, scale=...  5.16 us
  transfers between devices with their start and end apart: 24, of which 7 were waited for; matrix products, arithmetic and copies ran while one was open for 8% of the time, Pallas kernels for 30%

profile of v7, /device:TPU:3, one launch (start us, length us, event | category | flops | bytes accessed | tf_op | source)
XLA Modules:
  0.0 153.2 jit_solution(10253821606210665508)
XLA Ops:
  0.6 2.6 %memory_rows.1 = bf16[16,2048]{1,0:T(8,128)(2,1)} custom-call(s32[1]{0:T(128)} %bitcast.1.me_ref, s32[1,128]{1,0:T(1,128)} %slots_ref.5, bf16[512,1024]{1,0:T(8,128)(2,1)} %bitcast.68, bf16[512,1024]{1,0:T(8,128)(2,1)} %bitcast.75), custom_call_target="tpu_custom_call" | custom-call | tf_op jit(solution)/shard_map/memory_rows/pallas_call | solution.py:310
  4.4 2.1 %collective-permute-done.1 = bf16[16,2048]{1,0:T(8,128)(2,1)S(1)} collective-permute-done((bf16[16,2048]{1,0:T(8,128)(2,1)}, bf16[16,2048]{1,0:T(8,128)(2,1)S(1)}, u32[]{:S(2)}, u32[]{:S(2)}) %collective-permute-start.1) | collective-permute-done | bytes 65568 | tf_op jit(solution)/shard_map/ppermute | solution.py:454
  8.2 2.9 %halo_groups.1 = (bf16[512,768]{1,0:T(8,128)(2,1)}, bf16[512,1280]{1,0:T(8,128)(2,1)}) custom-call(bf16[512,1024]{1,0:T(8,128)(2,1)} %bitcast.69, bf16[512,1024]{1,0:T(8,128)(2,1)} %bitcast.76), custom_call_target="tpu_custom_call" | custom-call | bytes 4194304 | tf_op jit(solution)/shard_map/halo_groups/pallas_call | solution.py:330
  11.1 6.3 %collective-permute-start.4 = (bf16[512,1280]{1,0:T(8,128)(2,1)}, bf16[512,1280]{1,0:T(8,128)(2,1)}, u32[]{:S(2)}, u32[]{:S(2)}) collective-permute-start(bf16[512,1280]{1,0:T(8,128)(2,1)} %get-tuple-element.31), channel_id=1, source_target_pairs={{0,1},{1,2},{2,3},{3,4},{4,5},{5,6},{6,7},{8,9},{9,10},{10,11},{11... | collective-permute-start | bytes 3932168 | tf_op jit(solution)/shard_map/ppermute | solution.py:516
  21.1 4.2 %convolution_convert_fusion.g_ref = bf16[512,1024]{1,0:T(8,128)(2,1)} fusion(bf16[1024,1024]{1,0:T(8,128)(2,1)} %param.12, bf16[1,512,1024]{2,1,0:T(8,128)(2,1)} %param.11), kind=kOutput, calls=%fused_computation | convolution fusion | flops 1074266112 | bytes 4194304 | tf_op jit(solution)/shard_map/dot_general | solution.py:26
  26.2 14.5 %collective-permute-done.kh_ref.vh_ref = bf16[512,768]{1,0:T(8,128)(2,1)} collective-permute-done((bf16[512,768]{1,0:T(8,128)(2,1)}, bf16[512,768]{1,0:T(8,128)(2,1)}, u32[]{:S(2)}, u32[]{:S(2)}) %collective-permute-start) | collective-permute-done | bytes 786464 | tf_op jit(solution)/shard_map/ppermute | solution.py:516
  40.6 12.9 %band_forward.2 = (bf16[4,160,1024]{2,1,0:T(8,128)(2,1)}, bf16[4,160,1024]{2,1,0:T(8,128)(2,1)}, bf16[3,1152,1024]{2,1,0:T(8,128)(2,1)}, bf16[3,1024,256]{2,1,0:T(8,128)(2,1)}) custom-call(s32[1]{0:T(128)} %bitcast.1.me_ref, s32[1,8]{1,0:T(1,128)} %blocks_ref.3, s32[1,8]{1,0:T(1,128)} %fill_ref.3, bf16[512,1024]{1,0:T(8,128)(2,1)} %bitcast.82, ...), custom_call_target="tpu_custom_call" | custom-call | flops 4831838208 | bytes 12582912 | tf_op jit(solution)/shard_map/band_forward/pallas_call | solution.py:265
  53.5 18.7 %band_forward.3 = (bf16[4,160,1024]{2,1,0:T(8,128)(2,1)}, bf16[4,160,1024]{2,1,0:T(8,128)(2,1)}, bf16[5,1152,1024]{2,1,0:T(8,128)(2,1)}, bf16[5,1024,256]{2,1,0:T(8,128)(2,1)}) custom-call(s32[1]{0:T(128)} %bitcast.1.me_ref, s32[1,8]{1,0:T(1,128)} %blocks_ref.3, s32[1,8]{1,0:T(1,128)} %fill_ref.3, ...), custom_call_target="tpu_custom_call", output_to_operand_aliasing={{0}: (13, {}), {1}: (14, {})} | custom-call | flops 8053063680 | bytes 20971520 | tf_op jit(solution)/shard_map/band_forward/pallas_call | solution.py:265
  72.3 4.5 %band_backward.3 = (bf16[512,1024]{1,0:T(8,128)(2,1)}, bf16[512,1024]{1,0:T(8,128)(2,1)}, bf16[512,1024]{1,0:T(8,128)(2,1)}, bf16[1024,768]{1,0:T(8,128)(2,1)}) custom-call(bf16[512,1024]{1,0:T(8,128)(2,1)} %bitcast.84, bf16[3,1152,1024]{2,1,0:T(8,128)(2,1)} %get-tuple-element.29.pt_ref, bf16[3,1024,256]{2,1,0:T(8,128)(2,1)} %get-tuple-element.30.ga_ref, ...), custom_call_target="tpu_custom_call" | custom-call | flops 2684354560 | bytes 6291456 | tf_op jit(solution)/shard_map/band_backward/pallas_call | solution.py:359
  76.9 3.2 %fusion = (bf16[160,1024]{1,0:T(8,128)(2,1)}, bf16[160,1024]{1,0:T(8,128)(2,1)}, bf16[160,1024]{1,0:T(8,128)(2,1)}, f32[1,160,1024]{2,1,0:T(8,128)}) fusion(bf16[4,160,1024]{2,1,0:T(8,128)(2,1)} %get-tuple-element.47, s32[]{:T(128)S(6)} %select_n.76, bf16[4,160,1024]{2,1,0:T(8,128)(2,1)} %collective-permute-done.5, s32[]{:T(128)S(6)} %select_n.78, ...), kind=kLoop, calls=%fused_computation.6 | loop fusion | flops 2457600 | bytes 4259856 | tf_op jit(solution)/shard_map/convert_element_type | solution.py:481
  80.1 3.4 %collective-permute-start.8 = (bf16[160,1024]{1,0:T(8,128)(2,1)}, bf16[160,1024]{1,0:T(8,128)(2,1)}, u32[]{:S(2)}, u32[]{:S(2)}) collective-permute-start(bf16[160,1024]{1,0:T(8,128)(2,1)} %get-tuple-element.53), channel_id=1, source_target_pairs={{0,6},{1,7},{2,4},{3,5},{4,2},{5,3},{6,0},{7,1},{8,14},{9,15},{10,... | collective-permute-start | bytes 983048 | tf_op jit(solution)/shard_map/ppermute | solution.py:454
  83.8 12.4 %band_backward.4 = (bf16[512,1024]{1,0:T(8,128)(2,1)}, bf16[512,1024]{1,0:T(8,128)(2,1)}, bf16[512,1024]{1,0:T(8,128)(2,1)}, bf16[1024,768]{1,0:T(8,128)(2,1)}) custom-call(bf16[512,1024]{1,0:T(8,128)(2,1)} %bitcast.85, bf16[5,1152,1024]{2,1,0:T(8,128)(2,1)} %get-tuple-element.34.pt_ref, ...), custom_call_target="tpu_custom_call", output_to_operand_aliasing={{0}: (8, {}), {1}: (9, {}), {2}: (10, {}), {3}: (11, {})} | custom-call | flops 13421772800 | bytes 31457280 | tf_op jit(solution)/shard_map/band_backward/pallas_call | solution.py:359
  96.1 2.7 %collective-permute-start.9 = (bf16[1024,768]{1,0:T(8,128)(2,1)}, bf16[1024,768]{1,0:T(8,128)(2,1)}, u32[]{:S(2)}, u32[]{:S(2)}) collective-permute-start(bf16[1024,768]{1,0:T(8,128)(2,1)} %get-tuple-element.48), channel_id=1, source_target_pairs={{1,0},{2,1},{3,2},{4,3},{5,4},{6,5},{7,6},{9,8},{10,9},{11,10},{12... | collective-permute-start | bytes 4718600 | tf_op jit(solution)/shard_map/ppermute | solution.py:541
  101.0 3.3 %collective-permute-start.13 = (bf16[32,1024]{1,0:T(8,128)(2,1)}, bf16[32,1024]{1,0:T(8,128)(2,1)}, u32[]{:S(2)}, u32[]{:S(2)}) collective-permute-start(bf16[32,1024]{1,0:T(8,128)(2,1)} %get-tuple-element.59), channel_id=1, source_target_pairs={{0,24},{8,16},{16,8},{24,0},{1,25},{9,17},{17,9},{25,1},{2,26},{10... | collective-permute-start | bytes 196616 | tf_op jit(solution)/shard_map/ppermute | solution.py:454
  104.6 6.4 %band_backward.5 = (bf16[512,1024]{1,0:T(8,128)(2,1)}, bf16[512,1024]{1,0:T(8,128)(2,1)}, bf16[512,1024]{1,0:T(8,128)(2,1)}, bf16[1024,256]{1,0:T(8,128)(2,1)}) custom-call(bf16[512,1024]{1,0:T(8,128)(2,1)} %bitcast.86, bf16[3,1152,1024]{2,1,0:T(8,128)(2,1)} %get-tuple-element.29.pt_ref, ...), custom_call_target="tpu_custom_call", output_to_operand_aliasing={{0}: (8, {}), {1}: (9, {}), {2}: (10, {})} | custom-call | flops 5368709120 | bytes 12582912 | tf_op jit(solution)/shard_map/band_backward/pallas_call | solution.py:359
  111.1 3.5 %collective-permute-start.10 = (bf16[1024,256]{1,0:T(8,128)(2,1)}, bf16[1024,256]{1,0:T(8,128)(2,1)}, u32[]{:S(2)}, u32[]{:S(2)}) collective-permute-start(bf16[1024,256]{1,0:T(8,128)(2,1)} %get-tuple-element.49), channel_id=1, source_target_pairs={{1,0},{2,1},{3,2},{4,3},{5,4},{6,5},{7,6},{9,8},{10,9},{11,10},{12... | collective-permute-start | bytes 1572872 | tf_op jit(solution)/shard_map/ppermute | solution.py:541
  116.5 3.3 %collective-permute-start.16 = (bf16[32,1024]{1,0:T(8,128)(2,1)S(1)}, bf16[32,1024]{1,0:T(8,128)(2,1)S(1)}, u32[]{:S(2)}, u32[]{:S(2)}) collective-permute-start(bf16[32,1024]{1,0:T(8,128)(2,1)S(1)} %get-tuple-element.56), channel_id=1, source_target_pairs={{0,24},{8,16},{16,8},{24,0},{1,25},{9,17},{17,9},{25,1},{2,26},{10... | collective-permute-start | bytes 196616 | tf_op jit(solution)/shard_map/ppermute | solution.py:454
  122.1 3.3 %collective-permute-done.15 = bf16[32,1024]{1,0:T(8,128)(2,1)S(1)} collective-permute-done((bf16[32,1024]{1,0:T(8,128)(2,1)S(1)}, bf16[32,1024]{1,0:T(8,128)(2,1)S(1)}, u32[]{:S(2)}, u32[]{:S(2)}) %collective-permute-start.15) | collective-permute-done | bytes 65568 | tf_op jit(solution)/shard_map/ppermute | solution.py:454
  130.6 3.1 %collective-permute-done.18.rest_1_ = bf16[128,1024]{1,0:T(8,128)(2,1)} collective-permute-done((bf16[128,1024]{1,0:T(8,128)(2,1)}, bf16[128,1024]{1,0:T(8,128)(2,1)}, u32[]{:S(2)}, u32[]{:S(2)}) %collective-permute-start.18) | collective-permute-done | bytes 262176 | tf_op jit(solution)/shard_map/ppermute | solution.py:454
  133.7 2.5 %collective-permute-start.19 = (bf16[128,1024]{1,0:T(8,128)(2,1)}, bf16[128,1024]{1,0:T(8,128)(2,1)}, u32[]{:S(2)}, u32[]{:S(2)}) collective-permute-start(bf16[128,1024]{1,0:T(8,128)(2,1)} %collective-permute-done.18.rest_1_), channel_id=1, source_target_pairs={{0,1},{1,0},{2,3},{3,2},{4,5},{5,4},{6,7},{7,6},{8,9},{9,8},{10,11... | collective-permute-start | bytes 786440 | tf_op jit(solution)/shard_map/ppermute | solution.py:454
  136.2 4.7 %collective-permute-start.21 = (bf16[128,1024]{1,0:T(8,128)(2,1)}, bf16[128,1024]{1,0:T(8,128)(2,1)}, u32[]{:S(2)}, u32[]{:S(2)}) collective-permute-start(bf16[128,1024]{1,0:T(8,128)(2,1)} %collective-permute-done.20.rest_2_), channel_id=1, source_target_pairs={{0,1},{1,0},{2,3},{3,2},{4,5},{5,4},{6,7},{7,6},{8,9},{9,8},{10,11... | collective-permute-start | bytes 786440 | tf_op jit(solution)/shard_map/ppermute | solution.py:454
  144.1 3.7 %finish_rows.1 = (bf16[512,1024]{1,0:T(8,128)(2,1)}, bf16[512,1024]{1,0:T(8,128)(2,1)}) custom-call(s32[1,16]{1,0:T(1,128)} %constant_dynamic-slice_fusion.slot_ref, bf16[512,1024]{1,0:T(8,128)(2,1)} %get-tuple-element.44.dk_in, bf16[512,1024]{1,0:T(8,128)(2,1)} %get-tuple-element.45.dv_in, bf16[32,1024]{1,0:T(8,128)(2,1)} %get-tuple-element.57.dm_ref, ...), custom_call_target="tpu_custom_call" | custom-call | flops 67108864 | bytes 6291456 | tf_op jit(solution)/shard_map/finish_rows/pallas_call | solution.py:406
  147.8 2.6 %place_rows.2.rest_4_ = f32[1024,1024]{1,0:T(8,128)} custom-call(s32[2]{0:T(128)} %pad_add_fusion.where_ref, bf16[128,1024]{1,0:T(8,128)(2,1)} %pad_maximum_fusion.rest_0_, bf16[128,1024]{1,0:T(8,128)(2,1)} %collective-permute-done.18.rest_1_, bf16[128,1024]{1,0:T(8,128)(2,1)} %collective-permute-done.20.rest_2_, ...), custom_call_target="tpu_custom_call" | custom-call | flops 1048576 | bytes 3145728 | tf_op jit(solution)/shard_map/place_rows/pallas_call | solution.py:440
  150.4 2.6 %place_rows.3 = f32[1024,1024]{1,0:T(8,128)} custom-call(s32[2]{0:T(128)} %pad_add_fusion.where_ref, bf16[128,1024]{1,0:T(8,128)(2,1)} %collective-permute-done.17.rest_0_, bf16[128,1024]{1,0:T(8,128)(2,1)} %collective-permute-done.19.rest_1_, bf16[128,1024]{1,0:T(8,128)(2,1)} %collective-permute-done.21.rest_2_, ...), custom_call_target="tpu_custom_call", output_to_operand_aliasing={{}: (5, {})} | custom-call | flops 1048576 | bytes 3145728 | tf_op jit(solution)/shard_map/place_rows/pallas_call | solution.py:440
  (46 shorter events, 22.8 us)
Async XLA Ops:
  3.2 3.3 %collective-permute-start.1 = (bf16[16,2048]{1,0:T(8,128)(2,1)}, bf16[16,2048]{1,0:T(8,128)(2,1)S(1)}, u32[]{:S(2)}, u32[]{:S(2)}) collective-permute-start(bf16[16,2048]{1,0:T(8,128)(2,1)} %memory_rows.1), channel_id=1, source_target_pairs={{0,4},{1,5},{2,6},{3,7},{4,0},{5,1},{6,2},{7,3},{8,12},{9,13},{10,... | collective-permute-start | bytes 196616 | tf_op jit(solution)/shard_map/ppermute | solution.py:454
  8.1 11.2 %collective-permute-start.2 = (bf16[32,2048]{1,0:T(8,128)(2,1)}, bf16[32,2048]{1,0:T(8,128)(2,1)}, u32[]{:S(2)}, u32[]{:S(2)}) collective-permute-start(bf16[32,2048]{1,0:T(8,128)(2,1)} %maximum_select_fusion.2), channel_id=1, source_target_pairs={{0,2},{1,3},{2,0},{3,1},{4,6},{5,7},{6,4},{7,5},{8,10},{9,11},{10,... | collective-permute-start | bytes 393224 | tf_op jit(solution)/shard_map/ppermute | solution.py:454
  11.1 42.4 %collective-permute-start.4 = (bf16[512,1280]{1,0:T(8,128)(2,1)}, bf16[512,1280]{1,0:T(8,128)(2,1)}, u32[]{:S(2)}, u32[]{:S(2)}) collective-permute-start(bf16[512,1280]{1,0:T(8,128)(2,1)} %get-tuple-element.31), channel_id=1, source_target_pairs={{0,1},{1,2},{2,3},{3,4},{4,5},{5,6},{6,7},{8,9},{9,10},{10,11},{11... | collective-permute-start | bytes 3932168 | tf_op jit(solution)/shard_map/ppermute | solution.py:516
  17.4 23.3 %collective-permute-start = (bf16[512,768]{1,0:T(8,128)(2,1)}, bf16[512,768]{1,0:T(8,128)(2,1)}, u32[]{:S(2)}, u32[]{:S(2)}) collective-permute-start(bf16[512,768]{1,0:T(8,128)(2,1)} %get-tuple-element.28), channel_id=1, source_target_pairs={{0,1},{1,2},{2,3},{3,4},{4,5},{5,6},{6,7},{8,9},{9,10},{10,11},{11... | collective-permute-start | bytes 2359304 | tf_op jit(solution)/shard_map/ppermute | solution.py:516
  20.5 4.7 %collective-permute-start.3 = (bf16[64,2048]{1,0:T(8,128)(2,1)S(1)}, bf16[64,2048]{1,0:T(8,128)(2,1)S(1)}, u32[]{:S(2)}, u32[]{:S(2)}) collective-permute-start(bf16[64,2048]{1,0:T(8,128)(2,1)S(1)} %maximum_select_fusion.1), channel_id=1, source_target_pairs={{0,1},{1,0},{2,3},{3,2},{4,5},{5,4},{6,7},{7,6},{8,9},{9,8},{10,11... | collective-permute-start | bytes 786440 | tf_op jit(solution)/shard_map/ppermute | solution.py:454
  72.2 4.6 %collective-permute-start.5 = (bf16[4,160,1024]{2,1,0:T(8,128)(2,1)}, bf16[4,160,1024]{2,1,0:T(8,128)(2,1)}, u32[]{:S(2)}, u32[]{:S(2)}) collective-permute-start(bf16[4,160,1024]{2,1,0:T(8,128)(2,1)} %get-tuple-element.46), channel_id=1, source_target_pairs={{0,1},{1,0},{2,3},{3,2},{4,5},{5,4},{6,7},{7,6},{8,9},{9,8},{10,11... | collective-permute-start | bytes 3932168 | tf_op jit(solution)/shard_map/ppermute | solution.py:454
  80.1 18.8 %collective-permute-start.8 = (bf16[160,1024]{1,0:T(8,128)(2,1)}, bf16[160,1024]{1,0:T(8,128)(2,1)}, u32[]{:S(2)}, u32[]{:S(2)}) collective-permute-start(bf16[160,1024]{1,0:T(8,128)(2,1)} %get-tuple-element.53), channel_id=1, source_target_pairs={{0,6},{1,7},{2,4},{3,5},{4,2},{5,3},{6,0},{7,1},{8,14},{9,15},{10,... | collective-permute-start | bytes 983048 | tf_op jit(solution)/shard_map/ppermute | solution.py:454
  83.5 15.5 %collective-permute-start.7 = (bf16[160,1024]{1,0:T(8,128)(2,1)}, bf16[160,1024]{1,0:T(8,128)(2,1)}, u32[]{:S(2)}, u32[]{:S(2)}) collective-permute-start(bf16[160,1024]{1,0:T(8,128)(2,1)} %get-tuple-element.54), channel_id=1, source_target_pairs={{0,4},{1,5},{2,6},{3,7},{4,0},{5,1},{6,2},{7,3},{8,12},{9,13},{10,... | collective-permute-start | bytes 983048 | tf_op jit(solution)/shard_map/ppermute | solution.py:454
  83.5 15.5 %collective-permute-start.6 = (bf16[160,1024]{1,0:T(8,128)(2,1)}, bf16[160,1024]{1,0:T(8,128)(2,1)}, u32[]{:S(2)}, u32[]{:S(2)}) collective-permute-start(bf16[160,1024]{1,0:T(8,128)(2,1)} %get-tuple-element.52), channel_id=1, source_target_pairs={{0,2},{1,3},{2,0},{3,1},{4,6},{5,7},{6,4},{7,5},{8,10},{9,11},{10,... | collective-permute-start | bytes 983048 | tf_op jit(solution)/shard_map/ppermute | solution.py:454
  96.1 48.0 %collective-permute-start.9 = (bf16[1024,768]{1,0:T(8,128)(2,1)}, bf16[1024,768]{1,0:T(8,128)(2,1)}, u32[]{:S(2)}, u32[]{:S(2)}) collective-permute-start(bf16[1024,768]{1,0:T(8,128)(2,1)} %get-tuple-element.48), channel_id=1, source_target_pairs={{1,0},{2,1},{3,2},{4,3},{5,4},{6,5},{7,6},{9,8},{10,9},{11,10},{12... | collective-permute-start | bytes 4718600 | tf_op jit(solution)/shard_map/ppermute | solution.py:541
  101.0 13.6 %collective-permute-start.13 = (bf16[32,1024]{1,0:T(8,128)(2,1)}, bf16[32,1024]{1,0:T(8,128)(2,1)}, u32[]{:S(2)}, u32[]{:S(2)}) collective-permute-start(bf16[32,1024]{1,0:T(8,128)(2,1)} %get-tuple-element.59), channel_id=1, source_target_pairs={{0,24},{8,16},{16,8},{24,0},{1,25},{9,17},{17,9},{25,1},{2,26},{10... | collective-permute-start | bytes 196616 | tf_op jit(solution)/shard_map/ppermute | solution.py:454
  104.3 10.3 %collective-permute-start.12 = (bf16[32,1024]{1,0:T(8,128)(2,1)}, bf16[32,1024]{1,0:T(8,128)(2,1)}, u32[]{:S(2)}, u32[]{:S(2)}) collective-permute-start(bf16[32,1024]{1,0:T(8,128)(2,1)} %get-tuple-element.60), channel_id=1, source_target_pairs={{0,16},{8,24},{16,0},{24,8},{1,17},{9,25},{17,1},{25,9},{2,18},{10... | collective-permute-start | bytes 196616 | tf_op jit(solution)/shard_map/ppermute | solution.py:454
  104.3 10.3 %collective-permute-start.11 = (bf16[32,1024]{1,0:T(8,128)(2,1)}, bf16[32,1024]{1,0:T(8,128)(2,1)}, u32[]{:S(2)}, u32[]{:S(2)}) collective-permute-start(bf16[32,1024]{1,0:T(8,128)(2,1)} %get-tuple-element.58), channel_id=1, source_target_pairs={{0,8},{8,0},{16,24},{24,16},{1,9},{9,1},{17,25},{25,17},{2,10},{10... | collective-permute-start | bytes 196616 | tf_op jit(solution)/shard_map/ppermute | solution.py:454
  111.1 18.6 %collective-permute-start.10 = (bf16[1024,256]{1,0:T(8,128)(2,1)}, bf16[1024,256]{1,0:T(8,128)(2,1)}, u32[]{:S(2)}, u32[]{:S(2)}) collective-permute-start(bf16[1024,256]{1,0:T(8,128)(2,1)} %get-tuple-element.49), channel_id=1, source_target_pairs={{1,0},{2,1},{3,2},{4,3},{5,4},{6,5},{7,6},{9,8},{10,9},{11,10},{12... | collective-permute-start | bytes 1572872 | tf_op jit(solution)/shard_map/ppermute | solution.py:541
  116.5 5.6 %collective-permute-start.16 = (bf16[32,1024]{1,0:T(8,128)(2,1)S(1)}, bf16[32,1024]{1,0:T(8,128)(2,1)S(1)}, u32[]{:S(2)}, u32[]{:S(2)}) collective-permute-start(bf16[32,1024]{1,0:T(8,128)(2,1)S(1)} %get-tuple-element.56), channel_id=1, source_target_pairs={{0,24},{8,16},{16,8},{24,0},{1,25},{9,17},{17,9},{25,1},{2,26},{10... | collective-permute-start | bytes 196616 | tf_op jit(solution)/shard_map/ppermute | solution.py:454
  119.8 5.6 %collective-permute-start.15 = (bf16[32,1024]{1,0:T(8,128)(2,1)S(1)}, bf16[32,1024]{1,0:T(8,128)(2,1)S(1)}, u32[]{:S(2)}, u32[]{:S(2)}) collective-permute-start(bf16[32,1024]{1,0:T(8,128)(2,1)S(1)} %get-tuple-element.56), channel_id=1, source_target_pairs={{0,16},{8,24},{16,0},{24,8},{1,17},{9,25},{17,1},{25,9},{2,18},{10... | collective-permute-start | bytes 196616 | tf_op jit(solution)/shard_map/ppermute | solution.py:454
  119.8 5.6 %collective-permute-start.14 = (bf16[32,1024]{1,0:T(8,128)(2,1)S(1)}, bf16[32,1024]{1,0:T(8,128)(2,1)S(1)}, u32[]{:S(2)}, u32[]{:S(2)}) collective-permute-start(bf16[32,1024]{1,0:T(8,128)(2,1)S(1)} %get-tuple-element.56), channel_id=1, source_target_pairs={{0,8},{8,0},{16,24},{24,16},{1,9},{9,1},{17,25},{25,17},{2,10},{10... | collective-permute-start | bytes 196616 | tf_op jit(solution)/shard_map/ppermute | solution.py:454
  126.1 7.6 %collective-permute-start.18 = (bf16[128,1024]{1,0:T(8,128)(2,1)}, bf16[128,1024]{1,0:T(8,128)(2,1)}, u32[]{:S(2)}, u32[]{:S(2)}) collective-permute-start(bf16[128,1024]{1,0:T(8,128)(2,1)} %pad_maximum_fusion.rest_0_), channel_id=1, source_target_pairs={{0,2},{1,3},{2,0},{3,1},{4,6},{5,7},{6,4},{7,5},{8,10},{9,11},{10,... | collective-permute-start | bytes 786440 | tf_op jit(solution)/shard_map/ppermute | solution.py:454
  127.1 9.2 %collective-permute-start.20 = (bf16[128,1024]{1,0:T(8,128)(2,1)}, bf16[128,1024]{1,0:T(8,128)(2,1)}, u32[]{:S(2)}, u32[]{:S(2)}) collective-permute-start(bf16[128,1024]{1,0:T(8,128)(2,1)} %pad_maximum_fusion.rest_0_), channel_id=1, source_target_pairs={{0,4},{1,5},{2,6},{3,7},{4,0},{5,1},{6,2},{7,3},{8,12},{9,13},{10,... | collective-permute-start | bytes 786440 | tf_op jit(solution)/shard_map/ppermute | solution.py:454
  128.5 13.1 %collective-permute-start.22 = (bf16[128,1024]{1,0:T(8,128)(2,1)}, bf16[128,1024]{1,0:T(8,128)(2,1)}, u32[]{:S(2)}, u32[]{:S(2)}) collective-permute-start(bf16[128,1024]{1,0:T(8,128)(2,1)} %pad_maximum_fusion.rest_0_), channel_id=1, source_target_pairs={{0,6},{1,7},{2,4},{3,5},{4,2},{5,3},{6,0},{7,1},{8,14},{9,15},{10,... | collective-permute-start | bytes 786440 | tf_op jit(solution)/shard_map/ppermute | solution.py:454
  129.7 20.7 %collective-permute-start.17 = (bf16[128,1024]{1,0:T(8,128)(2,1)}, bf16[128,1024]{1,0:T(8,128)(2,1)}, u32[]{:S(2)}, u32[]{:S(2)}) collective-permute-start(bf16[128,1024]{1,0:T(8,128)(2,1)} %pad_maximum_fusion.rest_0_), channel_id=1, source_target_pairs={{0,1},{1,0},{2,3},{3,2},{4,5},{5,4},{6,7},{7,6},{8,9},{9,8},{10,11... | collective-permute-start | bytes 786440 | tf_op jit(solution)/shard_map/ppermute | solution.py:454
  133.7 16.7 %collective-permute-start.19 = (bf16[128,1024]{1,0:T(8,128)(2,1)}, bf16[128,1024]{1,0:T(8,128)(2,1)}, u32[]{:S(2)}, u32[]{:S(2)}) collective-permute-start(bf16[128,1024]{1,0:T(8,128)(2,1)} %collective-permute-done.18.rest_1_), channel_id=1, source_target_pairs={{0,1},{1,0},{2,3},{3,2},{4,5},{5,4},{6,7},{7,6},{8,9},{9,8},{10,11... | collective-permute-start | bytes 786440 | tf_op jit(solution)/shard_map/ppermute | solution.py:454
  136.2 14.2 %collective-permute-start.21 = (bf16[128,1024]{1,0:T(8,128)(2,1)}, bf16[128,1024]{1,0:T(8,128)(2,1)}, u32[]{:S(2)}, u32[]{:S(2)}) collective-permute-start(bf16[128,1024]{1,0:T(8,128)(2,1)} %collective-permute-done.20.rest_2_), channel_id=1, source_target_pairs={{0,1},{1,0},{2,3},{3,2},{4,5},{5,4},{6,7},{7,6},{8,9},{9,8},{10,11... | collective-permute-start | bytes 786440 | tf_op jit(solution)/shard_map/ppermute | solution.py:454
  141.6 8.8 %collective-permute-start.23 = (bf16[128,1024]{1,0:T(8,128)(2,1)}, bf16[128,1024]{1,0:T(8,128)(2,1)}, u32[]{:S(2)}, u32[]{:S(2)}) collective-permute-start(bf16[128,1024]{1,0:T(8,128)(2,1)} %collective-permute-done.22.rest_3_), channel_id=1, source_target_pairs={{0,1},{1,0},{2,3},{3,2},{4,5},{5,4},{6,7},{7,6},{8,9},{9,8},{10,11... | collective-permute-start | bytes 786440 | tf_op jit(solution)/shard_map/ppermute | solution.py:454
  (1 other events, 38.2 us)

commit v8 on v7

--- a/solution.py
+++ b/solution.py
@@ -416,14 +416,44 @@
     )(slots[None, :], dko, dvo, dmem, *backs)
 
 
-def place_kernel(where_ref, *rest, plane, nfam, scale, flip):
-    parts, (out_ref, buf, sems) = rest[:plane], rest[-3:]
+def finish_rest_kernel(slot_ref, dk_in, dv_in, mk_ref, mv_ref, back_ref, dk_old, dv_old, dk_ref, dv_ref):
+    tokens, mine = dk_in.shape[0], slot_ref.shape[1]
+    pick = (lax.broadcasted_iota(jnp.int32, (tokens, mine), 0) == slot_ref[...]).astype(f32).astype(bf16)
+    dk = dk_in[...].astype(f32) + dot(pick, mk_ref[...], NN)
+    dv = dv_in[...].astype(f32) + dot(pick, mv_ref[...], NN)
+    dk_ref[...] = (dk + back_ref[0].astype(f32)).astype(bf16)
+    dv_ref[...] = (dv + back_ref[1].astype(f32)).astype(bf16)
+
+
+def finish_rest(slots, dko, dvo, dmem, back, pair, count, carry):
+    tokens, width = dko.shape
+    mine = slots.shape[0]
+    col = lambda rows, j: pl.BlockSpec((rows, SPAN), lambda p: (j, p + pair))
+    return pl.pallas_call(
+        finish_rest_kernel,
+        grid=(count,),
+        in_specs=[
+            pl.BlockSpec((1, mine), lambda p: (0, 0)), col(tokens, 0), col(tokens, 0), col(mine, 0), col(mine, 1),
+            pl.BlockSpec((2, tokens, SPAN), lambda p: (0, 0, p)), ANY, ANY,
+        ],
+        out_specs=[col(tokens, 0), col(tokens, 0)],
+        out_shape=[jax.ShapeDtypeStruct((tokens, width), bf16)] * 2,
+        input_output_aliases={6: 0, 7: 1},
+        compiler_params=pltpu.CompilerParams(vmem_limit_bytes=67_000_000),
+        cost_estimate=pl.CostEstimate(flops=1 << 24, bytes_accessed=2 << 20, transcendentals=0),
+        name="finish_rest",
+    )(slots[None, :], dko, dvo, dmem, dmem, back, *carry)
+
+
+def place_kernel(me_ref, fam_ref, *rest, spots, plane, nfam, scale):
+    n = len(spots)
+    parts, (out_ref, buf, sems) = rest[:n], rest[-3:]
     rows = parts[0].shape[0]
     piece = rows // nfam
-    side, spot, fam = (where_ref[0] & 1) ^ flip, lax.div(where_ref[0], 2), where_ref[1]
+    core, spot, fam = me_ref[0] & 1, lax.div(me_ref[0], 2), fam_ref[0]
     copies = []
-    for i, part in enumerate(parts):
-        at = pl.multiple_of((side * plane + (spot ^ i)) * rows, rows)
+    for i, (part, (flip, other)) in enumerate(zip(parts, spots)):
+        at = pl.multiple_of(((core ^ flip) * plane + (spot ^ other)) * rows, rows)
         for k in range(nfam):
             row = pl.multiple_of((fam ^ k) * piece, piece)
             buf[i, pl.ds(row, piece), :] = part[k * piece : (k + 1) * piece, :].astype(f32) * scale
@@ -433,21 +463,22 @@
         copy.wait()
 
 
-def place(where, parts, nfam, scale, flip, carry):
+def place(me, fam, parts, spots, plane, nfam, scale, carry):
     rows, width = parts[0].shape
     n = len(parts)
     more = [] if carry is None else [carry]
+    smem, vmem = pl.BlockSpec(memory_space=pltpu.SMEM), pl.BlockSpec(memory_space=pltpu.VMEM)
     return pl.pallas_call(
-        functools.partial(place_kernel, plane=n, nfam=nfam, scale=scale, flip=flip),
-        in_specs=[pl.BlockSpec(memory_space=pltpu.SMEM)] + [pl.BlockSpec(memory_space=pltpu.VMEM)] * n + [ANY] * len(more),
+        functools.partial(place_kernel, spots=spots, plane=plane, nfam=nfam, scale=scale),
+        in_specs=[smem, smem] + [vmem] * n + [ANY] * len(more),
         out_specs=ANY,
-        out_shape=jax.ShapeDtypeStruct((2 * n * rows, width), f32),
+        out_shape=jax.ShapeDtypeStruct((2 * plane * rows, width), f32),
         scratch_shapes=[pltpu.VMEM((n, rows, width), f32), pltpu.SemaphoreType.DMA((n,))],
-        input_output_aliases={1 + n: 0} if more else {},
+        input_output_aliases={2 + n: 0} if more else {},
         compiler_params=pltpu.CompilerParams(vmem_limit_bytes=67_000_000),
         cost_estimate=pl.CostEstimate(flops=1 << 20, bytes_accessed=3 << 20, transcendentals=0),
         name="place_rows",
-    )(where, *parts, *more)
+    )(me, fam, *parts, *more)
 
 
 def swap(x, axis, bits):
@@ -493,7 +524,7 @@
     if pairs % 8:
         return [pairs], [(0, 0, pairs)], [pairs]
     u = pairs // 8
-    return [3 * u, 5 * u], [(0, 0, u), (1, 0, 5 * u), (0, u, 2 * u)], [6 * u, 2 * u]
+    return [3 * u, 5 * u], [(0, 0, u), (1, 0, 5 * u), (0, u, u), (0, 2 * u, u)], [7 * u, u]
 
 
 def per_device(queries, key_rows, value_rows, cotangent, out_weight, prot_blocks, last_fill, memory_slots):
@@ -548,12 +579,18 @@
     parts = spread(w, "ctx", 1, plane)
     others = [swap(x, "ctx", 1) for x in parts]
     scale = (nfam * nctx * tokens) ** -0.5
-    where = jnp.stack([me, fam]).astype(jnp.int32)
-    weight = place(where, parts, nfam, scale, 0, None)
-    weight = place(where, others, nfam, scale, 1, weight)
+    who = jnp.stack([fam]).astype(jnp.int32)
+    weight = place(where, who, [parts[0], others[0]], [(0, 0), (1, 0)], plane, nfam, scale, None)
+    spots = [(flip, k) for flip in range(2) for k in range(1, plane)]
+    weight = place(where, who, parts[1:] + others[1:], spots, plane, nfam, scale, weight)
     dq, dko, dvo = carry
     backs = [x.reshape(2, W, -1) for x in backs]
-    dk, dv = finish(lax.dynamic_slice_in_dim(slots, me * mine, mine), dko, dvo, mem_grad, backs, segments)
+    own_slots = lax.dynamic_slice_in_dim(slots, me * mine, mine)
+    grads = finish(own_slots, dko, dvo, mem_grad, backs[:1], [x for x in segments if x[0] == 0])
+    for i, x in enumerate(backs[1:], 1):
+        _, pair, _, count = [x for x in segments if x[0] == i][0]
+        grads = finish_rest(own_slots, dko, dvo, mem_grad, x, pair, count, grads)
+    dk, dv = grads
     return dq[None], dk[None], dv[None], weight
 
 

time: 155 us -> 170 us (1.097)
  waiting for transfers between devices: 25.8 us -> 46.9 us
  starting transfers between devices: 40.2 us -> 35 us
  Pallas kernels: 69.2 us -> 73.9 us
  other arithmetic: 12 us -> 7.39 us
    ppermute x20, waiting for transfers between devices: 11.3 us -> 46.4 us  [swap(): lax.ppermute(x, axis, [(i, i ^ bits) for i in range(lax.axis_size(axis))])]
    ppermute x2, waiting for transfers between devices: 14.5 us -> 0.48 us  [per_device(): halos = [lax.ppermute(x, 'ctx', shift) for x in halos]]
    ppermute x20, starting transfers between devices: 25.9 us -> 20.4 us  [swap(): lax.ppermute(x, axis, [(i, i ^ bits) for i in range(lax.axis_size(axis))])]
    convert_element_type x2, other arithmetic: 5.12 us -> 2.29 us  [exchange(): part(me ^ k).astype(bf16)]
    pallas_call x3 -> x4, Pallas kernels: 23.3 us -> 26 us  [backward(): pl.pallas_call(functools.partial(backward_kernel, nb=nb), grid=(count,),...]
    pallas_call x2 -> x3, Pallas kernels: 5.16 us -> 7.16 us  [the longest x2 5.14 us: place(): pl.pallas_call(functools.partial(place_kernel, spots=spots, plane=plane,...]
  transfers between devices with their start and end apart: 24 -> 24, of which waited for: 7 -> 9; matrix products, arithmetic and copies ran while one was open for 8% -> 6% of each run, Pallas kernels for 30% -> 29%
where the time goes in v8:
time: 170 us; the launch traced here: 169 us
  Pallas kernels  73.9 us (43%)
  waiting for transfers between devices  46.9 us (28%)
  starting transfers between devices  35 us (21%)
  other arithmetic  7.39 us (4%)
  matrix products  4.18 us (2%)
    ppermute x20, waiting for transfers between devices, swap(): lax.ppermute(x, axis, [(i, i ^ bits) for i in range(lax.axis_size(axis))])  46.4 us
    pallas_call x2, Pallas kernels, forward(): pl.pallas_call(functools.partial(forward_kernel, nb=nb, order=order, star...  31.7 us
    pallas_call x4, Pallas kernels, backward(): pl.pallas_call(functools.partial(backward_kernel, nb=nb), grid=(count,),...  26 us
    ppermute x20, starting transfers between devices, swap(): lax.ppermute(x, axis, [(i, i ^ bits) for i in range(lax.axis_size(axis))])  20.4 us
    ppermute x2, starting transfers between devices, per_device(): halos = [lax.ppermute(x, 'ctx', shift) for x in halos]  8.2 us
    ppermute x2, starting transfers between devices, per_device(): backs.append(lax.ppermute(carry.pop(), 'ctx', back))  6.36 us
    pallas_call x2, Pallas kernels, place(): pl.pallas_call(functools.partial(place_kernel, spots=spots, plane=plane,...  5.14 us
    dot_general x1, matrix products, dot(): return lax.dot_general(a, b, dims, preferred_element_type=f32)  4.18 us
  transfers between devices with their start and end apart: 24, of which 9 were waited for; matrix products, arithmetic and copies ran while one was open for 6% of the time, Pallas kernels for 29%

profile of v8, /device:TPU:3, one launch (start us, length us, event | category | flops | bytes accessed | tf_op | source)
XLA Modules:
  0.0 169.0 jit_solution(7665371047055421945)
XLA Ops:
  0.6 2.6 %memory_rows.1 = bf16[16,2048]{1,0:T(8,128)(2,1)} custom-call(s32[1]{0:T(128)} %bitcast.1.me_ref, s32[1,128]{1,0:T(1,128)} %slots_ref.5, bf16[512,1024]{1,0:T(8,128)(2,1)} %bitcast.68, bf16[512,1024]{1,0:T(8,128)(2,1)} %bitcast.76), custom_call_target="tpu_custom_call" | custom-call | tf_op jit(solution)/shard_map/memory_rows/pallas_call | solution.py:310
  4.4 2.1 %collective-permute-done.1 = bf16[16,2048]{1,0:T(8,128)(2,1)S(1)} collective-permute-done((bf16[16,2048]{1,0:T(8,128)(2,1)}, bf16[16,2048]{1,0:T(8,128)(2,1)S(1)}, u32[]{:S(2)}, u32[]{:S(2)}) %collective-permute-start.1) | collective-permute-done | bytes 65568 | tf_op jit(solution)/shard_map/ppermute | solution.py:485
  8.2 2.9 %halo_groups.1 = (bf16[512,768]{1,0:T(8,128)(2,1)}, bf16[512,1280]{1,0:T(8,128)(2,1)}) custom-call(bf16[512,1024]{1,0:T(8,128)(2,1)} %bitcast.69, bf16[512,1024]{1,0:T(8,128)(2,1)} %bitcast.77), custom_call_target="tpu_custom_call" | custom-call | bytes 4194304 | tf_op jit(solution)/shard_map/halo_groups/pallas_call | solution.py:330
  11.1 6.3 %collective-permute-start = (bf16[512,768]{1,0:T(8,128)(2,1)}, bf16[512,768]{1,0:T(8,128)(2,1)}, u32[]{:S(2)}, u32[]{:S(2)}) collective-permute-start(bf16[512,768]{1,0:T(8,128)(2,1)} %get-tuple-element.34), channel_id=1, source_target_pairs={{0,1},{1,2},{2,3},{3,4},{4,5},{5,6},{6,7},{8,9},{9,10},{10,11},{11... | collective-permute-start | bytes 2359304 | tf_op jit(solution)/shard_map/ppermute | solution.py:547
  21.1 4.2 %convolution_convert_fusion.g_ref = bf16[512,1024]{1,0:T(8,128)(2,1)} fusion(bf16[1024,1024]{1,0:T(8,128)(2,1)} %param.12, bf16[1,512,1024]{2,1,0:T(8,128)(2,1)} %param.11), kind=kOutput, calls=%fused_computation | convolution fusion | flops 1074266112 | bytes 4194304 | tf_op jit(solution)/shard_map/dot_general | solution.py:26
  26.6 13.0 %band_forward.2 = (bf16[4,160,1024]{2,1,0:T(8,128)(2,1)}, bf16[4,160,1024]{2,1,0:T(8,128)(2,1)}, bf16[3,1152,1024]{2,1,0:T(8,128)(2,1)}, bf16[3,1024,256]{2,1,0:T(8,128)(2,1)}) custom-call(s32[1]{0:T(128)} %bitcast.1.me_ref, s32[1,8]{1,0:T(1,128)} %blocks_ref.3, s32[1,8]{1,0:T(1,128)} %fill_ref.3, bf16[512,1024]{1,0:T(8,128)(2,1)} %bitcast.84, ...), custom_call_target="tpu_custom_call" | custom-call | flops 4831838208 | bytes 12582912 | tf_op jit(solution)/shard_map/band_forward/pallas_call | solution.py:265
  39.6 4.5 %band_backward.4 = (bf16[512,1024]{1,0:T(8,128)(2,1)}, bf16[512,1024]{1,0:T(8,128)(2,1)}, bf16[512,1024]{1,0:T(8,128)(2,1)}, bf16[1024,896]{1,0:T(8,128)(2,1)}) custom-call(bf16[512,1024]{1,0:T(8,128)(2,1)} %bitcast.85, bf16[3,1152,1024]{2,1,0:T(8,128)(2,1)} %get-tuple-element.35.pt_ref, bf16[3,1024,256]{2,1,0:T(8,128)(2,1)} %get-tuple-element.36.ga_ref, ...), custom_call_target="tpu_custom_call" | custom-call | flops 2684354560 | bytes 6291456 | tf_op jit(solution)/shard_map/band_backward/pallas_call | solution.py:359
  44.2 18.7 %band_forward.3 = (bf16[4,160,1024]{2,1,0:T(8,128)(2,1)}, bf16[4,160,1024]{2,1,0:T(8,128)(2,1)}, bf16[5,1152,1024]{2,1,0:T(8,128)(2,1)}, bf16[5,1024,256]{2,1,0:T(8,128)(2,1)}) custom-call(s32[1]{0:T(128)} %bitcast.1.me_ref, s32[1,8]{1,0:T(1,128)} %blocks_ref.3, s32[1,8]{1,0:T(1,128)} %fill_ref.3, ...), custom_call_target="tpu_custom_call", output_to_operand_aliasing={{0}: (13, {}), {1}: (14, {})} | custom-call | flops 8053063680 | bytes 20971520 | tf_op jit(solution)/shard_map/band_forward/pallas_call | solution.py:265
  62.9 12.4 %band_backward.5 = (bf16[512,1024]{1,0:T(8,128)(2,1)}, bf16[512,1024]{1,0:T(8,128)(2,1)}, bf16[512,1024]{1,0:T(8,128)(2,1)}, bf16[1024,896]{1,0:T(8,128)(2,1)}) custom-call(bf16[512,1024]{1,0:T(8,128)(2,1)} %bitcast.87, bf16[5,1152,1024]{2,1,0:T(8,128)(2,1)} %get-tuple-element.40.pt_ref, ...), custom_call_target="tpu_custom_call", output_to_operand_aliasing={{0}: (8, {}), {1}: (9, {}), {2}: (10, {}), {3}: (11, {})} | custom-call | flops 13421772800 | bytes 31457280 | tf_op jit(solution)/shard_map/band_backward/pallas_call | solution.py:359
  75.3 4.5 %band_backward.6 = (bf16[512,1024]{1,0:T(8,128)(2,1)}, bf16[512,1024]{1,0:T(8,128)(2,1)}, bf16[512,1024]{1,0:T(8,128)(2,1)}, bf16[1024,896]{1,0:T(8,128)(2,1)}) custom-call(bf16[512,1024]{1,0:T(8,128)(2,1)} %bitcast.88, bf16[3,1152,1024]{2,1,0:T(8,128)(2,1)} %get-tuple-element.35.pt_ref, ...), custom_call_target="tpu_custom_call", output_to_operand_aliasing={{0}: (8, {}), {1}: (9, {}), {2}: (10, {}), {3}: (11, {})} | custom-call | flops 2684354560 | bytes 6291456 | tf_op jit(solution)/shard_map/band_backward/pallas_call | solution.py:359
  79.8 2.6 %collective-permute-start.10 = (bf16[1024,896]{1,0:T(8,128)(2,1)}, bf16[1024,896]{1,0:T(8,128)(2,1)}, u32[]{:S(2)}, u32[]{:S(2)}) collective-permute-start(bf16[1024,896]{1,0:T(8,128)(2,1)} %get-tuple-element.59), channel_id=1, source_target_pairs={{1,0},{2,1},{3,2},{4,3},{5,4},{6,5},{7,6},{9,8},{10,9},{11,10},{12... | collective-permute-start | bytes 5505032 | tf_op jit(solution)/shard_map/ppermute | solution.py:572
  82.5 2.2 %fusion = (bf16[160,1024]{1,0:T(8,128)(2,1)S(1)}, bf16[160,1024]{1,0:T(8,128)(2,1)S(1)}, bf16[160,1024]{1,0:T(8,128)(2,1)S(1)}, f32[1,160,1024]{2,1,0:T(8,128)S(1)}) fusion(bf16[4,160,1024]{2,1,0:T(8,128)(2,1)} %get-tuple-element.57, s32[]{:T(128)S(6)} %select_n.76, bf16[4,160,1024]{2,1,0:T(8,128)(2,1)} %collective-permute-done.5, s32[]{:T(128)S(6)} %select_n.78, ...), kind=kLoop, calls=%fused_computation.6 | loop fusion | flops 2457600 | bytes 4259856 | tf_op jit(solution)/shard_map/convert_element_type | solution.py:512
  84.7 3.1 %collective-permute-start.8 = (bf16[160,1024]{1,0:T(8,128)(2,1)S(1)}, bf16[160,1024]{1,0:T(8,128)(2,1)S(1)}, u32[]{:S(2)}, u32[]{:S(2)}) collective-permute-start(bf16[160,1024]{1,0:T(8,128)(2,1)S(1)} %get-tuple-element.65), channel_id=1, source_target_pairs={{0,6},{1,7},{2,4},{3,5},{4,2},{5,3},{6,0},{7,1},{8,14},{9,15},{10,... | collective-permute-start | bytes 983048 | tf_op jit(solution)/shard_map/ppermute | solution.py:485
  88.1 7.7 %collective-permute-done.8 = bf16[160,1024]{1,0:T(8,128)(2,1)S(1)} collective-permute-done((bf16[160,1024]{1,0:T(8,128)(2,1)S(1)}, bf16[160,1024]{1,0:T(8,128)(2,1)S(1)}, u32[]{:S(2)}, u32[]{:S(2)}) %collective-permute-start.8) | collective-permute-done | bytes 327712 | tf_op jit(solution)/shard_map/ppermute | solution.py:485
  95.8 24.7 %collective-permute-done.7 = bf16[160,1024]{1,0:T(8,128)(2,1)S(1)} collective-permute-done((bf16[160,1024]{1,0:T(8,128)(2,1)S(1)}, bf16[160,1024]{1,0:T(8,128)(2,1)S(1)}, u32[]{:S(2)}, u32[]{:S(2)}) %collective-permute-start.7) | collective-permute-done | bytes 327712 | tf_op jit(solution)/shard_map/ppermute | solution.py:485
  120.6 3.4 %collective-permute-start.13 = (bf16[32,1024]{1,0:T(8,128)(2,1)S(1)}, bf16[32,1024]{1,0:T(8,128)(2,1)S(1)}, u32[]{:S(2)}, u32[]{:S(2)}) collective-permute-start(bf16[32,1024]{1,0:T(8,128)(2,1)S(1)} %get-tuple-element.71), channel_id=1, source_target_pairs={{0,24},{8,16},{16,8},{24,0},{1,25},{9,17},{17,9},{25,1},{2,26},{10... | collective-permute-start | bytes 196616 | tf_op jit(solution)/shard_map/ppermute | solution.py:485
  125.7 4.0 %collective-permute-done.12 = bf16[32,1024]{1,0:T(8,128)(2,1)S(1)} collective-permute-done((bf16[32,1024]{1,0:T(8,128)(2,1)S(1)}, bf16[32,1024]{1,0:T(8,128)(2,1)S(1)}, u32[]{:S(2)}, u32[]{:S(2)}) %collective-permute-start.12) | collective-permute-done | bytes 65568 | tf_op jit(solution)/shard_map/ppermute | solution.py:485
  135.4 3.8 %collective-permute-done.15 = bf16[32,1024]{1,0:T(8,128)(2,1)S(1)} collective-permute-done((bf16[32,1024]{1,0:T(8,128)(2,1)S(1)}, bf16[32,1024]{1,0:T(8,128)(2,1)S(1)}, u32[]{:S(2)}, u32[]{:S(2)}) %collective-permute-start.15) | collective-permute-done | bytes 65568 | tf_op jit(solution)/shard_map/ppermute | solution.py:485
  140.0 2.6 %collective-permute-start.19 = (bf16[128,1024]{1,0:T(8,128)(2,1)}, bf16[128,1024]{1,0:T(8,128)(2,1)}, u32[]{:S(2)}, u32[]{:S(2)}) collective-permute-start(bf16[128,1024]{1,0:T(8,128)(2,1)} %pad_maximum_fusion.rest_0_), channel_id=1, source_target_pairs={{0,6},{1,7},{2,4},{3,5},{4,2},{5,3},{6,0},{7,1},{8,14},{9,15},{10,... | collective-permute-start | bytes 786440 | tf_op jit(solution)/shard_map/ppermute | solution.py:485
  142.6 4.6 %band_backward.7 = (bf16[512,1024]{1,0:T(8,128)(2,1)}, bf16[512,1024]{1,0:T(8,128)(2,1)}, bf16[512,1024]{1,0:T(8,128)(2,1)}, bf16[1024,128]{1,0:T(8,128)(2,1)}) custom-call(bf16[512,1024]{1,0:T(8,128)(2,1)} %bitcast.89, bf16[3,1152,1024]{2,1,0:T(8,128)(2,1)} %get-tuple-element.35.pt_ref, ...), custom_call_target="tpu_custom_call", output_to_operand_aliasing={{0}: (8, {}), {1}: (9, {}), {2}: (10, {})} | custom-call | flops 2684354560 | bytes 6291456 | tf_op jit(solution)/shard_map/band_backward/pallas_call | solution.py:359
  147.2 3.8 %collective-permute-start.9 = (bf16[1024,128]{1,0:T(8,128)(2,1)}, bf16[1024,128]{1,0:T(8,128)(2,1)}, u32[]{:S(2)}, u32[]{:S(2)}) collective-permute-start(bf16[1024,128]{1,0:T(8,128)(2,1)} %get-tuple-element.58), channel_id=1, source_target_pairs={{1,0},{2,1},{3,2},{4,3},{5,4},{6,5},{7,6},{9,8},{10,9},{11,10},{12... | collective-permute-start | bytes 786440 | tf_op jit(solution)/shard_map/ppermute | solution.py:572
  152.9 4.6 %collective-permute-start.21 = (bf16[128,1024]{1,0:T(8,128)(2,1)}, bf16[128,1024]{1,0:T(8,128)(2,1)}, u32[]{:S(2)}, u32[]{:S(2)}) collective-permute-start(bf16[128,1024]{1,0:T(8,128)(2,1)} %collective-permute-done.18.rest_1_), channel_id=1, source_target_pairs={{0,1},{1,0},{2,3},{3,2},{4,5},{5,4},{6,7},{7,6},{8,9},{9,8},{10,11... | collective-permute-start | bytes 786440 | tf_op jit(solution)/shard_map/ppermute | solution.py:485
  158.1 3.6 %finish_rows.1 = (bf16[512,1024]{1,0:T(8,128)(2,1)}, bf16[512,1024]{1,0:T(8,128)(2,1)}) custom-call(s32[1,16]{1,0:T(1,128)} %constant_dynamic-slice_fusion.slot_ref, bf16[512,1024]{1,0:T(8,128)(2,1)} %get-tuple-element.54.dk_in, bf16[512,1024]{1,0:T(8,128)(2,1)} %get-tuple-element.55.dv_in, bf16[32,1024]{1,0:T(8,128)(2,1)} %get-tuple-element.69.dm_ref.mk_ref.mv_ref, ...), custom_call_target="tpu_custom_call" | custom-call | flops 67108864 | bytes 6291456 | tf_op jit(solution)/shard_map/finish_rows/pallas_call | solution.py:406
  165.7 3.1 %place_rows.3 = f32[1024,1024]{1,0:T(8,128)} custom-call(s32[1]{0:T(128)} %bitcast.1.me_ref, s32[1]{0:T(128)} %bitcast.14.fam_ref, bf16[128,1024]{1,0:T(8,128)(2,1)} %collective-permute-done.17.rest_0_, bf16[128,1024]{1,0:T(8,128)(2,1)} %collective-permute-done.18.rest_1_, ...), custom_call_target="tpu_custom_call", output_to_operand_aliasing={{}: (8, {})} | custom-call | flops 1048576 | bytes 3145728 | tf_op jit(solution)/shard_map/place_rows/pallas_call | solution.py:471
  (47 shorter events, 23.2 us)
Async XLA Ops:
  3.2 3.3 %collective-permute-start.1 = (bf16[16,2048]{1,0:T(8,128)(2,1)}, bf16[16,2048]{1,0:T(8,128)(2,1)S(1)}, u32[]{:S(2)}, u32[]{:S(2)}) collective-permute-start(bf16[16,2048]{1,0:T(8,128)(2,1)} %memory_rows.1), channel_id=1, source_target_pairs={{0,4},{1,5},{2,6},{3,7},{4,0},{5,1},{6,2},{7,3},{8,12},{9,13},{10,... | collective-permute-start | bytes 196616 | tf_op jit(solution)/shard_map/ppermute | solution.py:485
  8.1 11.2 %collective-permute-start.2 = (bf16[32,2048]{1,0:T(8,128)(2,1)}, bf16[32,2048]{1,0:T(8,128)(2,1)}, u32[]{:S(2)}, u32[]{:S(2)}) collective-permute-start(bf16[32,2048]{1,0:T(8,128)(2,1)} %maximum_select_fusion.2), channel_id=1, source_target_pairs={{0,2},{1,3},{2,0},{3,1},{4,6},{5,7},{6,4},{7,5},{8,10},{9,11},{10,... | collective-permute-start | bytes 393224 | tf_op jit(solution)/shard_map/ppermute | solution.py:485
  11.1 15.5 %collective-permute-start = (bf16[512,768]{1,0:T(8,128)(2,1)}, bf16[512,768]{1,0:T(8,128)(2,1)}, u32[]{:S(2)}, u32[]{:S(2)}) collective-permute-start(bf16[512,768]{1,0:T(8,128)(2,1)} %get-tuple-element.34), channel_id=1, source_target_pairs={{0,1},{1,2},{2,3},{3,4},{4,5},{5,6},{6,7},{8,9},{9,10},{10,11},{11... | collective-permute-start | bytes 2359304 | tf_op jit(solution)/shard_map/ppermute | solution.py:547
  17.4 26.8 %collective-permute-start.4 = (bf16[512,1280]{1,0:T(8,128)(2,1)}, bf16[512,1280]{1,0:T(8,128)(2,1)}, u32[]{:S(2)}, u32[]{:S(2)}) collective-permute-start(bf16[512,1280]{1,0:T(8,128)(2,1)} %get-tuple-element.37), channel_id=1, source_target_pairs={{0,1},{1,2},{2,3},{3,4},{4,5},{5,6},{6,7},{8,9},{9,10},{10,11},{11... | collective-permute-start | bytes 3932168 | tf_op jit(solution)/shard_map/ppermute | solution.py:547
  20.5 4.7 %collective-permute-start.3 = (bf16[64,2048]{1,0:T(8,128)(2,1)S(1)}, bf16[64,2048]{1,0:T(8,128)(2,1)S(1)}, u32[]{:S(2)}, u32[]{:S(2)}) collective-permute-start(bf16[64,2048]{1,0:T(8,128)(2,1)S(1)} %maximum_select_fusion.1), channel_id=1, source_target_pairs={{0,1},{1,0},{2,3},{3,2},{4,5},{5,4},{6,7},{7,6},{8,9},{9,8},{10,11... | collective-permute-start | bytes 786440 | tf_op jit(solution)/shard_map/ppermute | solution.py:485
  62.8 19.6 %collective-permute-start.5 = (bf16[4,160,1024]{2,1,0:T(8,128)(2,1)}, bf16[4,160,1024]{2,1,0:T(8,128)(2,1)}, u32[]{:S(2)}, u32[]{:S(2)}) collective-permute-start(bf16[4,160,1024]{2,1,0:T(8,128)(2,1)} %get-tuple-element.56), channel_id=1, source_target_pairs={{0,1},{1,0},{2,3},{3,2},{4,5},{5,4},{6,7},{7,6},{8,9},{9,8},{10,11... | collective-permute-start | bytes 3932168 | tf_op jit(solution)/shard_map/ppermute | solution.py:485
  79.8 71.1 %collective-permute-start.10 = (bf16[1024,896]{1,0:T(8,128)(2,1)}, bf16[1024,896]{1,0:T(8,128)(2,1)}, u32[]{:S(2)}, u32[]{:S(2)}) collective-permute-start(bf16[1024,896]{1,0:T(8,128)(2,1)} %get-tuple-element.59), channel_id=1, source_target_pairs={{1,0},{2,1},{3,2},{4,3},{5,4},{6,5},{7,6},{9,8},{10,9},{11,10},{12... | collective-permute-start | bytes 5505032 | tf_op jit(solution)/shard_map/ppermute | solution.py:572
  84.7 11.2 %collective-permute-start.8 = (bf16[160,1024]{1,0:T(8,128)(2,1)S(1)}, bf16[160,1024]{1,0:T(8,128)(2,1)S(1)}, u32[]{:S(2)}, u32[]{:S(2)}) collective-permute-start(bf16[160,1024]{1,0:T(8,128)(2,1)S(1)} %get-tuple-element.65), channel_id=1, source_target_pairs={{0,6},{1,7},{2,4},{3,5},{4,2},{5,3},{6,0},{7,1},{8,14},{9,15},{10,... | collective-permute-start | bytes 983048 | tf_op jit(solution)/shard_map/ppermute | solution.py:485
  87.8 32.7 %collective-permute-start.7 = (bf16[160,1024]{1,0:T(8,128)(2,1)S(1)}, bf16[160,1024]{1,0:T(8,128)(2,1)S(1)}, u32[]{:S(2)}, u32[]{:S(2)}) collective-permute-start(bf16[160,1024]{1,0:T(8,128)(2,1)S(1)} %get-tuple-element.66), channel_id=1, source_target_pairs={{0,4},{1,5},{2,6},{3,7},{4,0},{5,1},{6,2},{7,3},{8,12},{9,13},{10,... | collective-permute-start | bytes 983048 | tf_op jit(solution)/shard_map/ppermute | solution.py:485
  87.8 32.7 %collective-permute-start.6 = (bf16[160,1024]{1,0:T(8,128)(2,1)S(1)}, bf16[160,1024]{1,0:T(8,128)(2,1)S(1)}, u32[]{:S(2)}, u32[]{:S(2)}) collective-permute-start(bf16[160,1024]{1,0:T(8,128)(2,1)S(1)} %get-tuple-element.64), channel_id=1, source_target_pairs={{0,2},{1,3},{2,0},{3,1},{4,6},{5,7},{6,4},{7,5},{8,10},{9,11},{10,... | collective-permute-start | bytes 983048 | tf_op jit(solution)/shard_map/ppermute | solution.py:485
  120.6 5.1 %collective-permute-start.13 = (bf16[32,1024]{1,0:T(8,128)(2,1)S(1)}, bf16[32,1024]{1,0:T(8,128)(2,1)S(1)}, u32[]{:S(2)}, u32[]{:S(2)}) collective-permute-start(bf16[32,1024]{1,0:T(8,128)(2,1)S(1)} %get-tuple-element.71), channel_id=1, source_target_pairs={{0,24},{8,16},{16,8},{24,0},{1,25},{9,17},{17,9},{25,1},{2,26},{10... | collective-permute-start | bytes 196616 | tf_op jit(solution)/shard_map/ppermute | solution.py:485
  124.0 5.7 %collective-permute-start.12 = (bf16[32,1024]{1,0:T(8,128)(2,1)S(1)}, bf16[32,1024]{1,0:T(8,128)(2,1)S(1)}, u32[]{:S(2)}, u32[]{:S(2)}) collective-permute-start(bf16[32,1024]{1,0:T(8,128)(2,1)S(1)} %get-tuple-element.72), channel_id=1, source_target_pairs={{0,16},{8,24},{16,0},{24,8},{1,17},{9,25},{17,1},{25,9},{2,18},{10... | collective-permute-start | bytes 196616 | tf_op jit(solution)/shard_map/ppermute | solution.py:485
  124.0 5.7 %collective-permute-start.11 = (bf16[32,1024]{1,0:T(8,128)(2,1)S(1)}, bf16[32,1024]{1,0:T(8,128)(2,1)S(1)}, u32[]{:S(2)}, u32[]{:S(2)}) collective-permute-start(bf16[32,1024]{1,0:T(8,128)(2,1)S(1)} %get-tuple-element.70), channel_id=1, source_target_pairs={{0,8},{8,0},{16,24},{24,16},{1,9},{9,1},{17,25},{25,17},{2,10},{10... | collective-permute-start | bytes 196616 | tf_op jit(solution)/shard_map/ppermute | solution.py:485
  130.4 5.0 %collective-permute-start.16 = (bf16[32,1024]{1,0:T(8,128)(2,1)S(1)}, bf16[32,1024]{1,0:T(8,128)(2,1)S(1)}, u32[]{:S(2)}, u32[]{:S(2)}) collective-permute-start(bf16[32,1024]{1,0:T(8,128)(2,1)S(1)} %get-tuple-element.68), channel_id=1, source_target_pairs={{0,24},{8,16},{16,8},{24,0},{1,25},{9,17},{17,9},{25,1},{2,26},{10... | collective-permute-start | bytes 196616 | tf_op jit(solution)/shard_map/ppermute | solution.py:485
  132.2 7.0 %collective-permute-start.15 = (bf16[32,1024]{1,0:T(8,128)(2,1)S(1)}, bf16[32,1024]{1,0:T(8,128)(2,1)S(1)}, u32[]{:S(2)}, u32[]{:S(2)}) collective-permute-start(bf16[32,1024]{1,0:T(8,128)(2,1)S(1)} %get-tuple-element.68), channel_id=1, source_target_pairs={{0,16},{8,24},{16,0},{24,8},{1,17},{9,25},{17,1},{25,9},{2,18},{10... | collective-permute-start | bytes 196616 | tf_op jit(solution)/shard_map/ppermute | solution.py:485
  132.2 7.0 %collective-permute-start.14 = (bf16[32,1024]{1,0:T(8,128)(2,1)S(1)}, bf16[32,1024]{1,0:T(8,128)(2,1)S(1)}, u32[]{:S(2)}, u32[]{:S(2)}) collective-permute-start(bf16[32,1024]{1,0:T(8,128)(2,1)S(1)} %get-tuple-element.68), channel_id=1, source_target_pairs={{0,8},{8,0},{16,24},{24,16},{1,9},{9,1},{17,25},{25,17},{2,10},{10... | collective-permute-start | bytes 196616 | tf_op jit(solution)/shard_map/ppermute | solution.py:485
  140.0 11.1 %collective-permute-start.17 = (bf16[128,1024]{1,0:T(8,128)(2,1)}, bf16[128,1024]{1,0:T(8,128)(2,1)}, u32[]{:S(2)}, u32[]{:S(2)}) collective-permute-start(bf16[128,1024]{1,0:T(8,128)(2,1)} %pad_maximum_fusion.rest_0_), channel_id=1, source_target_pairs={{0,2},{1,3},{2,0},{3,1},{4,6},{5,7},{6,4},{7,5},{8,10},{9,11},{10,... | collective-permute-start | bytes 786440 | tf_op jit(solution)/shard_map/ppermute | solution.py:485
  140.0 12.9 %collective-permute-start.18 = (bf16[128,1024]{1,0:T(8,128)(2,1)}, bf16[128,1024]{1,0:T(8,128)(2,1)}, u32[]{:S(2)}, u32[]{:S(2)}) collective-permute-start(bf16[128,1024]{1,0:T(8,128)(2,1)} %pad_maximum_fusion.rest_0_), channel_id=1, source_target_pairs={{0,4},{1,5},{2,6},{3,7},{4,0},{5,1},{6,2},{7,3},{8,12},{9,13},{10,... | collective-permute-start | bytes 786440 | tf_op jit(solution)/shard_map/ppermute | solution.py:485
  140.0 17.5 %collective-permute-start.19 = (bf16[128,1024]{1,0:T(8,128)(2,1)}, bf16[128,1024]{1,0:T(8,128)(2,1)}, u32[]{:S(2)}, u32[]{:S(2)}) collective-permute-start(bf16[128,1024]{1,0:T(8,128)(2,1)} %pad_maximum_fusion.rest_0_), channel_id=1, source_target_pairs={{0,6},{1,7},{2,4},{3,5},{4,2},{5,3},{6,0},{7,1},{8,14},{9,15},{10,... | collective-permute-start | bytes 786440 | tf_op jit(solution)/shard_map/ppermute | solution.py:485
  147.2 14.5 %collective-permute-start.9 = (bf16[1024,128]{1,0:T(8,128)(2,1)}, bf16[1024,128]{1,0:T(8,128)(2,1)}, u32[]{:S(2)}, u32[]{:S(2)}) collective-permute-start(bf16[1024,128]{1,0:T(8,128)(2,1)} %get-tuple-element.58), channel_id=1, source_target_pairs={{1,0},{2,1},{3,2},{4,3},{5,4},{6,5},{7,6},{9,8},{10,9},{11,10},{12... | collective-permute-start | bytes 786440 | tf_op jit(solution)/shard_map/ppermute | solution.py:572
  150.9 12.7 %collective-permute-start.23 = (bf16[128,1024]{1,0:T(8,128)(2,1)}, bf16[128,1024]{1,0:T(8,128)(2,1)}, u32[]{:S(2)}, u32[]{:S(2)}) collective-permute-start(bf16[128,1024]{1,0:T(8,128)(2,1)} %pad_maximum_fusion.rest_0_), channel_id=1, source_target_pairs={{0,1},{1,0},{2,3},{3,2},{4,5},{5,4},{6,7},{7,6},{8,9},{9,8},{10,11... | collective-permute-start | bytes 786440 | tf_op jit(solution)/shard_map/ppermute | solution.py:485
  151.0 14.7 %collective-permute-start.20 = (bf16[128,1024]{1,0:T(8,128)(2,1)}, bf16[128,1024]{1,0:T(8,128)(2,1)}, u32[]{:S(2)}, u32[]{:S(2)}) collective-permute-start(bf16[128,1024]{1,0:T(8,128)(2,1)} %collective-permute-done.17.rest_0_), channel_id=1, source_target_pairs={{0,1},{1,0},{2,3},{3,2},{4,5},{5,4},{6,7},{7,6},{8,9},{9,8},{10,11... | collective-permute-start | bytes 786440 | tf_op jit(solution)/shard_map/ppermute | solution.py:485
  152.9 12.8 %collective-permute-start.21 = (bf16[128,1024]{1,0:T(8,128)(2,1)}, bf16[128,1024]{1,0:T(8,128)(2,1)}, u32[]{:S(2)}, u32[]{:S(2)}) collective-permute-start(bf16[128,1024]{1,0:T(8,128)(2,1)} %collective-permute-done.18.rest_1_), channel_id=1, source_target_pairs={{0,1},{1,0},{2,3},{3,2},{4,5},{5,4},{6,7},{7,6},{8,9},{9,8},{10,11... | collective-permute-start | bytes 786440 | tf_op jit(solution)/shard_map/ppermute | solution.py:485
  157.4 8.3 %collective-permute-start.22 = (bf16[128,1024]{1,0:T(8,128)(2,1)}, bf16[128,1024]{1,0:T(8,128)(2,1)}, u32[]{:S(2)}, u32[]{:S(2)}) collective-permute-start(bf16[128,1024]{1,0:T(8,128)(2,1)} %collective-permute-done.19.rest_2_), channel_id=1, source_target_pairs={{0,1},{1,0},{2,3},{3,2},{4,5},{5,4},{6,7},{7,6},{8,9},{9,8},{10,11... | collective-permute-start | bytes 786440 | tf_op jit(solution)/shard_map/ppermute | solution.py:485
  (1 other events, 14.8 us)

commit v9 on v8

--- a/solution.py
+++ b/solution.py
@@ -383,12 +383,20 @@
     )(*args)
 
 
-def finish_kernel(slot_ref, dk_in, dv_in, dm_ref, *rest, segments):
+def picks(me, slots_ref, base, rows, mine):
+    column = lax.broadcasted_iota(jnp.int32, (rows, mine), 1)
+    slot = jnp.zeros((rows, mine), jnp.int32)
+    for r in range(mine):
+        slot = jnp.where(column == r, slots_ref[0, me * mine + r], slot)
+    at = lax.broadcasted_iota(jnp.int32, (rows, mine), 0) + base
+    return (at == slot).astype(f32).astype(bf16)
+
+
+def finish_kernel(me_ref, slots_ref, dk_in, dv_in, dm_ref, *rest, segments):
     backs, (dk_ref, dv_ref) = rest[:-2], rest[-2:]
     rows = dk_in.shape[0]
-    mine = slot_ref.shape[1]
-    at = lax.broadcasted_iota(jnp.int32, (rows, mine), 0) + pl.program_id(0) * rows
-    pick = (at == slot_ref[...]).astype(f32).astype(bf16)
+    mine = dm_ref.shape[0] // 2
+    pick = picks(me_ref[0], slots_ref, pl.program_id(0) * rows, rows, mine)
     for g, pair, pos, count in segments:
         to, of = slice(pair * SPAN, (pair + count) * SPAN), slice(pos * SPAN, (pos + count) * SPAN)
         back = backs[g]
@@ -398,51 +406,52 @@
         dv_ref[:, to] = (dv + back[1, :, of].astype(f32)).astype(bf16)
 
 
-def finish(slots, dko, dvo, dmem, backs, segments):
+def finish(me, slots, dko, dvo, dmem, backs, segments):
     tokens, width = dko.shape
-    mine = slots.shape[0]
+    mine = dmem.shape[0] // 2
+    smem = pl.BlockSpec(memory_space=pltpu.SMEM)
     step = 2 * BLK
     row = pl.BlockSpec((step, width), lambda r: (r, 0))
     return pl.pallas_call(
         functools.partial(finish_kernel, segments=segments),
         grid=(tokens // step,),
-        in_specs=[pl.BlockSpec((1, mine), lambda r: (0, 0)), row, row, pl.BlockSpec((2 * mine, width), lambda r: (0, 0))]
+        in_specs=[smem, smem, row, row, pl.BlockSpec((2 * mine, width), lambda r: (0, 0))]
         + [pl.BlockSpec((2, step, b.shape[-1]), lambda r: (0, r, 0)) for b in backs],
         out_specs=[row, row],
         out_shape=[jax.ShapeDtypeStruct((tokens, width), bf16)] * 2,
         compiler_params=pltpu.CompilerParams(vmem_limit_bytes=67_000_000),
         cost_estimate=pl.CostEstimate(flops=1 << 26, bytes_accessed=6 << 20, transcendentals=0),
         name="finish_rows",
-    )(slots[None, :], dko, dvo, dmem, *backs)
-
-
-def finish_rest_kernel(slot_ref, dk_in, dv_in, mk_ref, mv_ref, back_ref, dk_old, dv_old, dk_ref, dv_ref):
-    tokens, mine = dk_in.shape[0], slot_ref.shape[1]
-    pick = (lax.broadcasted_iota(jnp.int32, (tokens, mine), 0) == slot_ref[...]).astype(f32).astype(bf16)
+    )(me, slots, dko, dvo, dmem, *backs)
+
+
+def finish_rest_kernel(me_ref, slots_ref, dk_in, dv_in, mk_ref, mv_ref, back_ref, dk_old, dv_old, dk_ref, dv_ref):
+    pick = picks(me_ref[0], slots_ref, 0, dk_in.shape[0], mk_ref.shape[0])
     dk = dk_in[...].astype(f32) + dot(pick, mk_ref[...], NN)
     dv = dv_in[...].astype(f32) + dot(pick, mv_ref[...], NN)
     dk_ref[...] = (dk + back_ref[0].astype(f32)).astype(bf16)
     dv_ref[...] = (dv + back_ref[1].astype(f32)).astype(bf16)
 
 
-def finish_rest(slots, dko, dvo, dmem, back, pair, count, carry):
+def finish_rest(me, slots, dko, dvo, dmem, back, pair, count, carry):
     tokens, width = dko.shape
-    mine = slots.shape[0]
+    mine = dmem.shape[0] // 2
+    smem = pl.BlockSpec(memory_space=pltpu.SMEM)
     col = lambda rows, j: pl.BlockSpec((rows, SPAN), lambda p: (j, p + pair))
     return pl.pallas_call(
         finish_rest_kernel,
         grid=(count,),
         in_specs=[
-            pl.BlockSpec((1, mine), lambda p: (0, 0)), col(tokens, 0), col(tokens, 0), col(mine, 0), col(mine, 1),
+            smem, smem, col(tokens, 0), col(tokens, 0), col(mine, 0), col(mine, 1),
             pl.BlockSpec((2, tokens, SPAN), lambda p: (0, 0, p)), ANY, ANY,
         ],
         out_specs=[col(tokens, 0), col(tokens, 0)],
         out_shape=[jax.ShapeDtypeStruct((tokens, width), bf16)] * 2,
-        input_output_aliases={6: 0, 7: 1},
+        input_output_aliases={7: 0, 8: 1},
         compiler_params=pltpu.CompilerParams(vmem_limit_bytes=67_000_000),
         cost_estimate=pl.CostEstimate(flops=1 << 24, bytes_accessed=2 << 20, transcendentals=0),
         name="finish_rest",
-    )(slots[None, :], dko, dvo, dmem, dmem, back, *carry)
+    )(me, slots, dko, dvo, dmem, dmem, back, *carry)
 
 
 def place_kernel(me_ref, fam_ref, *rest, spots, plane, nfam, scale):
@@ -570,7 +579,9 @@
             segments.append((len(backs), fstarts[j] + r, done, count))
             done, i = done + count, i + 1
         backs.append(lax.ppermute(carry.pop(), "ctx", back))
-    got = exchange(lambda j: at(sent, j, 0).astype(f32) + at(kept, j, 0).astype(f32), "ctx", 1, spot, plane)
+    both = lambda j, x, y: at(x, j, 0).astype(f32) + at(y, j, 0).astype(f32)
+    got = exchange(lambda j: both(j, sent, kept), "ctx", 1, spot, plane)
+    got[0] = both(spot, *lax.optimization_barrier((sent, kept)))
     rows = width // nctx
     mem_grad = total_of([x[rows:] for x in got]).astype(bf16)
     piece = lambda j: total_of([lax.dynamic_slice_in_dim(x, j * (rows // nfam), rows // nfam) for x in got])
@@ -585,11 +596,10 @@
     weight = place(where, who, parts[1:] + others[1:], spots, plane, nfam, scale, weight)
     dq, dko, dvo = carry
     backs = [x.reshape(2, W, -1) for x in backs]
-    own_slots = lax.dynamic_slice_in_dim(slots, me * mine, mine)
-    grads = finish(own_slots, dko, dvo, mem_grad, backs[:1], [x for x in segments if x[0] == 0])
+    grads = finish(where, memory_slots, dko, dvo, mem_grad, backs[:1], [x for x in segments if x[0] == 0])
     for i, x in enumerate(backs[1:], 1):
         _, pair, _, count = [x for x in segments if x[0] == i][0]
-        grads = finish_rest(own_slots, dko, dvo, mem_grad, x, pair, count, grads)
+        grads = finish_rest(where, memory_slots, dko, dvo, mem_grad, x, pair, count, grads)
     dk, dv = grads
     return dq[None], dk[None], dv[None], weight
 

time: 170 us -> 169 us (level)
  no operation moved by 1% of the time
where the time goes in v9:
time: 169 us; the launch traced here: 168 us
  Pallas kernels  73.9 us (44%)
  waiting for transfers between devices  46.1 us (27%)
  starting transfers between devices  35 us (21%)
  other arithmetic  8.18 us (5%)
  matrix products  4.18 us (2%)
    ppermute x20, waiting for transfers between devices, swap(): lax.ppermute(x, axis, [(i, i ^ bits) for i in range(lax.axis_size(axis))])  45.6 us
    pallas_call x2, Pallas kernels, forward(): pl.pallas_call(functools.partial(forward_kernel, nb=nb, order=order, star...  31.7 us
    pallas_call x4, Pallas kernels, backward(): pl.pallas_call(functools.partial(backward_kernel, nb=nb), grid=(count,),...  26 us
    ppermute x20, starting transfers between devices, swap(): lax.ppermute(x, axis, [(i, i ^ bits) for i in range(lax.axis_size(axis))])  20.4 us
    ppermute x2, starting transfers between devices, per_device(): halos = [lax.ppermute(x, 'ctx', shift) for x in halos]  8.2 us
    ppermute x2, starting transfers between devices, per_device(): backs.append(lax.ppermute(carry.pop(), 'ctx', back))  6.36 us
    pallas_call x2, Pallas kernels, place(): pl.pallas_call(functools.partial(place_kernel, spots=spots, plane=plane,...  5.14 us
    dot_general x1, matrix products, dot(): return lax.dot_general(a, b, dims, preferred_element_type=f32)  4.18 us
  transfers between devices with their start and end apart: 24, of which 9 were waited for; matrix products, arithmetic and copies ran while one was open for 6% of the time, Pallas kernels for 29%

profile of v9, /device:TPU:3, one launch (start us, length us, event | category | flops | bytes accessed | tf_op | source)
XLA Modules:
  0.0 168.4 jit_solution(2146369340969491896)
XLA Ops:
  0.6 2.6 %memory_rows.1 = bf16[16,2048]{1,0:T(8,128)(2,1)} custom-call(s32[1]{0:T(128)} %bitcast.1.me_ref, s32[1,128]{1,0:T(1,128)} %slots_ref.9, bf16[512,1024]{1,0:T(8,128)(2,1)} %bitcast.68, bf16[512,1024]{1,0:T(8,128)(2,1)} %bitcast.76), custom_call_target="tpu_custom_call" | custom-call | tf_op jit(solution)/shard_map/memory_rows/pallas_call | solution.py:310
  4.4 2.1 %collective-permute-done.1 = bf16[16,2048]{1,0:T(8,128)(2,1)S(1)} collective-permute-done((bf16[16,2048]{1,0:T(8,128)(2,1)}, bf16[16,2048]{1,0:T(8,128)(2,1)S(1)}, u32[]{:S(2)}, u32[]{:S(2)}) %collective-permute-start.1) | collective-permute-done | bytes 65568 | tf_op jit(solution)/shard_map/ppermute | solution.py:494
  8.2 2.9 %halo_groups.1 = (bf16[512,768]{1,0:T(8,128)(2,1)}, bf16[512,1280]{1,0:T(8,128)(2,1)}) custom-call(bf16[512,1024]{1,0:T(8,128)(2,1)} %bitcast.69, bf16[512,1024]{1,0:T(8,128)(2,1)} %bitcast.77), custom_call_target="tpu_custom_call" | custom-call | bytes 4194304 | tf_op jit(solution)/shard_map/halo_groups/pallas_call | solution.py:330
  11.1 6.3 %collective-permute-start = (bf16[512,768]{1,0:T(8,128)(2,1)}, bf16[512,768]{1,0:T(8,128)(2,1)}, u32[]{:S(2)}, u32[]{:S(2)}) collective-permute-start(bf16[512,768]{1,0:T(8,128)(2,1)} %get-tuple-element.36), channel_id=1, source_target_pairs={{0,1},{1,2},{2,3},{3,4},{4,5},{5,6},{6,7},{8,9},{9,10},{10,11},{11... | collective-permute-start | bytes 2359304 | tf_op jit(solution)/shard_map/ppermute | solution.py:556
  21.1 4.2 %convolution_convert_fusion.g_ref = bf16[512,1024]{1,0:T(8,128)(2,1)} fusion(bf16[1024,1024]{1,0:T(8,128)(2,1)} %param.12, bf16[1,512,1024]{2,1,0:T(8,128)(2,1)} %param.11), kind=kOutput, calls=%fused_computation | convolution fusion | flops 1074266112 | bytes 4194304 | tf_op jit(solution)/shard_map/dot_general | solution.py:26
  26.6 13.0 %band_forward.2 = (bf16[4,160,1024]{2,1,0:T(8,128)(2,1)}, bf16[4,160,1024]{2,1,0:T(8,128)(2,1)}, bf16[3,1152,1024]{2,1,0:T(8,128)(2,1)}, bf16[3,1024,256]{2,1,0:T(8,128)(2,1)}) custom-call(s32[1]{0:T(128)} %bitcast.1.me_ref, s32[1,8]{1,0:T(1,128)} %blocks_ref.3, s32[1,8]{1,0:T(1,128)} %fill_ref.3, bf16[512,1024]{1,0:T(8,128)(2,1)} %bitcast.84, ...), custom_call_target="tpu_custom_call" | custom-call | flops 4831838208 | bytes 12582912 | tf_op jit(solution)/shard_map/band_forward/pallas_call | solution.py:265
  39.6 4.5 %band_backward.4 = (bf16[512,1024]{1,0:T(8,128)(2,1)}, bf16[512,1024]{1,0:T(8,128)(2,1)}, bf16[512,1024]{1,0:T(8,128)(2,1)}, bf16[1024,896]{1,0:T(8,128)(2,1)}) custom-call(bf16[512,1024]{1,0:T(8,128)(2,1)} %bitcast.85, bf16[3,1152,1024]{2,1,0:T(8,128)(2,1)} %get-tuple-element.37.pt_ref, bf16[3,1024,256]{2,1,0:T(8,128)(2,1)} %get-tuple-element.38.ga_ref, ...), custom_call_target="tpu_custom_call" | custom-call | flops 2684354560 | bytes 6291456 | tf_op jit(solution)/shard_map/band_backward/pallas_call | solution.py:359
  44.1 18.7 %band_forward.3 = (bf16[4,160,1024]{2,1,0:T(8,128)(2,1)}, bf16[4,160,1024]{2,1,0:T(8,128)(2,1)}, bf16[5,1152,1024]{2,1,0:T(8,128)(2,1)}, bf16[5,1024,256]{2,1,0:T(8,128)(2,1)}) custom-call(s32[1]{0:T(128)} %bitcast.1.me_ref, s32[1,8]{1,0:T(1,128)} %blocks_ref.3, s32[1,8]{1,0:T(1,128)} %fill_ref.3, ...), custom_call_target="tpu_custom_call", output_to_operand_aliasing={{0}: (13, {}), {1}: (14, {})} | custom-call | flops 8053063680 | bytes 20971520 | tf_op jit(solution)/shard_map/band_forward/pallas_call | solution.py:265
  62.9 12.4 %band_backward.5 = (bf16[512,1024]{1,0:T(8,128)(2,1)}, bf16[512,1024]{1,0:T(8,128)(2,1)}, bf16[512,1024]{1,0:T(8,128)(2,1)}, bf16[1024,896]{1,0:T(8,128)(2,1)}) custom-call(bf16[512,1024]{1,0:T(8,128)(2,1)} %bitcast.87, bf16[5,1152,1024]{2,1,0:T(8,128)(2,1)} %get-tuple-element.42.pt_ref, ...), custom_call_target="tpu_custom_call", output_to_operand_aliasing={{0}: (8, {}), {1}: (9, {}), {2}: (10, {}), {3}: (11, {})} | custom-call | flops 13421772800 | bytes 31457280 | tf_op jit(solution)/shard_map/band_backward/pallas_call | solution.py:359
  75.3 4.6 %band_backward.6 = (bf16[512,1024]{1,0:T(8,128)(2,1)}, bf16[512,1024]{1,0:T(8,128)(2,1)}, bf16[512,1024]{1,0:T(8,128)(2,1)}, bf16[1024,896]{1,0:T(8,128)(2,1)}) custom-call(bf16[512,1024]{1,0:T(8,128)(2,1)} %bitcast.88, bf16[3,1152,1024]{2,1,0:T(8,128)(2,1)} %get-tuple-element.37.pt_ref, ...), custom_call_target="tpu_custom_call", output_to_operand_aliasing={{0}: (8, {}), {1}: (9, {}), {2}: (10, {}), {3}: (11, {})} | custom-call | flops 2684354560 | bytes 6291456 | tf_op jit(solution)/shard_map/band_backward/pallas_call | solution.py:359
  79.9 2.6 %collective-permute-start.10 = (bf16[1024,896]{1,0:T(8,128)(2,1)}, bf16[1024,896]{1,0:T(8,128)(2,1)}, u32[]{:S(2)}, u32[]{:S(2)}) collective-permute-start(bf16[1024,896]{1,0:T(8,128)(2,1)} %get-tuple-element.63), channel_id=1, source_target_pairs={{1,0},{2,1},{3,2},{4,3},{5,4},{6,5},{7,6},{9,8},{10,9},{11,10},{12... | collective-permute-start | bytes 5505032 | tf_op jit(solution)/shard_map/ppermute | solution.py:581
  84.3 3.1 %collective-permute-start.8 = (bf16[160,1024]{1,0:T(8,128)(2,1)S(1)}, bf16[160,1024]{1,0:T(8,128)(2,1)S(1)}, u32[]{:S(2)}, u32[]{:S(2)}) collective-permute-start(bf16[160,1024]{1,0:T(8,128)(2,1)S(1)} %get-tuple-element.69), channel_id=1, source_target_pairs={{0,6},{1,7},{2,4},{3,5},{4,2},{5,3},{6,0},{7,1},{8,14},{9,15},{10,... | collective-permute-start | bytes 983048 | tf_op jit(solution)/shard_map/ppermute | solution.py:494
  88.9 6.6 %collective-permute-done.8 = bf16[160,1024]{1,0:T(8,128)(2,1)S(1)} collective-permute-done((bf16[160,1024]{1,0:T(8,128)(2,1)S(1)}, bf16[160,1024]{1,0:T(8,128)(2,1)S(1)}, u32[]{:S(2)}, u32[]{:S(2)}) %collective-permute-start.8) | collective-permute-done | bytes 327712 | tf_op jit(solution)/shard_map/ppermute | solution.py:494
  95.5 25.0 %collective-permute-done.7 = bf16[160,1024]{1,0:T(8,128)(2,1)S(1)} collective-permute-done((bf16[160,1024]{1,0:T(8,128)(2,1)S(1)}, bf16[160,1024]{1,0:T(8,128)(2,1)S(1)}, u32[]{:S(2)}, u32[]{:S(2)}) %collective-permute-start.7) | collective-permute-done | bytes 327712 | tf_op jit(solution)/shard_map/ppermute | solution.py:494
  120.6 3.4 %collective-permute-start.13 = (bf16[32,1024]{1,0:T(8,128)(2,1)S(1)}, bf16[32,1024]{1,0:T(8,128)(2,1)S(1)}, u32[]{:S(2)}, u32[]{:S(2)}) collective-permute-start(bf16[32,1024]{1,0:T(8,128)(2,1)S(1)} %get-tuple-element.74), channel_id=1, source_target_pairs={{0,24},{8,16},{16,8},{24,0},{1,25},{9,17},{17,9},{25,1},{2,26},{10... | collective-permute-start | bytes 196616 | tf_op jit(solution)/shard_map/ppermute | solution.py:494
  125.7 4.0 %collective-permute-done.12 = bf16[32,1024]{1,0:T(8,128)(2,1)S(1)} collective-permute-done((bf16[32,1024]{1,0:T(8,128)(2,1)S(1)}, bf16[32,1024]{1,0:T(8,128)(2,1)S(1)}, u32[]{:S(2)}, u32[]{:S(2)}) %collective-permute-start.12) | collective-permute-done | bytes 65568 | tf_op jit(solution)/shard_map/ppermute | solution.py:494
  135.4 3.8 %collective-permute-done.15 = bf16[32,1024]{1,0:T(8,128)(2,1)S(1)} collective-permute-done((bf16[32,1024]{1,0:T(8,128)(2,1)S(1)}, bf16[32,1024]{1,0:T(8,128)(2,1)S(1)}, u32[]{:S(2)}, u32[]{:S(2)}) %collective-permute-start.15) | collective-permute-done | bytes 65568 | tf_op jit(solution)/shard_map/ppermute | solution.py:494
  140.0 2.6 %collective-permute-start.19 = (bf16[128,1024]{1,0:T(8,128)(2,1)}, bf16[128,1024]{1,0:T(8,128)(2,1)}, u32[]{:S(2)}, u32[]{:S(2)}) collective-permute-start(bf16[128,1024]{1,0:T(8,128)(2,1)} %pad_maximum_fusion.rest_0_), channel_id=1, source_target_pairs={{0,6},{1,7},{2,4},{3,5},{4,2},{5,3},{6,0},{7,1},{8,14},{9,15},{10,... | collective-permute-start | bytes 786440 | tf_op jit(solution)/shard_map/ppermute | solution.py:494
  142.6 4.5 %band_backward.7 = (bf16[512,1024]{1,0:T(8,128)(2,1)}, bf16[512,1024]{1,0:T(8,128)(2,1)}, bf16[512,1024]{1,0:T(8,128)(2,1)}, bf16[1024,128]{1,0:T(8,128)(2,1)}) custom-call(bf16[512,1024]{1,0:T(8,128)(2,1)} %bitcast.89, bf16[3,1152,1024]{2,1,0:T(8,128)(2,1)} %get-tuple-element.37.pt_ref, ...), custom_call_target="tpu_custom_call", output_to_operand_aliasing={{0}: (8, {}), {1}: (9, {}), {2}: (10, {})} | custom-call | flops 2684354560 | bytes 6291456 | tf_op jit(solution)/shard_map/band_backward/pallas_call | solution.py:359
  147.1 3.8 %collective-permute-start.9 = (bf16[1024,128]{1,0:T(8,128)(2,1)}, bf16[1024,128]{1,0:T(8,128)(2,1)}, u32[]{:S(2)}, u32[]{:S(2)}) collective-permute-start(bf16[1024,128]{1,0:T(8,128)(2,1)} %get-tuple-element.62), channel_id=1, source_target_pairs={{1,0},{2,1},{3,2},{4,3},{5,4},{6,5},{7,6},{9,8},{10,9},{11,10},{12... | collective-permute-start | bytes 786440 | tf_op jit(solution)/shard_map/ppermute | solution.py:581
  152.9 4.6 %collective-permute-start.21 = (bf16[128,1024]{1,0:T(8,128)(2,1)}, bf16[128,1024]{1,0:T(8,128)(2,1)}, u32[]{:S(2)}, u32[]{:S(2)}) collective-permute-start(bf16[128,1024]{1,0:T(8,128)(2,1)} %collective-permute-done.18.rest_1_), channel_id=1, source_target_pairs={{0,1},{1,0},{2,3},{3,2},{4,5},{5,4},{6,7},{7,6},{8,9},{9,8},{10,11... | collective-permute-start | bytes 786440 | tf_op jit(solution)/shard_map/ppermute | solution.py:494
  157.4 3.6 %finish_rows.1 = (bf16[512,1024]{1,0:T(8,128)(2,1)}, bf16[512,1024]{1,0:T(8,128)(2,1)}) custom-call(s32[1]{0:T(128)} %bitcast.1.me_ref, s32[1,128]{1,0:T(1,128)} %slots_ref.9, bf16[512,1024]{1,0:T(8,128)(2,1)} %get-tuple-element.56.dk_in, bf16[512,1024]{1,0:T(8,128)(2,1)} %get-tuple-element.57.dv_in, ...), custom_call_target="tpu_custom_call" | custom-call | flops 67108864 | bytes 6291456 | tf_op jit(solution)/shard_map/finish_rows/pallas_call | solution.py:415
  163.0 2.0 %place_rows.2.rest_6_ = f32[1024,1024]{1,0:T(8,128)} custom-call(s32[1]{0:T(128)} %bitcast.1.me_ref, s32[1]{0:T(128)} %bitcast.14.fam_ref, bf16[128,1024]{1,0:T(8,128)(2,1)} %pad_maximum_fusion.rest_0_, bf16[128,1024]{1,0:T(8,128)(2,1)} %collective-permute-done.23.rest_1_), custom_call_target="tpu_custom_call" | custom-call | flops 1048576 | bytes 3145728 | tf_op jit(solution)/shard_map/place_rows/pallas_call | solution.py:480
  165.1 3.1 %place_rows.3 = f32[1024,1024]{1,0:T(8,128)} custom-call(s32[1]{0:T(128)} %bitcast.1.me_ref, s32[1]{0:T(128)} %bitcast.14.fam_ref, bf16[128,1024]{1,0:T(8,128)(2,1)} %collective-permute-done.17.rest_0_, bf16[128,1024]{1,0:T(8,128)(2,1)} %collective-permute-done.18.rest_1_, ...), custom_call_target="tpu_custom_call", output_to_operand_aliasing={{}: (8, {})} | custom-call | flops 1048576 | bytes 3145728 | tf_op jit(solution)/shard_map/place_rows/pallas_call | solution.py:480
  (45 shorter events, 23.6 us)
Async XLA Ops:
  3.2 3.3 %collective-permute-start.1 = (bf16[16,2048]{1,0:T(8,128)(2,1)}, bf16[16,2048]{1,0:T(8,128)(2,1)S(1)}, u32[]{:S(2)}, u32[]{:S(2)}) collective-permute-start(bf16[16,2048]{1,0:T(8,128)(2,1)} %memory_rows.1), channel_id=1, source_target_pairs={{0,4},{1,5},{2,6},{3,7},{4,0},{5,1},{6,2},{7,3},{8,12},{9,13},{10,... | collective-permute-start | bytes 196616 | tf_op jit(solution)/shard_map/ppermute | solution.py:494
  8.1 11.2 %collective-permute-start.2 = (bf16[32,2048]{1,0:T(8,128)(2,1)}, bf16[32,2048]{1,0:T(8,128)(2,1)}, u32[]{:S(2)}, u32[]{:S(2)}) collective-permute-start(bf16[32,2048]{1,0:T(8,128)(2,1)} %maximum_select_fusion.2), channel_id=1, source_target_pairs={{0,2},{1,3},{2,0},{3,1},{4,6},{5,7},{6,4},{7,5},{8,10},{9,11},{10,... | collective-permute-start | bytes 393224 | tf_op jit(solution)/shard_map/ppermute | solution.py:494
  11.1 15.5 %collective-permute-start = (bf16[512,768]{1,0:T(8,128)(2,1)}, bf16[512,768]{1,0:T(8,128)(2,1)}, u32[]{:S(2)}, u32[]{:S(2)}) collective-permute-start(bf16[512,768]{1,0:T(8,128)(2,1)} %get-tuple-element.36), channel_id=1, source_target_pairs={{0,1},{1,2},{2,3},{3,4},{4,5},{5,6},{6,7},{8,9},{9,10},{10,11},{11... | collective-permute-start | bytes 2359304 | tf_op jit(solution)/shard_map/ppermute | solution.py:556
  17.4 26.8 %collective-permute-start.4 = (bf16[512,1280]{1,0:T(8,128)(2,1)}, bf16[512,1280]{1,0:T(8,128)(2,1)}, u32[]{:S(2)}, u32[]{:S(2)}) collective-permute-start(bf16[512,1280]{1,0:T(8,128)(2,1)} %get-tuple-element.39), channel_id=1, source_target_pairs={{0,1},{1,2},{2,3},{3,4},{4,5},{5,6},{6,7},{8,9},{9,10},{10,11},{11... | collective-permute-start | bytes 3932168 | tf_op jit(solution)/shard_map/ppermute | solution.py:556
  20.5 4.7 %collective-permute-start.3 = (bf16[64,2048]{1,0:T(8,128)(2,1)S(1)}, bf16[64,2048]{1,0:T(8,128)(2,1)S(1)}, u32[]{:S(2)}, u32[]{:S(2)}) collective-permute-start(bf16[64,2048]{1,0:T(8,128)(2,1)S(1)} %maximum_select_fusion.1), channel_id=1, source_target_pairs={{0,1},{1,0},{2,3},{3,2},{4,5},{5,4},{6,7},{7,6},{8,9},{9,8},{10,11... | collective-permute-start | bytes 786440 | tf_op jit(solution)/shard_map/ppermute | solution.py:494
  62.8 19.6 %collective-permute-start.5 = (bf16[4,160,1024]{2,1,0:T(8,128)(2,1)}, bf16[4,160,1024]{2,1,0:T(8,128)(2,1)}, u32[]{:S(2)}, u32[]{:S(2)}) collective-permute-start(bf16[4,160,1024]{2,1,0:T(8,128)(2,1)} %get-tuple-element.58), channel_id=1, source_target_pairs={{0,1},{1,0},{2,3},{3,2},{4,5},{5,4},{6,7},{7,6},{8,9},{9,8},{10,11... | collective-permute-start | bytes 3932168 | tf_op jit(solution)/shard_map/ppermute | solution.py:494
  79.9 71.1 %collective-permute-start.10 = (bf16[1024,896]{1,0:T(8,128)(2,1)}, bf16[1024,896]{1,0:T(8,128)(2,1)}, u32[]{:S(2)}, u32[]{:S(2)}) collective-permute-start(bf16[1024,896]{1,0:T(8,128)(2,1)} %get-tuple-element.63), channel_id=1, source_target_pairs={{1,0},{2,1},{3,2},{4,3},{5,4},{6,5},{7,6},{9,8},{10,9},{11,10},{12... | collective-permute-start | bytes 5505032 | tf_op jit(solution)/shard_map/ppermute | solution.py:581
  84.3 11.1 %collective-permute-start.8 = (bf16[160,1024]{1,0:T(8,128)(2,1)S(1)}, bf16[160,1024]{1,0:T(8,128)(2,1)S(1)}, u32[]{:S(2)}, u32[]{:S(2)}) collective-permute-start(bf16[160,1024]{1,0:T(8,128)(2,1)S(1)} %get-tuple-element.69), channel_id=1, source_target_pairs={{0,6},{1,7},{2,4},{3,5},{4,2},{5,3},{6,0},{7,1},{8,14},{9,15},{10,... | collective-permute-start | bytes 983048 | tf_op jit(solution)/shard_map/ppermute | solution.py:494
  87.4 33.1 %collective-permute-start.7 = (bf16[160,1024]{1,0:T(8,128)(2,1)S(1)}, bf16[160,1024]{1,0:T(8,128)(2,1)S(1)}, u32[]{:S(2)}, u32[]{:S(2)}) collective-permute-start(bf16[160,1024]{1,0:T(8,128)(2,1)S(1)} %get-tuple-element.70), channel_id=1, source_target_pairs={{0,4},{1,5},{2,6},{3,7},{4,0},{5,1},{6,2},{7,3},{8,12},{9,13},{10,... | collective-permute-start | bytes 983048 | tf_op jit(solution)/shard_map/ppermute | solution.py:494
  87.4 33.1 %collective-permute-start.6 = (bf16[160,1024]{1,0:T(8,128)(2,1)S(1)}, bf16[160,1024]{1,0:T(8,128)(2,1)S(1)}, u32[]{:S(2)}, u32[]{:S(2)}) collective-permute-start(bf16[160,1024]{1,0:T(8,128)(2,1)S(1)} %get-tuple-element.68), channel_id=1, source_target_pairs={{0,2},{1,3},{2,0},{3,1},{4,6},{5,7},{6,4},{7,5},{8,10},{9,11},{10,... | collective-permute-start | bytes 983048 | tf_op jit(solution)/shard_map/ppermute | solution.py:494
  120.6 5.1 %collective-permute-start.13 = (bf16[32,1024]{1,0:T(8,128)(2,1)S(1)}, bf16[32,1024]{1,0:T(8,128)(2,1)S(1)}, u32[]{:S(2)}, u32[]{:S(2)}) collective-permute-start(bf16[32,1024]{1,0:T(8,128)(2,1)S(1)} %get-tuple-element.74), channel_id=1, source_target_pairs={{0,24},{8,16},{16,8},{24,0},{1,25},{9,17},{17,9},{25,1},{2,26},{10... | collective-permute-start | bytes 196616 | tf_op jit(solution)/shard_map/ppermute | solution.py:494
  124.0 5.7 %collective-permute-start.12 = (bf16[32,1024]{1,0:T(8,128)(2,1)S(1)}, bf16[32,1024]{1,0:T(8,128)(2,1)S(1)}, u32[]{:S(2)}, u32[]{:S(2)}) collective-permute-start(bf16[32,1024]{1,0:T(8,128)(2,1)S(1)} %get-tuple-element.75), channel_id=1, source_target_pairs={{0,16},{8,24},{16,0},{24,8},{1,17},{9,25},{17,1},{25,9},{2,18},{10... | collective-permute-start | bytes 196616 | tf_op jit(solution)/shard_map/ppermute | solution.py:494
  124.0 5.7 %collective-permute-start.11 = (bf16[32,1024]{1,0:T(8,128)(2,1)S(1)}, bf16[32,1024]{1,0:T(8,128)(2,1)S(1)}, u32[]{:S(2)}, u32[]{:S(2)}) collective-permute-start(bf16[32,1024]{1,0:T(8,128)(2,1)S(1)} %get-tuple-element.73), channel_id=1, source_target_pairs={{0,8},{8,0},{16,24},{24,16},{1,9},{9,1},{17,25},{25,17},{2,10},{10... | collective-permute-start | bytes 196616 | tf_op jit(solution)/shard_map/ppermute | solution.py:494
  130.4 5.0 %collective-permute-start.16 = (bf16[32,1024]{1,0:T(8,128)(2,1)S(1)}, bf16[32,1024]{1,0:T(8,128)(2,1)S(1)}, u32[]{:S(2)}, u32[]{:S(2)}) collective-permute-start(bf16[32,1024]{1,0:T(8,128)(2,1)S(1)} %get-tuple-element.71), channel_id=1, source_target_pairs={{0,24},{8,16},{16,8},{24,0},{1,25},{9,17},{17,9},{25,1},{2,26},{10... | collective-permute-start | bytes 196616 | tf_op jit(solution)/shard_map/ppermute | solution.py:494
  132.2 7.0 %collective-permute-start.15 = (bf16[32,1024]{1,0:T(8,128)(2,1)S(1)}, bf16[32,1024]{1,0:T(8,128)(2,1)S(1)}, u32[]{:S(2)}, u32[]{:S(2)}) collective-permute-start(bf16[32,1024]{1,0:T(8,128)(2,1)S(1)} %get-tuple-element.71), channel_id=1, source_target_pairs={{0,16},{8,24},{16,0},{24,8},{1,17},{9,25},{17,1},{25,9},{2,18},{10... | collective-permute-start | bytes 196616 | tf_op jit(solution)/shard_map/ppermute | solution.py:494
  132.2 7.0 %collective-permute-start.14 = (bf16[32,1024]{1,0:T(8,128)(2,1)S(1)}, bf16[32,1024]{1,0:T(8,128)(2,1)S(1)}, u32[]{:S(2)}, u32[]{:S(2)}) collective-permute-start(bf16[32,1024]{1,0:T(8,128)(2,1)S(1)} %get-tuple-element.71), channel_id=1, source_target_pairs={{0,8},{8,0},{16,24},{24,16},{1,9},{9,1},{17,25},{25,17},{2,10},{10... | collective-permute-start | bytes 196616 | tf_op jit(solution)/shard_map/ppermute | solution.py:494
  140.0 11.1 %collective-permute-start.17 = (bf16[128,1024]{1,0:T(8,128)(2,1)}, bf16[128,1024]{1,0:T(8,128)(2,1)}, u32[]{:S(2)}, u32[]{:S(2)}) collective-permute-start(bf16[128,1024]{1,0:T(8,128)(2,1)} %pad_maximum_fusion.rest_0_), channel_id=1, source_target_pairs={{0,2},{1,3},{2,0},{3,1},{4,6},{5,7},{6,4},{7,5},{8,10},{9,11},{10,... | collective-permute-start | bytes 786440 | tf_op jit(solution)/shard_map/ppermute | solution.py:494
  140.0 12.9 %collective-permute-start.18 = (bf16[128,1024]{1,0:T(8,128)(2,1)}, bf16[128,1024]{1,0:T(8,128)(2,1)}, u32[]{:S(2)}, u32[]{:S(2)}) collective-permute-start(bf16[128,1024]{1,0:T(8,128)(2,1)} %pad_maximum_fusion.rest_0_), channel_id=1, source_target_pairs={{0,4},{1,5},{2,6},{3,7},{4,0},{5,1},{6,2},{7,3},{8,12},{9,13},{10,... | collective-permute-start | bytes 786440 | tf_op jit(solution)/shard_map/ppermute | solution.py:494
  140.0 17.5 %collective-permute-start.19 = (bf16[128,1024]{1,0:T(8,128)(2,1)}, bf16[128,1024]{1,0:T(8,128)(2,1)}, u32[]{:S(2)}, u32[]{:S(2)}) collective-permute-start(bf16[128,1024]{1,0:T(8,128)(2,1)} %pad_maximum_fusion.rest_0_), channel_id=1, source_target_pairs={{0,6},{1,7},{2,4},{3,5},{4,2},{5,3},{6,0},{7,1},{8,14},{9,15},{10,... | collective-permute-start | bytes 786440 | tf_op jit(solution)/shard_map/ppermute | solution.py:494
  147.1 13.9 %collective-permute-start.9 = (bf16[1024,128]{1,0:T(8,128)(2,1)}, bf16[1024,128]{1,0:T(8,128)(2,1)}, u32[]{:S(2)}, u32[]{:S(2)}) collective-permute-start(bf16[1024,128]{1,0:T(8,128)(2,1)} %get-tuple-element.62), channel_id=1, source_target_pairs={{1,0},{2,1},{3,2},{4,3},{5,4},{6,5},{7,6},{9,8},{10,9},{11,10},{12... | collective-permute-start | bytes 786440 | tf_op jit(solution)/shard_map/ppermute | solution.py:581
  150.9 12.1 %collective-permute-start.23 = (bf16[128,1024]{1,0:T(8,128)(2,1)}, bf16[128,1024]{1,0:T(8,128)(2,1)}, u32[]{:S(2)}, u32[]{:S(2)}) collective-permute-start(bf16[128,1024]{1,0:T(8,128)(2,1)} %pad_maximum_fusion.rest_0_), channel_id=1, source_target_pairs={{0,1},{1,0},{2,3},{3,2},{4,5},{5,4},{6,7},{7,6},{8,9},{9,8},{10,11... | collective-permute-start | bytes 786440 | tf_op jit(solution)/shard_map/ppermute | solution.py:494
  151.0 14.1 %collective-permute-start.20 = (bf16[128,1024]{1,0:T(8,128)(2,1)}, bf16[128,1024]{1,0:T(8,128)(2,1)}, u32[]{:S(2)}, u32[]{:S(2)}) collective-permute-start(bf16[128,1024]{1,0:T(8,128)(2,1)} %collective-permute-done.17.rest_0_), channel_id=1, source_target_pairs={{0,1},{1,0},{2,3},{3,2},{4,5},{5,4},{6,7},{7,6},{8,9},{9,8},{10,11... | collective-permute-start | bytes 786440 | tf_op jit(solution)/shard_map/ppermute | solution.py:494
  152.9 12.2 %collective-permute-start.21 = (bf16[128,1024]{1,0:T(8,128)(2,1)}, bf16[128,1024]{1,0:T(8,128)(2,1)}, u32[]{:S(2)}, u32[]{:S(2)}) collective-permute-start(bf16[128,1024]{1,0:T(8,128)(2,1)} %collective-permute-done.18.rest_1_), channel_id=1, source_target_pairs={{0,1},{1,0},{2,3},{3,2},{4,5},{5,4},{6,7},{7,6},{8,9},{9,8},{10,11... | collective-permute-start | bytes 786440 | tf_op jit(solution)/shard_map/ppermute | solution.py:494
  157.4 7.7 %collective-permute-start.22 = (bf16[128,1024]{1,0:T(8,128)(2,1)}, bf16[128,1024]{1,0:T(8,128)(2,1)}, u32[]{:S(2)}, u32[]{:S(2)}) collective-permute-start(bf16[128,1024]{1,0:T(8,128)(2,1)} %collective-permute-done.19.rest_2_), channel_id=1, source_target_pairs={{0,1},{1,0},{2,3},{3,2},{4,5},{5,4},{6,7},{7,6},{8,9},{9,8},{10,11... | collective-permute-start | bytes 786440 | tf_op jit(solution)/shard_map/ppermute | solution.py:494

commit v10 on v9

--- a/solution.py
+++ b/solution.py
@@ -425,35 +425,6 @@
     )(me, slots, dko, dvo, dmem, *backs)
 
 
-def finish_rest_kernel(me_ref, slots_ref, dk_in, dv_in, mk_ref, mv_ref, back_ref, dk_old, dv_old, dk_ref, dv_ref):
-    pick = picks(me_ref[0], slots_ref, 0, dk_in.shape[0], mk_ref.shape[0])
-    dk = dk_in[...].astype(f32) + dot(pick, mk_ref[...], NN)
-    dv = dv_in[...].astype(f32) + dot(pick, mv_ref[...], NN)
-    dk_ref[...] = (dk + back_ref[0].astype(f32)).astype(bf16)
-    dv_ref[...] = (dv + back_ref[1].astype(f32)).astype(bf16)
-
-
-def finish_rest(me, slots, dko, dvo, dmem, back, pair, count, carry):
-    tokens, width = dko.shape
-    mine = dmem.shape[0] // 2
-    smem = pl.BlockSpec(memory_space=pltpu.SMEM)
-    col = lambda rows, j: pl.BlockSpec((rows, SPAN), lambda p: (j, p + pair))
-    return pl.pallas_call(
-        finish_rest_kernel,
-        grid=(count,),
-        in_specs=[
-            smem, smem, col(tokens, 0), col(tokens, 0), col(mine, 0), col(mine, 1),
-            pl.BlockSpec((2, tokens, SPAN), lambda p: (0, 0, p)), ANY, ANY,
-        ],
-        out_specs=[col(tokens, 0), col(tokens, 0)],
-        out_shape=[jax.ShapeDtypeStruct((tokens, width), bf16)] * 2,
-        input_output_aliases={7: 0, 8: 1},
-        compiler_params=pltpu.CompilerParams(vmem_limit_bytes=67_000_000),
-        cost_estimate=pl.CostEstimate(flops=1 << 24, bytes_accessed=2 << 20, transcendentals=0),
-        name="finish_rest",
-    )(me, slots, dko, dvo, dmem, dmem, back, *carry)
-
-
 def place_kernel(me_ref, fam_ref, *rest, spots, plane, nfam, scale):
     n = len(spots)
     parts, (out_ref, buf, sems) = rest[:n], rest[-3:]
@@ -533,7 +504,7 @@
     if pairs % 8:
         return [pairs], [(0, 0, pairs)], [pairs]
     u = pairs // 8
-    return [3 * u, 5 * u], [(0, 0, u), (1, 0, 5 * u), (0, u, u), (0, 2 * u, u)], [7 * u, u]
+    return [3 * u, 5 * u], [(0, 0, u), (1, 0, 5 * u), (0, u, 2 * u)], [6 * u, 2 * u]
 
 
 def per_device(queries, key_rows, value_rows, cotangent, out_weight, prot_blocks, last_fill, memory_slots):
@@ -581,7 +552,6 @@
         backs.append(lax.ppermute(carry.pop(), "ctx", back))
     both = lambda j, x, y: at(x, j, 0).astype(f32) + at(y, j, 0).astype(f32)
     got = exchange(lambda j: both(j, sent, kept), "ctx", 1, spot, plane)
-    got[0] = both(spot, *lax.optimization_barrier((sent, kept)))
     rows = width // nctx
     mem_grad = total_of([x[rows:] for x in got]).astype(bf16)
     piece = lambda j: total_of([lax.dynamic_slice_in_dim(x, j * (rows // nfam), rows // nfam) for x in got])
@@ -596,11 +566,7 @@
     weight = place(where, who, parts[1:] + others[1:], spots, plane, nfam, scale, weight)
     dq, dko, dvo = carry
     backs = [x.reshape(2, W, -1) for x in backs]
-    grads = finish(where, memory_slots, dko, dvo, mem_grad, backs[:1], [x for x in segments if x[0] == 0])
-    for i, x in enumerate(backs[1:], 1):
-        _, pair, _, count = [x for x in segments if x[0] == i][0]
-        grads = finish_rest(where, memory_slots, dko, dvo, mem_grad, x, pair, count, grads)
-    dk, dv = grads
+    dk, dv = finish(where, memory_slots, dko, dvo, mem_grad, backs, segments)
     return dq[None], dk[None], dv[None], weight
 
 

time: 169 us -> 154 us (0.911)
  waiting for transfers between devices: 46.1 us -> 25.8 us
  starting transfers between devices: 35 us -> 40.2 us
  Pallas kernels: 73.9 us -> 69.2 us
  other arithmetic: 8.18 us -> 11.4 us
    ppermute x20, waiting for transfers between devices: 45.6 us -> 11.3 us  [swap(): lax.ppermute(x, axis, [(i, i ^ bits) for i in range(lax.axis_size(axis))])]
    ppermute x2, waiting for transfers between devices: 0.49 us -> 14.5 us  [per_device(): halos = [lax.ppermute(x, 'ctx', shift) for x in halos]]
    ppermute x20, starting transfers between devices: 20.4 us -> 25.9 us  [swap(): lax.ppermute(x, axis, [(i, i ^ bits) for i in range(lax.axis_size(axis))])]
    convert_element_type x2, other arithmetic: 1.94 us -> 5.12 us  [exchange(): part(me ^ k).astype(bf16)]
    pallas_call x4 -> x3, Pallas kernels: 26 us -> 23.3 us  [backward(): pl.pallas_call(functools.partial(backward_kernel, nb=nb), grid=(count,),...]
    pallas_call x1 -> x0, Pallas kernels: 2.03 us -> none  [finish_rest(): pl.pallas_call(finish_rest_kernel, grid=(count,), in_specs=[smem, smem, c...]
  transfers between devices with their start and end apart: 24 -> 24, of which waited for: 9 -> 7; matrix products, arithmetic and copies ran while one was open for 6% -> 7% of each run, Pallas kernels for 29% -> 30%
where the time goes in v10:
time: 154 us; the launch traced here: 152 us
  Pallas kernels  69.2 us (45%)
  starting transfers between devices  40.2 us (26%)
  waiting for transfers between devices  25.8 us (17%)
  other arithmetic  11.4 us (7%)
  matrix products  4.18 us (3%)
    pallas_call x2, Pallas kernels, forward(): pl.pallas_call(functools.partial(forward_kernel, nb=nb, order=order, star...  31.6 us
    ppermute x20, starting transfers between devices, swap(): lax.ppermute(x, axis, [(i, i ^ bits) for i in range(lax.axis_size(axis))])  25.9 us
    pallas_call x3, Pallas kernels, backward(): pl.pallas_call(functools.partial(backward_kernel, nb=nb), grid=(count,),...  23.3 us
    ppermute x2, waiting for transfers between devices, per_device(): halos = [lax.ppermute(x, 'ctx', shift) for x in halos]  14.5 us
    ppermute x20, waiting for transfers between devices, swap(): lax.ppermute(x, axis, [(i, i ^ bits) for i in range(lax.axis_size(axis))])  11.3 us
    ppermute x2, starting transfers between devices, per_device(): halos = [lax.ppermute(x, 'ctx', shift) for x in halos]  8.2 us
    ppermute x2, starting transfers between devices, per_device(): backs.append(lax.ppermute(carry.pop(), 'ctx', back))  6.18 us
    pallas_call x2, Pallas kernels, place(): pl.pallas_call(functools.partial(place_kernel, spots=spots, plane=plane,...  5.14 us
  transfers between devices with their start and end apart: 24, of which 7 were waited for; matrix products, arithmetic and copies ran while one was open for 7% of the time, Pallas kernels for 30%

profile of v10, /device:TPU:3, one launch (start us, length us, event | category | flops | bytes accessed | tf_op | source)
XLA Modules:
  0.0 151.9 jit_solution(1801425784898438657)
XLA Ops:
  0.6 2.6 %memory_rows.1 = bf16[16,2048]{1,0:T(8,128)(2,1)} custom-call(s32[1]{0:T(128)} %bitcast.1.me_ref, s32[1,128]{1,0:T(1,128)} %slots_ref.7, bf16[512,1024]{1,0:T(8,128)(2,1)} %bitcast.68, bf16[512,1024]{1,0:T(8,128)(2,1)} %bitcast.75), custom_call_target="tpu_custom_call" | custom-call | tf_op jit(solution)/shard_map/memory_rows/pallas_call | solution.py:310
  4.4 2.1 %collective-permute-done.1 = bf16[16,2048]{1,0:T(8,128)(2,1)S(1)} collective-permute-done((bf16[16,2048]{1,0:T(8,128)(2,1)}, bf16[16,2048]{1,0:T(8,128)(2,1)S(1)}, u32[]{:S(2)}, u32[]{:S(2)}) %collective-permute-start.1) | collective-permute-done | bytes 65568 | tf_op jit(solution)/shard_map/ppermute | solution.py:465
  8.2 2.9 %halo_groups.1 = (bf16[512,768]{1,0:T(8,128)(2,1)}, bf16[512,1280]{1,0:T(8,128)(2,1)}) custom-call(bf16[512,1024]{1,0:T(8,128)(2,1)} %bitcast.69, bf16[512,1024]{1,0:T(8,128)(2,1)} %bitcast.76), custom_call_target="tpu_custom_call" | custom-call | bytes 4194304 | tf_op jit(solution)/shard_map/halo_groups/pallas_call | solution.py:330
  11.1 6.3 %collective-permute-start.4 = (bf16[512,1280]{1,0:T(8,128)(2,1)}, bf16[512,1280]{1,0:T(8,128)(2,1)}, u32[]{:S(2)}, u32[]{:S(2)}) collective-permute-start(bf16[512,1280]{1,0:T(8,128)(2,1)} %get-tuple-element.31), channel_id=1, source_target_pairs={{0,1},{1,2},{2,3},{3,4},{4,5},{5,6},{6,7},{8,9},{9,10},{10,11},{11... | collective-permute-start | bytes 3932168 | tf_op jit(solution)/shard_map/ppermute | solution.py:527
  21.1 4.2 %convolution_convert_fusion.g_ref = bf16[512,1024]{1,0:T(8,128)(2,1)} fusion(bf16[1024,1024]{1,0:T(8,128)(2,1)} %param.12, bf16[1,512,1024]{2,1,0:T(8,128)(2,1)} %param.11), kind=kOutput, calls=%fused_computation | convolution fusion | flops 1074266112 | bytes 4194304 | tf_op jit(solution)/shard_map/dot_general | solution.py:26
  26.2 14.5 %collective-permute-done.kh_ref.vh_ref = bf16[512,768]{1,0:T(8,128)(2,1)} collective-permute-done((bf16[512,768]{1,0:T(8,128)(2,1)}, bf16[512,768]{1,0:T(8,128)(2,1)}, u32[]{:S(2)}, u32[]{:S(2)}) %collective-permute-start) | collective-permute-done | bytes 786464 | tf_op jit(solution)/shard_map/ppermute | solution.py:527
  40.6 12.9 %band_forward.2 = (bf16[4,160,1024]{2,1,0:T(8,128)(2,1)}, bf16[4,160,1024]{2,1,0:T(8,128)(2,1)}, bf16[3,1152,1024]{2,1,0:T(8,128)(2,1)}, bf16[3,1024,256]{2,1,0:T(8,128)(2,1)}) custom-call(s32[1]{0:T(128)} %bitcast.1.me_ref, s32[1,8]{1,0:T(1,128)} %blocks_ref.3, s32[1,8]{1,0:T(1,128)} %fill_ref.3, bf16[512,1024]{1,0:T(8,128)(2,1)} %bitcast.82, ...), custom_call_target="tpu_custom_call" | custom-call | flops 4831838208 | bytes 12582912 | tf_op jit(solution)/shard_map/band_forward/pallas_call | solution.py:265
  53.5 18.7 %band_forward.3 = (bf16[4,160,1024]{2,1,0:T(8,128)(2,1)}, bf16[4,160,1024]{2,1,0:T(8,128)(2,1)}, bf16[5,1152,1024]{2,1,0:T(8,128)(2,1)}, bf16[5,1024,256]{2,1,0:T(8,128)(2,1)}) custom-call(s32[1]{0:T(128)} %bitcast.1.me_ref, s32[1,8]{1,0:T(1,128)} %blocks_ref.3, s32[1,8]{1,0:T(1,128)} %fill_ref.3, ...), custom_call_target="tpu_custom_call", output_to_operand_aliasing={{0}: (13, {}), {1}: (14, {})} | custom-call | flops 8053063680 | bytes 20971520 | tf_op jit(solution)/shard_map/band_forward/pallas_call | solution.py:265
  72.3 4.5 %band_backward.3 = (bf16[512,1024]{1,0:T(8,128)(2,1)}, bf16[512,1024]{1,0:T(8,128)(2,1)}, bf16[512,1024]{1,0:T(8,128)(2,1)}, bf16[1024,768]{1,0:T(8,128)(2,1)}) custom-call(bf16[512,1024]{1,0:T(8,128)(2,1)} %bitcast.84, bf16[3,1152,1024]{2,1,0:T(8,128)(2,1)} %get-tuple-element.29.pt_ref, bf16[3,1024,256]{2,1,0:T(8,128)(2,1)} %get-tuple-element.30.ga_ref, ...), custom_call_target="tpu_custom_call" | custom-call | flops 2684354560 | bytes 6291456 | tf_op jit(solution)/shard_map/band_backward/pallas_call | solution.py:359
  76.9 3.2 %fusion = (bf16[160,1024]{1,0:T(8,128)(2,1)}, bf16[160,1024]{1,0:T(8,128)(2,1)}, bf16[160,1024]{1,0:T(8,128)(2,1)}, f32[1,160,1024]{2,1,0:T(8,128)}) fusion(bf16[4,160,1024]{2,1,0:T(8,128)(2,1)} %get-tuple-element.47, s32[]{:T(128)S(6)} %select_n.72, bf16[4,160,1024]{2,1,0:T(8,128)(2,1)} %collective-permute-done.5, s32[]{:T(128)S(6)} %select_n.74, ...), kind=kLoop, calls=%fused_computation.6 | loop fusion | flops 2457600 | bytes 4259856 | tf_op jit(solution)/shard_map/convert_element_type | solution.py:492
  80.0 3.4 %collective-permute-start.8 = (bf16[160,1024]{1,0:T(8,128)(2,1)}, bf16[160,1024]{1,0:T(8,128)(2,1)}, u32[]{:S(2)}, u32[]{:S(2)}) collective-permute-start(bf16[160,1024]{1,0:T(8,128)(2,1)} %get-tuple-element.53), channel_id=1, source_target_pairs={{0,6},{1,7},{2,4},{3,5},{4,2},{5,3},{6,0},{7,1},{8,14},{9,15},{10,... | collective-permute-start | bytes 983048 | tf_op jit(solution)/shard_map/ppermute | solution.py:465
  83.8 12.4 %band_backward.4 = (bf16[512,1024]{1,0:T(8,128)(2,1)}, bf16[512,1024]{1,0:T(8,128)(2,1)}, bf16[512,1024]{1,0:T(8,128)(2,1)}, bf16[1024,768]{1,0:T(8,128)(2,1)}) custom-call(bf16[512,1024]{1,0:T(8,128)(2,1)} %bitcast.85, bf16[5,1152,1024]{2,1,0:T(8,128)(2,1)} %get-tuple-element.34.pt_ref, ...), custom_call_target="tpu_custom_call", output_to_operand_aliasing={{0}: (8, {}), {1}: (9, {}), {2}: (10, {}), {3}: (11, {})} | custom-call | flops 13421772800 | bytes 31457280 | tf_op jit(solution)/shard_map/band_backward/pallas_call | solution.py:359
  96.1 2.7 %collective-permute-start.9 = (bf16[1024,768]{1,0:T(8,128)(2,1)}, bf16[1024,768]{1,0:T(8,128)(2,1)}, u32[]{:S(2)}, u32[]{:S(2)}) collective-permute-start(bf16[1024,768]{1,0:T(8,128)(2,1)} %get-tuple-element.48), channel_id=1, source_target_pairs={{1,0},{2,1},{3,2},{4,3},{5,4},{6,5},{7,6},{9,8},{10,9},{11,10},{12... | collective-permute-start | bytes 4718600 | tf_op jit(solution)/shard_map/ppermute | solution.py:552
  101.0 3.3 %collective-permute-start.13 = (bf16[32,1024]{1,0:T(8,128)(2,1)}, bf16[32,1024]{1,0:T(8,128)(2,1)}, u32[]{:S(2)}, u32[]{:S(2)}) collective-permute-start(bf16[32,1024]{1,0:T(8,128)(2,1)} %get-tuple-element.59), channel_id=1, source_target_pairs={{0,24},{8,16},{16,8},{24,0},{1,25},{9,17},{17,9},{25,1},{2,26},{10... | collective-permute-start | bytes 196616 | tf_op jit(solution)/shard_map/ppermute | solution.py:465
  104.6 6.4 %band_backward.5 = (bf16[512,1024]{1,0:T(8,128)(2,1)}, bf16[512,1024]{1,0:T(8,128)(2,1)}, bf16[512,1024]{1,0:T(8,128)(2,1)}, bf16[1024,256]{1,0:T(8,128)(2,1)}) custom-call(bf16[512,1024]{1,0:T(8,128)(2,1)} %bitcast.86, bf16[3,1152,1024]{2,1,0:T(8,128)(2,1)} %get-tuple-element.29.pt_ref, ...), custom_call_target="tpu_custom_call", output_to_operand_aliasing={{0}: (8, {}), {1}: (9, {}), {2}: (10, {})} | custom-call | flops 5368709120 | bytes 12582912 | tf_op jit(solution)/shard_map/band_backward/pallas_call | solution.py:359
  111.1 3.5 %collective-permute-start.10 = (bf16[1024,256]{1,0:T(8,128)(2,1)}, bf16[1024,256]{1,0:T(8,128)(2,1)}, u32[]{:S(2)}, u32[]{:S(2)}) collective-permute-start(bf16[1024,256]{1,0:T(8,128)(2,1)} %get-tuple-element.49), channel_id=1, source_target_pairs={{1,0},{2,1},{3,2},{4,3},{5,4},{6,5},{7,6},{9,8},{10,9},{11,10},{12... | collective-permute-start | bytes 1572872 | tf_op jit(solution)/shard_map/ppermute | solution.py:552
  116.5 3.3 %collective-permute-start.16 = (bf16[32,1024]{1,0:T(8,128)(2,1)S(1)}, bf16[32,1024]{1,0:T(8,128)(2,1)S(1)}, u32[]{:S(2)}, u32[]{:S(2)}) collective-permute-start(bf16[32,1024]{1,0:T(8,128)(2,1)S(1)} %get-tuple-element.56), channel_id=1, source_target_pairs={{0,24},{8,16},{16,8},{24,0},{1,25},{9,17},{17,9},{25,1},{2,26},{10... | collective-permute-start | bytes 196616 | tf_op jit(solution)/shard_map/ppermute | solution.py:465
  122.1 3.3 %collective-permute-done.15 = bf16[32,1024]{1,0:T(8,128)(2,1)S(1)} collective-permute-done((bf16[32,1024]{1,0:T(8,128)(2,1)S(1)}, bf16[32,1024]{1,0:T(8,128)(2,1)S(1)}, u32[]{:S(2)}, u32[]{:S(2)}) %collective-permute-start.15) | collective-permute-done | bytes 65568 | tf_op jit(solution)/shard_map/ppermute | solution.py:465
  130.6 3.1 %collective-permute-done.17.rest_0_ = bf16[128,1024]{1,0:T(8,128)(2,1)} collective-permute-done((bf16[128,1024]{1,0:T(8,128)(2,1)}, bf16[128,1024]{1,0:T(8,128)(2,1)}, u32[]{:S(2)}, u32[]{:S(2)}) %collective-permute-start.17) | collective-permute-done | bytes 262176 | tf_op jit(solution)/shard_map/ppermute | solution.py:465
  133.7 2.5 %collective-permute-start.20 = (bf16[128,1024]{1,0:T(8,128)(2,1)}, bf16[128,1024]{1,0:T(8,128)(2,1)}, u32[]{:S(2)}, u32[]{:S(2)}) collective-permute-start(bf16[128,1024]{1,0:T(8,128)(2,1)} %collective-permute-done.17.rest_0_), channel_id=1, source_target_pairs={{0,1},{1,0},{2,3},{3,2},{4,5},{5,4},{6,7},{7,6},{8,9},{9,8},{10,11... | collective-permute-start | bytes 786440 | tf_op jit(solution)/shard_map/ppermute | solution.py:465
  136.2 4.7 %collective-permute-start.21 = (bf16[128,1024]{1,0:T(8,128)(2,1)}, bf16[128,1024]{1,0:T(8,128)(2,1)}, u32[]{:S(2)}, u32[]{:S(2)}) collective-permute-start(bf16[128,1024]{1,0:T(8,128)(2,1)} %collective-permute-done.18.rest_1_), channel_id=1, source_target_pairs={{0,1},{1,0},{2,3},{3,2},{4,5},{5,4},{6,7},{7,6},{8,9},{9,8},{10,11... | collective-permute-start | bytes 786440 | tf_op jit(solution)/shard_map/ppermute | solution.py:465
  142.8 3.7 %finish_rows.1 = (bf16[512,1024]{1,0:T(8,128)(2,1)}, bf16[512,1024]{1,0:T(8,128)(2,1)}) custom-call(s32[1]{0:T(128)} %bitcast.1.me_ref, s32[1,128]{1,0:T(1,128)} %slots_ref.7, bf16[512,1024]{1,0:T(8,128)(2,1)} %get-tuple-element.44.dk_in, bf16[512,1024]{1,0:T(8,128)(2,1)} %get-tuple-element.45.dv_in, bf16[32,1024]{1,0:T(8,128)(2,1)} %get-tuple-element.57.dm_ref, ...), custom_call_target="tpu_custom_call" | custom-call | flops 67108864 | bytes 6291456 | tf_op jit(solution)/shard_map/finish_rows/pallas_call | solution.py:415
  146.5 2.0 %place_rows.2.rest_6_ = f32[1024,1024]{1,0:T(8,128)} custom-call(s32[1]{0:T(128)} %bitcast.1.me_ref, s32[1]{0:T(128)} %bitcast.14.fam_ref, bf16[128,1024]{1,0:T(8,128)(2,1)} %pad_maximum_fusion.rest_0_, bf16[128,1024]{1,0:T(8,128)(2,1)} %collective-permute-done.23.rest_1_), custom_call_target="tpu_custom_call" | custom-call | flops 1048576 | bytes 3145728 | tf_op jit(solution)/shard_map/place_rows/pallas_call | solution.py:451
  148.6 3.1 %place_rows.3 = f32[1024,1024]{1,0:T(8,128)} custom-call(s32[1]{0:T(128)} %bitcast.1.me_ref, s32[1]{0:T(128)} %bitcast.14.fam_ref, bf16[128,1024]{1,0:T(8,128)(2,1)} %collective-permute-done.17.rest_0_, bf16[128,1024]{1,0:T(8,128)(2,1)} %collective-permute-done.18.rest_1_, ...), custom_call_target="tpu_custom_call", output_to_operand_aliasing={{}: (8, {})} | custom-call | flops 1048576 | bytes 3145728 | tf_op jit(solution)/shard_map/place_rows/pallas_call | solution.py:451
  (42 shorter events, 21.6 us)
Async XLA Ops:
  3.2 3.3 %collective-permute-start.1 = (bf16[16,2048]{1,0:T(8,128)(2,1)}, bf16[16,2048]{1,0:T(8,128)(2,1)S(1)}, u32[]{:S(2)}, u32[]{:S(2)}) collective-permute-start(bf16[16,2048]{1,0:T(8,128)(2,1)} %memory_rows.1), channel_id=1, source_target_pairs={{0,4},{1,5},{2,6},{3,7},{4,0},{5,1},{6,2},{7,3},{8,12},{9,13},{10,... | collective-permute-start | bytes 196616 | tf_op jit(solution)/shard_map/ppermute | solution.py:465
  8.1 11.2 %collective-permute-start.2 = (bf16[32,2048]{1,0:T(8,128)(2,1)}, bf16[32,2048]{1,0:T(8,128)(2,1)}, u32[]{:S(2)}, u32[]{:S(2)}) collective-permute-start(bf16[32,2048]{1,0:T(8,128)(2,1)} %maximum_select_fusion.2), channel_id=1, source_target_pairs={{0,2},{1,3},{2,0},{3,1},{4,6},{5,7},{6,4},{7,5},{8,10},{9,11},{10,... | collective-permute-start | bytes 393224 | tf_op jit(solution)/shard_map/ppermute | solution.py:465
  11.1 42.4 %collective-permute-start.4 = (bf16[512,1280]{1,0:T(8,128)(2,1)}, bf16[512,1280]{1,0:T(8,128)(2,1)}, u32[]{:S(2)}, u32[]{:S(2)}) collective-permute-start(bf16[512,1280]{1,0:T(8,128)(2,1)} %get-tuple-element.31), channel_id=1, source_target_pairs={{0,1},{1,2},{2,3},{3,4},{4,5},{5,6},{6,7},{8,9},{9,10},{10,11},{11... | collective-permute-start | bytes 3932168 | tf_op jit(solution)/shard_map/ppermute | solution.py:527
  17.4 23.3 %collective-permute-start = (bf16[512,768]{1,0:T(8,128)(2,1)}, bf16[512,768]{1,0:T(8,128)(2,1)}, u32[]{:S(2)}, u32[]{:S(2)}) collective-permute-start(bf16[512,768]{1,0:T(8,128)(2,1)} %get-tuple-element.28), channel_id=1, source_target_pairs={{0,1},{1,2},{2,3},{3,4},{4,5},{5,6},{6,7},{8,9},{9,10},{10,11},{11... | collective-permute-start | bytes 2359304 | tf_op jit(solution)/shard_map/ppermute | solution.py:527
  20.5 4.7 %collective-permute-start.3 = (bf16[64,2048]{1,0:T(8,128)(2,1)S(1)}, bf16[64,2048]{1,0:T(8,128)(2,1)S(1)}, u32[]{:S(2)}, u32[]{:S(2)}) collective-permute-start(bf16[64,2048]{1,0:T(8,128)(2,1)S(1)} %maximum_select_fusion.1), channel_id=1, source_target_pairs={{0,1},{1,0},{2,3},{3,2},{4,5},{5,4},{6,7},{7,6},{8,9},{9,8},{10,11... | collective-permute-start | bytes 786440 | tf_op jit(solution)/shard_map/ppermute | solution.py:465
  72.2 4.6 %collective-permute-start.5 = (bf16[4,160,1024]{2,1,0:T(8,128)(2,1)}, bf16[4,160,1024]{2,1,0:T(8,128)(2,1)}, u32[]{:S(2)}, u32[]{:S(2)}) collective-permute-start(bf16[4,160,1024]{2,1,0:T(8,128)(2,1)} %get-tuple-element.46), channel_id=1, source_target_pairs={{0,1},{1,0},{2,3},{3,2},{4,5},{5,4},{6,7},{7,6},{8,9},{9,8},{10,11... | collective-permute-start | bytes 3932168 | tf_op jit(solution)/shard_map/ppermute | solution.py:465
  80.0 18.8 %collective-permute-start.8 = (bf16[160,1024]{1,0:T(8,128)(2,1)}, bf16[160,1024]{1,0:T(8,128)(2,1)}, u32[]{:S(2)}, u32[]{:S(2)}) collective-permute-start(bf16[160,1024]{1,0:T(8,128)(2,1)} %get-tuple-element.53), channel_id=1, source_target_pairs={{0,6},{1,7},{2,4},{3,5},{4,2},{5,3},{6,0},{7,1},{8,14},{9,15},{10,... | collective-permute-start | bytes 983048 | tf_op jit(solution)/shard_map/ppermute | solution.py:465
  83.5 15.5 %collective-permute-start.7 = (bf16[160,1024]{1,0:T(8,128)(2,1)}, bf16[160,1024]{1,0:T(8,128)(2,1)}, u32[]{:S(2)}, u32[]{:S(2)}) collective-permute-start(bf16[160,1024]{1,0:T(8,128)(2,1)} %get-tuple-element.54), channel_id=1, source_target_pairs={{0,4},{1,5},{2,6},{3,7},{4,0},{5,1},{6,2},{7,3},{8,12},{9,13},{10,... | collective-permute-start | bytes 983048 | tf_op jit(solution)/shard_map/ppermute | solution.py:465
  83.5 15.5 %collective-permute-start.6 = (bf16[160,1024]{1,0:T(8,128)(2,1)}, bf16[160,1024]{1,0:T(8,128)(2,1)}, u32[]{:S(2)}, u32[]{:S(2)}) collective-permute-start(bf16[160,1024]{1,0:T(8,128)(2,1)} %get-tuple-element.52), channel_id=1, source_target_pairs={{0,2},{1,3},{2,0},{3,1},{4,6},{5,7},{6,4},{7,5},{8,10},{9,11},{10,... | collective-permute-start | bytes 983048 | tf_op jit(solution)/shard_map/ppermute | solution.py:465
  96.1 46.7 %collective-permute-start.9 = (bf16[1024,768]{1,0:T(8,128)(2,1)}, bf16[1024,768]{1,0:T(8,128)(2,1)}, u32[]{:S(2)}, u32[]{:S(2)}) collective-permute-start(bf16[1024,768]{1,0:T(8,128)(2,1)} %get-tuple-element.48), channel_id=1, source_target_pairs={{1,0},{2,1},{3,2},{4,3},{5,4},{6,5},{7,6},{9,8},{10,9},{11,10},{12... | collective-permute-start | bytes 4718600 | tf_op jit(solution)/shard_map/ppermute | solution.py:552
  101.0 13.6 %collective-permute-start.13 = (bf16[32,1024]{1,0:T(8,128)(2,1)}, bf16[32,1024]{1,0:T(8,128)(2,1)}, u32[]{:S(2)}, u32[]{:S(2)}) collective-permute-start(bf16[32,1024]{1,0:T(8,128)(2,1)} %get-tuple-element.59), channel_id=1, source_target_pairs={{0,24},{8,16},{16,8},{24,0},{1,25},{9,17},{17,9},{25,1},{2,26},{10... | collective-permute-start | bytes 196616 | tf_op jit(solution)/shard_map/ppermute | solution.py:465
  104.3 10.3 %collective-permute-start.12 = (bf16[32,1024]{1,0:T(8,128)(2,1)}, bf16[32,1024]{1,0:T(8,128)(2,1)}, u32[]{:S(2)}, u32[]{:S(2)}) collective-permute-start(bf16[32,1024]{1,0:T(8,128)(2,1)} %get-tuple-element.60), channel_id=1, source_target_pairs={{0,16},{8,24},{16,0},{24,8},{1,17},{9,25},{17,1},{25,9},{2,18},{10... | collective-permute-start | bytes 196616 | tf_op jit(solution)/shard_map/ppermute | solution.py:465
  104.3 10.3 %collective-permute-start.11 = (bf16[32,1024]{1,0:T(8,128)(2,1)}, bf16[32,1024]{1,0:T(8,128)(2,1)}, u32[]{:S(2)}, u32[]{:S(2)}) collective-permute-start(bf16[32,1024]{1,0:T(8,128)(2,1)} %get-tuple-element.58), channel_id=1, source_target_pairs={{0,8},{8,0},{16,24},{24,16},{1,9},{9,1},{17,25},{25,17},{2,10},{10... | collective-permute-start | bytes 196616 | tf_op jit(solution)/shard_map/ppermute | solution.py:465
  111.1 18.6 %collective-permute-start.10 = (bf16[1024,256]{1,0:T(8,128)(2,1)}, bf16[1024,256]{1,0:T(8,128)(2,1)}, u32[]{:S(2)}, u32[]{:S(2)}) collective-permute-start(bf16[1024,256]{1,0:T(8,128)(2,1)} %get-tuple-element.49), channel_id=1, source_target_pairs={{1,0},{2,1},{3,2},{4,3},{5,4},{6,5},{7,6},{9,8},{10,9},{11,10},{12... | collective-permute-start | bytes 1572872 | tf_op jit(solution)/shard_map/ppermute | solution.py:552
  116.5 5.6 %collective-permute-start.16 = (bf16[32,1024]{1,0:T(8,128)(2,1)S(1)}, bf16[32,1024]{1,0:T(8,128)(2,1)S(1)}, u32[]{:S(2)}, u32[]{:S(2)}) collective-permute-start(bf16[32,1024]{1,0:T(8,128)(2,1)S(1)} %get-tuple-element.56), channel_id=1, source_target_pairs={{0,24},{8,16},{16,8},{24,0},{1,25},{9,17},{17,9},{25,1},{2,26},{10... | collective-permute-start | bytes 196616 | tf_op jit(solution)/shard_map/ppermute | solution.py:465
  119.8 5.6 %collective-permute-start.15 = (bf16[32,1024]{1,0:T(8,128)(2,1)S(1)}, bf16[32,1024]{1,0:T(8,128)(2,1)S(1)}, u32[]{:S(2)}, u32[]{:S(2)}) collective-permute-start(bf16[32,1024]{1,0:T(8,128)(2,1)S(1)} %get-tuple-element.56), channel_id=1, source_target_pairs={{0,16},{8,24},{16,0},{24,8},{1,17},{9,25},{17,1},{25,9},{2,18},{10... | collective-permute-start | bytes 196616 | tf_op jit(solution)/shard_map/ppermute | solution.py:465
  119.8 5.6 %collective-permute-start.14 = (bf16[32,1024]{1,0:T(8,128)(2,1)S(1)}, bf16[32,1024]{1,0:T(8,128)(2,1)S(1)}, u32[]{:S(2)}, u32[]{:S(2)}) collective-permute-start(bf16[32,1024]{1,0:T(8,128)(2,1)S(1)} %get-tuple-element.56), channel_id=1, source_target_pairs={{0,8},{8,0},{16,24},{24,16},{1,9},{9,1},{17,25},{25,17},{2,10},{10... | collective-permute-start | bytes 196616 | tf_op jit(solution)/shard_map/ppermute | solution.py:465
  126.1 7.6 %collective-permute-start.17 = (bf16[128,1024]{1,0:T(8,128)(2,1)}, bf16[128,1024]{1,0:T(8,128)(2,1)}, u32[]{:S(2)}, u32[]{:S(2)}) collective-permute-start(bf16[128,1024]{1,0:T(8,128)(2,1)} %pad_maximum_fusion.rest_0_), channel_id=1, source_target_pairs={{0,2},{1,3},{2,0},{3,1},{4,6},{5,7},{6,4},{7,5},{8,10},{9,11},{10,... | collective-permute-start | bytes 786440 | tf_op jit(solution)/shard_map/ppermute | solution.py:465
  127.0 9.2 %collective-permute-start.18 = (bf16[128,1024]{1,0:T(8,128)(2,1)}, bf16[128,1024]{1,0:T(8,128)(2,1)}, u32[]{:S(2)}, u32[]{:S(2)}) collective-permute-start(bf16[128,1024]{1,0:T(8,128)(2,1)} %pad_maximum_fusion.rest_0_), channel_id=1, source_target_pairs={{0,4},{1,5},{2,6},{3,7},{4,0},{5,1},{6,2},{7,3},{8,12},{9,13},{10,... | collective-permute-start | bytes 786440 | tf_op jit(solution)/shard_map/ppermute | solution.py:465
  128.5 13.1 %collective-permute-start.19 = (bf16[128,1024]{1,0:T(8,128)(2,1)}, bf16[128,1024]{1,0:T(8,128)(2,1)}, u32[]{:S(2)}, u32[]{:S(2)}) collective-permute-start(bf16[128,1024]{1,0:T(8,128)(2,1)} %pad_maximum_fusion.rest_0_), channel_id=1, source_target_pairs={{0,6},{1,7},{2,4},{3,5},{4,2},{5,3},{6,0},{7,1},{8,14},{9,15},{10,... | collective-permute-start | bytes 786440 | tf_op jit(solution)/shard_map/ppermute | solution.py:465
  129.7 16.9 %collective-permute-start.23 = (bf16[128,1024]{1,0:T(8,128)(2,1)}, bf16[128,1024]{1,0:T(8,128)(2,1)}, u32[]{:S(2)}, u32[]{:S(2)}) collective-permute-start(bf16[128,1024]{1,0:T(8,128)(2,1)} %pad_maximum_fusion.rest_0_), channel_id=1, source_target_pairs={{0,1},{1,0},{2,3},{3,2},{4,5},{5,4},{6,7},{7,6},{8,9},{9,8},{10,11... | collective-permute-start | bytes 786440 | tf_op jit(solution)/shard_map/ppermute | solution.py:465
  133.7 14.9 %collective-permute-start.20 = (bf16[128,1024]{1,0:T(8,128)(2,1)}, bf16[128,1024]{1,0:T(8,128)(2,1)}, u32[]{:S(2)}, u32[]{:S(2)}) collective-permute-start(bf16[128,1024]{1,0:T(8,128)(2,1)} %collective-permute-done.17.rest_0_), channel_id=1, source_target_pairs={{0,1},{1,0},{2,3},{3,2},{4,5},{5,4},{6,7},{7,6},{8,9},{9,8},{10,11... | collective-permute-start | bytes 786440 | tf_op jit(solution)/shard_map/ppermute | solution.py:465
  136.2 12.4 %collective-permute-start.21 = (bf16[128,1024]{1,0:T(8,128)(2,1)}, bf16[128,1024]{1,0:T(8,128)(2,1)}, u32[]{:S(2)}, u32[]{:S(2)}) collective-permute-start(bf16[128,1024]{1,0:T(8,128)(2,1)} %collective-permute-done.18.rest_1_), channel_id=1, source_target_pairs={{0,1},{1,0},{2,3},{3,2},{4,5},{5,4},{6,7},{7,6},{8,9},{9,8},{10,11... | collective-permute-start | bytes 786440 | tf_op jit(solution)/shard_map/ppermute | solution.py:465
  141.6 7.0 %collective-permute-start.22 = (bf16[128,1024]{1,0:T(8,128)(2,1)}, bf16[128,1024]{1,0:T(8,128)(2,1)}, u32[]{:S(2)}, u32[]{:S(2)}) collective-permute-start(bf16[128,1024]{1,0:T(8,128)(2,1)} %collective-permute-done.19.rest_2_), channel_id=1, source_target_pairs={{0,1},{1,0},{2,3},{3,2},{4,5},{5,4},{6,7},{7,6},{8,9},{9,8},{10,11... | collective-permute-start | bytes 786440 | tf_op jit(solution)/shard_map/ppermute | solution.py:465
